TPU v7x, 32 devices: a whole 2x2x4 slice. The times are simulated.
32 devices in a mesh: rep: 8 (over y, x, core), shard: 4 (over z).
Axes of the slice: x: 2, y: 2, z: 4, core: 2. Of those that a mesh axis runs over, the one named last changes fastest.
Arguments:
- inputs: bfloat16 [8192, 2048], P(('rep', 'shard')), may hold values from -6 to 6
- segments: int32 [8192], P(('rep', 'shard')), may hold values from 0 to 23, as said below
- positions: int32 [8192], P(('rep', 'shard')), may hold values from 0 to 1021, as said below
- ln_gain: float32 [2048], P('shard'), may hold values from 0.5 to 1.5
- ln_bias: float32 [2048], P('shard'), may hold values from -1 to 1
- w_qkv: bfloat16 [2048, 6144], P('shard'), may hold values from -0.125 to 0.125
- b_qkv: float32 [6144], P('shard'), may hold values from -1.5 to 1.5
- w_dense: bfloat16 [2048, 2048], P('shard'), may hold values from -0.75 to 0.75
- b_dense: float32 [2048], P('shard'), may hold values from -1.5 to 1.5
- w_fc1: bfloat16 [2048, 8192], P('shard'), may hold values from -0.125 to 0.125
- b_fc1: float32 [8192], P('shard'), may hold values from -1.5 to 1.5
- w_fc2: bfloat16 [8192, 2048], P('shard'), may hold values from -0.0625 to 0.0625
- b_fc2: float32 [2048], P('shard'), may hold values from -1.5 to 1.5
- cotangent: bfloat16 [8192, 2048], P(('rep', 'shard')), may hold values from -6 to 6
Outputs:
- block_out: float32 [8192, 2048], P(('rep', 'shard'))
- grad_inputs: float32 [8192, 2048], P(('rep', 'shard'))
- grad_ln_gain: float32 [2048], P('shard')
- grad_ln_bias: float32 [2048], P('shard')
- grad_w_qkv: float32 [2048, 6144], P('shard')
- grad_b_qkv: float32 [6144], P('shard')
- grad_w_dense: float32 [2048, 2048], P('shard')
- grad_b_dense: float32 [2048], P('shard')
- grad_w_fc1: float32 [2048, 8192], P('shard')
- grad_b_fc1: float32 [8192], P('shard')
- grad_w_fc2: float32 [8192, 2048], P('shard')
- grad_b_fc2: float32 [2048], P('shard')
Inputs may be any that keep to these rules, and one draw needn't show every extreme that they name: `segments`: document numbers never fall along the tokens; each aligned block of 1024 tokens holds exactly three documents, numbered 3 b, 3 b + 1 and 3 b + 2 in block b. `positions`: A token's offset from the first token of its document.
All inputs are finite; a program needn't handle non-finite values.
Results may differ from a plain program's by a relative error of at most 0.0089.
Values may be sent and summed in bfloat16 or wider, within the bound.
No kernel may reach another device: no remote copies, remote signals or barrier semaphores. Data moves between devices by JAX's collectives and lax.ppermute only.
A program may use at most 640 MiB of HBM per device.

v0:
```python
import jax
import jax.numpy as jnp
from jax import lax
from jax.sharding import PartitionSpec as P

HEAD_DIM = 64
ROT = 32
SEQ = 1024


def from_behind(block, axis, distance):
    devices = range(lax.axis_size(axis))
    route = [(i - distance, i) for i in devices if i - distance in devices]
    return lax.ppermute(block, axis, route)


def rotary(per_head, positions):
    halfway = ROT // 2
    frequency = 10000.0 ** (-(jnp.arange(halfway, dtype=jnp.float32) * 2.0) / ROT)
    angles = positions.astype(jnp.float32)[:, None] * frequency[None, :]
    cosine = jnp.cos(angles)[:, None, :]
    sine_part = jnp.sin(angles)[:, None, :]
    leading = per_head[..., :halfway]
    trailing = per_head[..., halfway:ROT]
    return jnp.concatenate(
        [
            leading * cosine - trailing * sine_part,
            trailing * cosine + leading * sine_part,
            per_head[..., ROT:],
        ],
        axis=-1,
    )


def layer_norm(inputs_wide, norm_gain, norm_shift):
    average = jnp.mean(inputs_wide, axis=-1, keepdims=True)
    centred = inputs_wide - average
    spread = jnp.mean(centred * centred, axis=-1, keepdims=True)
    return centred * lax.rsqrt(spread + 1e-05) * norm_gain + norm_shift


def gelu_tanh(pre_act):
    return jax.nn.gelu(pre_act, approximate=True)


def contract_rows(left_side, right_side):
    return lax.dot_general(
        left_side, right_side, (((0,), (0,)), ((), ())), preferred_element_type=jnp.float32
    )


def times_transpose(left_side, right_side):
    return lax.dot_general(
        left_side, right_side, (((1,), (1,)), ((), ())), preferred_element_type=jnp.float32
    )


def attend_forward(queries, key_heads, value_heads, allowed):
    scaling = queries.shape[-1] ** (-0.5)
    scores = (
        jnp.einsum("hqd,hkd->hqk", queries, key_heads, preferred_element_type=jnp.float32) * scaling
    )
    masked = jnp.where(allowed[None], scores, -1e30)
    row_max = jnp.max(masked, axis=-1, keepdims=True)
    exponent = jnp.exp(masked - row_max)
    row_total = jnp.sum(exponent, axis=-1, keepdims=True)
    attention = (exponent / row_total).astype(jnp.bfloat16)
    attended = jnp.einsum(
        "hqk,hkd->hqd", attention, value_heads, preferred_element_type=jnp.float32
    )
    return (attended, row_max + jnp.log(row_total))


def attend_backward(queries, key_heads, value_heads, allowed, logsum, d_attended):
    scaling = queries.shape[-1] ** (-0.5)
    scores = (
        jnp.einsum("hqd,hkd->hqk", queries, key_heads, preferred_element_type=jnp.float32) * scaling
    )
    softmax = jnp.exp(jnp.where(allowed[None], scores, -1e30) - logsum)
    attention = softmax.astype(jnp.bfloat16)
    d_attention = jnp.einsum(
        "hqd,hkd->hqk", d_attended, value_heads, preferred_element_type=jnp.float32
    )
    d_values = jnp.einsum("hqk,hqd->hkd", attention, d_attended, preferred_element_type=jnp.float32)
    d_scores = (
        softmax * (d_attention - jnp.sum(softmax * d_attention, axis=-1, keepdims=True))
    ).astype(jnp.bfloat16)
    d_queries = (
        jnp.einsum("hqk,hkd->hqd", d_scores, key_heads, preferred_element_type=jnp.float32)
        * scaling
    )
    d_keys = (
        jnp.einsum("hqk,hqd->hkd", d_scores, queries, preferred_element_type=jnp.float32) * scaling
    )
    return (d_queries, d_keys, d_values)


def shards(
    inputs,
    segments,
    positions,
    ln_gain,
    ln_bias,
    w_qkv,
    b_qkv,
    w_dense,
    b_dense,
    w_fc1,
    b_fc1,
    w_fc2,
    b_fc2,
    cotangent,
):
    tokens = inputs.shape[0]
    model_width = w_dense.shape[1]
    head_count = model_width // HEAD_DIM
    group_size = min(8, head_count)
    group_count = head_count // group_size
    span_count = SEQ // tokens
    key_count = span_count * tokens
    gain_full, shift_full, bias_qkv, bias_dense, bias_fc1, bias_fc2 = (
        lax.all_gather(ln_gain, "shard", axis=0, tiled=True),
        lax.all_gather(ln_bias, "shard", axis=0, tiled=True),
        lax.all_gather(b_qkv, "shard", axis=0, tiled=True),
        lax.all_gather(b_dense, "shard", axis=0, tiled=True),
        lax.all_gather(b_fc1, "shard", axis=0, tiled=True),
        lax.all_gather(b_fc2, "shard", axis=0, tiled=True),
    )
    inputs_wide = inputs.astype(jnp.float32)
    normed_low = layer_norm(inputs_wide, gain_full, shift_full).astype(jnp.bfloat16)
    pieces = (
        lax.all_gather(w_qkv, "shard", axis=0, tiled=True),
        lax.all_gather(w_fc1, "shard", axis=0, tiled=True),
    )
    columns = normed_low
    summed = (
        jnp.dot(columns, pieces[0], preferred_element_type=jnp.float32),
        jnp.dot(columns, pieces[1], preferred_element_type=jnp.float32),
    )
    folded = summed
    projected = folded[0] + bias_qkv
    pre_act = folded[1] + bias_fc1
    query_low = (
        rotary(projected[:, :model_width].reshape(tokens, head_count, HEAD_DIM), positions)
        .astype(jnp.bfloat16)
        .transpose(1, 0, 2)
    )
    key_low = (
        rotary(
            projected[:, model_width : 2 * model_width].reshape(tokens, head_count, HEAD_DIM),
            positions,
        )
        .astype(jnp.bfloat16)
        .reshape(tokens, model_width)
    )
    value_low = projected[:, 2 * model_width :].astype(jnp.bfloat16)
    carried = (jnp.concatenate([key_low, value_low], axis=1), segments)
    received = [carried]
    for repeat in range(span_count - 1):
        carried = from_behind((carried[0], carried[1]), ("rep", "shard"), 1)
        received.append(carried)
    received = received[::-1]
    keys_all = jnp.concatenate([member[0] for member in received], axis=0)
    key_segments = jnp.concatenate([member[1] for member in received], axis=0)
    device_index = lax.axis_index(("rep", "shard"))
    query_place = device_index * tokens + jnp.arange(tokens, dtype=jnp.int32)
    key_place = (device_index - (span_count - 1)) * tokens + jnp.arange(key_count, dtype=jnp.int32)
    allowed = (
        (segments[:, None] == key_segments[None, :])
        & (key_place[None, :] <= query_place[:, None])
        & (jnp.floor_divide(key_place, SEQ)[None, :] == jnp.floor_divide(query_place, SEQ)[:, None])
    )
    key_heads = (
        keys_all[:, :model_width].reshape(key_count, head_count, HEAD_DIM).transpose(1, 0, 2)
    )
    value_heads = (
        keys_all[:, model_width:].reshape(key_count, head_count, HEAD_DIM).transpose(1, 0, 2)
    )

    def grouped(array):
        return array.reshape((group_count, group_size) + array.shape[1:])

    attended, logsum = lax.map(
        lambda operands: attend_forward(operands[0], operands[1], operands[2], allowed),
        (grouped(query_low), grouped(key_heads), grouped(value_heads)),
    )
    attended_low = (
        attended.reshape(head_count, tokens, HEAD_DIM)
        .transpose(1, 0, 2)
        .reshape(tokens, model_width)
        .astype(jnp.bfloat16)
    )
    columns = attended_low
    summed = jnp.dot(
        columns,
        lax.all_gather(w_dense, "shard", axis=0, tiled=True),
        preferred_element_type=jnp.float32,
    )
    dense_fold = (summed,)
    activation_low = gelu_tanh(pre_act).astype(jnp.bfloat16)
    columns = activation_low
    summed = jnp.dot(
        columns,
        lax.all_gather(w_fc2, "shard", axis=0, tiled=True),
        preferred_element_type=jnp.float32,
    )
    block_out = inputs_wide + dense_fold[0] + bias_dense + summed + bias_fc2
    cot_wide = cotangent.astype(jnp.float32)

    def place_columns(piece):
        return times_transpose(cotangent, piece)

    d_attended = place_columns(lax.all_gather(w_dense, "shard", axis=0, tiled=True))
    d_activation = place_columns(lax.all_gather(w_fc2, "shard", axis=0, tiled=True))
    d_pre_low = jax.vjp(gelu_tanh, pre_act)[1](d_activation)[0].astype(jnp.bfloat16)
    d_attended_low = (
        d_attended.astype(jnp.bfloat16).reshape(tokens, head_count, HEAD_DIM).transpose(1, 0, 2)
    )
    d_queries, d_keys, d_values = lax.map(
        lambda operands: attend_backward(
            operands[0], operands[1], operands[2], allowed, operands[3], operands[4]
        ),
        (
            grouped(query_low),
            grouped(key_heads),
            grouped(value_heads),
            logsum,
            grouped(d_attended_low),
        ),
    )
    key_grads = jnp.concatenate(
        [
            d_keys.reshape(head_count, key_count, HEAD_DIM)
            .transpose(1, 0, 2)
            .reshape(key_count, model_width),
            d_values.reshape(head_count, key_count, HEAD_DIM)
            .transpose(1, 0, 2)
            .reshape(key_count, model_width),
        ],
        axis=1,
    )
    returned = key_grads[0:tokens]
    for repeat in range(span_count - 1):
        returned = from_behind(returned, ("rep", "shard"), -1)
        returned = returned + key_grads[(repeat + 1) * tokens : (repeat + 2) * tokens]
    rotate_back = jax.vjp(
        lambda per_head: rotary(per_head, positions),
        jnp.zeros((tokens, head_count, HEAD_DIM), jnp.float32),
    )[1]
    d_query_raw = rotate_back(d_queries.reshape(head_count, tokens, HEAD_DIM).transpose(1, 0, 2))[
        0
    ].reshape(tokens, model_width)
    d_key_raw = rotate_back(returned[:, :model_width].reshape(tokens, head_count, HEAD_DIM))[
        0
    ].reshape(tokens, model_width)
    d_projected_low = jnp.concatenate(
        [d_query_raw, d_key_raw, returned[:, model_width:]], axis=1
    ).astype(jnp.bfloat16)
    pieces = (
        lax.all_gather(w_qkv, "shard", axis=0, tiled=True),
        lax.all_gather(w_fc1, "shard", axis=0, tiled=True),
    )
    d_normed = times_transpose(d_projected_low, pieces[0]) + times_transpose(d_pre_low, pieces[1])
    norm_pull = jax.vjp(layer_norm, inputs_wide, gain_full, shift_full)[1]
    d_inputs, d_gain, d_shift = norm_pull(d_normed)
    grad_inputs = cot_wide + d_inputs
    joined = jnp.concatenate([d_projected_low, d_pre_low], axis=1)
    inner_grad = lax.psum_scatter(
        contract_rows(normed_low, joined), "shard", scatter_dimension=0, tiled=True
    )
    dense_grad = lax.psum_scatter(
        contract_rows(attended_low, cotangent), "shard", scatter_dimension=0, tiled=True
    )
    output_grad = lax.psum_scatter(
        contract_rows(activation_low, cotangent), "shard", scatter_dimension=0, tiled=True
    )
    gain_part, shift_part, qkv_bias_part, cot_bias_part, fc1_bias_part = (
        lax.psum_scatter(d_gain, "shard", scatter_dimension=0, tiled=True),
        lax.psum_scatter(d_shift, "shard", scatter_dimension=0, tiled=True),
        lax.psum_scatter(
            jnp.sum(d_projected_low, axis=0, dtype=jnp.float32),
            "shard",
            scatter_dimension=0,
            tiled=True,
        ),
        lax.psum_scatter(jnp.sum(cot_wide, axis=0), "shard", scatter_dimension=0, tiled=True),
        lax.psum_scatter(
            jnp.sum(d_pre_low, axis=0, dtype=jnp.float32), "shard", scatter_dimension=0, tiled=True
        ),
    )
    (
        inner_total,
        dense_total,
        output_total,
        gain_total,
        shift_total,
        qkv_bias_total,
        cot_bias_total,
        fc1_bias_total,
    ) = lax.psum(
        (
            inner_grad,
            dense_grad,
            output_grad,
            gain_part,
            shift_part,
            qkv_bias_part,
            cot_bias_part,
            fc1_bias_part,
        ),
        "rep",
    )
    return (
        block_out,
        grad_inputs,
        gain_total,
        shift_total,
        inner_total[:, : 3 * model_width],
        qkv_bias_total,
        dense_total,
        cot_bias_total,
        inner_total[:, 3 * model_width :],
        fc1_bias_total,
        output_total,
        cot_bias_total,
    )


def solution(mesh):
    return jax.shard_map(
        shards,
        mesh=mesh,
        in_specs=(
            P(("rep", "shard"), None),
            P(("rep", "shard")),
            P(("rep", "shard")),
            P("shard"),
            P("shard"),
            P("shard", None),
            P("shard"),
            P("shard", None),
            P("shard"),
            P("shard", None),
            P("shard"),
            P("shard", None),
            P("shard"),
            P(("rep", "shard"), None),
        ),
        out_specs=(
            P(("rep", "shard"), None),
            P(("rep", "shard"), None),
            P("shard"),
            P("shard"),
            P("shard", None),
            P("shard"),
            P("shard", None),
            P("shard"),
            P("shard", None),
            P("shard"),
            P("shard", None),
            P("shard"),
        ),
        check_vma=False,
    )
```

profile of v0, /device:TPU:0, one launch (start us, length us, event | category | flops | bytes accessed | tf_op | source)
XLA Modules:
  0.0 6058.3 jit_solution(3112275199614578343)
XLA Ops:
  9.6 13.5 all-gather.1
  23.1 12.0 all-gather
  35.1 32.5 all-gather.2
  68.5 369.4 %all-gather.10.cloned.1.call-done = bf16[2048,6144]{1,0:T(8,128)(2,1)} async-done(((bf16[512,6144]{1,0:T(8,128)(2,1)}), bf16[2048,6144]{1,0:T(8,128)(2,1)}) %all-gather.10.cloned.1.call-update) | async-done | bytes 25165840 | tf_op jit(solution)/shard_map/all_gather | solution.py:132
  437.9 13.3 convolution_add_fusion.1
  468.6 90.7 %collective-permute-done.3 = bf16[256,4096]{1,0:T(8,128)(2,1)S(1)} collective-permute-done((bf16[256,4096]{1,0:T(8,128)(2,1)S(1)}, bf16[256,4096]{1,0:T(8,128)(2,1)S(1)}, u32[]{:S(2)}, u32[]{:S(2)}) %collective-permute-start.3) | collective-permute-done | bytes 2097184 | tf_op jit(solution)/shard_map/ppermute | solution.py:14
  560.7 35.3 collective-permute-start.4
  596.0 89.3 %collective-permute-done.4 = bf16[256,4096]{1,0:T(8,128)(2,1)} collective-permute-done((bf16[256,4096]{1,0:T(8,128)(2,1)S(1)}, bf16[256,4096]{1,0:T(8,128)(2,1)}, u32[]{:S(2)}, u32[]{:S(2)}) %collective-permute-start.4) | collective-permute-done | bytes 2097184 | tf_op jit(solution)/shard_map/ppermute | solution.py:14
  685.3 76.4 %collective-permute-start.5 = (bf16[256,4096]{1,0:T(8,128)(2,1)}, bf16[256,4096]{1,0:T(8,128)(2,1)}, u32[]{:S(2)}, u32[]{:S(2)}) collective-permute-start(bf16[256,4096]{1,0:T(8,128)(2,1)} %collective-permute-done.4), channel_id=1, source_target_pairs={{0,1},{1,2},{2,3},{3,4},{4,5},{5,6},{6,7},{7,8},{8,9},{9,10},{10,1... | collective-permute-start | bytes 6291464 | tf_op jit(solution)/shard_map/ppermute | solution.py:14
  765.0 85.7 %collective-permute-done = s32[256]{0:T(256)S(1)} collective-permute-done((s32[256]{0:T(256)S(1)}, s32[256]{0:T(256)S(1)}, u32[]{:S(2)}, u32[]{:S(2)}) %collective-permute-start) | collective-permute-done | bytes 1056 | tf_op jit(solution)/shard_map/ppermute | solution.py:14
  850.7 49.4 collective-permute-start.1
  901.4 4.6 collective-permute-start.2
  909.5 7.6 maximum_maximum_fusion
  920.8 6.4 copy.49
  927.2 6.4 copy.50
  933.6 36.2 while.30
  969.8 10.1 fusion.102
  980.6 63.6 %all_gather.41 = f32[8192]{0:T(1024)S(1)} all-gather(f32[2048]{0:T(1024)S(1)} %copy-done.30), channel_id=1, replica_groups=mesh['rep'=8,'shard'=4] {'shard'}, dimensions={0}, use_global_device_ids=true | all-gather | bytes 40960 | tf_op jit(solution)/shard_map/all_gather | solution.py:126
  1044.2 90.2 %all-gather.16.cloned.1.call-done = bf16[8192,2048]{1,0:T(8,128)(2,1)} async-done(((bf16[2048,2048]{1,0:T(8,128)(2,1)}), bf16[8192,2048]{1,0:T(8,128)(2,1)}) %all-gather.16.cloned.1.call-update) | async-done | bytes 33554448 | tf_op jit(solution)/shard_map/all_gather | solution.py:204
  1134.4 21.8 fusion.100
  1156.2 539.1 %all-gather.14.cloned.1.call-done = bf16[2048,8192]{1,0:T(8,128)(2,1)} async-done(((bf16[512,8192]{1,0:T(8,128)(2,1)}), bf16[2048,8192]{1,0:T(8,128)(2,1)}) %all-gather.14.cloned.1.call-update) | async-done | bytes 33554448 | tf_op jit(solution)/shard_map/all_gather | solution.py:133
  1695.3 25.8 convert_reduce_fusion
  1721.1 27.6 fusion.95
  1749.0 95.6 %all-gather.12.cloned.1.call-done = bf16[2048,2048]{1,0:T(8,128)(2,1)} async-done(((bf16[512,2048]{1,0:T(8,128)(2,1)}), bf16[2048,2048]{1,0:T(8,128)(2,1)}) %all-gather.12.cloned.1.call-update) | async-done | bytes 8388624 | tf_op jit(solution)/shard_map/all_gather | solution.py:196
  1844.6 6.7 convolution_convert_fusion
  1853.0 75.6 %while.31 = (s32[]{:T(128)}, f32[4,8,256,64]{2,3,1,0:T(8,128)}, f32[4,8,1024,64]{2,3,1,0:T(8,128)}, f32[4,8,1024,64]{2,3,1,0:T(8,128)}, bf16[4,8,256,64]{2,3,1,0...) while((s32[]{:T(128)}, f32[4,8,256,64]{2,3,1,0:T(8,128)}, ...), condition=%wide.region_8.9_spmd.clone.clone, body=%wide.region_6.8_spmd.clone.sunk.clone | while | flops 1375598592 | bytes 72954008 | solution.py:219
  1855.9 4.5 multiply_reduce_fusion.3
  1874.8 4.5 multiply_reduce_fusion.3
  1912.5 4.5 multiply_reduce_fusion.3
  1928.6 9.1 copy.52
  1937.7 9.1 copy.53
  1951.3 231.2 %collective-permute-done.6 = f32[256,4096]{1,0:T(8,128)S(1)} collective-permute-done((f32[256,4096]{1,0:T(8,128)S(1)}, f32[256,4096]{1,0:T(8,128)S(1)}, u32[]{:S(2)}, u32[]{:S(2)}) %collective-permute-start.6) | collective-permute-done | bytes 4194336 | tf_op jit(solution)/shard_map/ppermute | solution.py:14
  2184.5 175.5 %collective-permute-done.7 = f32[256,4096]{1,0:T(8,128)} collective-permute-done((f32[256,4096]{1,0:T(8,128)S(1)}, f32[256,4096]{1,0:T(8,128)}, u32[]{:S(2)}, u32[]{:S(2)}) %collective-permute-start.7) | collective-permute-done | bytes 4194336 | tf_op jit(solution)/shard_map/ppermute | solution.py:14
  2365.7 243.5 %collective-permute-done.8 = f32[256,4096]{1,0:T(8,128)S(1)} collective-permute-done((f32[256,4096]{1,0:T(8,128)S(1)}, f32[256,4096]{1,0:T(8,128)S(1)}, u32[]{:S(2)}, u32[]{:S(2)}) %collective-permute-start.8) | collective-permute-done | bytes 4194336 | tf_op jit(solution)/shard_map/ppermute | solution.py:14
  2626.2 43.2 fusion.58
  2669.8 17.1 fusion.101
  2686.9 14.0 fusion.96
  2708.4 771.8 %reduce-scatter.10.cloned.1.call-done = f32[2048,2048]{1,0:T(8,128)} async-done(((f32[8192,2048]{1,0:T(8,128)}), f32[2048,2048]{1,0:T(8,128)}) %reduce-scatter.10.cloned.1.call-update) | async-done | bytes 16777232
  3480.3 1907.0 %reduce-scatter.6.cloned.1.call-done = f32[512,14336]{1,0:T(8,128)} async-done(((f32[2048,14336]{1,0:T(8,128)}), f32[512,14336]{1,0:T(8,128)}) %reduce-scatter.6.cloned.1.call-update) | async-done | bytes 29360144 | tf_op jit(solution)/shard_map/reduce_scatter | solution.py:268
  5390.5 14.1 all-gather.3
  5404.5 12.2 all-gather.4
  5416.7 7.1 fusion.77
  5423.8 20.0 fusion.76
  5447.5 24.7 all-reduce.12
  5472.2 542.0 %all-reduce.18.cloned.1.call-done = (f32[512,14336]{1,0:T(8,128)}, f32[512,2048]{1,0:T(8,128)}, f32[2048,2048]{1,0:T(8,128)}) async-done(((f32[512,14336]{1,0:T(8,128)}, f32[512,2048]{1,0:T(8,128)}, f32[2048,2048]{1,0:T(8,128)}), (f32[512,14336]{1,0:T(8,128)}, f32[512,2048]{1,0:T(8,128)}, f32[2048,2048]{1,0:T(8,128)})) %all-reduce.18.cloned.1.call-update) | async-done | bytes 50331664 | tf_op jit(solution)/shard_map/psum | solution.py:300
  6014.2 10.8 slice.99
  6025.1 11.8 slice.100
  6039.5 11.8 copy.102
  (215 shorter events, 178.3 us)
Async XLA Ops:
  7.2 430.7 %all-gather.10.cloned.1.call-start = ((), (), s32[]{:S(2)}) async-start(), calls=%async_computation.3 | async-start | bytes 31457280 | tf_op jit(solution)/shard_map/all_gather | solution.py:132
  7.9 1126.4 %all-gather.16.cloned.1.call-start = ((), (), s32[]{:S(2)}) async-start(), calls=%async_computation.6 | async-start | bytes 41943040 | tf_op jit(solution)/shard_map/all_gather | solution.py:204
  8.7 14.4 copy-start.33
  8.7 58.9 copy-start.2
  8.7 1686.6 %all-gather.14.cloned.1.call-start = ((), (), s32[]{:S(2)}) async-start(), calls=%async_computation.5 | async-start | bytes 41943040 | tf_op jit(solution)/shard_map/all_gather | solution.py:133
  9.4 1835.1 %all-gather.12.cloned.1.call-start = ((), (), s32[]{:S(2)}) async-start(), calls=%async_computation.4 | async-start | bytes 10485760 | tf_op jit(solution)/shard_map/all_gather | solution.py:196
  23.1 1672.2 %copy-start.17 = (f32[4,1,512]{2,1,0:T(1,128)}, f32[4,1,512]{2,1,0:T(1,128)S(1)}, u32[]{:S(2)}) copy-start(f32[4,1,512]{2,1,0:T(1,128)S(1)} %all-gather.1) | copy-start | bytes 24580
  35.1 1660.2 %copy-start.15 = (f32[4,1,512]{2,1,0:T(1,128)}, f32[4,1,512]{2,1,0:T(1,128)S(1)}, u32[]{:S(2)}) copy-start(f32[4,1,512]{2,1,0:T(1,128)S(1)} %all-gather) | copy-start | bytes 24580
  67.8 1627.5 %copy-start.19 = (f32[256]{0:T(256)}, f32[256]{0:T(256)S(1)}, u32[]{:S(2)}) copy-start(f32[256]{0:T(256)S(1)} %broadcast_multiply_fusion) | copy-start | bytes 3076
  68.3 383.0 %copy-start.28 = (f32[256]{0:T(256)}, f32[256]{0:T(256)S(1)}, u32[]{:S(2)}) copy-start(f32[256]{0:T(256)S(1)} %fusion.83) | copy-start | bytes 3076
  68.3 1627.0 %copy-start.21 = (f32[256]{0:T(256)}, f32[256]{0:T(256)S(1)}, u32[]{:S(2)}) copy-start(f32[256]{0:T(256)S(1)} %fusion.88) | copy-start | bytes 3076
  68.4 393.2 %copy-start.23 = (f32[256,16]{0,1:T(8,128)}, f32[256,16]{0,1:T(8,128)S(1)}, u32[]{:S(2)}) copy-start(f32[256,16]{0,1:T(8,128)S(1)} %get-tuple-element.274) | copy-start | bytes 49156
  68.4 393.2 %copy-start.25 = (f32[256,16]{0,1:T(8,128)}, f32[256,16]{0,1:T(8,128)S(1)}, u32[]{:S(2)}) copy-start(f32[256,16]{0,1:T(8,128)S(1)} %get-tuple-element.275) | copy-start | bytes 49156
  451.4 15.6 copy-start.9
  460.2 301.5 %copy-start.27 = (s32[256]{0:T(256)S(1)}, s32[256]{0:T(256)}, u32[]{:S(2)}) copy-start(s32[256]{0:T(256)} %param.19) | copy-start | bytes 3076
  467.0 297.8 %copy-start.10 = (bf16[256,2048]{1,0:T(8,128)(2,1)}, bf16[256,2048]{1,0:T(8,128)(2,1)S(1)}, u32[]{:S(2)}) copy-start(bf16[256,2048]{1,0:T(8,128)(2,1)S(1)} %copy.48) | copy-start | bytes 3145732
  467.2 92.2 %collective-permute-start.3 = (bf16[256,4096]{1,0:T(8,128)(2,1)S(1)}, bf16[256,4096]{1,0:T(8,128)(2,1)S(1)}, u32[]{:S(2)}, u32[]{:S(2)}) collective-permute-start(bf16[256,4096]{1,0:T(8,128)(2,1)S(1)} %pad_maximum_fusion.2), channel_id=1, source_target_pairs={{0,1},{1,2},{2,3},{3,4},{4,5},{5,6},{6,7},{7,8},{8,9},{9,10},{10,1... | collective-permute-start | bytes 6291464 | tf_op jit(solution)/shard_map/ppermute | solution.py:14
  560.7 124.6 %collective-permute-start.4 = (bf16[256,4096]{1,0:T(8,128)(2,1)S(1)}, bf16[256,4096]{1,0:T(8,128)(2,1)}, u32[]{:S(2)}, u32[]{:S(2)}) collective-permute-start(bf16[256,4096]{1,0:T(8,128)(2,1)S(1)} %collective-permute-done.3), channel_id=1, source_target_pairs={{0,1},{1,2},{2,3},{3,4},{4,5},{5,6},{6,7},{7,8},{8,9},{9,10},{10,1... | collective-permute-start | bytes 6291464 | tf_op jit(solution)/shard_map/ppermute | solution.py:14
  685.3 224.2 %collective-permute-start.5 = (bf16[256,4096]{1,0:T(8,128)(2,1)}, bf16[256,4096]{1,0:T(8,128)(2,1)}, u32[]{:S(2)}, u32[]{:S(2)}) collective-permute-start(bf16[256,4096]{1,0:T(8,128)(2,1)} %collective-permute-done.4), channel_id=1, source_target_pairs={{0,1},{1,2},{2,3},{3,4},{4,5},{5,6},{6,7},{7,8},{8,9},{9,10},{10,1... | collective-permute-start | bytes 6291464 | tf_op jit(solution)/shard_map/ppermute | solution.py:14
  761.6 89.1 %collective-permute-start = (s32[256]{0:T(256)S(1)}, s32[256]{0:T(256)S(1)}, u32[]{:S(2)}, u32[]{:S(2)}) collective-permute-start(s32[256]{0:T(256)S(1)} %copy-done.27), channel_id=1, source_target_pairs={{0,1},{1,2},{2,3},{3,4},{4,5},{5,6},{6,7},{7,8},{8,9},{9,10},{10,1... | collective-permute-start | bytes 3080 | tf_op jit(solution)/shard_map/ppermute | solution.py:14
  764.8 1943.6 %reduce-scatter.8.cloned.1.call-start = ((), (), s32[]{:S(2)}) async-start(), calls=%async_computation.8 | async-start | bytes 20971520 | tf_op jit(solution)/shard_map/reduce_scatter | solution.py:271
  850.7 50.7 collective-permute-start.1
  901.4 5.7 collective-permute-start.2
  969.8 10.1 copy-start.4
  979.9 154.4 %copy-start.7 = (bf16[256,2048]{1,0:T(8,128)(2,1)S(1)}, bf16[256,2048]{1,0:T(8,128)(2,1)}, u32[]{:S(2)}) copy-start(bf16[256,2048]{1,0:T(8,128)(2,1)} %param.31) | copy-start | bytes 3145732
  979.9 2500.3 %reduce-scatter.10.cloned.1.call-start = ((), (), s32[]{:S(2)}) async-start(), calls=%async_computation.9 | async-start | bytes 83886080
  1748.7 3638.6 %reduce-scatter.6.cloned.1.call-start = ((), (), s32[]{:S(2)}) async-start(), calls=%async_computation.7 | async-start | bytes 146800640 | tf_op jit(solution)/shard_map/reduce_scatter | solution.py:268
  1946.8 235.6 %copy-start = (f32[1024,2048]{1,0:T(8,128)S(1)}, f32[1024,2048]{1,0:T(8,128)}, u32[]{:S(2)}) copy-start(f32[1024,2048]{1,0:T(8,128)} %copy.52) | copy-start | bytes 25165828
  1946.8 235.6 %copy-start.1 = (f32[1024,2048]{1,0:T(8,128)S(1)}, f32[1024,2048]{1,0:T(8,128)}, u32[]{:S(2)}) copy-start(f32[1024,2048]{1,0:T(8,128)} %copy.53) | copy-start | bytes 25165828
  1949.7 232.7 %collective-permute-start.6 = (f32[256,4096]{1,0:T(8,128)S(1)}, f32[256,4096]{1,0:T(8,128)S(1)}, u32[]{:S(2)}, u32[]{:S(2)}) collective-permute-start(f32[256,4096]{1,0:T(8,128)S(1)} %fusion.68), channel_id=1, source_target_pairs={{1,0},{2,1},{3,2},{4,3},{5,4},{6,5},{7,6},{8,7},{9,8},{10,9},{11,1... | collective-permute-start | bytes 12582920 | tf_op jit(solution)/shard_map/ppermute | solution.py:14
  2183.1 181.5 %copy-start.13 = (f32[4,8,256,64]{2,3,1,0:T(8,128)S(1)}, f32[4,8,256,64]{2,3,1,0:T(8,128)}, u32[]{:S(2)}) copy-start(f32[4,8,256,64]{2,3,1,0:T(8,128)} %get-tuple-element.106) | copy-start | bytes 6291460
  2183.1 176.9 %collective-permute-start.7 = (f32[256,4096]{1,0:T(8,128)S(1)}, f32[256,4096]{1,0:T(8,128)}, u32[]{:S(2)}, u32[]{:S(2)}) collective-permute-start(f32[256,4096]{1,0:T(8,128)S(1)} %fusion.70), channel_id=1, source_target_pairs={{1,0},{2,1},{3,2},{4,3},{5,4},{6,5},{7,6},{8,7},{9,8},{10,9},{11,1... | collective-permute-start | bytes 12582920 | tf_op jit(solution)/shard_map/ppermute | solution.py:14
  2363.1 246.1 %collective-permute-start.8 = (f32[256,4096]{1,0:T(8,128)S(1)}, f32[256,4096]{1,0:T(8,128)S(1)}, u32[]{:S(2)}, u32[]{:S(2)}) collective-permute-start(f32[256,4096]{1,0:T(8,128)S(1)} %fusion.67), channel_id=1, source_target_pairs={{1,0},{2,1},{3,2},{4,3},{5,4},{6,5},{7,6},{8,7},{9,8},{10,9},{11,1... | collective-permute-start | bytes 12582920 | tf_op jit(solution)/shard_map/ppermute | solution.py:14
  2609.9 5.9 copy-start.24
  2609.9 5.9 copy-start.26
  2618.6 7.6 copy-start.3
  2618.6 7.6 copy-start.16
  2618.6 7.6 copy-start.18
  2618.6 7.6 copy-start.20
  2618.6 7.6 copy-start.22
  2669.5 2774.3 %all-reduce.20.cloned.1.call-start = ((), (), s32[]{:S(2)}) async-start(), calls=%async_computation.11 | async-start | bytes 163840
  2669.8 17.1 copy-start.6
  2686.9 14.0 copy-start.29
  2708.4 3305.9 %all-reduce.18.cloned.1.call-start = ((), (), s32[]{:S(2)}) async-start(), calls=%async_computation.10 | async-start | bytes 100663296 | tf_op jit(solution)/shard_map/psum | solution.py:300
  5387.3 17.3 copy-start.35
  5387.3 29.4 copy-start.5
  5472.2 564.6 %copy-start.36 = (f32[512]{0:T(512)}, f32[512]{0:T(512)S(1)}, u32[]{:S(2)}) copy-start(f32[512]{0:T(512)S(1)} %get-tuple-element.628) | copy-start | bytes 6148
  6025.1 12.4 copy-start.12
  (9 other events, 17.3 us)
Sparse Core Ops, SparseCore 0:
  9.6 428.2 all-gather.9
  439.4 694.8 all-gather.15
  1135.9 559.2 all-gather.13
  1696.7 147.8 all-gather.11
  1847.3 412.8 reduce-scatter.7
  2262.6 1217.6 reduce-scatter.9
  3482.6 1904.6 reduce-scatter.5
  5391.4 36.6 all-reduce.19
  5432.3 581.8 all-reduce.17
where the time goes:
time: 6070 us; the launch traced here: 6060 us
  waiting for transfers between devices  5240 us (86%)
  matrix products  298 us (5%)
  starting transfers between devices  175 us (3%)
  blocking collectives  173 us (3%)
  local copies, waits for them, and re-layouts  104 us (2%)
    reduce_scatter x1, waiting for transfers between devices, shards(): lax.psum_scatter(contract_rows(normed_low, joined), 'shard', scatter_dime...  1910 us
    ppermute x9, waiting for transfers between devices, from_behind(): return lax.ppermute(block, axis, route)  918 us
    unnamed x11, waiting for transfers between devices  774 us
    psum x1, waiting for transfers between devices, shards(): lax.psum((inner_grad, dense_grad, output_grad, gain_part, shift_part, qkv...  542 us
    all_gather x1, waiting for transfers between devices, shards(): lax.all_gather(w_fc1, 'shard', axis=0, tiled=True)  539 us
    all_gather x1, waiting for transfers between devices, shards(): lax.all_gather(w_qkv, 'shard', axis=0, tiled=True)  369 us
    ppermute x9, starting transfers between devices, from_behind(): return lax.ppermute(block, axis, route)  175 us
  transfers between devices with their start and end apart: 18, of which 15 were waited for; matrix products, arithmetic and copies ran while one was open for 7% of the time, Pallas kernels for 0%

commit v1 on v0

v1 whole, which is shorter than its diff:
```python
import functools

import jax
import jax.numpy as jnp
from jax import lax
from jax.experimental import pallas as pl
from jax.experimental.pallas import tpu as pltpu
from jax.sharding import PartitionSpec as P

HEAD_DIM = 64
ROT = 32
SEQ = 1024
PAIR = 2 * HEAD_DIM
BF = jnp.bfloat16
F32 = jnp.float32


def ring(array, axis, distance):
    size = lax.axis_size(axis)
    return lax.ppermute(array, axis, [(i, (i + distance) % size) for i in range(size)])


def swap(array, axis, bit):
    size = lax.axis_size(axis)
    return lax.ppermute(array, axis, [(i, i ^ bit) for i in range(size)])


def contract_rows(left_side, right_side):
    return lax.dot_general(
        left_side, right_side, (((0,), (0,)), ((), ())), preferred_element_type=F32
    )


def times_transpose(left_side, right_side):
    return lax.dot_general(
        left_side, right_side, (((1,), (1,)), ((), ())), preferred_element_type=F32
    )


def times(left_side, right_side):
    return jnp.dot(left_side, right_side, preferred_element_type=F32)


def gelu_tanh(pre_act):
    return jax.nn.gelu(pre_act, approximate=True)


def ring_gather(block, place):
    size = lax.axis_size("shard")
    whole = jnp.zeros((size,) + block.shape, block.dtype)
    held = block
    for hop in range(size):
        whole = lax.dynamic_update_index_in_dim(whole, held, (place - hop) % size, 0)
        if hop < size - 1:
            held = ring(held, "shard", 1)
    return whole.reshape((size * block.shape[0],) + block.shape[1:])


def exchange(pick, place):
    size = lax.axis_size("shard")
    own = pick(place)
    whole = jnp.zeros((size,) + own.shape, own.dtype)
    whole = lax.dynamic_update_index_in_dim(whole, own, place, 0)
    for hop in range(1, size):
        came = ring(pick((place + hop) % size), "shard", hop)
        whole = lax.dynamic_update_index_in_dim(whole, came, (place - hop) % size, 0)
    return whole


def scatter_sum(pick, place):
    size = lax.axis_size("shard")
    total = pick(place).astype(F32)
    for hop in range(1, size):
        total = total + ring(pick((place + hop) % size), "shard", hop).astype(F32)
    return total


def rep_sum(values):
    bit = 1
    while bit < lax.axis_size("rep"):
        values = values + swap(values, "rep", bit)
        bit *= 2
    return values


def attention_kernel(
    block,
    proj_ref,
    bias_ref,
    turn_ref,
    datt_ref,
    start_ref,
    att_ref,
    dproj_ref,
    bsum_ref,
    dq_ref,
    dk_ref,
    dv_ref,
):
    rows = proj_ref.shape[0]
    scaling = HEAD_DIM ** (-0.5)
    cosine = turn_ref[0]
    minus = turn_ref[1]
    plus = turn_ref[2]

    def turned(u):
        return (
            u * cosine
            + pltpu.roll(u, PAIR - ROT // 2, 1) * minus
            + pltpu.roll(u, ROT // 2, 1) * plus
        )

    def turned_back(u):
        return (
            u * cosine
            - pltpu.roll(u, PAIR - ROT // 2, 1) * minus
            - pltpu.roll(u, ROT // 2, 1) * plus
        )

    query = turned(proj_ref[:, :PAIR] + bias_ref[:, :PAIR]).astype(BF) * scaling
    query = query.astype(BF)
    key = turned(proj_ref[:, PAIR : 2 * PAIR] + bias_ref[:, PAIR : 2 * PAIR]).astype(BF)
    value = (proj_ref[:, 2 * PAIR :] + bias_ref[:, 2 * PAIR :]).astype(BF)
    d_att = datt_ref[...]
    start = start_ref[0]
    dk_ref[...] = jnp.zeros_like(dk_ref)
    dv_ref[...] = jnp.zeros_like(dv_ref)
    for head in range(2):
        lanes = slice(head * HEAD_DIM, (head + 1) * HEAD_DIM)
        key_h, value_h = key[:, lanes], value[:, lanes]
        key_t, value_t = key_h.T, value_h.T
        for part in range(rows // block):
            own = slice(part * block, (part + 1) * block)
            length = (part + 1) * block
            query_p = query[own, lanes]
            d_att_p = d_att[own, lanes]
            scores = times_transpose(key_h[:length], query_p)
            place = lax.broadcasted_iota(jnp.int32, (length, block), 0)
            asker = lax.broadcasted_iota(jnp.int32, (length, block), 1) + part * block
            allowed = (place >= start[:, own]) & (place <= asker)
            scores = jnp.where(allowed, scores, -1e30)
            exponent = jnp.exp(scores - jnp.max(scores, axis=0, keepdims=True))
            softmax = exponent * (1.0 / jnp.sum(exponent, axis=0, keepdims=True))
            attention = softmax.astype(BF)
            att_ref[own, lanes] = times(value_t[:, :length], attention).T.astype(BF)
            d_attention = times_transpose(value_h[:length], d_att_p)
            dv_ref[:length, lanes] += times(attention, d_att_p)
            weighted = softmax * d_attention
            d_scores = (
                weighted - softmax * jnp.sum(weighted, axis=0, keepdims=True)
            ).astype(BF)
            dq_ref[own, lanes] = times(key_t[:, :length], d_scores).T * scaling
            dk_ref[:length, lanes] += times(d_scores, query_p)
    d_query = turned_back(dq_ref[...]).astype(BF)
    d_key = turned_back(dk_ref[...]).astype(BF)
    d_value = dv_ref[...].astype(BF)
    for at, piece in enumerate((d_query, d_key, d_value)):
        lanes = slice(at * PAIR, (at + 1) * PAIR)
        dproj_ref[:, lanes] = piece
        bsum_ref[0, :, lanes] = jnp.sum(piece.astype(F32), axis=0, keepdims=True)


def attention(projected, bias, turns, d_attended, start):
    tokens, width = projected.shape
    pairs, seqs = width // (3 * PAIR), tokens // SEQ
    block = min(256, SEQ)
    return pl.pallas_call(
        functools.partial(attention_kernel, block),
        grid=(seqs, pairs),
        in_specs=[
            pl.BlockSpec((SEQ, 3 * PAIR), lambda s, p: (s, p)),
            pl.BlockSpec((1, 3 * PAIR), lambda s, p: (0, p)),
            pl.BlockSpec((3, SEQ, PAIR), lambda s, p: (0, s, 0)),
            pl.BlockSpec((SEQ, PAIR), lambda s, p: (s, p)),
            pl.BlockSpec((1, 1, SEQ), lambda s, p: (s, 0, 0)),
        ],
        out_specs=[
            pl.BlockSpec((SEQ, PAIR), lambda s, p: (s, p)),
            pl.BlockSpec((SEQ, 3 * PAIR), lambda s, p: (s, p)),
            pl.BlockSpec((1, 1, 3 * PAIR), lambda s, p: (s, 0, p)),
        ],
        out_shape=[
            jax.ShapeDtypeStruct((tokens, pairs * PAIR), BF),
            jax.ShapeDtypeStruct((tokens, width), BF),
            jax.ShapeDtypeStruct((seqs, 1, width), F32),
        ],
        scratch_shapes=[pltpu.VMEM((SEQ, PAIR), F32)] * 3,
        compiler_params=pltpu.CompilerParams(vmem_limit_bytes=48 * 2**20),
        name="attention",
    )(projected, bias, turns, d_attended, start)


def shards(
    inputs,
    segments,
    positions,
    ln_gain,
    ln_bias,
    w_qkv,
    b_qkv,
    w_dense,
    b_dense,
    w_fc1,
    b_fc1,
    w_fc2,
    b_fc2,
    cotangent,
):
    reps, group = lax.axis_size("rep"), lax.axis_size("shard")
    rep, place = lax.axis_index("rep"), lax.axis_index("shard")
    tokens, width = inputs.shape
    rows = width // group
    slab = rows // reps
    hidden = w_fc1.shape[1] // group
    heads_width = width // group
    pairs = heads_width // PAIR

    slab_fc1 = lax.dynamic_slice_in_dim(w_fc1, rep * slab, slab, 0)
    slab_qkv = lax.dynamic_slice_in_dim(w_qkv, rep * slab, slab, 0)

    def fc1_for(owner):
        return lax.dynamic_slice_in_dim(slab_fc1, owner * hidden, hidden, 1)

    def qkv_for(owner):
        split = slab_qkv.reshape(slab, 3, group, pairs, PAIR)
        return (
            lax.dynamic_index_in_dim(split, owner, 2, keepdims=False)
            .transpose(0, 2, 1, 3)
            .reshape(slab, 3 * heads_width)
        )

    fc1_cols = lax.all_gather(
        exchange(fc1_for, place).reshape(group * slab, hidden), "rep", axis=0, tiled=True
    )
    qkv_cols = lax.all_gather(
        exchange(qkv_for, place).reshape(group * slab, 3 * heads_width), "rep", axis=0, tiled=True
    )

    small = jnp.concatenate([ln_gain, ln_bias, b_qkv, b_dense + b_fc2])
    small = lax.all_gather(small, "shard", axis=0)
    all_positions = lax.all_gather(positions, "shard", axis=0, tiled=True)
    gain = small[:, :rows].reshape(width)
    shift = small[:, rows : 2 * rows].reshape(width)
    bias_qkv = (
        lax.dynamic_index_in_dim(
            small[:, 2 * rows : 5 * rows].reshape(3, group, pairs, PAIR), place, 1, keepdims=False
        )
        .transpose(1, 0, 2)
        .reshape(1, 3 * heads_width)
    )
    bias_out = small[:, 5 * rows :].reshape(width)

    inputs_wide = inputs.astype(F32)
    average = jnp.mean(inputs_wide, axis=-1, keepdims=True)
    centred = inputs_wide - average
    spread = jnp.mean(centred * centred, axis=-1, keepdims=True)
    inverse = lax.rsqrt(spread + 1e-05)
    normed = (centred * inverse * gain + shift).astype(BF)
    normed = normed.reshape(tokens, group, reps, slab).transpose(0, 2, 1, 3).reshape(tokens, width)
    normed_all = ring_gather(normed, place)
    cot_all = ring_gather(cotangent, place)

    frequency = 10000.0 ** (-(jnp.arange(ROT // 2, dtype=F32) * 2.0) / ROT)
    angles = all_positions.astype(F32)[:, None] * frequency[None, :]
    cosine, sine = jnp.cos(angles), jnp.sin(angles)
    none = jnp.zeros_like(sine)
    still = jnp.zeros((sine.shape[0], HEAD_DIM - ROT), F32)
    turns = jnp.stack(
        [
            jnp.concatenate([cosine, cosine, still + 1.0] * 2, axis=1),
            jnp.concatenate([-sine, none, still] * 2, axis=1),
            jnp.concatenate([none, sine, still] * 2, axis=1),
        ]
    )
    start = jnp.arange(SEQ, dtype=jnp.int32)[None, None] - all_positions.reshape(-1, 1, SEQ)

    pre_act = times(normed_all, fc1_cols) + b_fc1
    activation = gelu_tanh(pre_act).astype(BF)
    d_activation = times_transpose(cot_all, w_fc2)
    d_pre = jax.vjp(gelu_tanh, pre_act)[1](d_activation)[0].astype(BF)
    grad_fc2 = contract_rows(activation, cot_all).astype(BF)
    grad_fc1 = contract_rows(normed_all, d_pre).astype(BF)

    projected = times(normed_all, qkv_cols)
    d_attended = times_transpose(cot_all, w_dense).astype(BF)
    attended, d_projected, d_bias_qkv = attention(projected, bias_qkv, turns, d_attended, start)
    grad_qkv = contract_rows(normed_all, d_projected).astype(BF)
    grad_dense = contract_rows(attended, cot_all).astype(BF)

    out_part = (times(attended, w_dense) + times(activation, w_fc2)).astype(BF)
    d_normed_part = (
        times_transpose(d_projected, qkv_cols) + times_transpose(d_pre, fc1_cols)
    ).astype(BF)

    def rows_of(array):
        return lambda owner: lax.dynamic_slice_in_dim(array, owner * tokens, tokens, 0)

    block_out = inputs_wide + scatter_sum(rows_of(out_part), place) + bias_out
    d_normed = scatter_sum(rows_of(d_normed_part), place)
    d_normed = (
        d_normed.reshape(tokens, reps, group, slab).transpose(0, 2, 1, 3).reshape(tokens, width)
    )
    xhat = centred * inverse
    d_gain = jnp.sum(d_normed * xhat, axis=0)
    d_shift = jnp.sum(d_normed, axis=0)
    scaled = d_normed * gain
    grad_inputs = cotangent.astype(F32) + inverse * (
        scaled
        - jnp.mean(scaled, axis=-1, keepdims=True)
        - xhat * jnp.mean(scaled * xhat, axis=-1, keepdims=True)
    )

    def reduced(array):
        return lax.psum_scatter(array, "rep", scatter_dimension=0, tiled=True)

    def spread_out(array):
        return lax.all_gather(array, "rep", axis=0, tiled=True).astype(F32)

    def slab_of(array):
        return lambda owner: lax.dynamic_slice_in_dim(array, owner * slab, slab, 0)

    fc2_total = spread_out(reduced(grad_fc2))
    fc1_slab = exchange(slab_of(reduced(grad_fc1)), place)
    fc1_total = spread_out(fc1_slab.transpose(1, 0, 2).reshape(slab, group * hidden))
    dense_total = spread_out(reduced(grad_dense))
    qkv_slab = exchange(slab_of(reduced(grad_qkv)), place)
    qkv_total = spread_out(
        qkv_slab.reshape(group, slab, pairs, 3, PAIR)
        .transpose(1, 3, 0, 2, 4)
        .reshape(slab, 3 * width)
    )

    d_bias_qkv = jnp.sum(d_bias_qkv[:, 0], axis=0).reshape(pairs, 3, PAIR).transpose(1, 0, 2)
    d_bias_all = jnp.zeros((3, group, pairs, PAIR), F32)
    d_bias_all = lax.dynamic_update_index_in_dim(d_bias_all, d_bias_qkv, place, 1)
    early = jnp.concatenate(
        [
            d_bias_all.reshape(group, 3 * rows),
            jnp.sum(cotangent.astype(F32), axis=0).reshape(group, rows),
        ],
        axis=1,
    )
    pick = lambda array: lambda owner: lax.dynamic_index_in_dim(array, owner, 0, keepdims=False)
    early = scatter_sum(pick(early), place)
    early = rep_sum(jnp.concatenate([early, jnp.sum(d_pre.astype(F32), axis=0)]))
    late = jnp.concatenate([d_gain.reshape(group, rows), d_shift.reshape(group, rows)], axis=1)
    late = rep_sum(scatter_sum(pick(late), place))
    cot_total = early[3 * rows : 4 * rows]
    return (
        block_out,
        grad_inputs,
        late[:rows],
        late[rows:],
        qkv_total,
        early[: 3 * rows],
        dense_total,
        cot_total,
        fc1_total,
        early[4 * rows :],
        fc2_total,
        cot_total,
    )


def solution(mesh):
    both, shard = P(("rep", "shard")), P("shard")
    wide, held = P(("rep", "shard"), None), P("shard", None)
    return jax.shard_map(
        shards,
        mesh=mesh,
        in_specs=(
            wide, both, both, shard, shard, held, shard, held, shard, held, shard, held, shard, wide
        ),
        out_specs=(
            wide, wide, shard, shard, held, shard, held, shard, held, shard, held, shard
        ),
        check_vma=False,
    )
```

time: 6070 us -> 875 us (0.14)
  waiting for transfers between devices: 5240 us -> 364 us
  matrix products: 298 us -> 127 us
  blocking collectives: 173 us -> 62.4 us
  starting transfers between devices: 175 us -> 93.1 us
    reduce_scatter x2 -> x4, waiting for transfers between devices: 1910 us -> 155 us  [reduced(): return lax.psum_scatter(array, 'rep', scatter_dimension=0, tiled=True)]
    all_gather x4 -> x6, waiting for transfers between devices: 1090 us -> 0.05 us  [the longest x1 0.02 us: shards(): lax.all_gather(exchange(qkv_for, place).reshape(group * slab, 3 * heads_w...]
    unnamed x11 -> x10, waiting for transfers between devices: 774 us -> 0.82 us
    ppermute x9 -> x36, waiting for transfers between devices: 918 us -> 208 us  [the longest x30 200 us: ring(): lax.ppermute(array, axis, [(i, (i + distance) % size) for i in range(size)])]
    psum x1 -> x0, waiting for transfers between devices: 542 us -> none  [shards(): lax.psum((inner_grad, dense_grad, output_grad, gain_part, shift_part, qkv...]
    dot_general x32 -> x4, matrix products: 157 us -> 42.6 us  [times(): return jnp.dot(left_side, right_side, preferred_element_type=F32)]
    all_gather x6 -> x2, blocking collectives: 148 us -> 62.4 us  [the longest x1 46.8 us: shards(): all_positions = lax.all_gather(positions, 'shard', axis=0, tiled=True)]
    ppermute x9 -> x36, starting transfers between devices: 175 us -> 92.7 us  [the longest x30 87.1 us: ring(): lax.ppermute(array, axis, [(i, (i + distance) % size) for i in range(size)])]
  transfers between devices with their start and end apart: 18 -> 46, of which waited for: 15 -> 25; matrix products, arithmetic and copies ran while one was open for 7% -> 30% of each run, Pallas kernels for 0% -> 5%
where the time goes in v1:
time: 875 us; the launch traced here: 866 us
  waiting for transfers between devices  364 us (42%)
  matrix products  127 us (15%)
  local copies, waits for them, and re-layouts  104 us (12%)
  starting transfers between devices  93.1 us (11%)
  blocking collectives  62.4 us (7%)
  other arithmetic  60.5 us (7%)
  Pallas kernels  39.8 us (5%)
  between operations  15.3 us (2%)
    ppermute x30, waiting for transfers between devices, ring(): lax.ppermute(array, axis, [(i, (i + distance) % size) for i in range(size)])  200 us
    reduce_scatter x4, waiting for transfers between devices, reduced(): return lax.psum_scatter(array, 'rep', scatter_dimension=0, tiled=True)  155 us
    ppermute x30, starting transfers between devices, ring(): lax.ppermute(array, axis, [(i, (i + distance) % size) for i in range(size)])  87.1 us
    all_gather x1, blocking collectives, shards(): all_positions = lax.all_gather(positions, 'shard', axis=0, tiled=True)  46.8 us
    dot_general x4, matrix products, times_transpose(): lax.dot_general(left_side, right_side, (((1,), (1,)), ((), ())), preferre...  45.1 us
    dot_general x4, matrix products, times(): return jnp.dot(left_side, right_side, preferred_element_type=F32)  42.6 us
    pallas_call x1, Pallas kernels, attention(): pl.pallas_call(functools.partial(attention_kernel, block), grid=(seqs, pa...  39.8 us
    dot_general x4, matrix products, contract_rows(): lax.dot_general(left_side, right_side, (((0,), (0,)), ((), ())), preferre...  39.5 us
  transfers between devices with their start and end apart: 46, of which 25 were waited for; matrix products, arithmetic and copies ran while one was open for 30% of the time, Pallas kernels for 5%

profile of v1, /device:TPU:0, one launch (start us, length us, event | category | flops | bytes accessed | tf_op | source)
XLA Modules:
  0.0 865.9 jit_solution(3404149136995219013)
XLA Ops:
  12.5 3.1 collective-permute-start.3
  25.3 5.9 collective-permute-done.4
  37.0 3.1 collective-permute-start.9
  40.1 3.2 collective-permute-start.10
  46.2 4.2 collective-permute-done.9
  52.1 7.8 collective-permute-done.10
  63.1 15.5 %all-gather = f32[12288]{0:T(1024)S(1)} all-gather(f32[3072]{0:T(1024)S(1)} %pad_maximum_fusion.2), channel_id=2, replica_groups=mesh['rep'=8,'shard'=4] {'shard'}, dimensions={0}, use_global_device_ids=true | all-gather | bytes 61440 | tf_op jit(solution)/shard_map/all_gather | solution.py:240
  85.2 46.8 %all-gather.1 = s32[4,1,256]{2,1,0:T(1,128)S(1)} all-gather(s32[1,1,256]{2,1,0:T(1,128)S(1)} %bitcast.164), channel_id=1, replica_groups=mesh['rep'=8,'shard'=4] {'shard'}, dimensions={0}, use_global_device_ids=true | all-gather | bytes 5120 | tf_op jit(solution)/shard_map/all_gather | solution.py:241
  132.0 3.1 multiply_cosine_fusion
  138.3 2.9 concatenate.24
  141.3 3.0 concatenate.23
  152.1 11.2 %collective-permute-done.1 = bf16[256,2048]{0,1:T(8,128)(2,1)} collective-permute-done((bf16[256,2048]{0,1:T(8,128)(2,1)}, bf16[256,2048]{0,1:T(8,128)(2,1)}, u32[]{:S(2)}, u32[]{:S(2)}) %collective-permute-start.1) | collective-permute-done | bytes 1048608 | tf_op jit(solution)/shard_map/ppermute | solution.py:20
  168.2 17.6 %collective-permute-done.7 = bf16[256,2048]{1,0:T(8,128)(2,1)} collective-permute-done((bf16[256,2048]{1,0:T(8,128)(2,1)}, bf16[256,2048]{1,0:T(8,128)(2,1)}, u32[]{:S(2)}, u32[]{:S(2)}) %collective-permute-start.7) | collective-permute-done | bytes 1048608 | tf_op jit(solution)/shard_map/ppermute | solution.py:20
  192.2 16.0 %collective-permute-done.2 = bf16[256,2048]{0,1:T(8,128)(2,1)} collective-permute-done((bf16[256,2048]{0,1:T(8,128)(2,1)}, bf16[256,2048]{0,1:T(8,128)(2,1)}, u32[]{:S(2)}, u32[]{:S(2)}) %collective-permute-start.2) | collective-permute-done | bytes 1048608 | tf_op jit(solution)/shard_map/ppermute | solution.py:20
  210.9 13.2 %collective-permute-done.8 = bf16[256,2048]{1,0:T(8,128)(2,1)} collective-permute-done((bf16[256,2048]{1,0:T(8,128)(2,1)}, bf16[256,2048]{1,0:T(8,128)(2,1)}, u32[]{:S(2)}, u32[]{:S(2)}) %collective-permute-start.8) | collective-permute-done | bytes 1048608 | tf_op jit(solution)/shard_map/ppermute | solution.py:20
  226.4 4.5 convolution_convert_fusion.4.datt_ref
  231.0 11.8 %fusion.29.proj_ref = f32[1024,1536]{1,0:T(8,128)} fusion(bf16[1024,2048]{1,0:T(8,128)(2,1)} %bitcast.131, bf16[2048,1536]{1,0:T(8,128)(2,1)} %all-gather.9.cloned.1.call-done), kind=kOutput, calls=%fused_computation.120 | convolution fusion | flops 6442450944 | bytes 16777216 | tf_op jit(solution)/shard_map/dot_general | solution.py:41
  242.7 39.8 %attention.1 = (bf16[1024,512]{1,0:T(8,128)(2,1)S(1)}, bf16[1024,1536]{1,0:T(8,128)(2,1)}, f32[1,1,1536]{2,1,0:T(1,128)S(1)}) custom-call(f32[1024,1536]{1,0:T(8,128)} %fusion.29.proj_ref, f32[1,1536]{1,0:T(1,128)S(1)} %reshape.150.bias_ref, f32[3,1024,128]{2,1,0:T(8,128)S(1)} %copy-done.1, bf16[1024,512]{1,0:T(8,128)(2,1)S(1)} %convolution_convert_fusion.4.datt_ref, ...), custom_call_target="tpu_custom_call" | custom-call | tf_op jit(solution)/shard_map/attention/pallas_call | solution.py:167
  283.5 3.7 convolution_convert_fusion.3
  287.3 11.7 %convolution_convert_fusion.2 = bf16[2048,1536]{1,0:T(8,128)(2,1)} fusion(bf16[1024,2048]{1,0:T(8,128)(2,1)} %bitcast.132, bf16[1024,1536]{1,0:T(8,128)(2,1)} %get-tuple-element.16), kind=kOutput, calls=%fused_computation.15 | convolution fusion | flops 6445596672 | bytes 13631488 | tf_op jit(solution)/shard_map/dot_general | solution.py:29
  299.1 12.6 %fusion.30 = f32[1024,2048]{1,0:T(8,128)S(1)} fusion(bf16[1024,2048]{1,0:T(8,128)(2,1)} %bitcast.133, bf16[2048,2048]{1,0:T(8,128)(2,1)} %all-gather.11.cloned.1.call-done), kind=kOutput, calls=%fused_computation.121 | convolution fusion | flops 8589934592 | bytes 20971520 | tf_op jit(solution)/shard_map/dot_general | solution.py:41
  311.7 3.4 copy-done.28
  315.1 12.7 %convolution_convert_fusion = bf16[2048,2048]{1,0:T(8,128)(2,1)} fusion(bf16[1024,2048]{1,0:T(8,128)(2,1)S(1)} %bitcast.138, f32[1024,2048]{1,0:T(8,128)S(1)} %fusion.30, f32[2048]{0:T(1024)S(1)} %copy-done.27), kind=kOutput, calls=%fused_computation.13 | convolution fusion | flops 8615100416 | bytes 20979712 | tf_op jit(solution)/shard_map/dot_general | solution.py:29
  328.0 19.0 %convert_reduce_fusion = (f32[2048]{0:T(1024)S(1)}, bf16[1024,2048]{1,0:T(8,128)(2,1)S(1)}) fusion(f32[1024,2048]{1,0:T(8,128)} %copy-done.28, f32[2048]{0:T(1024)S(1)} %copy-done.27, bf16[1024,2048]{1,0:T(8,128)(2,1)} %bitcast.136, bf16[2048,2048]{1,0:T(8,128)(2,1)} %param.24), kind=kOutput, calls=%fused_computation.9 | convolution fusion | flops 8638167040 | bytes 25182208 | tf_op jit(solution)/shard_map/dot_general | solution.py:35
  348.9 11.4 %convolution_convert_fusion.1 = bf16[2048,2048]{1,0:T(8,128)(2,1)} fusion(bf16[1024,2048]{1,0:T(8,128)(2,1)S(1)} %bitcast.134, bf16[1024,2048]{1,0:T(8,128)(2,1)S(1)} %get-tuple-element.21), kind=kOutput, calls=%fused_computation.14 | convolution fusion | flops 8594128896 | bytes 16777216 | tf_op jit(solution)/shard_map/dot_general | solution.py:29
  361.2 31.0 %reduce-scatter.5.cloned.1.call-done = bf16[256,1536]{1,0:T(8,128)(2,1)} async-done(((bf16[2048,1536]{1,0:T(8,128)(2,1)}), bf16[256,1536]{1,0:T(8,128)(2,1)}) %reduce-scatter.5.cloned.1.call-update) | async-done | bytes 786448 | tf_op jit(solution)/shard_map/reduce_scatter | solution.py:314
  403.7 6.6 collective-permute-done.25
  411.7 3.1 reshape.157
  418.6 48.8 %reduce-scatter.11.cloned.1.call-done = bf16[256,2048]{1,0:T(8,128)(2,1)} async-done(((bf16[2048,2048]{1,0:T(8,128)(2,1)}), bf16[256,2048]{1,0:T(8,128)(2,1)}) %reduce-scatter.11.cloned.1.call-update) | async-done | bytes 1048592 | tf_op jit(solution)/shard_map/reduce_scatter | solution.py:314
  467.4 75.5 %reduce-scatter.9.cloned.1.call-done = bf16[256,2048]{1,0:T(8,128)(2,1)} async-done(((bf16[2048,2048]{1,0:T(8,128)(2,1)}), bf16[256,2048]{1,0:T(8,128)(2,1)}) %reduce-scatter.9.cloned.1.call-update) | async-done | bytes 1048592 | tf_op jit(solution)/shard_map/reduce_scatter | solution.py:314
  550.6 4.7 collective-permute-done.33
  555.3 10.0 %collective-permute-done.34 = bf16[64,2048]{1,0:T(8,128)(2,1)S(1)} collective-permute-done((bf16[64,2048]{1,0:T(8,128)(2,1)S(1)}, bf16[64,2048]{1,0:T(8,128)(2,1)S(1)}, u32[]{:S(2)}, u32[]{:S(2)}) %collective-permute-start.34) | collective-permute-done | bytes 262176 | tf_op jit(solution)/shard_map/ppermute | solution.py:20
  567.4 7.8 dynamic_update_slice.103
  577.1 12.7 %fusion.31 = f32[1024,2048]{1,0:T(8,128)S(1)} fusion(bf16[1024,2048]{1,0:T(8,128)(2,1)} %copy-done.29, bf16[2048,2048]{1,0:T(8,128)(2,1)} %all-gather.11.cloned.1.call-done), kind=kOutput, calls=%fused_computation.122 | convolution fusion | flops 8589934592 | bytes 20971520 | tf_op jit(solution)/shard_map/dot_general | solution.py:35
  589.9 8.8 %add_convert_fusion = bf16[1024,2048]{1,0:T(8,128)(2,1)S(1)} fusion(f32[1024,2048]{1,0:T(8,128)S(1)} %fusion.31, bf16[1024,1536]{1,0:T(8,128)(2,1)S(1)} %copy-done.26, bf16[2048,1536]{1,0:T(8,128)(2,1)} %all-gather.9.cloned.1.call-done), kind=kOutput, calls=%fused_computation.10 | convolution fusion | flops 6446645248 | bytes 22020096 | tf_op jit(solution)/shard_map/dot_general | solution.py:35
  599.1 7.7 collective-permute-start.17
  607.5 15.7 %fusion.24 = f32[1024,2048]{1,0:T(8,128)S(1)} fusion(bf16[2048,2048]{1,0:T(8,128)(2,1)} %param.24, f32[1024,2048]{1,0:T(8,128)} %copy-done.28, f32[2048]{0:T(1024)S(1)} %copy-done.27), kind=kOutput, calls=%fused_computation.116 | convolution fusion | flops 8610906112 | bytes 25174016 | tf_op jit(solution)/shard_map/dot_general | solution.py:41
  629.5 3.2 collective-permute-start.14
  633.8 41.8 %collective-permute-start.12 = (bf16[256,2048]{1,0:T(8,128)(2,1)}, bf16[256,2048]{1,0:T(8,128)(2,1)}, u32[]{:S(2)}, u32[]{:S(2)}) collective-permute-start(bf16[256,2048]{1,0:T(8,128)(2,1)} %get-tuple-element.28), channel_id=1, source_target_pairs={{0,1},{1,2},{2,3},{3,0},{4,5},{5,6},{6,7},{7,4},{8,9},{9,10},{10,1... | collective-permute-start | bytes 3145736 | tf_op jit(solution)/shard_map/ppermute | solution.py:20
  675.6 67.3 %collective-permute-done.16 = bf16[256,2048]{1,0:T(8,128)(2,1)S(1)} collective-permute-done((bf16[256,2048]{1,0:T(8,128)(2,1)S(1)}, bf16[256,2048]{1,0:T(8,128)(2,1)S(1)}, u32[]{:S(2)}, u32[]{:S(2)}) %collective-permute-start.16) | collective-permute-done | bytes 1048608 | tf_op jit(solution)/shard_map/ppermute | solution.py:20
  747.8 3.1 copy.158
  752.9 2.9 copy.159
  760.3 26.9 %collective-permute-done.13 = bf16[256,2048]{1,0:T(8,128)(2,1)} collective-permute-done((bf16[256,2048]{1,0:T(8,128)(2,1)}, bf16[256,2048]{1,0:T(8,128)(2,1)}, u32[]{:S(2)}, u32[]{:S(2)}) %collective-permute-start.13) | collective-permute-done | bytes 1048608 | tf_op jit(solution)/shard_map/ppermute | solution.py:20
  787.2 6.8 convert_reduce_fusion.2
  821.5 4.1 convert_element_type.100
  825.7 9.2 %convert_element_type.97 = f32[512,6144]{1,0:T(8,128)} convert(bf16[512,6144]{1,0:T(8,128)(2,1)} %all-gather.13.cloned.1.call-done) | non-fusion elementwise | flops 3145728 | bytes 18874368 | tf_op jit(solution)/shard_map/convert_element_type | solution.py:317
  834.9 11.7 %convert_element_type.104 = f32[2048,2048]{1,0:T(8,128)} convert(bf16[2048,2048]{1,0:T(8,128)(2,1)} %all-gather.19.cloned.1.call-done) | non-fusion elementwise | flops 4194304 | bytes 25165824 | tf_op jit(solution)/shard_map/convert_element_type | solution.py:317
  846.5 11.7 %convert_element_type.102 = f32[512,8192]{1,0:T(8,128)} convert(bf16[512,8192]{1,0:T(8,128)(2,1)} %all-gather.17.cloned.1.call-done) | non-fusion elementwise | flops 4194304 | bytes 25165824 | tf_op jit(solution)/shard_map/convert_element_type | solution.py:317
  (262 shorter events, 141.9 us)
Async XLA Ops:
  7.2 219.2 %copy-start = (bf16[512,2048]{1,0:T(8,128)(2,1)S(1)}, bf16[512,2048]{1,0:T(8,128)(2,1)}, u32[]{:S(2)}) copy-start(bf16[512,2048]{1,0:T(8,128)(2,1)} %param.20) | copy-start | bytes 6291460
  7.2 223.8 %all-gather.9.cloned.1.call-start = ((), (), s32[]{:S(2)}) async-start(), calls=%async_computation.4 | async-start | bytes 7077888 | tf_op jit(solution)/shard_map/all_gather | solution.py:235
  12.5 11.1 %collective-permute-start.3 = (bf16[64,1536]{1,0:T(8,128)(2,1)S(1)}, bf16[64,1536]{1,0:T(8,128)(2,1)}, u32[]{:S(2)}, u32[]{:S(2)}) collective-permute-start(bf16[64,1536]{1,0:T(8,128)(2,1)S(1)} %reshape.145), channel_id=1, source_target_pairs={{0,1},{1,2},{2,3},{3,0},{4,5},{5,6},{6,7},{7,4},{8,9},{9,10},{10,1... | collective-permute-start | bytes 589832 | tf_op jit(solution)/shard_map/ppermute | solution.py:20
  16.7 14.5 %collective-permute-start.4 = (bf16[64,1536]{1,0:T(8,128)(2,1)}, bf16[64,1536]{1,0:T(8,128)(2,1)}, u32[]{:S(2)}, u32[]{:S(2)}) collective-permute-start(bf16[64,1536]{1,0:T(8,128)(2,1)} %reshape.146), channel_id=1, source_target_pairs={{0,2},{1,3},{2,0},{3,1},{4,6},{5,7},{6,4},{7,5},{8,10},{9,11},{10,... | collective-permute-start | bytes 589832 | tf_op jit(solution)/shard_map/ppermute | solution.py:20
  20.3 12.5 %collective-permute-start.5 = (bf16[64,1536]{1,0:T(8,128)(2,1)}, bf16[64,1536]{1,0:T(8,128)(2,1)}, u32[]{:S(2)}, u32[]{:S(2)}) collective-permute-start(bf16[64,1536]{1,0:T(8,128)(2,1)} %reshape.147), channel_id=1, source_target_pairs={{0,3},{1,0},{2,1},{3,2},{4,7},{5,4},{6,5},{7,6},{8,11},{9,8},{10,9... | collective-permute-start | bytes 589832 | tf_op jit(solution)/shard_map/ppermute | solution.py:20
  23.0 55.7 %copy-start.4 = (bf16[256,2048]{1,0:T(8,128)(2,1)S(1)}, bf16[256,2048]{1,0:T(8,128)(2,1)}, u32[]{:S(2)}) copy-start(bf16[256,2048]{1,0:T(8,128)(2,1)} %param.14) | copy-start | bytes 3145732
  34.5 264.6 %all-gather.11.cloned.1.call-start = ((), (), s32[]{:S(2)}) async-start(), calls=%async_computation.5 | async-start | bytes 9437184 | tf_op jit(solution)/shard_map/all_gather | solution.py:232
  37.0 13.4 %collective-permute-start.9 = (bf16[64,2048]{1,0:T(8,128)(2,1)}, bf16[64,2048]{1,0:T(8,128)(2,1)}, u32[]{:S(2)}, u32[]{:S(2)}) collective-permute-start(bf16[64,2048]{1,0:T(8,128)(2,1)} %get-tuple-element.23), channel_id=1, source_target_pairs={{0,1},{1,2},{2,3},{3,0},{4,5},{5,6},{6,7},{7,4},{8,9},{9,10},{10,1... | collective-permute-start | bytes 786440 | tf_op jit(solution)/shard_map/ppermute | solution.py:20
  40.1 19.8 %collective-permute-start.10 = (bf16[64,2048]{1,0:T(8,128)(2,1)}, bf16[64,2048]{1,0:T(8,128)(2,1)}, u32[]{:S(2)}, u32[]{:S(2)}) collective-permute-start(bf16[64,2048]{1,0:T(8,128)(2,1)} %get-tuple-element.24), channel_id=1, source_target_pairs={{0,2},{1,3},{2,0},{3,1},{4,6},{5,7},{6,4},{7,5},{8,10},{9,11},{10,... | collective-permute-start | bytes 786440 | tf_op jit(solution)/shard_map/ppermute | solution.py:20
  43.3 18.2 %collective-permute-start.11 = (bf16[64,2048]{1,0:T(8,128)(2,1)}, bf16[64,2048]{1,0:T(8,128)(2,1)S(1)}, u32[]{:S(2)}, u32[]{:S(2)}) collective-permute-start(bf16[64,2048]{1,0:T(8,128)(2,1)} %get-tuple-element.22), channel_id=1, source_target_pairs={{0,3},{1,0},{2,1},{3,2},{4,7},{5,4},{6,5},{7,6},{8,11},{9,8},{10,9... | collective-permute-start | bytes 786440 | tf_op jit(solution)/shard_map/ppermute | solution.py:20
  62.2 298.2 %reduce-scatter.7.cloned.1.call-start = ((), (), s32[]{:S(2)}) async-start(), calls=%async_computation.8 | async-start | bytes 2359296 | tf_op jit(solution)/shard_map/reduce_scatter | solution.py:314
  83.0 52.1 %collective-permute-start = (bf16[256,2048]{0,1:T(8,128)(2,1)S(1)}, bf16[256,2048]{0,1:T(8,128)(2,1)}, u32[]{:S(2)}, u32[]{:S(2)}) collective-permute-start(bf16[256,2048]{0,1:T(8,128)(2,1)S(1)} %bitcast.140), channel_id=1, source_target_pairs={{0,1},{1,2},{2,3},{3,0},{4,5},{5,6},{6,7},{7,4},{8,9},{9,10},{10,1... | collective-permute-start | bytes 3145736 | tf_op jit(solution)/shard_map/ppermute | solution.py:20
  85.1 64.3 %collective-permute-start.6 = (bf16[256,2048]{1,0:T(8,128)(2,1)}, bf16[256,2048]{1,0:T(8,128)(2,1)}, u32[]{:S(2)}, u32[]{:S(2)}) collective-permute-start(bf16[256,2048]{1,0:T(8,128)(2,1)} %param.26), channel_id=1, source_target_pairs={{0,1},{1,2},{2,3},{3,0},{4,5},{5,6},{6,7},{7,4},{8,9},{9,10},{10,1... | collective-permute-start | bytes 3145736 | tf_op jit(solution)/shard_map/ppermute | solution.py:20
  135.1 28.2 %collective-permute-start.1 = (bf16[256,2048]{0,1:T(8,128)(2,1)}, bf16[256,2048]{0,1:T(8,128)(2,1)}, u32[]{:S(2)}, u32[]{:S(2)}) collective-permute-start(bf16[256,2048]{0,1:T(8,128)(2,1)} %collective-permute-done), channel_id=1, source_target_pairs={{0,1},{1,2},{2,3},{3,0},{4,5},{5,6},{6,7},{7,4},{8,9},{9,10},{10,1... | collective-permute-start | bytes 3145736 | tf_op jit(solution)/shard_map/ppermute | solution.py:20
  149.5 36.4 %collective-permute-start.7 = (bf16[256,2048]{1,0:T(8,128)(2,1)}, bf16[256,2048]{1,0:T(8,128)(2,1)}, u32[]{:S(2)}, u32[]{:S(2)}) collective-permute-start(bf16[256,2048]{1,0:T(8,128)(2,1)} %collective-permute-done.6), channel_id=1, source_target_pairs={{0,1},{1,2},{2,3},{3,0},{4,5},{5,6},{6,7},{7,4},{8,9},{9,10},{10,1... | collective-permute-start | bytes 3145736 | tf_op jit(solution)/shard_map/ppermute | solution.py:20
  163.3 44.9 %collective-permute-start.2 = (bf16[256,2048]{0,1:T(8,128)(2,1)}, bf16[256,2048]{0,1:T(8,128)(2,1)}, u32[]{:S(2)}, u32[]{:S(2)}) collective-permute-start(bf16[256,2048]{0,1:T(8,128)(2,1)} %collective-permute-done.1), channel_id=1, source_target_pairs={{0,1},{1,2},{2,3},{3,0},{4,5},{5,6},{6,7},{7,4},{8,9},{9,10},{10,1... | collective-permute-start | bytes 3145736 | tf_op jit(solution)/shard_map/ppermute | solution.py:20
  185.8 38.3 %collective-permute-start.8 = (bf16[256,2048]{1,0:T(8,128)(2,1)}, bf16[256,2048]{1,0:T(8,128)(2,1)}, u32[]{:S(2)}, u32[]{:S(2)}) collective-permute-start(bf16[256,2048]{1,0:T(8,128)(2,1)} %collective-permute-done.7), channel_id=1, source_target_pairs={{0,1},{1,2},{2,3},{3,0},{4,5},{5,6},{6,7},{7,4},{8,9},{9,10},{10,1... | collective-permute-start | bytes 3145736 | tf_op jit(solution)/shard_map/ppermute | solution.py:20
  287.2 104.9 %reduce-scatter.5.cloned.1.call-start = ((), (), s32[]{:S(2)}) async-start(), calls=%async_computation.6 | async-start | bytes 7077888 | tf_op jit(solution)/shard_map/reduce_scatter | solution.py:314
  299.0 168.3 %reduce-scatter.11.cloned.1.call-start = ((), (), s32[]{:S(2)}) async-start(), calls=%async_computation.12 | async-start | bytes 9437184 | tf_op jit(solution)/shard_map/reduce_scatter | solution.py:314
  327.9 215.1 %reduce-scatter.9.cloned.1.call-start = ((), (), s32[]{:S(2)}) async-start(), calls=%async_computation.10 | async-start | bytes 9437184 | tf_op jit(solution)/shard_map/reduce_scatter | solution.py:314
  360.3 461.2 %all-gather.15.cloned.1.call-start = ((), (), s32[]{:S(2)}) async-start(), calls=%async_computation.9 | async-start | bytes 2359296 | tf_op jit(solution)/shard_map/all_gather | solution.py:317
  361.1 464.6 %all-gather.13.cloned.1.call-start = ((), (), s32[]{:S(2)}) async-start(), calls=%async_computation.7 | async-start | bytes 7077888 | tf_op jit(solution)/shard_map/all_gather | solution.py:317
  393.3 9.8 %collective-permute-start.24 = (bf16[64,1536]{1,0:T(8,128)(2,1)S(1)}, bf16[64,1536]{1,0:T(8,128)(2,1)S(1)}, u32[]{:S(2)}, u32[]{:S(2)}) collective-permute-start(bf16[64,1536]{1,0:T(8,128)(2,1)S(1)} %get-tuple-element.39), channel_id=1, source_target_pairs={{0,1},{1,2},{2,3},{3,0},{4,5},{5,6},{6,7},{7,4},{8,9},{9,10},{10,1... | collective-permute-start | bytes 589832 | tf_op jit(solution)/shard_map/ppermute | solution.py:20
  394.9 15.5 %collective-permute-start.25 = (bf16[64,1536]{1,0:T(8,128)(2,1)S(1)}, bf16[64,1536]{1,0:T(8,128)(2,1)S(1)}, u32[]{:S(2)}, u32[]{:S(2)}) collective-permute-start(bf16[64,1536]{1,0:T(8,128)(2,1)S(1)} %get-tuple-element.38), channel_id=1, source_target_pairs={{0,2},{1,3},{2,0},{3,1},{4,6},{5,7},{6,4},{7,5},{8,10},{9,11},{10,... | collective-permute-start | bytes 589832 | tf_op jit(solution)/shard_map/ppermute | solution.py:20
  397.3 13.8 %collective-permute-start.26 = (bf16[64,1536]{1,0:T(8,128)(2,1)S(1)}, bf16[64,1536]{1,0:T(8,128)(2,1)S(1)}, u32[]{:S(2)}, u32[]{:S(2)}) collective-permute-start(bf16[64,1536]{1,0:T(8,128)(2,1)S(1)} %get-tuple-element.37), channel_id=1, source_target_pairs={{0,3},{1,0},{2,1},{3,2},{4,7},{5,4},{6,5},{7,6},{8,11},{9,8},{10,9... | collective-permute-start | bytes 589832 | tf_op jit(solution)/shard_map/ppermute | solution.py:20
  418.5 416.3 %all-gather.19.cloned.1.call-start = ((), (), s32[]{:S(2)}) async-start(), calls=%async_computation.13 | async-start | bytes 9437184 | tf_op jit(solution)/shard_map/all_gather | solution.py:317
  467.4 379.2 %all-gather.17.cloned.1.call-start = ((), (), s32[]{:S(2)}) async-start(), calls=%async_computation.11 | async-start | bytes 9437184 | tf_op jit(solution)/shard_map/all_gather | solution.py:317
  544.1 11.2 %collective-permute-start.33 = (bf16[64,2048]{1,0:T(8,128)(2,1)S(1)}, bf16[64,2048]{1,0:T(8,128)(2,1)S(1)}, u32[]{:S(2)}, u32[]{:S(2)}) collective-permute-start(bf16[64,2048]{1,0:T(8,128)(2,1)S(1)} %get-tuple-element.33), channel_id=1, source_target_pairs={{0,1},{1,2},{2,3},{3,0},{4,5},{5,6},{6,7},{7,4},{8,9},{9,10},{10,1... | collective-permute-start | bytes 786440 | tf_op jit(solution)/shard_map/ppermute | solution.py:20
  545.7 19.7 %collective-permute-start.34 = (bf16[64,2048]{1,0:T(8,128)(2,1)S(1)}, bf16[64,2048]{1,0:T(8,128)(2,1)S(1)}, u32[]{:S(2)}, u32[]{:S(2)}) collective-permute-start(bf16[64,2048]{1,0:T(8,128)(2,1)S(1)} %get-tuple-element.32), channel_id=1, source_target_pairs={{0,2},{1,3},{2,0},{3,1},{4,6},{5,7},{6,4},{7,5},{8,10},{9,11},{10,... | collective-permute-start | bytes 786440 | tf_op jit(solution)/shard_map/ppermute | solution.py:20
  548.1 18.2 %collective-permute-start.35 = (bf16[64,2048]{1,0:T(8,128)(2,1)S(1)}, bf16[64,2048]{1,0:T(8,128)(2,1)S(1)}, u32[]{:S(2)}, u32[]{:S(2)}) collective-permute-start(bf16[64,2048]{1,0:T(8,128)(2,1)S(1)} %get-tuple-element.31), channel_id=1, source_target_pairs={{0,3},{1,0},{2,1},{3,2},{4,7},{5,4},{6,5},{7,6},{8,11},{9,8},{10,9... | collective-permute-start | bytes 786440 | tf_op jit(solution)/shard_map/ppermute | solution.py:20
  599.1 34.6 %collective-permute-start.17 = (bf16[256,2048]{1,0:T(8,128)(2,1)S(1)}, bf16[256,2048]{1,0:T(8,128)(2,1)S(1)}, u32[]{:S(2)}, u32[]{:S(2)}) collective-permute-start(bf16[256,2048]{1,0:T(8,128)(2,1)S(1)} %get-tuple-element.26), channel_id=1, source_target_pairs={{0,3},{1,0},{2,1},{3,2},{4,7},{5,4},{6,5},{7,6},{8,11},{9,8},{10,9... | collective-permute-start | bytes 3145736 | tf_op jit(solution)/shard_map/ppermute | solution.py:20
  606.9 136.1 %collective-permute-start.16 = (bf16[256,2048]{1,0:T(8,128)(2,1)S(1)}, bf16[256,2048]{1,0:T(8,128)(2,1)S(1)}, u32[]{:S(2)}, u32[]{:S(2)}) collective-permute-start(bf16[256,2048]{1,0:T(8,128)(2,1)S(1)} %get-tuple-element.27), channel_id=1, source_target_pairs={{0,2},{1,3},{2,0},{3,1},{4,6},{5,7},{6,4},{7,5},{8,10},{9,11},{10,... | collective-permute-start | bytes 3145736 | tf_op jit(solution)/shard_map/ppermute | solution.py:20
  606.9 136.0 %collective-permute-start.15 = (bf16[256,2048]{1,0:T(8,128)(2,1)S(1)}, bf16[256,2048]{1,0:T(8,128)(2,1)S(1)}, u32[]{:S(2)}, u32[]{:S(2)}) collective-permute-start(bf16[256,2048]{1,0:T(8,128)(2,1)S(1)} %get-tuple-element.25), channel_id=1, source_target_pairs={{0,1},{1,2},{2,3},{3,0},{4,5},{5,6},{6,7},{7,4},{8,9},{9,10},{10,1... | collective-permute-start | bytes 3145736 | tf_op jit(solution)/shard_map/ppermute | solution.py:20
  629.5 130.8 %collective-permute-start.14 = (bf16[256,2048]{1,0:T(8,128)(2,1)}, bf16[256,2048]{1,0:T(8,128)(2,1)}, u32[]{:S(2)}, u32[]{:S(2)}) collective-permute-start(bf16[256,2048]{1,0:T(8,128)(2,1)} %get-tuple-element.29), channel_id=1, source_target_pairs={{0,3},{1,0},{2,1},{3,2},{4,7},{5,4},{6,5},{7,6},{8,11},{9,8},{10,9... | collective-permute-start | bytes 3145736 | tf_op jit(solution)/shard_map/ppermute | solution.py:20
  632.6 154.5 %collective-permute-start.13 = (bf16[256,2048]{1,0:T(8,128)(2,1)}, bf16[256,2048]{1,0:T(8,128)(2,1)}, u32[]{:S(2)}, u32[]{:S(2)}) collective-permute-start(bf16[256,2048]{1,0:T(8,128)(2,1)} %get-tuple-element.30), channel_id=1, source_target_pairs={{0,2},{1,3},{2,0},{3,1},{4,6},{5,7},{6,4},{7,5},{8,10},{9,11},{10,... | collective-permute-start | bytes 3145736 | tf_op jit(solution)/shard_map/ppermute | solution.py:20
  633.8 153.4 %collective-permute-start.12 = (bf16[256,2048]{1,0:T(8,128)(2,1)}, bf16[256,2048]{1,0:T(8,128)(2,1)}, u32[]{:S(2)}, u32[]{:S(2)}) collective-permute-start(bf16[256,2048]{1,0:T(8,128)(2,1)} %get-tuple-element.28), channel_id=1, source_target_pairs={{0,1},{1,2},{2,3},{3,0},{4,5},{5,6},{6,7},{7,4},{8,9},{9,10},{10,1... | collective-permute-start | bytes 3145736 | tf_op jit(solution)/shard_map/ppermute | solution.py:20
  794.0 3.7 collective-permute-start.29
  794.1 4.6 collective-permute-start.28
  795.3 5.4 collective-permute-start.27
  800.7 2.4 collective-permute-start.30
  800.8 3.7 collective-permute-start.20
  802.3 4.5 collective-permute-start.19
  802.5 5.6 collective-permute-start.18
  803.1 13.4 %collective-permute-start.31 = (f32[4096]{0:T(1024)S(1)}, f32[4096]{0:T(1024)S(1)}, u32[]{:S(2)}, u32[]{:S(2)}) collective-permute-start(f32[4096]{0:T(1024)S(1)} %fusion.23), channel_id=1, source_target_pairs={{0,8},{4,12},{8,0},{12,4},{16,24},{20,28},{24,16},{28,20},{1,9},{5... | collective-permute-start | bytes 49160 | tf_op jit(solution)/shard_map/ppermute | solution.py:25
  808.1 1.2 collective-permute-start.21
  809.3 3.6 collective-permute-start.22
  812.9 3.6 collective-permute-start.23
  816.5 3.8 collective-permute-start.32
  (28 other events, 388.6 us)
Sparse Core Ops, SparseCore 0:
  34.6 48.8 all-gather.8
  86.0 54.3 all-gather.10
  287.3 39.3 reduce-scatter.6
  330.4 61.7 reduce-scatter.4
  396.0 71.2 reduce-scatter.10
  471.6 71.2 reduce-scatter.8
  544.8 27.8 all-gather.14
  574.6 45.5 all-gather.12
  622.1 54.3 all-gather.18
  678.2 54.3 all-gather.16

commit v2 on v1

v2 whole, which is shorter than its diff:
```python
import functools

import jax
import jax.numpy as jnp
from jax import lax
from jax.experimental import pallas as pl
from jax.experimental.pallas import tpu as pltpu
from jax.sharding import PartitionSpec as P

HEAD_DIM = 64
ROT = 32
SEQ = 1024
PAIR = 2 * HEAD_DIM
BF = jnp.bfloat16
F32 = jnp.float32


def ring(array, axis, distance):
    size = lax.axis_size(axis)
    return lax.ppermute(array, axis, [(i, (i + distance) % size) for i in range(size)])


def swap(array, axis, bit):
    size = lax.axis_size(axis)
    return lax.ppermute(array, axis, [(i, i ^ bit) for i in range(size)])


def contract_rows(left_side, right_side):
    return lax.dot_general(
        left_side, right_side, (((0,), (0,)), ((), ())), preferred_element_type=F32
    )


def times_transpose(left_side, right_side):
    return lax.dot_general(
        left_side, right_side, (((1,), (1,)), ((), ())), preferred_element_type=F32
    )


def times(left_side, right_side):
    return jnp.dot(left_side, right_side, preferred_element_type=F32)


def gelu_tanh(pre_act):
    return jax.nn.gelu(pre_act, approximate=True)


class Order:
    def __init__(self):
        self.last = None

    def step(self, work, *operands):
        if self.last is not None:
            *operands, _ = lax.optimization_barrier((*operands, self.last))
        result = work(*operands)
        self.last = jax.tree.leaves(result)[0]
        return result

    def hold(self, array):
        return self.step(lambda a: a, array)


def after(array, *others):
    return lax.optimization_barrier((array, *others))[0]


def placed(pieces, place, axis):
    size, length = len(pieces), pieces[0].shape[axis]
    shape = list(pieces[0].shape)
    shape[axis] *= size
    whole = jnp.zeros(shape, pieces[0].dtype)
    for hop, piece in enumerate(pieces):
        whole = lax.dynamic_update_slice_in_dim(
            whole, piece, (place - hop) % size * length, axis
        )
    return whole


def direct(pick, place):
    size = lax.axis_size("shard")
    return [pick(place)] + [
        ring(pick((place + hop) % size), "shard", hop) for hop in range(1, size)
    ]


def doubled(row, place):
    bit = 1
    while bit < lax.axis_size("shard"):
        other = swap(row, "shard", bit)
        upper = (place & bit) > 0
        row = jnp.concatenate([jnp.where(upper, other, row), jnp.where(upper, row, other)])
        bit *= 2
    return row


def rep_sum(values):
    bit = 1
    while bit < lax.axis_size("rep"):
        values = values + swap(values, "rep", bit)
        bit *= 2
    return values


class Halving:
    def __init__(self, rep, array, parts):
        count = lax.axis_size("rep").bit_length() - 2
        self.rep = rep
        array = array.reshape((2,) * count + (array.shape[0] >> count,) + array.shape[1:])
        rows = array.shape[count] // parts
        self.arrays = [array] * parts
        self.spans = [(part * rows, rows) for part in range(parts)]
        bits = list(range(count, 0, -1))
        self.bits = [list(bits) for _ in range(parts)]
        self.todo = [
            bits[::-1][part % count :] + bits[::-1][: part % count] for part in range(parts)
        ]

    def pick(self, part, array, mine):
        axis = self.bits[part].index(self.todo[part][0])
        bit = (self.rep >> self.todo[part][0]) & 1
        starts, sizes = [0] * array.ndim, list(array.shape)
        starts[axis], sizes[axis] = (bit if mine else 1 - bit), 1
        starts[len(self.bits[part])], sizes[len(self.bits[part])] = self.spans[part]
        half = lax.dynamic_slice(array, starts, sizes)
        return half.reshape(half.shape[:axis] + half.shape[axis + 1 :])

    def outgoing(self, *arrays):
        return tuple(self.pick(part, array, False) for part, array in enumerate(arrays))

    def added(self, *operands):
        count = len(operands) // 2
        return tuple(
            (self.pick(part, operands[part], True).astype(F32) + operands[count + part].astype(F32))
            .astype(BF)
            for part in range(count)
        )

    def send(self, line):
        sent = line.step(self.outgoing, *self.arrays)
        self.came = [
            swap(piece, "rep", 1 << todo[0]) for piece, todo in zip(sent, self.todo)
        ]

    def take(self, line):
        self.arrays = line.step(self.added, *self.arrays, *self.came)
        for part, todo in enumerate(self.todo):
            self.bits[part].remove(todo[0])
            self.todo[part] = todo[1:]
            self.spans[part] = (0, self.spans[part][1])

    def further(self, line):
        self.take(line)
        self.send(line)

    def end(self, line):
        while len(self.todo[0]) > 1:
            self.further(line)
        self.take(line)
        return jnp.concatenate(self.arrays, axis=0)


def grad_kernel(which_ref, left_ref, right_ref, *refs):
    total = contract_rows(left_ref[...], right_ref[...])
    if len(refs) > 1:
        total = total + refs[0][...].astype(F32)
    refs[-1][...] = total.astype(BF)


def half_grads(left, right, which, reps, by_rows, came=None):
    tokens, height = left.shape
    length = right.shape[1]
    if by_rows:
        height //= reps
    else:
        length //= reps
    if (height if by_rows else length) % 128:
        side = left if by_rows else right
        split = side.reshape(tokens, reps // 2, 2, -1)
        split = lax.dynamic_index_in_dim(split, which, 2, keepdims=False)
        total = lax.dot_general(
            split if by_rows else left,
            right if by_rows else split,
            (((0,), (0,)), ((), ())),
            preferred_element_type=F32,
        )
        if not by_rows:
            total = total.transpose(1, 0, 2)
        total = total.reshape(-1, length)
        return (total if came is None else total + came.astype(F32)).astype(BF)
    chosen = lambda b, w: (0, 2 * b + w[0])
    fixed = lambda b, w: (0, 0)
    block = pl.BlockSpec((height, length), lambda b, w: (b, 0))
    return pl.pallas_call(
        grad_kernel,
        grid_spec=pltpu.PrefetchScalarGridSpec(
            num_scalar_prefetch=1,
            grid=(reps // 2,),
            in_specs=[
                pl.BlockSpec((tokens, height), chosen if by_rows else fixed),
                pl.BlockSpec((tokens, length), fixed if by_rows else chosen),
            ]
            + ([] if came is None else [block]),
            out_specs=block,
        ),
        out_shape=jax.ShapeDtypeStruct((reps // 2 * height, length), BF),
        compiler_params=pltpu.CompilerParams(vmem_limit_bytes=48 * 2**20),
        name="half_grads",
    )(which.reshape(1), left, right, *([] if came is None else [came]))


def ln_forward_kernel(reps, group, x_ref, gain_ref, shift_ref, out_ref):
    x = x_ref[...].astype(F32)
    centred = x - jnp.mean(x, axis=-1, keepdims=True)
    spread = jnp.mean(centred * centred, axis=-1, keepdims=True)
    normed = (centred * lax.rsqrt(spread + 1e-05)) * gain_ref[...] + shift_ref[...]
    slab = x.shape[1] // (reps * group)
    out_ref[...] = jnp.concatenate(
        [
            normed[:, (g * reps + r) * slab : (g * reps + r + 1) * slab]
            for r in range(reps)
            for g in range(group)
        ],
        axis=1,
    ).astype(BF)


def ln_forward(inputs, gain, shift, reps, group):
    tokens, width = inputs.shape
    return pl.pallas_call(
        functools.partial(ln_forward_kernel, reps, group),
        out_shape=jax.ShapeDtypeStruct((tokens, width), BF),
        compiler_params=pltpu.CompilerParams(vmem_limit_bytes=48 * 2**20),
        name="ln_forward",
    )(inputs, gain.reshape(1, width), shift.reshape(1, width))


def ln_backward_kernel(reps, group, *refs):
    x_ref, gain_ref, cot_ref, *parts, out_ref, sums_ref = refs
    x = x_ref[...].astype(F32)
    centred = x - jnp.mean(x, axis=-1, keepdims=True)
    spread = jnp.mean(centred * centred, axis=-1, keepdims=True)
    inverse = lax.rsqrt(spread + 1e-05)
    xhat = centred * inverse
    mixed = parts[0][...].astype(F32)
    for part in parts[1:]:
        mixed = mixed + part[...].astype(F32)
    slab = x.shape[1] // (reps * group)
    d_normed = jnp.concatenate(
        [
            mixed[:, (r * group + g) * slab : (r * group + g + 1) * slab]
            for g in range(group)
            for r in range(reps)
        ],
        axis=1,
    )
    sums_ref[0:1] = jnp.sum(d_normed * xhat, axis=0, keepdims=True)
    sums_ref[1:2] = jnp.sum(d_normed, axis=0, keepdims=True)
    scaled = d_normed * gain_ref[...]
    out_ref[...] = cot_ref[...].astype(F32) + inverse * (
        scaled
        - jnp.mean(scaled, axis=-1, keepdims=True)
        - xhat * jnp.mean(scaled * xhat, axis=-1, keepdims=True)
    )


def ln_backward(inputs, gain, cotangent, parts, reps, group):
    tokens, width = inputs.shape
    return pl.pallas_call(
        functools.partial(ln_backward_kernel, reps, group),
        out_shape=[
            jax.ShapeDtypeStruct((tokens, width), F32),
            jax.ShapeDtypeStruct((2, width), F32),
        ],
        compiler_params=pltpu.CompilerParams(vmem_limit_bytes=56 * 2**20),
        name="ln_backward",
    )(inputs, gain.reshape(1, width), cotangent, *parts)


def attention_kernel(block, *refs):
    q_ref, k_ref, v_ref, turn_ref, datt_ref, start_ref = refs[:6]
    att_ref, dproj_ref, bsum_ref, dq_ref, dk_ref, dv_ref = refs[-6:]
    rows = q_ref.shape[0]
    scaling = HEAD_DIM ** (-0.5)
    stage = pl.program_id(1)

    @pl.when(stage == 0)
    def _():
        cosine = turn_ref[0]
        minus = turn_ref[1]
        plus = turn_ref[2]

        def turned(u, sign):
            return (
                u * cosine
                + sign * (pltpu.roll(u, PAIR - ROT // 2, 1) * minus)
                + sign * (pltpu.roll(u, ROT // 2, 1) * plus)
            )

        query = turned(q_ref[...], 1.0).astype(BF) * scaling
        query = query.astype(BF)
        key = turned(k_ref[...], 1.0).astype(BF)
        value = v_ref[...].astype(BF)
        d_att = datt_ref[...]
        start = start_ref[0]
        dk_ref[...] = jnp.zeros_like(dk_ref)
        dv_ref[...] = jnp.zeros_like(dv_ref)
        for head in range(2):
            lanes = slice(head * HEAD_DIM, (head + 1) * HEAD_DIM)
            key_h, value_h = key[:, lanes], value[:, lanes]
            key_t, value_t = key_h.T, value_h.T
            for part in range(rows // block):
                own = slice(part * block, (part + 1) * block)
                length = (part + 1) * block
                query_p = query[own, lanes]
                d_att_p = d_att[own, lanes]
                scores = times_transpose(key_h[:length], query_p)
                place = lax.broadcasted_iota(jnp.int32, (length, block), 0)
                asker = lax.broadcasted_iota(jnp.int32, (length, block), 1) + part * block
                allowed = (place >= start[:, own]) & (place <= asker)
                scores = jnp.where(allowed, scores, -1e30)
                exponent = jnp.exp(scores - jnp.max(scores, axis=0, keepdims=True))
                softmax = exponent * (1.0 / jnp.sum(exponent, axis=0, keepdims=True))
                attention = softmax.astype(BF)
                att_ref[own, lanes] = times(value_t[:, :length], attention).T.astype(BF)
                d_attention = times_transpose(value_h[:length], d_att_p)
                dv_ref[:length, lanes] += times(attention, d_att_p)
                weighted = softmax * d_attention
                d_scores = (
                    weighted - softmax * jnp.sum(weighted, axis=0, keepdims=True)
                ).astype(BF)
                dq_ref[own, lanes] = times(key_t[:, :length], d_scores).T * scaling
                dk_ref[:length, lanes] += times(d_scores, query_p)
        dq_ref[...] = turned(dq_ref[...], -1.0)
        dk_ref[...] = turned(dk_ref[...], -1.0)

    for at, held in enumerate((dq_ref, dk_ref, dv_ref)):

        @pl.when(stage == at)
        def _(held=held):
            piece = held[...].astype(BF)
            dproj_ref[...] = piece
            bsum_ref[0] = jnp.sum(piece.astype(F32), axis=0, keepdims=True)


def attention(projected, turns, d_attended, start, pair, before):
    tokens, width = projected.shape
    pairs, seqs = width // (3 * PAIR), tokens // SEQ
    block = min(256, SEQ)
    wide = lambda at: pl.BlockSpec((SEQ, PAIR), lambda s, j: (s, at * pairs + pair))
    aliases = {6 + k: k for k in range(3)} if before else {}
    return pl.pallas_call(
        functools.partial(attention_kernel, block),
        grid=(seqs, 3),
        in_specs=[
            wide(0),
            wide(1),
            wide(2),
            pl.BlockSpec((3, SEQ, PAIR), lambda s, j: (0, s, 0)),
            pl.BlockSpec((SEQ, PAIR), lambda s, j: (s, pair)),
            pl.BlockSpec((1, 1, SEQ), lambda s, j: (s, 0, 0)),
        ]
        + [pl.BlockSpec(memory_space=pl.ANY)] * len(before),
        out_specs=[
            pl.BlockSpec((SEQ, PAIR), lambda s, j: (s, pair)),
            pl.BlockSpec((SEQ, PAIR), lambda s, j: (s, j * pairs + pair)),
            pl.BlockSpec((1, 1, PAIR), lambda s, j: (s, 0, j * pairs + pair)),
        ],
        out_shape=[
            jax.ShapeDtypeStruct((tokens, pairs * PAIR), BF),
            jax.ShapeDtypeStruct((tokens, width), BF),
            jax.ShapeDtypeStruct((seqs, 1, width), F32),
        ],
        scratch_shapes=[pltpu.VMEM((SEQ, PAIR), F32)] * 3,
        input_output_aliases=aliases,
        compiler_params=pltpu.CompilerParams(vmem_limit_bytes=48 * 2**20),
        name="attention",
    )(projected, projected, projected, turns, d_attended, start, *before)


def shards(
    inputs,
    segments,
    positions,
    ln_gain,
    ln_bias,
    w_qkv,
    b_qkv,
    w_dense,
    b_dense,
    w_fc1,
    b_fc1,
    w_fc2,
    b_fc2,
    cotangent,
):
    reps, group = lax.axis_size("rep"), lax.axis_size("shard")
    rep, place = lax.axis_index("rep"), lax.axis_index("shard")
    core = rep & 1
    tokens, width = inputs.shape
    rows = width // group
    slab = rows // reps
    hidden = w_fc1.shape[1] // group
    pairs = rows // PAIR

    line = Order()
    owners = [(place + hop) % group for hop in range(group)]

    def sends(pieces):
        return [pieces[0]] + [ring(piece, "shard", k + 1) for k, piece in enumerate(pieces[1:])]

    def gathered(array):
        return lax.all_gather(array, "rep", axis=0, tiled=True)

    fc1_pieces = sends(
        line.step(
            lambda w: tuple(
                lax.dynamic_slice(w, (rep * slab, owner * hidden), (slab, hidden))
                for owner in owners
            ),
            w_fc1,
        )
    )
    small = jnp.concatenate(
        [ln_gain, ln_bias, b_qkv, b_dense + b_fc2, positions.astype(F32)]
    ).reshape(1, -1)
    small = doubled(line.hold(small), place)
    gain = small[:, :rows].reshape(width)
    shift = small[:, rows : 2 * rows].reshape(width)
    bias_qkv = lax.dynamic_slice_in_dim(
        small[:, 2 * rows : 5 * rows].reshape(3, width), place * rows, rows, 1
    ).reshape(3 * rows)
    bias_out = small[:, 5 * rows : 6 * rows].reshape(width)
    all_positions = small[:, 6 * rows :].reshape(group * tokens)

    normed = [line.step(lambda *o: ln_forward(*o, reps, group), inputs, gain, shift)]
    normed.append(ring(normed[0], "shard", 1))
    fc1_cols = gathered(line.step(lambda *p: placed(p, place, 0), *fc1_pieces))
    qkv_pieces = sends(
        line.step(
            lambda w: tuple(
                jnp.concatenate(
                    [
                        lax.dynamic_slice(w, (rep * slab, at * width + owner * rows), (slab, rows))
                        for at in range(3)
                    ],
                    axis=1,
                )
                for owner in owners
            ),
            w_qkv,
        )
    )
    qkv_cols = gathered(line.step(lambda *p: placed(p, place, 0), *qkv_pieces))

    def tables(all_positions):
        frequency = 10000.0 ** (-(jnp.arange(ROT // 2, dtype=F32) * 2.0) / ROT)
        angles = frequency[:, None] * all_positions[None, :]
        cosine, sine = jnp.cos(angles).T, jnp.sin(angles).T
        none = jnp.zeros_like(sine)
        still = jnp.zeros((sine.shape[0], HEAD_DIM - ROT), F32)
        return jnp.stack(
            [
                jnp.concatenate([cosine, cosine, still + 1.0] * 2, axis=1),
                jnp.concatenate([-sine, none, still] * 2, axis=1),
                jnp.concatenate([none, sine, still] * 2, axis=1),
            ]
        )

    def start_whole(block):
        whole = jnp.zeros((group * tokens, width), block.dtype)
        return lax.dynamic_update_slice_in_dim(whole, block, place * tokens, 0)

    def put(hop):
        return lambda whole, block: lax.dynamic_update_slice_in_dim(
            whole, block, (place - hop) % group * tokens, 0
        )

    for hop in range(1, group):
        normed[hop] = line.hold(normed[hop])
        if hop + 1 < group:
            normed.append(ring(normed[hop], "shard", 1))
        else:
            cots = [line.hold(cotangent)]
            cots.append(ring(cots[0], "shard", 1))
        if hop == 1:
            turns = line.step(tables, all_positions)
            normed_all = line.step(start_whole, normed[0])
        normed_all = line.step(put(hop), normed_all, normed[hop])
    start = (
        jnp.arange(SEQ, dtype=jnp.int32)[None, None]
        - all_positions.astype(jnp.int32).reshape(-1, 1, SEQ)
    )

    def feed_forward(normed_all, fc1_cols, bias):
        pre_act = times(normed_all, fc1_cols) + bias
        root = (2.0 / jnp.pi) ** 0.5
        square = pre_act * pre_act
        curve = jnp.tanh(root * pre_act * (1.0 + 0.044715 * square))
        activation = (0.5 * pre_act * (1.0 + curve)).astype(BF)
        slope = (
            0.5 * (1.0 + curve)
            + 0.5 * pre_act * (1.0 - curve * curve) * root * (1.0 + 3 * 0.044715 * square)
        ).astype(BF)
        return activation, slope

    for hop in range(1, group):
        if hop == 1:
            activation, slope = line.step(feed_forward, normed_all, fc1_cols, b_fc1)
        if hop == 2:
            projected = line.step(
                lambda a, b, c: times(a, b) + c, normed_all, qkv_cols, bias_qkv
            )
        cots[hop] = line.hold(cots[hop])
        if hop + 1 < group:
            cots.append(ring(cots[hop], "shard", 1))
        if hop == 1:
            cot_all = line.step(start_whole, cots[0])
        cot_all = line.step(put(hop), cot_all, cots[hop])

    def grad(left, right, by_rows=True):
        sent = line.step(
            lambda a, b: half_grads(a, b, 1 - core, reps, by_rows), left, right
        )
        return swap(sent, "rep", 1)

    def grad_sum(left, right, came, parts, by_rows=True):
        own = line.step(
            lambda a, b, c: half_grads(a, b, core, reps, by_rows, c), left, right, came
        )
        halving = Halving(rep, own, parts)
        halving.send(line)
        return halving

    def attend(pair, results):
        return line.step(
            lambda p, d, *r: attention(p, turns, d, start, pair, tuple(r)),
            projected,
            d_attended,
            *results,
        )

    def cut(array, count, owners):
        return line.step(
            lambda a: tuple(
                lax.dynamic_slice_in_dim(a, owner * count, count, 0) for owner in owners
            ),
            array,
        )

    class Passing:
        def __init__(self, array):
            self.own = cut(array, tokens, [(place - hop) % group for hop in range(1, group + 1)])
            self.hop = 1
            self.came = ring(self.own[0], "shard", 1)

        def further(self):
            sent = line.step(
                lambda a, b: (a.astype(F32) + b.astype(F32)).astype(BF),
                self.own[self.hop],
                self.came,
            )
            self.hop += 1
            self.came = ring(sent, "shard", 1)

        def end(self):
            while self.hop + 1 < group:
                self.further()
            return self.own[-1], self.came

    fc2_came = grad(activation, cot_all)
    d_pre = line.step(
        lambda c, w, s: (times_transpose(c, w) * s.astype(F32)).astype(BF), cot_all, w_fc2, slope
    )
    fc2_sum = grad_sum(activation, cot_all, fc2_came, 2)
    fc1_came = grad(normed_all, d_pre)
    d_attended = line.step(lambda c, w: times_transpose(c, w).astype(BF), cot_all, w_dense)
    results = attend(0, ())
    fc1_sum = grad_sum(normed_all, d_pre, fc1_came, 2)
    fc2_sum.further(line)
    if pairs > 1:
        results = attend(1, results)
    fc2_whole = gathered(line.hold(fc2_sum.end(line)))
    for pair in range(2, max(2, pairs - 1)):
        results = attend(pair, results)
    fc1_sum.further(line)
    for pair in range(max(2, pairs - 1), pairs):
        results = attend(pair, results)
    attended, d_projected, d_bias_qkv = results
    fc1_pieces = sends(cut(fc1_sum.end(line), slab, owners))

    qkv_came = grad(normed_all, d_projected)
    dense_came = grad(attended, cot_all, False)
    d_normed_first = line.step(times_transpose, d_pre, fc1_cols)
    fc1_whole = gathered(line.step(lambda *p: placed(p, place, 1), *fc1_pieces))
    d_normed_part = line.step(
        lambda a, b, c: (times_transpose(a, b) + c).astype(BF),
        d_projected,
        qkv_cols,
        d_normed_first,
    )
    d_normed_sum = Passing(d_normed_part)
    qkv_sum = grad_sum(normed_all, d_projected, qkv_came, 2)
    dense_sum = grad_sum(attended, cot_all, dense_came, 1, False)
    out_first = line.step(times, activation, w_fc2)
    d_normed_sum.further()
    out_part = line.step(
        lambda a, b, c: (times(a, b) + c).astype(BF), attended, w_dense, out_first
    )
    qkv_sum.further(line)
    dense_sum.further(line)
    out_sum = Passing(out_part)
    d_normed_sum.further()
    fc2_total = line.step(lambda a: a.astype(F32), fc2_whole)
    qkv_pieces = sends(cut(qkv_sum.end(line), slab, owners))
    dense_piece = line.hold(dense_sum.end(line))
    grad_inputs, norm_sums = line.step(
        lambda x, g, c, *p: ln_backward(x, g, c, p, reps, group),
        inputs,
        gain,
        cotangent,
        *d_normed_sum.end(),
    )

    def last_slab(dense_piece, *pieces):
        qkv_slab = placed([a.reshape(slab, 3, rows) for a in pieces], place, 2)
        dense_slab = dense_piece.reshape(reps, rows // reps, width // reps).transpose(1, 0, 2)
        return jnp.concatenate(
            [qkv_slab.reshape(slab, -1), dense_slab.reshape(slab, width)], axis=1
        )

    last_whole = gathered(line.step(last_slab, dense_piece, *qkv_pieces))
    out_sum.further()

    def all_sums(d_bias_qkv, cotangent, norm_sums, d_pre):
        d_bias_all = lax.dynamic_update_slice_in_dim(
            jnp.zeros((3, width), F32),
            jnp.sum(d_bias_qkv[:, 0], axis=0).reshape(3, rows),
            place * rows,
            1,
        )
        ones = jnp.ones((8, group * tokens), BF)
        return (
            jnp.concatenate(
                [
                    d_bias_all.reshape(group, 3 * rows),
                    jnp.sum(cotangent.astype(F32), axis=0).reshape(group, rows),
                    norm_sums[0].reshape(group, rows),
                    norm_sums[1].reshape(group, rows),
                ],
                axis=1,
            ),
            times(ones, d_pre)[0],
        )

    sums, d_bias_fc1 = line.step(all_sums, d_bias_qkv, cotangent, norm_sums, d_pre)
    came = [
        ring(lax.dynamic_slice_in_dim(sums, owners[hop], 1, 0), "shard", hop)
        for hop in range(1, group)
    ]
    sums = sum(came, lax.dynamic_slice_in_dim(sums, place, 1, 0))[0]
    sums = rep_sum(line.hold(jnp.concatenate([sums, d_bias_fc1])))
    out_sum.further()
    fc1_total = line.step(lambda a: a.astype(F32), fc1_whole)
    block_out = line.step(
        lambda x, b, *p: sum((a.astype(F32) for a in p), x.astype(F32) + b),
        inputs,
        bias_out,
        *out_sum.end(),
    )
    qkv_total, dense_total = line.step(
        lambda a: (
            a[:, : 3 * width].astype(F32),
            a[:, 3 * width :]
            .reshape(reps, slab, reps, width // reps)
            .transpose(2, 1, 0, 3)
            .reshape(rows, width)
            .astype(F32),
        ),
        last_whole,
    )
    cot_total = sums[3 * rows : 4 * rows]
    return (
        block_out,
        grad_inputs,
        sums[4 * rows : 5 * rows],
        sums[5 * rows : 6 * rows],
        qkv_total,
        sums[: 3 * rows],
        dense_total,
        cot_total,
        fc1_total,
        sums[6 * rows :],
        fc2_total,
        cot_total,
    )


def solution(mesh):
    both, shard = P(("rep", "shard")), P("shard")
    wide, held = P(("rep", "shard"), None), P("shard", None)
    return jax.shard_map(
        shards,
        mesh=mesh,
        in_specs=(
            wide, both, both, shard, shard, held, shard, held, shard, held, shard, held, shard, wide
        ),
        out_specs=(
            wide, wide, shard, shard, held, shard, held, shard, held, shard, held, shard
        ),
        check_vma=False,
    )
```

time: 875 us -> 681 us (0.78)
  waiting for transfers between devices: 364 us -> 228 us
  Pallas kernels: 39.8 us -> 111 us
  blocking collectives: 62.4 us -> 0 us
  matrix products: 127 us -> 90.7 us
  starting transfers between devices: 93.1 us -> 60.6 us
    reduce_scatter x4 -> x0, waiting for transfers between devices: 155 us -> none  [reduced(): return lax.psum_scatter(array, 'rep', scatter_dimension=0, tiled=True)]
    pallas_call x1 -> x14, Pallas kernels: 39.8 us -> 111 us  [the longest x8 54.2 us: half_grads(): pl.pallas_call(grad_kernel, grid_spec=pltpu.PrefetchScalarGridSpec(num_sc...]
    all_gather x2 -> x0, blocking collectives: 62.4 us -> none  [the longest x1 46.8 us: shards(): all_positions = lax.all_gather(positions, 'shard', axis=0, tiled=True)]
    ppermute x6 -> x23, waiting for transfers between devices: 7.43 us -> 63 us  [swap(): return lax.ppermute(array, axis, [(i, i ^ bit) for i in range(size)])]
    ppermute x30 -> x27, starting transfers between devices: 87.1 us -> 37.5 us  [ring(): lax.ppermute(array, axis, [(i, (i + distance) % size) for i in range(size)])]
    dot_general x4 -> x0, matrix products: 39.5 us -> none  [contract_rows(): lax.dot_general(left_side, right_side, (((0,), (0,)), ((), ())), preferre...]
    ppermute x30 -> x27, waiting for transfers between devices: 200 us -> 165 us  [ring(): lax.ppermute(array, axis, [(i, (i + distance) % size) for i in range(size)])]
    ppermute x6 -> x23, starting transfers between devices: 5.63 us -> 22.9 us  [swap(): return lax.ppermute(array, axis, [(i, i ^ bit) for i in range(size)])]
  transfers between devices with their start and end apart: 46 -> 55, of which waited for: 25 -> 28; matrix products, arithmetic and copies ran while one was open for 30% -> 30% of each run, Pallas kernels for 5% -> 13%
where the time goes in v2:
time: 681 us; the launch traced here: 671 us
  waiting for transfers between devices  228 us (33%)
  Pallas kernels  111 us (16%)
  local copies, waits for them, and re-layouts  98.1 us (14%)
  matrix products  90.7 us (13%)
  other arithmetic  66.6 us (10%)
  starting transfers between devices  60.6 us (9%)
  between operations  15.4 us (2%)
    ppermute x27, waiting for transfers between devices, ring(): lax.ppermute(array, axis, [(i, (i + distance) % size) for i in range(size)])  165 us
    ppermute x23, waiting for transfers between devices, swap(): return lax.ppermute(array, axis, [(i, i ^ bit) for i in range(size)])  63 us
    pallas_call x8, Pallas kernels, half_grads(): pl.pallas_call(grad_kernel, grid_spec=pltpu.PrefetchScalarGridSpec(num_sc...  54.2 us
    pallas_call x4, Pallas kernels, attention(): pl.pallas_call(functools.partial(attention_kernel, block), grid=(seqs, 3)...  50.3 us
    dot_general x5, matrix products, times(): return jnp.dot(left_side, right_side, preferred_element_type=F32)  46.9 us
    dot_general x4, matrix products, times_transpose(): lax.dot_general(left_side, right_side, (((1,), (1,)), ((), ())), preferre...  43.8 us
    ppermute x27, starting transfers between devices, ring(): lax.ppermute(array, axis, [(i, (i + distance) % size) for i in range(size)])  37.5 us
    unnamed x92, local copies, waits for them, and re-layouts  23.9 us
  transfers between devices with their start and end apart: 55, of which 28 were waited for; matrix products, arithmetic and copies ran while one was open for 30% of the time, Pallas kernels for 13%

profile of v2, /device:TPU:0, one launch (start us, length us, event | category | flops | bytes accessed | tf_op | source)
XLA Modules:
  0.0 670.6 jit_solution(10353269640441819660)
XLA Ops:
  27.7 4.6 collective-permute-done.3
  32.3 8.9 %collective-permute-done.4 = bf16[64,2048]{1,0:T(8,128)(2,1)} collective-permute-done((bf16[64,2048]{1,0:T(8,128)(2,1)}, bf16[64,2048]{1,0:T(8,128)(2,1)}, u32[]{:S(2)}, u32[]{:S(2)}) %collective-permute-start.4) | collective-permute-done | bytes 262176 | tf_op jit(solution)/shard_map/ppermute | solution.py:20
  49.4 6.6 collective-permute-start.8
  57.2 4.1 collective-permute-done.8
  61.3 13.1 %collective-permute-done.7 = bf16[64,1536]{1,0:T(8,128)(2,1)S(1)} collective-permute-done((bf16[64,1536]{1,0:T(8,128)(2,1)S(1)}, bf16[64,1536]{1,0:T(8,128)(2,1)S(1)}, u32[]{:S(2)}, u32[]{:S(2)}) %collective-permute-start.7) | collective-permute-done | bytes 196640 | tf_op jit(solution)/shard_map/ppermute | solution.py:20
  78.3 26.1 %collective-permute-done.2 = bf16[256,2048]{1,0:T(8,128)(2,1)} collective-permute-done((bf16[256,2048]{1,0:T(8,128)(2,1)S(1)}, bf16[256,2048]{1,0:T(8,128)(2,1)}, u32[]{:S(2)}, u32[]{:S(2)}) %collective-permute-start.2) | collective-permute-done | bytes 1048608 | tf_op jit(solution)/shard_map/ppermute | solution.py:20
  109.3 3.4 concatenate.56
  112.7 3.6 concatenate.57
  117.1 3.6 concatenate.55
  132.2 22.5 %collective-permute-done.10 = bf16[256,2048]{1,0:T(8,128)(2,1)} collective-permute-done((bf16[256,2048]{1,0:T(8,128)(2,1)}, bf16[256,2048]{1,0:T(8,128)(2,1)}, u32[]{:S(2)}, u32[]{:S(2)}) %collective-permute-start.10) | collective-permute-done | bytes 1048608 | tf_op jit(solution)/shard_map/ppermute | solution.py:20
  157.1 18.8 %add_convert_fusion.2 = (bf16[1024,2048]{1,0:T(8,128)(2,1)}, bf16[1024,2048]{1,0:T(8,128)(2,1)}) fusion(f32[2048]{0:T(1024)S(1)} %copy-done.37, bf16[1024,2048]{1,0:T(8,128)(2,1)} %constant_dynamic-update-slice_fusion.13.left_ref, bf16[2048,2048]{1,0:T(8,128)(2,1)} %all-gather.8.cloned.1.call-done), kind=kOutput, calls=%fused_computation.3 | convolution fusion | flops 8631877632 | bytes 20979712 | tf_op jit(solution)/shard_map/dot_general | solution.py:41
  184.6 11.7 %convolution_add_fusion.refs_0_.refs_1_.refs_2_ = f32[1024,1536]{1,0:T(8,128)} fusion(bf16[1024,2048]{1,0:T(8,128)(2,1)} %constant_dynamic-update-slice_fusion.13.left_ref, bf16[2048,1536]{1,0:T(8,128)(2,1)} %all-gather.6.cloned.1.call-done, f32[1536]{0:T(1024)S(1)} %reshape.240), kind=kOutput, calls=%fused_computation.7 | convolution fusion | flops 6444023808 | bytes 16783360 | tf_op jit(solution)/shard_map/dot_general | solution.py:41
  196.2 5.8 collective-permute-done.12
  204.4 19.7 %collective-permute-done.13 = bf16[256,2048]{1,0:T(8,128)(2,1)S(1)} collective-permute-done((bf16[256,2048]{1,0:T(8,128)(2,1)}, bf16[256,2048]{1,0:T(8,128)(2,1)S(1)}, u32[]{:S(2)}, u32[]{:S(2)}) %collective-permute-start.13) | collective-permute-done | bytes 1048608 | tf_op jit(solution)/shard_map/ppermute | solution.py:20
  225.1 8.7 %half_grads.8 = bf16[1024,2048]{1,0:T(8,128)(2,1)} custom-call(s32[1]{0:T(128)} %bitcast.5.which_ref, bf16[1024,2048]{1,0:T(8,128)(2,1)} %get-tuple-element.330.left_ref, bf16[1024,2048]{1,0:T(8,128)(2,1)} %constant_dynamic-update-slice_fusion.9.right_ref), custom_call_target="tpu_custom_call" | custom-call | tf_op jit(solution)/shard_map/half_grads/pallas_call | solution.py:193
  233.8 14.5 %multiply_convert_fusion.right_ref = bf16[1024,2048]{1,0:T(8,128)(2,1)} fusion(bf16[1024,2048]{1,0:T(8,128)(2,1)} %get-tuple-element.244, bf16[1024,2048]{1,0:T(8,128)(2,1)} %constant_dynamic-update-slice_fusion.9.right_ref, bf16[2048,2048]{1,0:T(8,128)(2,1)} %param.24), kind=kOutput, calls=%fused_computation.2 | convolution fusion | flops 8596226048 | bytes 20971520 | tf_op jit(solution)/shard_map/dot_general | solution.py:35
  248.4 8.0 %half_grads.9 = bf16[1024,2048]{1,0:T(8,128)(2,1)S(1)} custom-call(s32[1]{0:T(128)} %bitcast.6.which_ref, bf16[1024,2048]{1,0:T(8,128)(2,1)} %get-tuple-element.330.left_ref, bf16[1024,2048]{1,0:T(8,128)(2,1)} %constant_dynamic-update-slice_fusion.9.right_ref, bf16[1024,2048]{1,0:T(8,128)(2,1)} %collective-permute-done.14.refs_0_), custom_call_target="tpu_custom_call" | custom-call | tf_op jit(solution)/shard_map/half_grads/pallas_call | solution.py:193
  259.6 8.7 %half_grads.10 = bf16[1024,2048]{1,0:T(8,128)(2,1)} custom-call(s32[1]{0:T(128)} %bitcast.5.which_ref, bf16[1024,2048]{1,0:T(8,128)(2,1)} %constant_dynamic-update-slice_fusion.13.left_ref, bf16[1024,2048]{1,0:T(8,128)(2,1)} %multiply_convert_fusion.right_ref), custom_call_target="tpu_custom_call" | custom-call | tf_op jit(solution)/shard_map/half_grads/pallas_call | solution.py:193
  273.2 4.7 convolution_convert_fusion.refs_4_
  277.9 12.6 %attention.4 = (bf16[1024,512]{1,0:T(8,128)(2,1)S(1)}, bf16[1024,1536]{1,0:T(8,128)(2,1)}, f32[1,1,1536]{2,1,0:T(1,128)S(1)}) custom-call(f32[1024,1536]{1,0:T(8,128)} %convolution_add_fusion.refs_0_.refs_1_.refs_2_, f32[1024,1536]{1,0:T(8,128)} %convolution_add_fusion.refs_0_.refs_1_.refs_2_, f32[1024,1536]{1,0:T(8,128)} %convolution_add_fusion.refs_0_.refs_1_.refs_2_, ...), custom_call_target="tpu_custom_call" | custom-call | tf_op jit(solution)/shard_map/attention/pallas_call | solution.py:351
  290.5 8.2 %half_grads.11 = bf16[1024,2048]{1,0:T(8,128)(2,1)S(1)} custom-call(s32[1]{0:T(128)} %bitcast.6.which_ref, bf16[1024,2048]{1,0:T(8,128)(2,1)} %constant_dynamic-update-slice_fusion.13.left_ref, bf16[1024,2048]{1,0:T(8,128)(2,1)} %multiply_convert_fusion.right_ref, bf16[1024,2048]{1,0:T(8,128)(2,1)} %collective-permute-done.17.refs_0_), custom_call_target="tpu_custom_call" | custom-call | tf_op jit(solution)/shard_map/half_grads/pallas_call | solution.py:193
  305.8 12.4 %attention.5 = (bf16[1024,512]{1,0:T(8,128)(2,1)S(1)}, bf16[1024,1536]{1,0:T(8,128)(2,1)}, f32[1,1,1536]{2,1,0:T(1,128)S(1)}) custom-call(f32[1024,1536]{1,0:T(8,128)} %convolution_add_fusion.refs_0_.refs_1_.refs_2_, f32[1024,1536]{1,0:T(8,128)} %convolution_add_fusion.refs_0_.refs_1_.refs_2_, ...), custom_call_target="tpu_custom_call", output_to_operand_aliasing={{0}: (6, {}), {1}: (7, {}), {2}: (8, {})} | custom-call | tf_op jit(solution)/shard_map/attention/pallas_call | solution.py:351
  327.0 12.6 %attention.6 = (bf16[1024,512]{1,0:T(8,128)(2,1)S(1)}, bf16[1024,1536]{1,0:T(8,128)(2,1)}, f32[1,1,1536]{2,1,0:T(1,128)S(1)}) custom-call(f32[1024,1536]{1,0:T(8,128)} %convolution_add_fusion.refs_0_.refs_1_.refs_2_, f32[1024,1536]{1,0:T(8,128)} %convolution_add_fusion.refs_0_.refs_1_.refs_2_, ...), custom_call_target="tpu_custom_call", output_to_operand_aliasing={{0}: (6, {}), {1}: (7, {}), {2}: (8, {})} | custom-call | tf_op jit(solution)/shard_map/attention/pallas_call | solution.py:351
  339.5 16.8 %collective-permute-done.21 = bf16[2,128,2048]{2,1,0:T(8,128)(2,1)S(1)} collective-permute-done((bf16[2,128,2048]{2,1,0:T(8,128)(2,1)S(1)}, bf16[2,128,2048]{2,1,0:T(8,128)(2,1)S(1)}, u32[]{:S(2)}, u32[]{:S(2)}) %collective-permute-start.21) | collective-permute-done | bytes 1048608 | tf_op jit(solution)/shard_map/ppermute | solution.py:25
  365.3 12.7 %attention.7 = (bf16[1024,512]{1,0:T(8,128)(2,1)S(1)}, bf16[1024,1536]{1,0:T(8,128)(2,1)}, f32[1,1,1536]{2,1,0:T(1,128)S(1)}) custom-call(f32[1024,1536]{1,0:T(8,128)} %convolution_add_fusion.refs_0_.refs_1_.refs_2_, f32[1024,1536]{1,0:T(8,128)} %convolution_add_fusion.refs_0_.refs_1_.refs_2_, ...), custom_call_target="tpu_custom_call", output_to_operand_aliasing={{0}: (6, {}), {1}: (7, {}), {2}: (8, {})} | custom-call | tf_op jit(solution)/shard_map/attention/pallas_call | solution.py:351
  378.1 7.8 %collective-permute-done.23 = bf16[128,2048]{1,0:T(8,128)(2,1)} collective-permute-done((bf16[128,2048]{1,0:T(8,128)(2,1)}, bf16[128,2048]{1,0:T(8,128)(2,1)}, u32[]{:S(2)}, u32[]{:S(2)}) %collective-permute-start.23) | collective-permute-done | bytes 524320 | tf_op jit(solution)/shard_map/ppermute | solution.py:25
  389.9 6.2 half_grads.12
  397.8 3.8 half_grads.13
  402.1 3.3 collective-permute-start.28
  405.4 13.6 %fusion.25 = f32[1024,2048]{1,0:T(8,128)} fusion(bf16[1024,2048]{1,0:T(8,128)(2,1)S(1)} %copy-done.16, bf16[2048,2048]{1,0:T(8,128)(2,1)} %all-gather.8.cloned.1.call-done), kind=kOutput, calls=%fused_computation.152 | convolution fusion | flops 8589934592 | bytes 20971520 | tf_op jit(solution)/shard_map/dot_general | solution.py:35
  424.4 11.0 %add_convert_fusion.1 = bf16[1024,2048]{1,0:T(8,128)(2,1)S(1)} fusion(f32[1024,2048]{1,0:T(8,128)} %fusion.25, bf16[1024,1536]{1,0:T(8,128)(2,1)} %get-tuple-element.323.right_ref, bf16[2048,1536]{1,0:T(8,128)(2,1)} %all-gather.6.cloned.1.call-done), kind=kOutput, calls=%fused_computation.1 | convolution fusion | flops 6446645248 | bytes 22020096 | tf_op jit(solution)/shard_map/dot_general | solution.py:35
  436.9 5.4 collective-permute-start.29
  442.3 6.7 %half_grads.14 = bf16[1024,1536]{1,0:T(8,128)(2,1)S(1)} custom-call(s32[1]{0:T(128)} %bitcast.6.which_ref, bf16[1024,2048]{1,0:T(8,128)(2,1)} %constant_dynamic-update-slice_fusion.13.left_ref, bf16[1024,1536]{1,0:T(8,128)(2,1)} %get-tuple-element.323.right_ref, bf16[1024,1536]{1,0:T(8,128)(2,1)} %collective-permute-done.25.refs_0_), custom_call_target="tpu_custom_call" | custom-call | tf_op jit(solution)/shard_map/half_grads/pallas_call | solution.py:193
  450.3 3.9 half_grads.15
  455.9 11.2 %fusion.26 = f32[1024,2048]{1,0:T(8,128)S(1)} fusion(bf16[1024,2048]{1,0:T(8,128)(2,1)S(1)} %copy-done.17, bf16[2048,2048]{1,0:T(8,128)(2,1)} %param.24), kind=kOutput, calls=%fused_computation.153 | convolution fusion | flops 8589934592 | bytes 20971520 | tf_op jit(solution)/shard_map/dot_general | solution.py:41
  472.3 21.8 %collective-permute-done.32 = bf16[2,128,1536]{2,1,0:T(8,128)(2,1)S(1)} collective-permute-done((bf16[2,128,1536]{2,1,0:T(8,128)(2,1)S(1)}, bf16[2,128,1536]{2,1,0:T(8,128)(2,1)S(1)}, u32[]{:S(2)}, u32[]{:S(2)}) %collective-permute-start.32) | collective-permute-done | bytes 786464 | tf_op jit(solution)/shard_map/ppermute | solution.py:25
  496.9 6.3 collective-permute-done.30
  508.9 11.7 %convert_element_type.334 = f32[2048,2048]{1,0:T(8,128)} convert(bf16[2048,2048]{1,0:T(8,128)(2,1)} %all-gather.10.cloned.1.call-done) | non-fusion elementwise | flops 4194304 | bytes 25165824 | tf_op jit(solution)/shard_map/convert_element_type | solution.py:613
  522.1 4.1 collective-permute-start.39
  527.2 9.7 %collective-permute-done.41.refs_4_ = bf16[256,2048]{1,0:T(8,128)(2,1)} collective-permute-done((bf16[256,2048]{1,0:T(8,128)(2,1)}, bf16[256,2048]{1,0:T(8,128)(2,1)}, u32[]{:S(2)}, u32[]{:S(2)}) %collective-permute-start.41) | collective-permute-done | bytes 1048608 | tf_op jit(solution)/shard_map/ppermute | solution.py:20
  536.9 5.5 ln_backward.1
  542.4 4.4 collective-permute-done.39
  554.9 4.1 collective-permute-start.33
  559.0 23.1 %collective-permute-done.33 = bf16[256,2048]{1,0:T(8,128)(2,1)} collective-permute-done((bf16[256,2048]{1,0:T(8,128)(2,1)}, bf16[256,2048]{1,0:T(8,128)(2,1)}, u32[]{:S(2)}, u32[]{:S(2)}) %collective-permute-start.33) | collective-permute-done | bytes 1048608 | tf_op jit(solution)/shard_map/ppermute | solution.py:20
  594.7 17.0 %collective-permute-done.43 = f32[1,3072]{1,0:T(1,128)S(1)} collective-permute-done((f32[1,3072]{1,0:T(1,128)S(1)}, f32[1,3072]{1,0:T(1,128)S(1)}, u32[]{:S(2)}, u32[]{:S(2)}) %collective-permute-start.43) | collective-permute-done | bytes 12320 | tf_op jit(solution)/shard_map/ppermute | solution.py:20
  626.0 11.9 %convert_element_type.354 = f32[512,8192]{1,0:T(8,128)} convert(bf16[512,8192]{1,0:T(8,128)(2,1)} %all-gather.12.cloned.1.call-done) | non-fusion elementwise | flops 4194304 | bytes 25165824 | tf_op jit(solution)/shard_map/convert_element_type | solution.py:663
  645.2 9.2 %slice_convert_fusion = f32[512,6144]{1,0:T(8,128)} fusion(bf16[512,8192]{1,0:T(8,128)(2,1)} %all-gather.14.cloned.1.call-done), kind=kLoop, calls=%fused_computation.6 | loop fusion | flops 3145728 | bytes 18874368 | tf_op jit(solution)/shard_map/convert_element_type | solution.py:672
  659.1 4.0 copy.49
  (312 shorter events, 177.3 us)
Async XLA Ops:
  7.2 149.9 %all-gather.8.cloned.1.call-start = ((), (), s32[]{:S(2)}) async-start(), calls=%async_computation.1 | async-start | bytes 9437184 | tf_op jit(solution)/shard_map/all_gather | solution.py:412
  22.5 18.7 %collective-permute-start.4 = (bf16[64,2048]{1,0:T(8,128)(2,1)}, bf16[64,2048]{1,0:T(8,128)(2,1)}, u32[]{:S(2)}, u32[]{:S(2)}) collective-permute-start(bf16[64,2048]{1,0:T(8,128)(2,1)} %get-tuple-element.395), channel_id=1, source_target_pairs={{0,2},{1,3},{2,0},{3,1},{4,6},{5,7},{6,4},{7,5},{8,10},{9,11},{10,... | collective-permute-start | bytes 786440 | tf_op jit(solution)/shard_map/ppermute | solution.py:20
  22.8 18.4 %collective-permute-start.5 = (bf16[64,2048]{1,0:T(8,128)(2,1)}, bf16[64,2048]{1,0:T(8,128)(2,1)}, u32[]{:S(2)}, u32[]{:S(2)}) collective-permute-start(bf16[64,2048]{1,0:T(8,128)(2,1)} %get-tuple-element.392), channel_id=1, source_target_pairs={{0,3},{1,0},{2,1},{3,2},{4,7},{5,4},{6,5},{7,6},{8,11},{9,8},{10,9... | collective-permute-start | bytes 786440 | tf_op jit(solution)/shard_map/ppermute | solution.py:20
  48.0 136.6 %all-gather.6.cloned.1.call-start = ((), (), s32[]{:S(2)}) async-start(), calls=%async_computation | async-start | bytes 7077888 | tf_op jit(solution)/shard_map/all_gather | solution.py:412
  56.0 18.4 %collective-permute-start.7 = (bf16[64,1536]{1,0:T(8,128)(2,1)S(1)}, bf16[64,1536]{1,0:T(8,128)(2,1)S(1)}, u32[]{:S(2)}, u32[]{:S(2)}) collective-permute-start(bf16[64,1536]{1,0:T(8,128)(2,1)S(1)} %pad_maximum_fusion.6), channel_id=1, source_target_pairs={{0,2},{1,3},{2,0},{3,1},{4,6},{5,7},{6,4},{7,5},{8,10},{9,11},{10,... | collective-permute-start | bytes 589832 | tf_op jit(solution)/shard_map/ppermute | solution.py:20
  57.1 17.3 %collective-permute-start.6 = (bf16[64,1536]{1,0:T(8,128)(2,1)S(1)}, bf16[64,1536]{1,0:T(8,128)(2,1)S(1)}, u32[]{:S(2)}, u32[]{:S(2)}) collective-permute-start(bf16[64,1536]{1,0:T(8,128)(2,1)S(1)} %pad_maximum_fusion.5), channel_id=1, source_target_pairs={{0,1},{1,2},{2,3},{3,0},{4,5},{5,6},{6,7},{7,4},{8,9},{9,10},{10,1... | collective-permute-start | bytes 589832 | tf_op jit(solution)/shard_map/ppermute | solution.py:20
  78.2 430.7 %all-gather.10.cloned.1.call-start = ((), (), s32[]{:S(2)}) async-start(), calls=%async_computation.2 | async-start | bytes 9437184 | tf_op jit(solution)/shard_map/all_gather | solution.py:412
  78.2 26.2 %collective-permute-start.2 = (bf16[256,2048]{1,0:T(8,128)(2,1)S(1)}, bf16[256,2048]{1,0:T(8,128)(2,1)}, u32[]{:S(2)}, u32[]{:S(2)}) collective-permute-start(bf16[256,2048]{1,0:T(8,128)(2,1)S(1)} %ln_forward.1), channel_id=1, source_target_pairs={{0,1},{1,2},{2,3},{3,0},{4,5},{5,6},{6,7},{7,4},{8,9},{9,10},{10,1... | collective-permute-start | bytes 3145736 | tf_op jit(solution)/shard_map/ppermute | solution.py:20
  104.4 25.4 %collective-permute-start.9 = (bf16[256,2048]{1,0:T(8,128)(2,1)}, bf16[256,2048]{1,0:T(8,128)(2,1)}, u32[]{:S(2)}, u32[]{:S(2)}) collective-permute-start(bf16[256,2048]{1,0:T(8,128)(2,1)} %collective-permute-done.2), channel_id=1, source_target_pairs={{0,1},{1,2},{2,3},{3,0},{4,5},{5,6},{6,7},{7,4},{8,9},{9,10},{10,1... | collective-permute-start | bytes 3145736 | tf_op jit(solution)/shard_map/ppermute | solution.py:20
  129.9 24.9 %collective-permute-start.10 = (bf16[256,2048]{1,0:T(8,128)(2,1)}, bf16[256,2048]{1,0:T(8,128)(2,1)}, u32[]{:S(2)}, u32[]{:S(2)}) collective-permute-start(bf16[256,2048]{1,0:T(8,128)(2,1)} %collective-permute-done.9), channel_id=1, source_target_pairs={{0,1},{1,2},{2,3},{3,0},{4,5},{5,6},{6,7},{7,4},{8,9},{9,10},{10,1... | collective-permute-start | bytes 3145736 | tf_op jit(solution)/shard_map/ppermute | solution.py:20
  154.7 23.8 %collective-permute-start.11 = (bf16[256,2048]{1,0:T(8,128)(2,1)S(1)}, bf16[256,2048]{1,0:T(8,128)(2,1)}, u32[]{:S(2)}, u32[]{:S(2)}) collective-permute-start(bf16[256,2048]{1,0:T(8,128)(2,1)S(1)} %copy-done.18), channel_id=1, source_target_pairs={{0,1},{1,2},{2,3},{3,0},{4,5},{5,6},{6,7},{7,4},{8,9},{9,10},{10,1... | collective-permute-start | bytes 3145736 | tf_op jit(solution)/shard_map/ppermute | solution.py:20
  178.5 23.5 %collective-permute-start.12 = (bf16[256,2048]{1,0:T(8,128)(2,1)}, bf16[256,2048]{1,0:T(8,128)(2,1)}, u32[]{:S(2)}, u32[]{:S(2)}) collective-permute-start(bf16[256,2048]{1,0:T(8,128)(2,1)} %collective-permute-done.11), channel_id=1, source_target_pairs={{0,1},{1,2},{2,3},{3,0},{4,5},{5,6},{6,7},{7,4},{8,9},{9,10},{10,1... | collective-permute-start | bytes 3145736 | tf_op jit(solution)/shard_map/ppermute | solution.py:20
  202.0 22.1 %collective-permute-start.13 = (bf16[256,2048]{1,0:T(8,128)(2,1)}, bf16[256,2048]{1,0:T(8,128)(2,1)S(1)}, u32[]{:S(2)}, u32[]{:S(2)}) collective-permute-start(bf16[256,2048]{1,0:T(8,128)(2,1)} %collective-permute-done.12), channel_id=1, source_target_pairs={{0,1},{1,2},{2,3},{3,0},{4,5},{5,6},{6,7},{7,4},{8,9},{9,10},{10,1... | collective-permute-start | bytes 3145736 | tf_op jit(solution)/shard_map/ppermute | solution.py:20
  233.8 14.6 %collective-permute-start.14 = (bf16[1024,2048]{1,0:T(8,128)(2,1)}, bf16[1024,2048]{1,0:T(8,128)(2,1)}, u32[]{:S(2)}, u32[]{:S(2)}) collective-permute-start(bf16[1024,2048]{1,0:T(8,128)(2,1)} %half_grads.8), channel_id=1, source_target_pairs={{0,4},{4,0},{8,12},{12,8},{16,20},{20,16},{24,28},{28,24},{1,5},{5... | collective-permute-start | bytes 12582920 | tf_op jit(solution)/shard_map/ppermute | solution.py:25
  268.2 22.3 %collective-permute-start.17 = (bf16[1024,2048]{1,0:T(8,128)(2,1)}, bf16[1024,2048]{1,0:T(8,128)(2,1)}, u32[]{:S(2)}, u32[]{:S(2)}) collective-permute-start(bf16[1024,2048]{1,0:T(8,128)(2,1)} %half_grads.10), channel_id=1, source_target_pairs={{0,4},{4,0},{8,12},{12,8},{16,20},{20,16},{24,28},{28,24},{1,5},{5... | collective-permute-start | bytes 12582920 | tf_op jit(solution)/shard_map/ppermute | solution.py:25
  268.7 31.1 %collective-permute-start.15 = (bf16[2,128,2048]{2,1,0:T(8,128)(2,1)}, bf16[2,128,2048]{2,1,0:T(8,128)(2,1)S(1)}, u32[]{:S(2)}, u32[]{:S(2)}) collective-permute-start(bf16[2,128,2048]{2,1,0:T(8,128)(2,1)} %dynamic-slice_bitcast_fusion.3), channel_id=1, source_target_pairs={{0,8},{4,12},{8,0},{12,4},{16,24},{20,28},{24,16},{28,20},{1,9},{5... | collective-permute-start | bytes 3145736 | tf_op jit(solution)/shard_map/ppermute | solution.py:25
  271.6 28.3 %collective-permute-start.16 = (bf16[2,128,2048]{2,1,0:T(8,128)(2,1)S(1)}, bf16[2,128,2048]{2,1,0:T(8,128)(2,1)}, u32[]{:S(2)}, u32[]{:S(2)}) collective-permute-start(bf16[2,128,2048]{2,1,0:T(8,128)(2,1)S(1)} %dynamic-slice_bitcast_fusion.2), channel_id=1, source_target_pairs={{0,16},{4,20},{8,24},{12,28},{16,0},{20,4},{24,8},{28,12},{1,17},{... | collective-permute-start | bytes 3145736 | tf_op jit(solution)/shard_map/ppermute | solution.py:25
  304.7 13.5 %collective-permute-start.19 = (bf16[128,2048]{1,0:T(8,128)(2,1)S(1)}, bf16[128,2048]{1,0:T(8,128)(2,1)S(1)}, u32[]{:S(2)}, u32[]{:S(2)}) collective-permute-start(bf16[128,2048]{1,0:T(8,128)(2,1)S(1)} %dynamic-slice_bitcast_fusion.9), channel_id=1, source_target_pairs={{0,8},{4,12},{8,0},{12,4},{16,24},{20,28},{24,16},{28,20},{1,9},{5... | collective-permute-start | bytes 1572872 | tf_op jit(solution)/shard_map/ppermute | solution.py:25
  305.3 13.1 %collective-permute-start.18 = (bf16[128,2048]{1,0:T(8,128)(2,1)S(1)}, bf16[128,2048]{1,0:T(8,128)(2,1)S(1)}, u32[]{:S(2)}, u32[]{:S(2)}) collective-permute-start(bf16[128,2048]{1,0:T(8,128)(2,1)S(1)} %dynamic-slice_bitcast_fusion.10), channel_id=1, source_target_pairs={{0,16},{4,20},{8,24},{12,28},{16,0},{20,4},{24,8},{28,12},{1,17},{... | collective-permute-start | bytes 1572872 | tf_op jit(solution)/shard_map/ppermute | solution.py:25
  319.8 306.2 %all-gather.12.cloned.1.call-start = ((), (), s32[]{:S(2)}) async-start(), calls=%async_computation.3 | async-start | bytes 9437184 | tf_op jit(solution)/shard_map/all_gather | solution.py:412
  321.2 35.1 %collective-permute-start.21 = (bf16[2,128,2048]{2,1,0:T(8,128)(2,1)S(1)}, bf16[2,128,2048]{2,1,0:T(8,128)(2,1)S(1)}, u32[]{:S(2)}, u32[]{:S(2)}) collective-permute-start(bf16[2,128,2048]{2,1,0:T(8,128)(2,1)S(1)} %dynamic-slice_bitcast_fusion), channel_id=1, source_target_pairs={{0,16},{4,20},{8,24},{12,28},{16,0},{20,4},{24,8},{28,12},{1,17},{... | collective-permute-start | bytes 3145736 | tf_op jit(solution)/shard_map/ppermute | solution.py:25
  322.6 35.2 %collective-permute-start.20 = (bf16[2,128,2048]{2,1,0:T(8,128)(2,1)}, bf16[2,128,2048]{2,1,0:T(8,128)(2,1)S(1)}, u32[]{:S(2)}, u32[]{:S(2)}) collective-permute-start(bf16[2,128,2048]{2,1,0:T(8,128)(2,1)} %dynamic-slice_bitcast_fusion.1), channel_id=1, source_target_pairs={{0,8},{4,12},{8,0},{12,4},{16,24},{20,28},{24,16},{28,20},{1,9},{5... | collective-permute-start | bytes 3145736 | tf_op jit(solution)/shard_map/ppermute | solution.py:25
  360.7 25.2 %collective-permute-start.23 = (bf16[128,2048]{1,0:T(8,128)(2,1)}, bf16[128,2048]{1,0:T(8,128)(2,1)}, u32[]{:S(2)}, u32[]{:S(2)}) collective-permute-start(bf16[128,2048]{1,0:T(8,128)(2,1)} %dynamic-slice_bitcast_fusion.7), channel_id=1, source_target_pairs={{0,8},{4,12},{8,0},{12,4},{16,24},{20,28},{24,16},{28,20},{1,9},{5... | collective-permute-start | bytes 1572872 | tf_op jit(solution)/shard_map/ppermute | solution.py:25
  362.2 25.1 %collective-permute-start.22 = (bf16[128,2048]{1,0:T(8,128)(2,1)}, bf16[128,2048]{1,0:T(8,128)(2,1)}, u32[]{:S(2)}, u32[]{:S(2)}) collective-permute-start(bf16[128,2048]{1,0:T(8,128)(2,1)} %dynamic-slice_bitcast_fusion.8), channel_id=1, source_target_pairs={{0,16},{4,20},{8,24},{12,28},{16,0},{20,4},{24,8},{28,12},{1,17},{... | collective-permute-start | bytes 1572872 | tf_op jit(solution)/shard_map/ppermute | solution.py:25
  401.6 17.5 %collective-permute-start.26 = (bf16[64,2048]{1,0:T(8,128)(2,1)S(1)}, bf16[64,2048]{1,0:T(8,128)(2,1)S(1)}, u32[]{:S(2)}, u32[]{:S(2)}) collective-permute-start(bf16[64,2048]{1,0:T(8,128)(2,1)S(1)} %get-tuple-element.418), channel_id=1, source_target_pairs={{0,1},{1,2},{2,3},{3,0},{4,5},{5,6},{6,7},{7,4},{8,9},{9,10},{10,1... | collective-permute-start | bytes 786440 | tf_op jit(solution)/shard_map/ppermute | solution.py:20
  401.6 18.1 %collective-permute-start.27 = (bf16[64,2048]{1,0:T(8,128)(2,1)S(1)}, bf16[64,2048]{1,0:T(8,128)(2,1)S(1)}, u32[]{:S(2)}, u32[]{:S(2)}) collective-permute-start(bf16[64,2048]{1,0:T(8,128)(2,1)S(1)} %get-tuple-element.417), channel_id=1, source_target_pairs={{0,2},{1,3},{2,0},{3,1},{4,6},{5,7},{6,4},{7,5},{8,10},{9,11},{10,... | collective-permute-start | bytes 786440 | tf_op jit(solution)/shard_map/ppermute | solution.py:20
  402.1 17.6 %collective-permute-start.28 = (bf16[64,2048]{1,0:T(8,128)(2,1)S(1)}, bf16[64,2048]{1,0:T(8,128)(2,1)S(1)}, u32[]{:S(2)}, u32[]{:S(2)}) collective-permute-start(bf16[64,2048]{1,0:T(8,128)(2,1)S(1)} %get-tuple-element.416), channel_id=1, source_target_pairs={{0,3},{1,0},{2,1},{3,2},{4,7},{5,4},{6,5},{7,6},{8,11},{9,8},{10,9... | collective-permute-start | bytes 786440 | tf_op jit(solution)/shard_map/ppermute | solution.py:20
  423.8 219.3 %all-gather.14.cloned.1.call-start = ((), (), s32[]{:S(2)}) async-start(), calls=%async_computation.4 | async-start | bytes 9437184 | tf_op jit(solution)/shard_map/all_gather | solution.py:412
  423.8 18.5 %collective-permute-start.25 = (bf16[1024,1536]{1,0:T(8,128)(2,1)}, bf16[1024,1536]{1,0:T(8,128)(2,1)}, u32[]{:S(2)}, u32[]{:S(2)}) collective-permute-start(bf16[1024,1536]{1,0:T(8,128)(2,1)} %copy-done.13), channel_id=1, source_target_pairs={{0,4},{4,0},{8,12},{12,8},{16,20},{20,16},{24,28},{28,24},{1,5},{5... | collective-permute-start | bytes 9437192 | tf_op jit(solution)/shard_map/ppermute | solution.py:25
  424.0 26.4 %collective-permute-start.24 = (bf16[2048,256]{1,0:T(8,128)(2,1)}, bf16[2048,256]{1,0:T(8,128)(2,1)S(1)}, u32[]{:S(2)}, u32[]{:S(2)}) collective-permute-start(bf16[2048,256]{1,0:T(8,128)(2,1)} %copy-done.14), channel_id=1, source_target_pairs={{0,4},{4,0},{8,12},{12,8},{16,20},{20,16},{24,28},{28,24},{1,5},{5... | collective-permute-start | bytes 3145736 | tf_op jit(solution)/shard_map/ppermute | solution.py:25
  436.9 30.2 %collective-permute-start.29 = (bf16[256,2048]{1,0:T(8,128)(2,1)S(1)}, bf16[256,2048]{1,0:T(8,128)(2,1)}, u32[]{:S(2)}, u32[]{:S(2)}) collective-permute-start(bf16[256,2048]{1,0:T(8,128)(2,1)S(1)} %get-tuple-element.411), channel_id=1, source_target_pairs={{0,1},{1,2},{2,3},{3,0},{4,5},{5,6},{6,7},{7,4},{8,9},{9,10},{10,1... | collective-permute-start | bytes 3145736 | tf_op jit(solution)/shard_map/ppermute | solution.py:20
  450.0 44.1 %collective-permute-start.31 = (bf16[2,128,1536]{2,1,0:T(8,128)(2,1)}, bf16[2,128,1536]{2,1,0:T(8,128)(2,1)}, u32[]{:S(2)}, u32[]{:S(2)}) collective-permute-start(bf16[2,128,1536]{2,1,0:T(8,128)(2,1)} %dynamic-slice_bitcast_fusion.5), channel_id=1, source_target_pairs={{0,8},{4,12},{8,0},{12,4},{16,24},{20,28},{24,16},{28,20},{1,9},{5... | collective-permute-start | bytes 2359304 | tf_op jit(solution)/shard_map/ppermute | solution.py:25
  454.3 48.9 %collective-permute-start.30 = (bf16[2,512,256]{2,1,0:T(8,128)(2,1)S(1)}, bf16[2,512,256]{2,1,0:T(8,128)(2,1)S(1)}, u32[]{:S(2)}, u32[]{:S(2)}) collective-permute-start(bf16[2,512,256]{2,1,0:T(8,128)(2,1)S(1)} %dynamic-slice_bitcast_fusion.6), channel_id=1, source_target_pairs={{0,8},{4,12},{8,0},{12,4},{16,24},{20,28},{24,16},{28,20},{1,9},{5... | collective-permute-start | bytes 1572872 | tf_op jit(solution)/shard_map/ppermute | solution.py:25
  468.8 38.4 %collective-permute-start.37 = (bf16[256,2048]{1,0:T(8,128)(2,1)S(1)}, bf16[256,2048]{1,0:T(8,128)(2,1)S(1)}, u32[]{:S(2)}, u32[]{:S(2)}) collective-permute-start(bf16[256,2048]{1,0:T(8,128)(2,1)S(1)} %add_convert_fusion.6), channel_id=1, source_target_pairs={{0,1},{1,2},{2,3},{3,0},{4,5},{5,6},{6,7},{7,4},{8,9},{9,10},{10,1... | collective-permute-start | bytes 3145736 | tf_op jit(solution)/shard_map/ppermute | solution.py:20
  469.5 24.6 %collective-permute-start.32 = (bf16[2,128,1536]{2,1,0:T(8,128)(2,1)S(1)}, bf16[2,128,1536]{2,1,0:T(8,128)(2,1)S(1)}, u32[]{:S(2)}, u32[]{:S(2)}) collective-permute-start(bf16[2,128,1536]{2,1,0:T(8,128)(2,1)S(1)} %dynamic-slice_bitcast_fusion.4), channel_id=1, source_target_pairs={{0,16},{4,20},{8,24},{12,28},{16,0},{20,4},{24,8},{28,12},{1,17},{... | collective-permute-start | bytes 2359304 | tf_op jit(solution)/shard_map/ppermute | solution.py:25
  496.6 24.0 %collective-permute-start.35 = (bf16[128,1536]{1,0:T(8,128)(2,1)}, bf16[128,1536]{1,0:T(8,128)(2,1)S(1)}, u32[]{:S(2)}, u32[]{:S(2)}) collective-permute-start(bf16[128,1536]{1,0:T(8,128)(2,1)} %dynamic-slice_bitcast_fusion.12), channel_id=1, source_target_pairs={{0,16},{4,20},{8,24},{12,28},{16,0},{20,4},{24,8},{28,12},{1,17},{... | collective-permute-start | bytes 1179656 | tf_op jit(solution)/shard_map/ppermute | solution.py:25
  503.4 18.6 %collective-permute-start.34 = (bf16[512,256]{1,0:T(8,128)(2,1)S(1)}, bf16[512,256]{1,0:T(8,128)(2,1)}, u32[]{:S(2)}, u32[]{:S(2)}) collective-permute-start(bf16[512,256]{1,0:T(8,128)(2,1)S(1)} %dynamic-slice_bitcast_fusion.13), channel_id=1, source_target_pairs={{0,16},{4,20},{8,24},{12,28},{16,0},{20,4},{24,8},{28,12},{1,17},{... | collective-permute-start | bytes 786440 | tf_op jit(solution)/shard_map/ppermute | solution.py:25
  504.4 16.2 %collective-permute-start.36 = (bf16[128,1536]{1,0:T(8,128)(2,1)}, bf16[128,1536]{1,0:T(8,128)(2,1)}, u32[]{:S(2)}, u32[]{:S(2)}) collective-permute-start(bf16[128,1536]{1,0:T(8,128)(2,1)} %dynamic-slice_bitcast_fusion.11), channel_id=1, source_target_pairs={{0,8},{4,12},{8,0},{12,4},{16,24},{20,28},{24,16},{28,20},{1,9},{5... | collective-permute-start | bytes 1179656 | tf_op jit(solution)/shard_map/ppermute | solution.py:25
  508.6 28.4 %collective-permute-start.41 = (bf16[256,2048]{1,0:T(8,128)(2,1)}, bf16[256,2048]{1,0:T(8,128)(2,1)}, u32[]{:S(2)}, u32[]{:S(2)}) collective-permute-start(bf16[256,2048]{1,0:T(8,128)(2,1)} %add_convert_fusion.5), channel_id=1, source_target_pairs={{0,1},{1,2},{2,3},{3,0},{4,5},{5,6},{6,7},{7,4},{8,9},{9,10},{10,1... | collective-permute-start | bytes 3145736 | tf_op jit(solution)/shard_map/ppermute | solution.py:20
  522.0 20.4 %collective-permute-start.38 = (bf16[64,1536]{1,0:T(8,128)(2,1)S(1)}, bf16[64,1536]{1,0:T(8,128)(2,1)S(1)}, u32[]{:S(2)}, u32[]{:S(2)}) collective-permute-start(bf16[64,1536]{1,0:T(8,128)(2,1)S(1)} %get-tuple-element.422), channel_id=1, source_target_pairs={{0,1},{1,2},{2,3},{3,0},{4,5},{5,6},{6,7},{7,4},{8,9},{9,10},{10,1... | collective-permute-start | bytes 589832 | tf_op jit(solution)/shard_map/ppermute | solution.py:20
  522.1 24.7 %collective-permute-start.39 = (bf16[64,1536]{1,0:T(8,128)(2,1)S(1)}, bf16[64,1536]{1,0:T(8,128)(2,1)S(1)}, u32[]{:S(2)}, u32[]{:S(2)}) collective-permute-start(bf16[64,1536]{1,0:T(8,128)(2,1)S(1)} %get-tuple-element.421), channel_id=1, source_target_pairs={{0,2},{1,3},{2,0},{3,1},{4,6},{5,7},{6,4},{7,5},{8,10},{9,11},{10,... | collective-permute-start | bytes 589832 | tf_op jit(solution)/shard_map/ppermute | solution.py:20
  526.2 20.7 %collective-permute-start.40 = (bf16[64,1536]{1,0:T(8,128)(2,1)S(1)}, bf16[64,1536]{1,0:T(8,128)(2,1)S(1)}, u32[]{:S(2)}, u32[]{:S(2)}) collective-permute-start(bf16[64,1536]{1,0:T(8,128)(2,1)S(1)} %get-tuple-element.420), channel_id=1, source_target_pairs={{0,3},{1,0},{2,1},{3,2},{4,7},{5,4},{6,5},{7,6},{8,11},{9,8},{10,9... | collective-permute-start | bytes 589832 | tf_op jit(solution)/shard_map/ppermute | solution.py:20
  554.9 27.2 %collective-permute-start.33 = (bf16[256,2048]{1,0:T(8,128)(2,1)}, bf16[256,2048]{1,0:T(8,128)(2,1)}, u32[]{:S(2)}, u32[]{:S(2)}) collective-permute-start(bf16[256,2048]{1,0:T(8,128)(2,1)} %get-tuple-element.412), channel_id=1, source_target_pairs={{0,1},{1,2},{2,3},{3,0},{4,5},{5,6},{6,7},{7,4},{8,9},{9,10},{10,1... | collective-permute-start | bytes 3145736 | tf_op jit(solution)/shard_map/ppermute | solution.py:20
  585.0 27.1 %collective-permute-start.42 = (bf16[256,2048]{1,0:T(8,128)(2,1)}, bf16[256,2048]{1,0:T(8,128)(2,1)}, u32[]{:S(2)}, u32[]{:S(2)}) collective-permute-start(bf16[256,2048]{1,0:T(8,128)(2,1)} %add_convert_fusion.4), channel_id=1, source_target_pairs={{0,1},{1,2},{2,3},{3,0},{4,5},{5,6},{6,7},{7,4},{8,9},{9,10},{10,1... | collective-permute-start | bytes 3145736 | tf_op jit(solution)/shard_map/ppermute | solution.py:20
  587.8 24.0 %collective-permute-start.43 = (f32[1,3072]{1,0:T(1,128)S(1)}, f32[1,3072]{1,0:T(1,128)S(1)}, u32[]{:S(2)}, u32[]{:S(2)}) collective-permute-start(f32[1,3072]{1,0:T(1,128)S(1)} %get-tuple-element.429), channel_id=1, source_target_pairs={{0,1},{1,2},{2,3},{3,0},{4,5},{5,6},{6,7},{7,4},{8,9},{9,10},{10,1... | collective-permute-start | bytes 36872 | tf_op jit(solution)/shard_map/ppermute | solution.py:20
  588.1 23.9 %collective-permute-start.44 = (f32[1,3072]{1,0:T(1,128)S(1)}, f32[1,3072]{1,0:T(1,128)S(1)}, u32[]{:S(2)}, u32[]{:S(2)}) collective-permute-start(f32[1,3072]{1,0:T(1,128)S(1)} %get-tuple-element.431), channel_id=1, source_target_pairs={{0,2},{1,3},{2,0},{3,1},{4,6},{5,7},{6,4},{7,5},{8,10},{9,11},{10,... | collective-permute-start | bytes 36872 | tf_op jit(solution)/shard_map/ppermute | solution.py:20
  589.9 22.1 %collective-permute-start.45 = (f32[1,3072]{1,0:T(1,128)S(1)}, f32[1,3072]{1,0:T(1,128)S(1)}, u32[]{:S(2)}, u32[]{:S(2)}) collective-permute-start(f32[1,3072]{1,0:T(1,128)S(1)} %get-tuple-element.430), channel_id=1, source_target_pairs={{0,3},{1,0},{2,1},{3,2},{4,7},{5,4},{6,5},{7,6},{8,11},{9,8},{10,9... | collective-permute-start | bytes 36872 | tf_op jit(solution)/shard_map/ppermute | solution.py:20
  614.7 25.4 %collective-permute-start.46 = (bf16[256,2048]{1,0:T(8,128)(2,1)}, bf16[256,2048]{1,0:T(8,128)(2,1)}, u32[]{:S(2)}, u32[]{:S(2)}) collective-permute-start(bf16[256,2048]{1,0:T(8,128)(2,1)} %add_convert_fusion.3), channel_id=1, source_target_pairs={{0,1},{1,2},{2,3},{3,0},{4,5},{5,6},{6,7},{7,4},{8,9},{9,10},{10,1... | collective-permute-start | bytes 3145736 | tf_op jit(solution)/shard_map/ppermute | solution.py:20
  (45 other events, 774.8 us)
Sparse Core Ops, SparseCore 0:
  48.1 58.5 all-gather.7
  109.2 45.5 all-gather.5
  319.9 75.0 all-gather.9
  423.9 77.4 all-gather.11
  555.0 56.3 all-gather.13

commit v3 on v2

v3 whole, which is shorter than its diff:
```python
import functools

import jax
import jax.numpy as jnp
from jax import lax
from jax.experimental import pallas as pl
from jax.experimental.pallas import tpu as pltpu
from jax.sharding import PartitionSpec as P

HEAD_DIM = 64
ROT = 32
SEQ = 1024
PAIR = 2 * HEAD_DIM
BF = jnp.bfloat16
F32 = jnp.float32
ROOM = pltpu.CompilerParams(vmem_limit_bytes=56 * 2**20)
ANY = pl.BlockSpec(memory_space=pl.ANY)


def ring(array, axis, distance):
    size = lax.axis_size(axis)
    return lax.ppermute(array, axis, [(i, (i + distance) % size) for i in range(size)])


def swap(array, axis, mask):
    size = lax.axis_size(axis)
    return lax.ppermute(array, axis, [(i, i ^ mask) for i in range(size)])


def contract_rows(left_side, right_side):
    return lax.dot_general(
        left_side, right_side, (((0,), (0,)), ((), ())), preferred_element_type=F32
    )


def times_transpose(left_side, right_side):
    return lax.dot_general(
        left_side, right_side, (((1,), (1,)), ((), ())), preferred_element_type=F32
    )


def times(left_side, right_side):
    return jnp.dot(left_side, right_side, preferred_element_type=F32)


class Order:
    def __init__(self):
        self.last = None

    def step(self, work, *operands):
        if self.last is not None:
            operands, _ = lax.optimization_barrier((operands, self.last))
        result = work(*operands)
        self.last = jax.tree.leaves(result)
        return result

    def hold(self, array):
        return self.step(lambda a: a, array)


def doubled(row, place, line):
    bit = 1
    while bit < lax.axis_size("shard"):
        row = line.hold(row)
        other = swap(row, "shard", bit)
        upper = (place & bit) > 0
        row = jnp.concatenate([jnp.where(upper, other, row), jnp.where(upper, row, other)])
        bit *= 2
    return row


def owned_sum(line, values, place):
    bit = lax.axis_size("shard") >> 1
    while bit:
        upper = ((place & bit) > 0).astype(jnp.int32)
        count = values.shape[0] // 2
        sent, kept = (
            lax.dynamic_slice_in_dim(values, side * count, count, 0) for side in (1 - upper, upper)
        )
        values = line.hold(kept + swap(sent, "shard", bit))
        bit >>= 1
    return values[0]


class Halving:
    def __init__(self, rep, array, parts):
        count = lax.axis_size("rep").bit_length() - 2
        self.rep = rep
        array = array.reshape((2,) * count + (array.shape[0] >> count,) + array.shape[1:])
        rows = array.shape[count] // parts
        self.arrays = [array] * parts
        self.spans = [(part * rows, rows) for part in range(parts)]
        bits = list(range(count, 0, -1))
        self.bits = [list(bits) for _ in range(parts)]
        self.todo = [
            bits[::-1][part % count :] + bits[::-1][: part % count] for part in range(parts)
        ]

    def pick(self, part, array, mine):
        axis = self.bits[part].index(self.todo[part][0])
        bit = (self.rep >> self.todo[part][0]) & 1
        starts, sizes = [0] * array.ndim, list(array.shape)
        starts[axis], sizes[axis] = (bit if mine else 1 - bit), 1
        starts[len(self.bits[part])], sizes[len(self.bits[part])] = self.spans[part]
        half = lax.dynamic_slice(array, starts, sizes)
        return half.reshape(half.shape[:axis] + half.shape[axis + 1 :])

    def outgoing(self, *arrays):
        return tuple(self.pick(part, array, False) for part, array in enumerate(arrays))

    def added(self, *operands):
        count = len(operands) // 2
        return tuple(
            (self.pick(part, operands[part], True).astype(F32) + operands[count + part].astype(F32))
            .astype(BF)
            for part in range(count)
        )

    def send(self, line):
        sent = line.step(self.outgoing, *self.arrays)
        self.came = [
            swap(piece, "rep", 1 << todo[0]) for piece, todo in zip(sent, self.todo)
        ]

    def take(self, line):
        self.arrays = line.step(self.added, *self.arrays, *self.came)
        for part, todo in enumerate(self.todo):
            self.bits[part].remove(todo[0])
            self.todo[part] = todo[1:]
            self.spans[part] = (0, self.spans[part][1])

    def further(self, line):
        self.take(line)
        self.send(line)

    def end(self, line):
        while len(self.todo[0]) > 1:
            self.further(line)
        self.take(line)
        return jnp.concatenate(self.arrays, axis=0)


class Passing:
    def __init__(self, line, array, tokens):
        self.line, self.group = line, array.shape[0] // tokens
        self.block = lambda hop: (hop % self.group * tokens, tokens)
        self.array, self.hop = array, 1
        sent = line.step(lambda a: lax.slice_in_dim(a, tokens, 2 * tokens, axis=0), array)
        self.came = ring(sent, "shard", 1)

    def hold(self):
        self.came = self.line.hold(self.came)

    def further(self):
        self.hop += 1
        first, count = self.block(self.hop)
        sent = self.line.step(
            lambda a, b: (
                lax.slice_in_dim(a, first, first + count, axis=0).astype(F32) + b.astype(F32)
            ).astype(BF),
            self.array,
            self.came,
        )
        self.came = ring(sent, "shard", 1)

    def end(self):
        while self.hop + 1 < self.group:
            self.further()
        return lax.slice_in_dim(self.array, 0, self.block(0)[1], axis=0), self.came


def exchanged(array):
    return lax.all_to_all(array, "shard", 0, 0, tiled=True)


def widen_kernel(size, width, rows_ref, out_ref):
    length = rows_ref.shape[0] // size
    for owner in range(size):
        for at in range(rows_ref.shape[1] // width):
            first = (at * size + owner) * width
            out_ref[:, first : first + width] = rows_ref[
                owner * length : (owner + 1) * length, at * width : (at + 1) * width
            ]


def widened(array, size, width):
    rows, columns = array.shape
    return pl.pallas_call(
        functools.partial(widen_kernel, size, width),
        out_shape=jax.ShapeDtypeStruct((rows // size, columns * size), array.dtype),
        compiler_params=ROOM,
        name="widened",
    )(array)


def split_kernel(in_ref, *refs):
    first = 0
    for ref in refs:
        ref[...] = in_ref[first : first + ref.shape[0]].astype(F32)
        first += ref.shape[0]


def split_rows(array, reps, heights):
    rows, columns = array.shape
    return pl.pallas_call(
        split_kernel,
        grid=(reps,),
        in_specs=[pl.BlockSpec((rows // reps, columns), lambda r: (r, 0))],
        out_specs=[pl.BlockSpec((height, columns), lambda r: (r, 0)) for height in heights],
        out_shape=[jax.ShapeDtypeStruct((height * reps, columns), F32) for height in heights],
        compiler_params=ROOM,
        name="split_rows",
    )(array)


class Spread:
    def __init__(self, line, array):
        self.line, self.size = line, lax.axis_size("rep")
        self.pieces = {0: array}
        steps = (2, 4) if self.size == 8 else range(2, self.size, 2)
        for mask in steps:
            self.pieces[mask] = swap(array, "rep", mask)

    def across(self):
        if self.size != 8:
            return
        half = self.pieces[0].shape[0] // 2
        self.pieces[2], self.pieces[4], first, second = self.line.step(
            lambda a, b: (a, b, a[:half], b[half:]), self.pieces[2], self.pieces[4]
        )
        self.halves = (swap(first, "rep", 4), swap(second, "rep", 2))

    def shared(self):
        masks = range(0, self.size, 2)
        if self.size == 8:
            self.pieces[6] = self.line.step(lambda *h: jnp.concatenate(h), *self.halves)
        held = self.line.step(lambda *p: p, *[self.pieces[mask] for mask in masks])
        return [piece for one in held for piece in (one, swap(one, "rep", 1))]


def assemble_kernel(rep_ref, *refs):
    for mask, piece in enumerate(refs[:-1]):

        @pl.when(pl.program_id(0) == mask)
        def _(piece=piece):
            refs[-1][...] = piece[...].astype(F32)


def assemble(pieces, rep):
    size = len(pieces)
    rows, columns = pieces[0].shape
    whole = pl.BlockSpec((rows, columns), lambda m, r: (0, 0), pipeline_mode=pl.Buffered(1))
    return pl.pallas_call(
        assemble_kernel,
        grid_spec=pltpu.PrefetchScalarGridSpec(
            num_scalar_prefetch=1,
            grid=(size,),
            in_specs=[whole] * size,
            out_specs=pl.BlockSpec((rows, columns), lambda m, r: (r[0] ^ m, 0)),
        ),
        out_shape=jax.ShapeDtypeStruct((rows * size, columns), F32),
        compiler_params=ROOM,
        name="assemble",
    )(rep.reshape(1), *pieces)


def grad_kernel(which_ref, left_ref, right_ref, *refs):
    *more, out_ref = refs
    left = left_ref[...]
    if more and more[0].shape[0] == left.shape[0]:
        both = more.pop(0)
        lanes = both.shape[1] // 2
        left = jnp.concatenate(
            [left, jnp.where(which_ref[0] == 0, both[:, :lanes], both[:, lanes:])], axis=1
        )
    total = contract_rows(left, right_ref[...])
    if more:
        total = total + more[0][...].astype(F32)
    out_ref[...] = total.astype(BF)


def half_grads(left, right, which, reps, came=None, also=None):
    tokens, height = left.shape
    length = right.shape[1]
    height //= reps
    extra = 0 if also is None else also.shape[1] // reps
    if height % 128 or extra not in (0, 64):
        sides = [left] if also is None else [left, also]
        total = [
            contract_rows(
                lax.dynamic_index_in_dim(
                    side.reshape(tokens, reps // 2, 2, -1), which, 2, keepdims=False
                ).reshape(tokens, -1),
                right,
            ).reshape(reps // 2, -1, length)
            for side in sides
        ]
        total = jnp.concatenate(total, axis=1).reshape(-1, length)
        return (total if came is None else total + came.astype(F32)).astype(BF)
    block = pl.BlockSpec((height + extra, length), lambda b, w: (b, 0))
    more = [] if also is None else [also]
    more_specs = [] if also is None else [pl.BlockSpec((tokens, 128), lambda b, w: (0, b))]
    return pl.pallas_call(
        grad_kernel,
        grid_spec=pltpu.PrefetchScalarGridSpec(
            num_scalar_prefetch=1,
            grid=(reps // 2,),
            in_specs=[
                pl.BlockSpec((tokens, height), lambda b, w: (0, 2 * b + w[0])),
                pl.BlockSpec((tokens, length), lambda b, w: (0, 0)),
            ]
            + more_specs
            + ([] if came is None else [block]),
            out_specs=block,
        ),
        out_shape=jax.ShapeDtypeStruct((reps // 2 * (height + extra), length), BF),
        compiler_params=ROOM,
        name="half_grads",
    )(which.reshape(1), left, right, *more, *([] if came is None else [came]))


def ln_forward_kernel(reps, group, x_ref, gain_ref, shift_ref, out_ref):
    x = x_ref[...].astype(F32)
    centred = x - jnp.mean(x, axis=-1, keepdims=True)
    spread = jnp.mean(centred * centred, axis=-1, keepdims=True)
    normed = (centred * lax.rsqrt(spread + 1e-05)) * gain_ref[...] + shift_ref[...]
    slab = x.shape[1] // (reps * group)
    out_ref[...] = jnp.concatenate(
        [
            normed[:, (g * reps + r) * slab : (g * reps + r + 1) * slab]
            for r in range(reps)
            for g in range(group)
        ],
        axis=1,
    ).astype(BF)


def ln_forward(inputs, gain, shift, reps, group):
    tokens, width = inputs.shape
    return pl.pallas_call(
        functools.partial(ln_forward_kernel, reps, group),
        out_shape=jax.ShapeDtypeStruct((tokens, width), BF),
        compiler_params=ROOM,
        name="ln_forward",
    )(inputs, gain.reshape(1, width), shift.reshape(1, width))


def ln_backward_kernel(reps, group, x_ref, gain_ref, cot_ref, a_ref, b_ref, out_ref, sums_ref):
    x = x_ref[...].astype(F32)
    centred = x - jnp.mean(x, axis=-1, keepdims=True)
    spread = jnp.mean(centred * centred, axis=-1, keepdims=True)
    inverse = lax.rsqrt(spread + 1e-05)
    xhat = centred * inverse
    mixed = a_ref[...].astype(F32) + b_ref[...].astype(F32)
    slab = x.shape[1] // (reps * group)
    d_normed = jnp.concatenate(
        [
            mixed[:, (r * group + g) * slab : (r * group + g + 1) * slab]
            for g in range(group)
            for r in range(reps)
        ],
        axis=1,
    )
    sums_ref[0:1] = jnp.sum(d_normed * xhat, axis=0, keepdims=True)
    sums_ref[1:2] = jnp.sum(d_normed, axis=0, keepdims=True)
    scaled = d_normed * gain_ref[...]
    out_ref[...] = cot_ref[...].astype(F32) + inverse * (
        scaled
        - jnp.mean(scaled, axis=-1, keepdims=True)
        - xhat * jnp.mean(scaled * xhat, axis=-1, keepdims=True)
    )


def ln_backward(inputs, gain, cotangent, parts, reps, group):
    tokens, width = inputs.shape
    return pl.pallas_call(
        functools.partial(ln_backward_kernel, reps, group),
        out_shape=[
            jax.ShapeDtypeStruct((tokens, width), F32),
            jax.ShapeDtypeStruct((2, width), F32),
        ],
        compiler_params=ROOM,
        name="ln_backward",
    )(inputs, gain.reshape(1, width), cotangent, *parts)


def pull_kernel(cot_ref, weight_ref, *refs):
    total = times_transpose(cot_ref[...], weight_ref[...])
    if len(refs) > 1:
        total = total * refs[0][...].astype(F32)
    refs[-1][...] = total.astype(BF)


def pull(cot_all, weight, *slope):
    height, width = cot_all.shape
    hidden = weight.shape[0]
    tile = min(512, hidden)
    block = pl.BlockSpec((height, tile), lambda j: (0, j))
    return pl.pallas_call(
        pull_kernel,
        grid=(hidden // tile,),
        in_specs=[
            pl.BlockSpec((height, width), lambda j: (0, 0)),
            pl.BlockSpec((tile, width), lambda j: (j, 0)),
        ]
        + [block] * len(slope),
        out_specs=block,
        out_shape=jax.ShapeDtypeStruct((height, hidden), BF),
        compiler_params=ROOM,
        name="pull",
    )(cot_all, weight, *slope)


def push_kernel(transposed, size, place_ref, a_ref, b_ref, c_ref, d_ref, out_ref):
    product = times_transpose if transposed else times
    total = product(a_ref[...], b_ref[...]) + product(c_ref[...], d_ref[...])
    if size is None:
        out_ref[...] = total.astype(BF)
        return
    block = out_ref.shape[0] // size
    for hop in range(size):
        out_ref[token_block(place_ref[0], hop, size, block)] = total[
            hop * block : (hop + 1) * block
        ].astype(BF)


def push(a, b, c, d, transposed, place, size=None):
    height = a.shape[0]
    length = b.shape[0 if transposed else 1]
    tile = min(512, length)
    full = lambda x: pl.BlockSpec(x.shape, lambda j, z: (0, 0))
    if transposed:
        part = lambda x: pl.BlockSpec((tile, x.shape[1]), lambda j, z: (j, 0))
    else:
        part = lambda x: pl.BlockSpec((x.shape[0], tile), lambda j, z: (0, j))
    return pl.pallas_call(
        functools.partial(push_kernel, transposed, size),
        grid_spec=pltpu.PrefetchScalarGridSpec(
            num_scalar_prefetch=1,
            grid=(length // tile,),
            in_specs=[full(a), part(b), full(c), part(d)],
            out_specs=pl.BlockSpec((height, tile), lambda j, z: (0, j)),
        ),
        out_shape=jax.ShapeDtypeStruct((height, length), BF),
        compiler_params=ROOM,
        name="push",
    )(place.reshape(1), a, b, c, d)


def turned(u, turn, sign):
    return (
        u * turn[0]
        + sign * (pltpu.roll(u, PAIR - ROT // 2, 1) * turn[1])
        + sign * (pltpu.roll(u, ROT // 2, 1) * turn[2])
    )


def spans(rows, block):
    first = 0
    for part in range(rows // block):
        yield part, first, (part + 1) * block
        first += (part + 1) * block


def token_block(place, hop, count, block):
    return pl.ds(pl.multiple_of(lax.rem(place - hop + count, count) * block, block), block)


def attend_kernel(block, place_ref, q_ref, k_ref, v_ref, turn_ref, start_ref, *refs):
    att_ref, prob_ref, low_ref, out_ref = refs[-4:]
    rows = q_ref.shape[0]
    count = rows // block
    for hop in range(count):
        here, there = slice(hop * block, (hop + 1) * block), token_block(place_ref[0], hop, count, block)
        turn = [turn_ref[k, here] for k in range(3)]
        query = turned(q_ref[here], turn, 1.0).astype(BF)
        low_ref[0, there] = (query * HEAD_DIM ** (-0.5)).astype(BF)
        low_ref[1, there] = turned(k_ref[here], turn, 1.0).astype(BF)
        low_ref[2, there] = v_ref[here].astype(BF)
    start = start_ref[0]
    for head in range(2):
        lanes = slice(head * HEAD_DIM, (head + 1) * HEAD_DIM)
        key_h = low_ref[1, :, lanes]
        value_t = low_ref[2, :, lanes].T
        for part, first, length in spans(rows, block):
            own = slice(part * block, (part + 1) * block)
            scores = times_transpose(key_h[:length], low_ref[0, own, lanes])
            place = lax.broadcasted_iota(jnp.int32, (length, block), 0)
            asker = lax.broadcasted_iota(jnp.int32, (length, block), 1) + part * block
            allowed = (place >= start[:, own]) & (place <= asker)
            scores = jnp.where(allowed, scores, -1e30)
            exponent = jnp.exp(scores - jnp.max(scores, axis=0, keepdims=True))
            softmax = exponent * (1.0 / jnp.sum(exponent, axis=0, keepdims=True))
            attention = softmax.astype(BF)
            prob_ref[0, head, first : first + length] = attention
            out_ref[own, lanes] = times(value_t[:, :length], attention).T.astype(BF)
    for hop in range(count):
        att_ref[hop * block : (hop + 1) * block] = out_ref[token_block(place_ref[0], hop, count, block)]


def attend(projected, turns, start, place, first, count, block, before):
    tokens, width = projected.shape
    pairs, seqs = width // (3 * PAIR), tokens // SEQ
    stored = sum(length for _, _, length in spans(SEQ, block))
    wide = lambda at: pl.BlockSpec((SEQ, PAIR), lambda s, p, z: (s, at * pairs + first + p))
    return pl.pallas_call(
        functools.partial(attend_kernel, block),
        grid_spec=pltpu.PrefetchScalarGridSpec(
            num_scalar_prefetch=1,
            grid=(seqs, count),
            in_specs=[
                wide(0),
                wide(1),
                wide(2),
                pl.BlockSpec((3, SEQ, PAIR), lambda s, p, z: (0, s, 0)),
                pl.BlockSpec((1, 1, SEQ), lambda s, p, z: (s, 0, 0)),
            ]
            + [ANY] * len(before),
            out_specs=[
                pl.BlockSpec((SEQ, PAIR), lambda s, p, z: (s, first + p)),
                pl.BlockSpec((1, 2, stored, block), lambda s, p, z: (s, p, 0, 0)),
                pl.BlockSpec((3, SEQ, PAIR), lambda s, p, z: (0, s, p)),
            ],
            scratch_shapes=[pltpu.VMEM((SEQ, PAIR), BF)],
        ),
        out_shape=[
            jax.ShapeDtypeStruct((tokens, pairs * PAIR), BF),
            jax.ShapeDtypeStruct((seqs, 2 * count, stored, block), BF),
            jax.ShapeDtypeStruct((3, tokens, count * PAIR), BF),
        ],
        input_output_aliases={6: 0} if before else {},
        compiler_params=ROOM,
        name="attend",
    )(place.reshape(1), projected, projected, projected, turns, start, *before)


def attend_back_kernel(block, place_ref, prob_ref, low_ref, datt_ref, turn_ref, *refs):
    dproj_ref, bsum_ref, d_ref, dq_ref, dk_ref, dv_ref, done_ref = refs[-7:]
    rows = datt_ref.shape[0]
    count = rows // block
    stage = pl.program_id(2)

    @pl.when(stage == 0)
    def _():
        for hop in range(count):
            d_ref[token_block(place_ref[0], hop, count, block)] = datt_ref[
                hop * block : (hop + 1) * block
            ]
        for head in range(2):
            lanes = slice(head * HEAD_DIM, (head + 1) * HEAD_DIM)
            key_t = low_ref[1, :, lanes].T
            value_h = low_ref[2, :, lanes]
            for part, first, length in reversed(list(spans(rows, block))):
                own = slice(part * block, (part + 1) * block)
                query_p = low_ref[0, own, lanes]
                d_att_p = d_ref[own, lanes]
                attention = prob_ref[0, head, first : first + length]
                d_attention = times_transpose(value_h[:length], d_att_p)
                softmax = attention.astype(F32)
                weighted = softmax * d_attention
                d_scores = (
                    weighted - softmax * jnp.sum(weighted, axis=0, keepdims=True)
                ).astype(BF)
                dq_ref[own, lanes] = times(key_t[:, :length], d_scores).T * HEAD_DIM ** (-0.5)
                d_value = times(attention, d_att_p)
                d_key = times(d_scores, query_p)
                if length == rows:
                    dv_ref[:, lanes] = d_value
                    dk_ref[:, lanes] = d_key
                else:
                    dv_ref[:length, lanes] += d_value
                    dk_ref[:length, lanes] += d_key
        for hop in range(count):
            here = slice(hop * block, (hop + 1) * block)
            there = token_block(place_ref[0], hop, count, block)
            turn = [turn_ref[k, here] for k in range(3)]
            done_ref[0, here] = turned(dq_ref[there], turn, -1.0).astype(BF)
            done_ref[1, here] = turned(dk_ref[there], turn, -1.0).astype(BF)
            done_ref[2, here] = dv_ref[there].astype(BF)

    piece = done_ref[stage]
    dproj_ref[...] = piece
    bsum_ref[0] = jnp.sum(piece.astype(F32), axis=0, keepdims=True)


def attend_back(kept, d_attended, turns, place, first, block, pairs, before):
    prob, low = kept
    tokens = d_attended.shape[0]
    seqs, count = tokens // SEQ, prob.shape[1] // 2
    width = 3 * pairs * PAIR
    return pl.pallas_call(
        functools.partial(attend_back_kernel, block),
        grid_spec=pltpu.PrefetchScalarGridSpec(
            num_scalar_prefetch=1,
            grid=(seqs, count, 3),
            in_specs=[
                pl.BlockSpec((1, 2) + prob.shape[2:], lambda s, p, j, z: (s, p, 0, 0)),
                pl.BlockSpec((3, SEQ, PAIR), lambda s, p, j, z: (0, s, p)),
                pl.BlockSpec((SEQ, PAIR), lambda s, p, j, z: (s, first + p)),
                pl.BlockSpec((3, SEQ, PAIR), lambda s, p, j, z: (0, s, 0)),
            ]
            + [ANY] * len(before),
            out_specs=[
                pl.BlockSpec((SEQ, PAIR), lambda s, p, j, z: (s, j * pairs + first + p)),
                pl.BlockSpec((1, 1, PAIR), lambda s, p, j, z: (s, 0, j * pairs + first + p)),
            ],
            scratch_shapes=[pltpu.VMEM((SEQ, PAIR), BF)]
            + [pltpu.VMEM((SEQ, PAIR), F32)] * 3
            + [pltpu.VMEM((3, SEQ, PAIR), BF)],
        ),
        out_shape=[
            jax.ShapeDtypeStruct((tokens, width), BF),
            jax.ShapeDtypeStruct((seqs, 1, width), F32),
        ],
        input_output_aliases={5: 0, 6: 1} if before else {},
        compiler_params=ROOM,
        name="attend_back",
    )(place.reshape(1), prob, low, d_attended, turns, *before)


def tables(positions):
    frequency = 10000.0 ** (-(jnp.arange(ROT // 2, dtype=F32) * 2.0) / ROT)
    angles = frequency[:, None] * positions[None, :]
    cosine, sine = jnp.cos(angles).T, jnp.sin(angles).T
    none = jnp.zeros_like(sine)
    still = jnp.zeros((sine.shape[0], HEAD_DIM - ROT), F32)
    return jnp.stack(
        [
            jnp.concatenate([cosine, cosine, still + 1.0] * 2, axis=1),
            jnp.concatenate([-sine, none, still] * 2, axis=1),
            jnp.concatenate([none, sine, still] * 2, axis=1),
        ]
    )


def feed_forward(normed_all, fc1_cols, bias):
    pre_act = times(normed_all, fc1_cols) + bias
    root = (2.0 / jnp.pi) ** 0.5
    square = pre_act * pre_act
    curve = jnp.tanh(root * pre_act * (1.0 + 0.044715 * square))
    activation = (0.5 * pre_act * (1.0 + curve)).astype(BF)
    slope = (
        0.5 * (1.0 + curve)
        + 0.5 * pre_act * (1.0 - curve * curve) * root * (1.0 + 3 * 0.044715 * square)
    ).astype(BF)
    return activation, slope


def shards(
    inputs,
    segments,
    positions,
    ln_gain,
    ln_bias,
    w_qkv,
    b_qkv,
    w_dense,
    b_dense,
    w_fc1,
    b_fc1,
    w_fc2,
    b_fc2,
    cotangent,
):
    reps, group = lax.axis_size("rep"), lax.axis_size("shard")
    rep, place = lax.axis_index("rep"), lax.axis_index("shard")
    core = rep & 1
    tokens, width = inputs.shape
    rows = width // group
    slab = rows // reps
    hidden = w_fc1.shape[1] // group
    pairs = rows // PAIR
    line = Order()
    def gathered(array):
        return lax.all_gather(array, "rep", axis=0, tiled=True)

    small = jnp.concatenate(
        [ln_gain, ln_bias, b_qkv, b_dense + b_fc2, positions.astype(F32)]
    ).reshape(1, -1)
    small = doubled(small, place, line)
    def qkv_rows(w):
        return jnp.concatenate(
            [
                jnp.concatenate(
                    [
                        lax.dynamic_slice(w, (rep * slab, at * width + owner * rows), (slab, rows))
                        for at in range(3)
                    ],
                    axis=1,
                )
                for owner in range(group)
            ]
        )

    def fc1_rows(w):
        return jnp.concatenate(
            [
                lax.dynamic_slice(w, (rep * slab, owner * hidden), (slab, hidden))
                for owner in range(group)
            ]
        )

    qkv_pieces = exchanged(line.step(qkv_rows, w_qkv))
    fc1_pieces = exchanged(line.step(fc1_rows, w_fc1))
    gain = small[:, :rows].reshape(width)
    shift = small[:, rows : 2 * rows].reshape(width)
    bias_qkv = lax.dynamic_slice_in_dim(
        small[:, 2 * rows : 5 * rows].reshape(3, width), place * rows, rows, 1
    ).reshape(3 * rows)
    bias_out = small[:, 5 * rows : 6 * rows].reshape(width)
    group_positions = small[:, 6 * rows :]

    normed = [line.step(lambda *o: ln_forward(*o, reps, group), inputs, gain, shift)]
    normed.append(ring(line.hold(normed[0]), "shard", 1))
    qkv_cols = gathered(line.hold(qkv_pieces))

    ring_order = [(place - hop) % group for hop in range(group)]
    ring_positions = jnp.concatenate(
        [lax.dynamic_index_in_dim(group_positions, at, 0, keepdims=False) for at in ring_order]
    )
    start = (
        jnp.arange(SEQ, dtype=jnp.int32)[None, None]
        - group_positions.astype(jnp.int32).reshape(-1, 1, SEQ)
    )
    per_seq = SEQ // tokens
    if group == per_seq:
        turn_place = place
        by_seq = from_seq = lambda array, axis=0: array
    else:
        turn_place = jnp.zeros_like(place)
        seq_order = [at // per_seq * per_seq + (-at) % per_seq for at in range(group)]

        def taken(array, order, axis):
            return jnp.concatenate(
                [
                    lax.dynamic_slice_in_dim(array, at * tokens, tokens, axis)
                    for at in order
                ],
                axis=axis,
            )

        by_seq = lambda array, axis=0: taken(
            array, [(place - at) % group for at in seq_order], axis
        )
        from_seq = lambda array, axis=0: taken(
            array, [at // per_seq * per_seq + (-at) % per_seq for at in ring_order], axis
        )

    turns = line.step(lambda p: by_seq(tables(p), 1), ring_positions)

    def begin(block):
        return jnp.concatenate([block, jnp.zeros(((group - 1) * tokens, width), BF)])

    def put(hop):
        return lambda whole, block: lax.dynamic_update_slice_in_dim(
            whole, block, hop * tokens, 0
        )

    normed_all = line.step(begin, normed[0])
    cot_all = line.step(begin, cotangent)
    for hop in range(1, group):
        normed[hop] = line.hold(normed[hop])
        if hop == 1:
            fc1_cols = gathered(line.hold(fc1_pieces))
        if hop + 1 < group:
            normed.append(ring(normed[hop], "shard", 1))
        else:
            cots = [line.hold(cotangent)]
            cots.append(ring(cots[0], "shard", 1))
        normed_all = line.step(put(hop), normed_all, normed[hop])

    projected = line.step(
        lambda a, b, c: by_seq(times(a, b) + c), normed_all, qkv_cols, bias_qkv
    )
    calls = 2 if pairs > 1 else 1
    each = pairs // calls
    kept = []

    def attend_some(call, before):
        attended, *rest = line.step(
            lambda p, *b: attend(p, turns, start, turn_place, call * each, each, tokens, b),
            projected,
            *before,
        )
        kept.append(rest)
        return (attended,)

    attended = attend_some(0, ())
    for hop in range(1, group):
        cots[hop] = line.hold(cots[hop])
        if hop + 1 < group:
            cots.append(ring(cots[hop], "shard", 1))
        cot_all = line.step(put(hop), cot_all, cots[hop])
        if hop == 1:
            activation, slope = line.step(feed_forward, normed_all, fc1_cols, b_fc1)
        if hop == 2:
            if calls > 1:
                attended = attend_some(1, attended)
            out_part = line.step(
                lambda a, b, c, d: push(a, b, c, d, False, place, group),
                from_seq(attended[0]),
                w_dense,
                activation,
                w_fc2,
            )
            out_sum = lax.psum_scatter(out_part, "shard", scatter_dimension=0, tiled=True)
    (attended,) = attended
    attended = from_seq(attended)

    def grad(left, right, *also):
        sent = line.step(
            lambda a, b, *c: half_grads(a, b, 1 - core, reps, None, *c), left, right, *also
        )
        return swap(sent, "rep", 1)

    def grad_sum(left, right, came, *also):
        own = line.step(
            lambda a, b, c, *d: half_grads(a, b, core, reps, c, *d), left, right, came, *also
        )
        halving = Halving(rep, own, 2)
        halving.send(line)
        return halving

    def attend_back_some(call, before):
        return line.step(
            lambda d, t, *b: attend_back(
                kept[call], d, t, turn_place, call * each, tokens, pairs, b
            ),
            d_attended,
            turns,
            *before,
        )

    out_came = grad(activation, cot_all, attended)
    d_pre = line.step(pull, cot_all, w_fc2, slope)
    fc1_came = grad(normed_all, d_pre)
    out_grads = grad_sum(activation, cot_all, out_came, attended)
    d_attended = by_seq(line.step(pull, cot_all, w_dense))
    back = attend_back_some(0, ())
    fc1_sum = grad_sum(normed_all, d_pre, fc1_came)
    out_grads.further(line)
    for call in range(1, calls):
        back = attend_back_some(call, back)
    d_projected, d_bias_qkv = back
    d_projected = from_seq(d_projected)
    d_normed_part = line.step(
        lambda a, b, c, d: push(a, b, c, d, True, place), d_projected, qkv_cols, d_pre, fc1_cols
    )
    d_normed_sum = Passing(line, d_normed_part, tokens)
    out_piece = out_grads.end(line)
    fc1_sum.further(line)
    out_whole = gathered(line.hold(out_piece))
    qkv_came = grad(normed_all, d_projected)
    block_out = line.step(
        lambda x, b, p: x.astype(F32) + b + p.astype(F32), inputs, bias_out, out_sum
    )
    qkv_sum = grad_sum(normed_all, d_projected, qkv_came)
    fc1_pieces = exchanged(line.hold(fc1_sum.end(line)))
    d_normed_sum.further()
    qkv_sum.further(line)

    def bias_sums(d_bias_qkv, cotangent, d_pre):
        d_bias_all = lax.dynamic_update_slice_in_dim(
            jnp.zeros((3, width), F32),
            jnp.sum(d_bias_qkv[:, 0], axis=0).reshape(3, rows),
            place * rows,
            1,
        )
        ones = jnp.ones((8, group * tokens), BF)
        return (
            jnp.concatenate(
                [
                    d_bias_all.reshape(group, 3 * rows),
                    jnp.sum(cotangent.astype(F32), axis=0).reshape(group, rows),
                ],
                axis=1,
            ),
            times(ones, d_pre)[0],
        )

    early_sums, d_bias_fc1 = line.step(bias_sums, d_bias_qkv, cotangent, d_pre)
    qkv_piece = qkv_sum.end(line)
    d_normed_sum.hold()
    fc1_slab = line.step(lambda p: widened(p, group, hidden), fc1_pieces)
    qkv_pieces = exchanged(line.hold(qkv_piece))
    fc1_whole = gathered(line.hold(fc1_slab))
    qkv_spread = Spread(line, line.step(lambda p: widened(p, group, rows), qkv_pieces))
    d_normed_sum.further()
    fc2_total, dense_total = line.step(
        lambda a: split_rows(a, reps, (hidden // reps, slab)), out_whole
    )
    grad_inputs, norm_sums = line.step(
        lambda x, g, c, *p: ln_backward(x, g, c, p, reps, group),
        inputs,
        gain,
        cotangent,
        *d_normed_sum.end(),
    )

    sums = line.step(
        lambda early, norm_sums: jnp.concatenate(
            [early, norm_sums[0].reshape(group, rows), norm_sums[1].reshape(group, rows)], axis=1
        ),
        early_sums,
        norm_sums,
    )
    qkv_spread.across()
    sums = owned_sum(line, sums, place)
    sums = line.hold(jnp.concatenate([sums, d_bias_fc1]))
    sums = line.hold(sums + swap(sums, "rep", 1))
    fc1_total = line.step(lambda a: a.astype(F32), fc1_whole)
    qkv_spread = qkv_spread.shared()
    bit = 2
    while bit < reps:
        sums = line.hold(sums + swap(sums, "rep", bit))
        bit *= 2
    qkv_total = line.step(lambda *p: assemble(p, rep), *qkv_spread)
    cot_total = sums[3 * rows : 4 * rows]
    return (
        block_out,
        grad_inputs,
        sums[4 * rows : 5 * rows],
        sums[5 * rows : 6 * rows],
        qkv_total,
        sums[: 3 * rows],
        dense_total,
        cot_total,
        fc1_total,
        sums[6 * rows :],
        fc2_total,
        cot_total,
    )


def solution(mesh):
    both, shard = P(("rep", "shard")), P("shard")
    wide, held = P(("rep", "shard"), None), P("shard", None)
    return jax.shard_map(
        shards,
        mesh=mesh,
        in_specs=(
            wide, both, both, shard, shard, held, shard, held, shard, held, shard, held, shard, wide
        ),
        out_specs=(
            wide, wide, shard, shard, held, shard, held, shard, held, shard, held, shard
        ),
        check_vma=False,
    )
```

time: 681 us -> 595 us (0.87)
  Pallas kernels: 111 us -> 213 us
  waiting for transfers between devices: 228 us -> 163 us
  matrix products: 90.7 us -> 33.4 us
  local copies, waits for them, and re-layouts: 98.1 us -> 49.6 us
  blocking collectives: 0 us -> 23.7 us
  other arithmetic: 66.6 us -> 43.5 us
  starting transfers between devices: 60.6 us -> 46.2 us
    pallas_call x4 -> x12, Pallas kernels: 50.3 us -> 148 us  [the longest x2 37 us: push(): pl.pallas_call(functools.partial(push_kernel, transposed, size), grid_spe...]
    ppermute x27 -> x9, waiting for transfers between devices: 165 us -> 88.6 us  [ring(): lax.ppermute(array, axis, [(i, (i + distance) % size) for i in range(size)])]
    dot_general x4 -> x0, matrix products: 43.8 us -> none  [times_transpose(): lax.dot_general(left_side, right_side, (((1,), (1,)), ((), ())), preferre...]
    ppermute x27 -> x9, starting transfers between devices: 37.5 us -> 6.49 us  [ring(): lax.ppermute(array, axis, [(i, (i + distance) % size) for i in range(size)])]
    convert_element_type x8 -> x3, other arithmetic: 31.5 us -> 5.07 us  [the longest x2 5.06 us: further(): sent = self.line.step(lambda a, b: (lax.slice_in_dim(a, first, first + co...]
    all_to_all x0 -> x3, waiting for transfers between devices: none -> 24.2 us  [exchanged(): return lax.all_to_all(array, 'shard', 0, 0, tiled=True)]
    all_to_all x0 -> x1, blocking collectives: none -> 23.7 us  [exchanged(): return lax.all_to_all(array, 'shard', 0, 0, tiled=True)]
    dynamic_update_slice x25 -> x7, local copies, waits for them, and re-layouts: 26.8 us -> 7.55 us  [the longest x6 7.55 us: put(): lax.dynamic_update_slice_in_dim(whole, block, hop * tokens, 0)]
  transfers between devices with their start and end apart: 55 -> 47, of which waited for: 28 -> 22; matrix products, arithmetic and copies ran while one was open for 30% -> 20% of each run, Pallas kernels for 13% -> 33%
where the time goes in v3:
time: 595 us; the launch traced here: 588 us
  Pallas kernels  213 us (36%)
  waiting for transfers between devices  163 us (27%)
  local copies, waits for them, and re-layouts  49.6 us (8%)
  starting transfers between devices  46.2 us (8%)
  other arithmetic  43.5 us (7%)
  matrix products  33.4 us (6%)
  blocking collectives  23.7 us (4%)
  between operations  15 us (3%)
    ppermute x9, waiting for transfers between devices, ring(): lax.ppermute(array, axis, [(i, (i + distance) % size) for i in range(size)])  88.6 us
    pallas_call x6, Pallas kernels, half_grads(): pl.pallas_call(grad_kernel, grid_spec=pltpu.PrefetchScalarGridSpec(num_sc...  56.7 us
    ppermute x30, waiting for transfers between devices, swap(): return lax.ppermute(array, axis, [(i, i ^ mask) for i in range(size)])  50.1 us
    pallas_call x2, Pallas kernels, push(): pl.pallas_call(functools.partial(push_kernel, transposed, size), grid_spe...  37 us
    pallas_call x2, Pallas kernels, attend_back(): pl.pallas_call(functools.partial(attend_back_kernel, block), grid_spec=pl...  36.4 us
    dot_general x3, matrix products, times(): return jnp.dot(left_side, right_side, preferred_element_type=F32)  33.4 us
    pallas_call x2, Pallas kernels, attend(): pl.pallas_call(functools.partial(attend_kernel, block), grid_spec=pltpu.P...  29 us
    ppermute x30, starting transfers between devices, swap(): return lax.ppermute(array, axis, [(i, i ^ mask) for i in range(size)])  27.4 us
  transfers between devices with their start and end apart: 47, of which 22 were waited for; matrix products, arithmetic and copies ran while one was open for 20% of the time, Pallas kernels for 33%

profile of v3, /device:TPU:0, one launch (start us, length us, event | category | flops | bytes accessed | tf_op | source)
XLA Modules:
  0.0 587.8 jit_solution(13309985164619994085)
XLA Ops:
  10.7 3.1 collective-permute-start
  15.5 3.1 collective-permute-start.1
  22.0 3.5 all-to-all-start
  27.9 3.2 ln_forward.1
  31.1 13.4 %all-to-all-done = bf16[4,64,1536]{2,1,0:T(8,128)(2,1)S(1)} async-done(((bf16[4,64,1536]{2,1,0:T(8,128)(2,1)}), bf16[4,64,1536]{2,1,0:T(8,128)(2,1)S(1)}, u32[]{:S(2)}, u32[]{:S(2)}) %all-to-all-start) | async-done | bytes 786464 | tf_op jit(solution)/shard_map/all_to_all | solution.py:173
  45.4 4.3 all-to-all-start.1
  60.0 2.5 concatenate.79
  62.6 2.4 concatenate.80
  65.0 27.8 %collective-permute-done.2 = bf16[256,2048]{1,0:T(8,128)(2,1)} collective-permute-done((bf16[256,2048]{1,0:T(8,128)(2,1)}, bf16[256,2048]{1,0:T(8,128)(2,1)}, u32[]{:S(2)}, u32[]{:S(2)}) %collective-permute-start.2) | collective-permute-done | bytes 1048608 | tf_op jit(solution)/shard_map/ppermute | solution.py:22
  92.8 4.6 all-to-all-done.1
  99.9 23.8 %collective-permute-done.3 = bf16[256,2048]{1,0:T(8,128)(2,1)S(1)} collective-permute-done((bf16[256,2048]{1,0:T(8,128)(2,1)}, bf16[256,2048]{1,0:T(8,128)(2,1)S(1)}, u32[]{:S(2)}, u32[]{:S(2)}) %collective-permute-start.3) | collective-permute-done | bytes 1048608 | tf_op jit(solution)/shard_map/ppermute | solution.py:22
  125.4 23.2 %collective-permute-done.4 = bf16[256,2048]{1,0:T(8,128)(2,1)S(1)} collective-permute-done((bf16[256,2048]{1,0:T(8,128)(2,1)S(1)}, bf16[256,2048]{1,0:T(8,128)(2,1)S(1)}, u32[]{:S(2)}, u32[]{:S(2)}) %collective-permute-start.4) | collective-permute-done | bytes 1048608 | tf_op jit(solution)/shard_map/ppermute | solution.py:22
  149.9 11.6 %convolution_add_fusion.q_ref.k_ref.v_ref = f32[1024,1536]{1,0:T(8,128)} fusion(bf16[1024,2048]{1,0:T(8,128)(2,1)} %constant_dynamic-update-slice_fusion.10.left_ref, bf16[2048,1536]{1,0:T(8,128)(2,1)} %all-gather.5.cloned.1.call-done.b_ref, f32[1536]{0:T(1024)S(1)} %reshape.211), kind=kOutput, calls=%fused_computation.3 | convolution fusion | flops 6444023808 | bytes 16783360 | tf_op jit(solution)/shard_map/dot_general | solution.py:43
  161.5 14.5 %attend.2 = (bf16[1024,512]{1,0:T(8,128)(2,1)}, bf16[1,4,2560,256]{3,2,1,0:T(8,128)(2,1)}, bf16[3,1024,256]{2,1,0:T(8,128)(2,1)}) custom-call(s32[1]{0:T(128)} %bitcast.place_ref, f32[1024,1536]{1,0:T(8,128)} %convolution_add_fusion.q_ref.k_ref.v_ref, f32[1024,1536]{1,0:T(8,128)} %convolution_add_fusion.q_ref.k_ref.v_ref, ...), custom_call_target="tpu_custom_call" | custom-call | tf_op jit(solution)/shard_map/attend/pallas_call | solution.py:506
  177.5 18.9 %add_convert_fusion = (bf16[1024,2048]{1,0:T(8,128)(2,1)}, bf16[1024,2048]{1,0:T(8,128)(2,1)}) fusion(f32[2048]{0:T(1024)S(1)} %copy-done.22, bf16[1024,2048]{1,0:T(8,128)(2,1)} %constant_dynamic-update-slice_fusion.10.left_ref, bf16[2048,2048]{1,0:T(8,128)(2,1)} %all-gather.7.cloned.1.call-done.d_ref), kind=kOutput, calls=%fused_computation | convolution fusion | flops 8631877632 | bytes 20979712 | tf_op jit(solution)/shard_map/dot_general | solution.py:43
  196.4 4.2 collective-permute-done.6
  202.1 14.5 %attend.3 = (bf16[1024,512]{1,0:T(8,128)(2,1)}, bf16[1,4,2560,256]{3,2,1,0:T(8,128)(2,1)}, bf16[3,1024,256]{2,1,0:T(8,128)(2,1)}) custom-call(s32[1]{0:T(128)} %bitcast.place_ref, f32[1024,1536]{1,0:T(8,128)} %convolution_add_fusion.q_ref.k_ref.v_ref, f32[1024,1536]{1,0:T(8,128)} %convolution_add_fusion.q_ref.k_ref.v_ref, ...), custom_call_target="tpu_custom_call", output_to_operand_aliasing={{0}: (6, {})} | custom-call | tf_op jit(solution)/shard_map/attend/pallas_call | solution.py:506
  216.6 15.8 %push.2 = bf16[1024,2048]{1,0:T(8,128)(2,1)} custom-call(s32[1]{0:T(128)} %bitcast.place_ref, bf16[1024,512]{1,0:T(8,128)(2,1)} %get-tuple-element.247.a_ref.refs_0_, bf16[512,2048]{1,0:T(8,128)(2,1)} %weight_ref.1, bf16[1024,2048]{1,0:T(8,128)(2,1)} %get-tuple-element.245.c_ref.left_ref, bf16[2048,2048]{1,0:T(8,128)(2,1)} %weight_ref), custom_call_target="tpu_custom_call" | custom-call | tf_op jit(solution)/shard_map/push/pallas_call | solution.py:436
  233.4 10.9 %half_grads.6 = bf16[1280,2048]{1,0:T(8,128)(2,1)} custom-call(s32[1]{0:T(128)} %bitcast.14.which_ref, bf16[1024,2048]{1,0:T(8,128)(2,1)} %get-tuple-element.245.c_ref.left_ref, bf16[1024,2048]{1,0:T(8,128)(2,1)} %constant_dynamic-update-slice_fusion.7.right_ref.cot_ref, bf16[1024,512]{1,0:T(8,128)(2,1)} %get-tuple-element.247.a_ref.refs_0_), custom_call_target="tpu_custom_call" | custom-call | tf_op jit(solution)/shard_map/half_grads/pallas_call | solution.py:303
  244.3 14.4 %pull.2.right_ref.c_ref = bf16[1024,2048]{1,0:T(8,128)(2,1)} custom-call(bf16[1024,2048]{1,0:T(8,128)(2,1)} %constant_dynamic-update-slice_fusion.7.right_ref.cot_ref, bf16[2048,2048]{1,0:T(8,128)(2,1)} %weight_ref, bf16[1024,2048]{1,0:T(8,128)(2,1)} %get-tuple-element.242.refs_0_), custom_call_target="tpu_custom_call" | custom-call | tf_op jit(solution)/shard_map/pull/pallas_call | solution.py:399
  258.7 8.7 %half_grads.7 = bf16[1024,2048]{1,0:T(8,128)(2,1)} custom-call(s32[1]{0:T(128)} %bitcast.14.which_ref, bf16[1024,2048]{1,0:T(8,128)(2,1)} %constant_dynamic-update-slice_fusion.10.left_ref, bf16[1024,2048]{1,0:T(8,128)(2,1)} %pull.2.right_ref.c_ref), custom_call_target="tpu_custom_call" | custom-call | tf_op jit(solution)/shard_map/half_grads/pallas_call | solution.py:303
  268.2 11.9 %half_grads.8 = bf16[1280,2048]{1,0:T(8,128)(2,1)} custom-call(s32[1]{0:T(128)} %bitcast.15.which_ref, bf16[1024,2048]{1,0:T(8,128)(2,1)} %get-tuple-element.245.c_ref.left_ref, bf16[1024,2048]{1,0:T(8,128)(2,1)} %constant_dynamic-update-slice_fusion.7.right_ref.cot_ref, bf16[1024,512]{1,0:T(8,128)(2,1)} %get-tuple-element.247.a_ref.refs_0_, ...), custom_call_target="tpu_custom_call" | custom-call | tf_op jit(solution)/shard_map/half_grads/pallas_call | solution.py:303
  283.2 2.5 dynamic-slice_bitcast_fusion
  287.3 6.2 %pull.3.datt_ref = bf16[1024,512]{1,0:T(8,128)(2,1)} custom-call(bf16[1024,2048]{1,0:T(8,128)(2,1)} %constant_dynamic-update-slice_fusion.7.right_ref.cot_ref, bf16[512,2048]{1,0:T(8,128)(2,1)} %weight_ref.1), custom_call_target="tpu_custom_call" | custom-call | tf_op jit(solution)/shard_map/pull/pallas_call | solution.py:399
  293.5 18.2 %attend_back.2 = (bf16[1024,1536]{1,0:T(8,128)(2,1)}, f32[1,1,1536]{2,1,0:T(1,128)}) custom-call(s32[1]{0:T(128)} %bitcast.place_ref, bf16[1,4,2560,256]{3,2,1,0:T(8,128)(2,1)} %get-tuple-element.214.prob_ref, bf16[3,1024,256]{2,1,0:T(8,128)(2,1)} %get-tuple-element.215.low_ref, bf16[1024,512]{1,0:T(8,128)(2,1)} %pull.3.datt_ref, ...), custom_call_target="tpu_custom_call" | custom-call | tf_op jit(solution)/shard_map/attend_back/pallas_call | solution.py:591
  311.7 9.5 %half_grads.9 = bf16[1024,2048]{1,0:T(8,128)(2,1)} custom-call(s32[1]{0:T(128)} %bitcast.15.which_ref, bf16[1024,2048]{1,0:T(8,128)(2,1)} %constant_dynamic-update-slice_fusion.10.left_ref, bf16[1024,2048]{1,0:T(8,128)(2,1)} %pull.2.right_ref.c_ref, bf16[1024,2048]{1,0:T(8,128)(2,1)} %collective-permute-done.11.refs_0_), custom_call_target="tpu_custom_call" | custom-call | tf_op jit(solution)/shard_map/half_grads/pallas_call | solution.py:303
  332.6 18.2 %attend_back.3 = (bf16[1024,1536]{1,0:T(8,128)(2,1)}, f32[1,1,1536]{2,1,0:T(1,128)}) custom-call(s32[1]{0:T(128)} %bitcast.place_ref, bf16[1,4,2560,256]{3,2,1,0:T(8,128)(2,1)} %get-tuple-element.228.prob_ref, bf16[3,1024,256]{2,1,0:T(8,128)(2,1)} %get-tuple-element.229.low_ref, ...), custom_call_target="tpu_custom_call", output_to_operand_aliasing={{0}: (5, {}), {1}: (6, {})} | custom-call | tf_op jit(solution)/shard_map/attend_back/pallas_call | solution.py:591
  350.8 21.2 %push.3 = bf16[1024,2048]{1,0:T(8,128)(2,1)} custom-call(s32[1]{0:T(128)} %bitcast.place_ref, bf16[1024,1536]{1,0:T(8,128)(2,1)} %get-tuple-element.296.a_ref.right_ref, bf16[2048,1536]{1,0:T(8,128)(2,1)} %all-gather.5.cloned.1.call-done.b_ref, bf16[1024,2048]{1,0:T(8,128)(2,1)} %pull.2.right_ref.c_ref, bf16[2048,2048]{1,0:T(8,128)(2,1)} %all-gather.7.cloned.1.call-done.d_ref), custom_call_target="tpu_custom_call" | custom-call | tf_op jit(solution)/shard_map/push/pallas_call | solution.py:436
  372.0 2.5 slice.62
  378.7 7.5 %half_grads.10 = bf16[1024,1536]{1,0:T(8,128)(2,1)} custom-call(s32[1]{0:T(128)} %bitcast.14.which_ref, bf16[1024,2048]{1,0:T(8,128)(2,1)} %constant_dynamic-update-slice_fusion.10.left_ref, bf16[1024,1536]{1,0:T(8,128)(2,1)} %get-tuple-element.296.a_ref.right_ref), custom_call_target="tpu_custom_call" | custom-call | tf_op jit(solution)/shard_map/half_grads/pallas_call | solution.py:303
  388.5 2.9 convert_add_fusion.4
  392.1 8.2 %half_grads.11 = bf16[1024,1536]{1,0:T(8,128)(2,1)} custom-call(s32[1]{0:T(128)} %bitcast.15.which_ref, bf16[1024,2048]{1,0:T(8,128)(2,1)} %constant_dynamic-update-slice_fusion.10.left_ref, bf16[1024,1536]{1,0:T(8,128)(2,1)} %get-tuple-element.296.a_ref.right_ref, bf16[1024,1536]{1,0:T(8,128)(2,1)} %collective-permute-done.19.refs_0_), custom_call_target="tpu_custom_call" | custom-call | tf_op jit(solution)/shard_map/half_grads/pallas_call | solution.py:303
  406.7 6.6 %collective-permute-done.17 = bf16[128,2048]{1,0:T(8,128)(2,1)} collective-permute-done((bf16[128,2048]{1,0:T(8,128)(2,1)}, bf16[128,2048]{1,0:T(8,128)(2,1)}, u32[]{:S(2)}, u32[]{:S(2)}) %collective-permute-start.17) | collective-permute-done | bytes 524320 | tf_op jit(solution)/shard_map/ppermute | solution.py:27
  417.6 3.1 add_convert_fusion.2
  422.8 4.3 all-to-all-start.2
  427.1 10.5 %collective-permute-done.21 = bf16[2,128,1536]{2,1,0:T(8,128)(2,1)} collective-permute-done((bf16[2,128,1536]{2,1,0:T(8,128)(2,1)}, bf16[2,128,1536]{2,1,0:T(8,128)(2,1)}, u32[]{:S(2)}, u32[]{:S(2)}) %collective-permute-start.21) | collective-permute-done | bytes 786464 | tf_op jit(solution)/shard_map/ppermute | solution.py:27
  444.8 2.8 fusion.13
  447.7 13.7 %collective-permute-done.23 = bf16[128,1536]{1,0:T(8,128)(2,1)S(1)} collective-permute-done((bf16[128,1536]{1,0:T(8,128)(2,1)S(1)}, bf16[128,1536]{1,0:T(8,128)(2,1)S(1)}, u32[]{:S(2)}, u32[]{:S(2)}) %collective-permute-start.23) | collective-permute-done | bytes 393248 | tf_op jit(solution)/shard_map/ppermute | solution.py:27
  462.5 6.2 %all-to-all-done.2 = bf16[4,64,2048]{2,1,0:T(8,128)(2,1)} async-done(((bf16[4,64,2048]{2,1,0:T(8,128)(2,1)}), bf16[4,64,2048]{2,1,0:T(8,128)(2,1)}, u32[]{:S(2)}, u32[]{:S(2)}) %all-to-all-start.2) | async-done | bytes 1048608 | tf_op jit(solution)/shard_map/all_to_all | solution.py:173
  471.2 23.7 %all_to_all.48 = bf16[4,64,1536]{2,1,0:T(8,128)(2,1)} all-to-all(bf16[4,64,1536]{2,1,0:T(8,128)(2,1)S(1)} %bitcast.117), channel_id=1, replica_groups=mesh['rep'=8,'shard'=4] {'shard'}, dimensions={0} | all-to-all | bytes 1572864 | tf_op jit(solution)/shard_map/all_to_all | solution.py:173
  499.3 2.6 slice.78.a_ref
  503.5 12.1 %split_rows.1 = (f32[2048,2048]{1,0:T(8,128)}, f32[512,2048]{1,0:T(8,128)}) custom-call(bf16[2560,2048]{1,0:T(8,128)(2,1)} %all-gather.9.cloned.1.call-done.in_ref), custom_call_target="tpu_custom_call" | custom-call | tf_op jit(solution)/shard_map/split_rows/pallas_call | solution.py:205
  515.6 9.5 %collective-permute-done.25.b_ref = bf16[256,2048]{1,0:T(8,128)(2,1)} collective-permute-done((bf16[256,2048]{1,0:T(8,128)(2,1)S(1)}, bf16[256,2048]{1,0:T(8,128)(2,1)}, u32[]{:S(2)}, u32[]{:S(2)}) %collective-permute-start.25) | collective-permute-done | bytes 1048608 | tf_op jit(solution)/shard_map/ppermute | solution.py:22
  525.1 5.5 ln_backward.1
  531.6 6.7 %collective-permute-done.27.refs_2_ = bf16[64,6144]{1,0:T(8,128)(2,1)S(1)} collective-permute-done((bf16[64,6144]{1,0:T(8,128)(2,1)S(1)}, bf16[64,6144]{1,0:T(8,128)(2,1)S(1)}, u32[]{:S(2)}, u32[]{:S(2)}) %collective-permute-start.27) | collective-permute-done | bytes 786464 | tf_op jit(solution)/shard_map/ppermute | solution.py:27
  546.9 11.8 %convert_element_type.255 = f32[512,8192]{1,0:T(8,128)} convert(bf16[512,8192]{1,0:T(8,128)(2,1)} %all-gather.11.cloned.1.call-done) | non-fusion elementwise | flops 4194304 | bytes 25165824 | tf_op jit(solution)/shard_map/convert_element_type | solution.py:911
  565.6 2.8 collective-permute-done.34
  571.9 8.4 %assemble.1 = f32[512,6144]{1,0:T(8,128)} custom-call(s32[1]{0:T(128)} %bitcast.50.rep_ref, bf16[64,6144]{1,0:T(8,128)(2,1)} %widened.3.refs_0_, bf16[64,6144]{1,0:T(8,128)(2,1)} %copy-done.14, bf16[64,6144]{1,0:T(8,128)(2,1)} %copy-done.12, bf16[64,6144]{1,0:T(8,128)(2,1)} %copy-done.15, bf16[64,6144]{1,0:T(8,128)(2,1)} %copy-done.13, ...), custom_call_target="tpu_custom_call" | custom-call | tf_op jit(solution)/shard_map/assemble/pallas_call | solution.py:253
  (232 shorter events, 105.3 us)
Async XLA Ops:
  10.7 4.8 collective-permute-start
  15.5 11.1 %collective-permute-start.1 = (f32[2,3328]{1,0:T(2,128)S(1)}, f32[2,3328]{1,0:T(2,128)S(1)}, u32[]{:S(2)}, u32[]{:S(2)}) collective-permute-start(f32[2,3328]{1,0:T(2,128)S(1)} %pad_maximum_fusion.6), channel_id=1, source_target_pairs={{0,2},{1,3},{2,0},{3,1},{4,6},{5,7},{6,4},{7,5},{8,10},{9,11},{10,... | collective-permute-start | bytes 79880 | tf_op jit(solution)/shard_map/ppermute | solution.py:27
  22.0 22.4 %all-to-all-start = ((bf16[4,64,1536]{2,1,0:T(8,128)(2,1)}), bf16[4,64,1536]{2,1,0:T(8,128)(2,1)S(1)}, u32[]{:S(2)}, u32[]{:S(2)}) async-start(bf16[4,64,1536]{2,1,0:T(8,128)(2,1)} %bitcast.7), calls=%async_computation | async-start | bytes 1572864 | tf_op jit(solution)/shard_map/all_to_all | solution.py:173
  25.6 124.3 %all-gather.5.cloned.1.call-start = ((), (), s32[]{:S(2)}) async-start(), calls=%async_computation.5 | async-start | bytes 7077888 | tf_op jit(solution)/shard_map/all_gather | solution.py:675
  45.4 52.0 %all-to-all-start.1 = ((bf16[4,64,2048]{2,1,0:T(8,128)(2,1)}), bf16[4,64,2048]{2,1,0:T(8,128)(2,1)}, u32[]{:S(2)}, u32[]{:S(2)}) async-start(bf16[4,64,2048]{2,1,0:T(8,128)(2,1)} %bitcast.12), calls=%async_computation.1 | async-start | bytes 2097152 | tf_op jit(solution)/shard_map/all_to_all | solution.py:173
  49.7 127.8 %all-gather.7.cloned.1.call-start = ((), (), s32[]{:S(2)}) async-start(), calls=%async_computation.6 | async-start | bytes 9437184 | tf_op jit(solution)/shard_map/all_gather | solution.py:675
  49.7 43.1 %collective-permute-start.2 = (bf16[256,2048]{1,0:T(8,128)(2,1)}, bf16[256,2048]{1,0:T(8,128)(2,1)}, u32[]{:S(2)}, u32[]{:S(2)}) collective-permute-start(bf16[256,2048]{1,0:T(8,128)(2,1)} %ln_forward.1), channel_id=1, source_target_pairs={{0,1},{1,2},{2,3},{3,0},{4,5},{5,6},{6,7},{7,4},{8,9},{9,10},{10,1... | collective-permute-start | bytes 3145736 | tf_op jit(solution)/shard_map/ppermute | solution.py:22
  97.4 291.1 %reduce-scatter.2.cloned.1.call-start = ((), (), s32[]{:S(2)}) async-start(), calls=%async_computation.7 | async-start | bytes 5242880 | tf_op jit(solution)/shard_map/reduce_scatter | solution.py:806
  97.5 26.2 %collective-permute-start.3 = (bf16[256,2048]{1,0:T(8,128)(2,1)}, bf16[256,2048]{1,0:T(8,128)(2,1)S(1)}, u32[]{:S(2)}, u32[]{:S(2)}) collective-permute-start(bf16[256,2048]{1,0:T(8,128)(2,1)} %collective-permute-done.2), channel_id=1, source_target_pairs={{0,1},{1,2},{2,3},{3,0},{4,5},{5,6},{6,7},{7,4},{8,9},{9,10},{10,1... | collective-permute-start | bytes 3145736 | tf_op jit(solution)/shard_map/ppermute | solution.py:22
  123.6 25.0 %collective-permute-start.4 = (bf16[256,2048]{1,0:T(8,128)(2,1)S(1)}, bf16[256,2048]{1,0:T(8,128)(2,1)S(1)}, u32[]{:S(2)}, u32[]{:S(2)}) collective-permute-start(bf16[256,2048]{1,0:T(8,128)(2,1)S(1)} %collective-permute-done.3), channel_id=1, source_target_pairs={{0,1},{1,2},{2,3},{3,0},{4,5},{5,6},{6,7},{7,4},{8,9},{9,10},{10,1... | collective-permute-start | bytes 3145736 | tf_op jit(solution)/shard_map/ppermute | solution.py:22
  148.6 27.4 %collective-permute-start.5 = (bf16[256,2048]{1,0:T(8,128)(2,1)S(1)}, bf16[256,2048]{1,0:T(8,128)(2,1)S(1)}, u32[]{:S(2)}, u32[]{:S(2)}) collective-permute-start(bf16[256,2048]{1,0:T(8,128)(2,1)S(1)} %copy-done.3), channel_id=1, source_target_pairs={{0,1},{1,2},{2,3},{3,0},{4,5},{5,6},{6,7},{7,4},{8,9},{9,10},{10,1... | collective-permute-start | bytes 3145736 | tf_op jit(solution)/shard_map/ppermute | solution.py:22
  176.1 24.5 %collective-permute-start.6 = (bf16[256,2048]{1,0:T(8,128)(2,1)S(1)}, bf16[256,2048]{1,0:T(8,128)(2,1)S(1)}, u32[]{:S(2)}, u32[]{:S(2)}) collective-permute-start(bf16[256,2048]{1,0:T(8,128)(2,1)S(1)} %collective-permute-done.5), channel_id=1, source_target_pairs={{0,1},{1,2},{2,3},{3,0},{4,5},{5,6},{6,7},{7,4},{8,9},{9,10},{10,1... | collective-permute-start | bytes 3145736 | tf_op jit(solution)/shard_map/ppermute | solution.py:22
  200.6 31.8 %collective-permute-start.7 = (bf16[256,2048]{1,0:T(8,128)(2,1)S(1)}, bf16[256,2048]{1,0:T(8,128)(2,1)S(1)}, u32[]{:S(2)}, u32[]{:S(2)}) collective-permute-start(bf16[256,2048]{1,0:T(8,128)(2,1)S(1)} %collective-permute-done.6), channel_id=1, source_target_pairs={{0,1},{1,2},{2,3},{3,0},{4,5},{5,6},{6,7},{7,4},{8,9},{9,10},{10,1... | collective-permute-start | bytes 3145736 | tf_op jit(solution)/shard_map/ppermute | solution.py:22
  244.3 23.9 %collective-permute-start.8 = (bf16[1280,2048]{1,0:T(8,128)(2,1)}, bf16[1280,2048]{1,0:T(8,128)(2,1)}, u32[]{:S(2)}, u32[]{:S(2)}) collective-permute-start(bf16[1280,2048]{1,0:T(8,128)(2,1)} %half_grads.6), channel_id=1, source_target_pairs={{0,4},{4,0},{8,12},{12,8},{16,20},{20,16},{24,28},{28,24},{1,5},{5... | collective-permute-start | bytes 15728648 | tf_op jit(solution)/shard_map/ppermute | solution.py:27
  267.4 44.3 %collective-permute-start.11 = (bf16[1024,2048]{1,0:T(8,128)(2,1)}, bf16[1024,2048]{1,0:T(8,128)(2,1)}, u32[]{:S(2)}, u32[]{:S(2)}) collective-permute-start(bf16[1024,2048]{1,0:T(8,128)(2,1)} %half_grads.7), channel_id=1, source_target_pairs={{0,4},{4,0},{8,12},{12,8},{16,20},{20,16},{24,28},{28,24},{1,5},{5... | collective-permute-start | bytes 12582920 | tf_op jit(solution)/shard_map/ppermute | solution.py:27
  267.9 235.5 %all-gather.9.cloned.1.call-start = ((), (), s32[]{:S(2)}) async-start(), calls=%async_computation.8 | async-start | bytes 11796480 | tf_op jit(solution)/shard_map/all_gather | solution.py:675
  281.5 44.4 %collective-permute-start.9 = (bf16[2,160,2048]{2,1,0:T(8,128)(2,1)S(1)}, bf16[2,160,2048]{2,1,0:T(8,128)(2,1)S(1)}, u32[]{:S(2)}, u32[]{:S(2)}) collective-permute-start(bf16[2,160,2048]{2,1,0:T(8,128)(2,1)S(1)} %dynamic-slice_bitcast_fusion.1), channel_id=1, source_target_pairs={{0,8},{4,12},{8,0},{12,4},{16,24},{20,28},{24,16},{28,20},{1,9},{5... | collective-permute-start | bytes 3932168 | tf_op jit(solution)/shard_map/ppermute | solution.py:27
  285.8 40.1 %collective-permute-start.10 = (bf16[2,160,2048]{2,1,0:T(8,128)(2,1)}, bf16[2,160,2048]{2,1,0:T(8,128)(2,1)}, u32[]{:S(2)}, u32[]{:S(2)}) collective-permute-start(bf16[2,160,2048]{2,1,0:T(8,128)(2,1)} %dynamic-slice_bitcast_fusion), channel_id=1, source_target_pairs={{0,16},{4,20},{8,24},{12,28},{16,0},{20,4},{24,8},{28,12},{1,17},{... | collective-permute-start | bytes 3932168 | tf_op jit(solution)/shard_map/ppermute | solution.py:27
  293.5 32.4 %slice-start = ((s8[5242880]{0:T(1024)(128)(4,1)}), s8[4194304]{0:T(1024)(128)(4,1)S(1)}, s32[]{:S(2)}) async-start(s8[5242880]{0:T(1024)(128)(4,1)} %bitcast.103), calls=%async_computation.10 | async-start | bytes 8388608
  328.5 46.0 %collective-permute-start.12 = (bf16[160,2048]{1,0:T(8,128)(2,1)S(1)}, bf16[160,2048]{1,0:T(8,128)(2,1)S(1)}, u32[]{:S(2)}, u32[]{:S(2)}) collective-permute-start(bf16[160,2048]{1,0:T(8,128)(2,1)S(1)} %dynamic-slice_bitcast_fusion.7), channel_id=1, source_target_pairs={{0,16},{4,20},{8,24},{12,28},{16,0},{20,4},{24,8},{28,12},{1,17},{... | collective-permute-start | bytes 1966088 | tf_op jit(solution)/shard_map/ppermute | solution.py:27
  329.0 45.4 %collective-permute-start.13 = (bf16[160,2048]{1,0:T(8,128)(2,1)S(1)}, bf16[160,2048]{1,0:T(8,128)(2,1)S(1)}, u32[]{:S(2)}, u32[]{:S(2)}) collective-permute-start(bf16[160,2048]{1,0:T(8,128)(2,1)S(1)} %dynamic-slice_bitcast_fusion.6), channel_id=1, source_target_pairs={{0,8},{4,12},{8,0},{12,4},{16,24},{20,28},{24,16},{28,20},{1,9},{5... | collective-permute-start | bytes 1966088 | tf_op jit(solution)/shard_map/ppermute | solution.py:27
  329.5 45.4 %collective-permute-start.14 = (bf16[2,128,2048]{2,1,0:T(8,128)(2,1)}, bf16[2,128,2048]{2,1,0:T(8,128)(2,1)S(1)}, u32[]{:S(2)}, u32[]{:S(2)}) collective-permute-start(bf16[2,128,2048]{2,1,0:T(8,128)(2,1)} %dynamic-slice_bitcast_fusion.3), channel_id=1, source_target_pairs={{0,8},{4,12},{8,0},{12,4},{16,24},{20,28},{24,16},{28,20},{1,9},{5... | collective-permute-start | bytes 3145736 | tf_op jit(solution)/shard_map/ppermute | solution.py:27
  331.0 43.9 %collective-permute-start.15 = (bf16[2,128,2048]{2,1,0:T(8,128)(2,1)}, bf16[2,128,2048]{2,1,0:T(8,128)(2,1)S(1)}, u32[]{:S(2)}, u32[]{:S(2)}) collective-permute-start(bf16[2,128,2048]{2,1,0:T(8,128)(2,1)} %dynamic-slice_bitcast_fusion.2), channel_id=1, source_target_pairs={{0,16},{4,20},{8,24},{12,28},{16,0},{20,4},{24,8},{28,12},{1,17},{... | collective-permute-start | bytes 3145736 | tf_op jit(solution)/shard_map/ppermute | solution.py:27
  386.1 6.0 %collective-permute-start.19 = (bf16[1024,1536]{1,0:T(8,128)(2,1)}, bf16[1024,1536]{1,0:T(8,128)(2,1)}, u32[]{:S(2)}, u32[]{:S(2)}) collective-permute-start(bf16[1024,1536]{1,0:T(8,128)(2,1)} %half_grads.10), channel_id=1, source_target_pairs={{0,4},{4,0},{8,12},{12,8},{16,20},{20,16},{24,28},{28,24},{1,5},{5... | collective-permute-start | bytes 9437192 | tf_op jit(solution)/shard_map/ppermute | solution.py:27
  386.1 31.5 %collective-permute-start.16 = (bf16[256,2048]{1,0:T(8,128)(2,1)}, bf16[256,2048]{1,0:T(8,128)(2,1)}, u32[]{:S(2)}, u32[]{:S(2)}) collective-permute-start(bf16[256,2048]{1,0:T(8,128)(2,1)} %slice.62), channel_id=1, source_target_pairs={{0,1},{1,2},{2,3},{3,0},{4,5},{5,6},{6,7},{7,4},{8,9},{9,10},{10,1... | collective-permute-start | bytes 3145736 | tf_op jit(solution)/shard_map/ppermute | solution.py:22
  387.3 26.0 %collective-permute-start.17 = (bf16[128,2048]{1,0:T(8,128)(2,1)}, bf16[128,2048]{1,0:T(8,128)(2,1)}, u32[]{:S(2)}, u32[]{:S(2)}) collective-permute-start(bf16[128,2048]{1,0:T(8,128)(2,1)} %dynamic-slice_bitcast_fusion.9), channel_id=1, source_target_pairs={{0,16},{4,20},{8,24},{12,28},{16,0},{20,4},{24,8},{28,12},{1,17},{... | collective-permute-start | bytes 1572872 | tf_op jit(solution)/shard_map/ppermute | solution.py:27
  387.9 26.3 %collective-permute-start.18 = (bf16[128,2048]{1,0:T(8,128)(2,1)}, bf16[128,2048]{1,0:T(8,128)(2,1)}, u32[]{:S(2)}, u32[]{:S(2)}) collective-permute-start(bf16[128,2048]{1,0:T(8,128)(2,1)} %dynamic-slice_bitcast_fusion.8), channel_id=1, source_target_pairs={{0,8},{4,12},{8,0},{12,4},{16,24},{20,28},{24,16},{28,20},{1,9},{5... | collective-permute-start | bytes 1572872 | tf_op jit(solution)/shard_map/ppermute | solution.py:27
  402.4 35.2 %collective-permute-start.21 = (bf16[2,128,1536]{2,1,0:T(8,128)(2,1)}, bf16[2,128,1536]{2,1,0:T(8,128)(2,1)}, u32[]{:S(2)}, u32[]{:S(2)}) collective-permute-start(bf16[2,128,1536]{2,1,0:T(8,128)(2,1)} %dynamic-slice_bitcast_fusion.5), channel_id=1, source_target_pairs={{0,8},{4,12},{8,0},{12,4},{16,24},{20,28},{24,16},{28,20},{1,9},{5... | collective-permute-start | bytes 2359304 | tf_op jit(solution)/shard_map/ppermute | solution.py:27
  405.2 33.3 %collective-permute-start.22 = (bf16[2,128,1536]{2,1,0:T(8,128)(2,1)}, bf16[2,128,1536]{2,1,0:T(8,128)(2,1)}, u32[]{:S(2)}, u32[]{:S(2)}) collective-permute-start(bf16[2,128,1536]{2,1,0:T(8,128)(2,1)} %dynamic-slice_bitcast_fusion.4), channel_id=1, source_target_pairs={{0,16},{4,20},{8,24},{12,28},{16,0},{20,4},{24,8},{28,12},{1,17},{... | collective-permute-start | bytes 2359304 | tf_op jit(solution)/shard_map/ppermute | solution.py:27
  420.7 41.8 %collective-permute-start.20 = (bf16[256,2048]{1,0:T(8,128)(2,1)}, bf16[256,2048]{1,0:T(8,128)(2,1)}, u32[]{:S(2)}, u32[]{:S(2)}) collective-permute-start(bf16[256,2048]{1,0:T(8,128)(2,1)} %add_convert_fusion.2), channel_id=1, source_target_pairs={{0,1},{1,2},{2,3},{3,0},{4,5},{5,6},{6,7},{7,4},{8,9},{9,10},{10,1... | collective-permute-start | bytes 3145736 | tf_op jit(solution)/shard_map/ppermute | solution.py:22
  422.8 46.0 %all-to-all-start.2 = ((bf16[4,64,2048]{2,1,0:T(8,128)(2,1)}), bf16[4,64,2048]{2,1,0:T(8,128)(2,1)}, u32[]{:S(2)}, u32[]{:S(2)}) async-start(bf16[4,64,2048]{2,1,0:T(8,128)(2,1)} %bitcast.115), calls=%async_computation.3 | async-start | bytes 2097152 | tf_op jit(solution)/shard_map/all_to_all | solution.py:173
  427.1 119.8 %all-gather.11.cloned.1.call-start = ((), (), s32[]{:S(2)}) async-start(), calls=%async_computation.9 | async-start | bytes 9437184 | tf_op jit(solution)/shard_map/all_gather | solution.py:675
  441.6 19.9 %collective-permute-start.23 = (bf16[128,1536]{1,0:T(8,128)(2,1)S(1)}, bf16[128,1536]{1,0:T(8,128)(2,1)S(1)}, u32[]{:S(2)}, u32[]{:S(2)}) collective-permute-start(bf16[128,1536]{1,0:T(8,128)(2,1)S(1)} %dynamic-slice_bitcast_fusion.11), channel_id=1, source_target_pairs={{0,16},{4,20},{8,24},{12,28},{16,0},{20,4},{24,8},{28,12},{1,17},{... | collective-permute-start | bytes 1179656 | tf_op jit(solution)/shard_map/ppermute | solution.py:27
  442.4 19.8 %collective-permute-start.24 = (bf16[128,1536]{1,0:T(8,128)(2,1)S(1)}, bf16[128,1536]{1,0:T(8,128)(2,1)S(1)}, u32[]{:S(2)}, u32[]{:S(2)}) collective-permute-start(bf16[128,1536]{1,0:T(8,128)(2,1)S(1)} %dynamic-slice_bitcast_fusion.10), channel_id=1, source_target_pairs={{0,8},{4,12},{8,0},{12,4},{16,24},{20,28},{24,16},{28,20},{1,9},{5... | collective-permute-start | bytes 1179656 | tf_op jit(solution)/shard_map/ppermute | solution.py:27
  499.0 26.1 %collective-permute-start.25 = (bf16[256,2048]{1,0:T(8,128)(2,1)S(1)}, bf16[256,2048]{1,0:T(8,128)(2,1)}, u32[]{:S(2)}, u32[]{:S(2)}) collective-permute-start(bf16[256,2048]{1,0:T(8,128)(2,1)S(1)} %add_convert_fusion.1), channel_id=1, source_target_pairs={{0,1},{1,2},{2,3},{3,0},{4,5},{5,6},{6,7},{7,4},{8,9},{9,10},{10,1... | collective-permute-start | bytes 3145736 | tf_op jit(solution)/shard_map/ppermute | solution.py:22
  501.9 36.4 %collective-permute-start.27 = (bf16[64,6144]{1,0:T(8,128)(2,1)S(1)}, bf16[64,6144]{1,0:T(8,128)(2,1)S(1)}, u32[]{:S(2)}, u32[]{:S(2)}) collective-permute-start(bf16[64,6144]{1,0:T(8,128)(2,1)S(1)} %copy-done.5), channel_id=1, source_target_pairs={{0,8},{4,12},{8,0},{12,4},{16,24},{20,28},{24,16},{28,20},{1,9},{5... | collective-permute-start | bytes 2359304 | tf_op jit(solution)/shard_map/ppermute | solution.py:27
  502.3 36.5 %collective-permute-start.28 = (bf16[64,6144]{1,0:T(8,128)(2,1)S(1)}, bf16[64,6144]{1,0:T(8,128)(2,1)S(1)}, u32[]{:S(2)}, u32[]{:S(2)}) collective-permute-start(bf16[64,6144]{1,0:T(8,128)(2,1)S(1)} %copy-done.5), channel_id=1, source_target_pairs={{0,16},{4,20},{8,24},{12,28},{16,0},{20,4},{24,8},{28,12},{1,17},{... | collective-permute-start | bytes 2359304 | tf_op jit(solution)/shard_map/ppermute | solution.py:27
  531.5 7.3 %collective-permute-start.26 = (f32[2,3072]{1,0:T(2,128)S(1)}, f32[2,3072]{1,0:T(2,128)S(1)}, u32[]{:S(2)}, u32[]{:S(2)}) collective-permute-start(f32[2,3072]{1,0:T(2,128)S(1)} %constant_dynamic-slice_fusion.5), channel_id=1, source_target_pairs={{0,2},{1,3},{2,0},{3,1},{4,6},{5,7},{6,4},{7,5},{8,10},{9,11},{10,... | collective-permute-start | bytes 73736 | tf_op jit(solution)/shard_map/ppermute | solution.py:27
  540.2 4.0 collective-permute-start.29
  540.8 17.9 %collective-permute-start.32 = (bf16[32,6144]{1,0:T(8,128)(2,1)S(1)}, bf16[32,6144]{1,0:T(8,128)(2,1)S(1)}, u32[]{:S(2)}, u32[]{:S(2)}) collective-permute-start(bf16[32,6144]{1,0:T(8,128)(2,1)S(1)} %slice.69), channel_id=1, source_target_pairs={{0,16},{4,20},{8,24},{12,28},{16,0},{20,4},{24,8},{28,12},{1,17},{... | collective-permute-start | bytes 1179656 | tf_op jit(solution)/shard_map/ppermute | solution.py:27
  541.8 16.8 %collective-permute-start.33 = (bf16[32,6144]{1,0:T(8,128)(2,1)S(1)}, bf16[32,6144]{1,0:T(8,128)(2,1)}, u32[]{:S(2)}, u32[]{:S(2)}) collective-permute-start(bf16[32,6144]{1,0:T(8,128)(2,1)S(1)} %slice.70), channel_id=1, source_target_pairs={{0,8},{4,12},{8,0},{12,4},{16,24},{20,28},{24,16},{28,20},{1,9},{5... | collective-permute-start | bytes 1179656 | tf_op jit(solution)/shard_map/ppermute | solution.py:27
  545.0 1.3 collective-permute-start.30
  559.7 10.5 %collective-permute-start.35 = (bf16[64,6144]{1,0:T(8,128)(2,1)S(1)}, bf16[64,6144]{1,0:T(8,128)(2,1)S(1)}, u32[]{:S(2)}, u32[]{:S(2)}) collective-permute-start(bf16[64,6144]{1,0:T(8,128)(2,1)S(1)} %copy-done.5), channel_id=1, source_target_pairs={{0,4},{4,0},{8,12},{12,8},{16,20},{20,16},{24,28},{28,24},{1,5},{5... | collective-permute-start | bytes 2359304 | tf_op jit(solution)/shard_map/ppermute | solution.py:27
  559.9 10.2 %collective-permute-start.36 = (bf16[64,6144]{1,0:T(8,128)(2,1)S(1)}, bf16[64,6144]{1,0:T(8,128)(2,1)S(1)}, u32[]{:S(2)}, u32[]{:S(2)}) collective-permute-start(bf16[64,6144]{1,0:T(8,128)(2,1)S(1)} %collective-permute-done.27.refs_2_), channel_id=1, source_target_pairs={{0,4},{4,0},{8,12},{12,8},{16,20},{20,16},{24,28},{28,24},{1,5},{5... | collective-permute-start | bytes 2359304 | tf_op jit(solution)/shard_map/ppermute | solution.py:27
  560.3 9.9 %collective-permute-start.37 = (bf16[64,6144]{1,0:T(8,128)(2,1)S(1)}, bf16[64,6144]{1,0:T(8,128)(2,1)S(1)}, u32[]{:S(2)}, u32[]{:S(2)}) collective-permute-start(bf16[64,6144]{1,0:T(8,128)(2,1)S(1)} %collective-permute-done.28.refs_4_), channel_id=1, source_target_pairs={{0,4},{4,0},{8,12},{12,8},{16,20},{20,16},{24,28},{28,24},{1,5},{5... | collective-permute-start | bytes 2359304 | tf_op jit(solution)/shard_map/ppermute | solution.py:27
  560.4 9.8 %collective-permute-start.38 = (bf16[64,6144]{1,0:T(8,128)(2,1)S(1)}, bf16[64,6144]{1,0:T(8,128)(2,1)S(1)}, u32[]{:S(2)}, u32[]{:S(2)}) collective-permute-start(bf16[64,6144]{1,0:T(8,128)(2,1)S(1)} %pad_maximum_fusion.5.refs_6_), channel_id=1, source_target_pairs={{0,4},{4,0},{8,12},{12,8},{16,20},{20,16},{24,28},{28,24},{1,5},{5... | collective-permute-start | bytes 2359304 | tf_op jit(solution)/shard_map/ppermute | solution.py:27
  560.8 3.8 collective-permute-start.31
  564.6 3.8 collective-permute-start.34
  (24 other events, 217.1 us)
Sparse Core Ops, SparseCore 0:
  45.5 44.6 all-gather.4
  97.5 52.6 all-gather.6
  268.0 78.2 reduce-scatter.1
  378.8 91.7 all-gather.8
  472.5 70.3 all-gather.10

commit v4 on v3

--- a/solution.py
+++ b/solution.py
@@ -116,8 +116,9 @@
             for part in range(count)
         )
 
-    def send(self, line):
-        sent = line.step(self.outgoing, *self.arrays)
+    def send(self, line, sent=None):
+        if sent is None:
+            sent = line.step(self.outgoing, *self.arrays)
         self.came = [
             swap(piece, "rep", 1 << todo[0]) for piece, todo in zip(sent, self.todo)
         ]
@@ -169,6 +170,37 @@
         return lax.slice_in_dim(self.array, 0, self.block(0)[1], axis=0), self.came
 
 
+def place_kernel(width, place_ref, *refs):
+    *pieces, out_ref = refs
+    size = len(pieces)
+    length, columns = pieces[0].shape
+    for hop, piece in enumerate(pieces):
+        owner = lax.rem(place_ref[0] - hop + size, size)
+        if width is None:
+            out_ref[pl.ds(pl.multiple_of(owner * length, length), length), :] = piece[...]
+        else:
+            count = columns // width
+            for at in range(count):
+                first = pl.multiple_of((at * size + owner) * width, width)
+                out_ref[:, pl.ds(first, width)] = piece[:, at * width : (at + 1) * width]
+
+
+def placed(pieces, place, width=None):
+    length, columns = pieces[0].shape
+    shape = (
+        (length * len(pieces), columns) if width is None else (length, columns * len(pieces))
+    )
+    whole = pl.BlockSpec(memory_space=pltpu.VMEM)
+    return pl.pallas_call(
+        functools.partial(place_kernel, width),
+        in_specs=[pl.BlockSpec(memory_space=pltpu.SMEM)] + [whole] * len(pieces),
+        out_specs=whole,
+        out_shape=jax.ShapeDtypeStruct(shape, pieces[0].dtype),
+        compiler_params=ROOM,
+        name="placed",
+    )(place.reshape(1), *pieces)
+
+
 def exchanged(array):
     return lax.all_to_all(array, "shard", 0, 0, tiled=True)
 
@@ -277,6 +309,78 @@
     if more:
         total = total + more[0][...].astype(F32)
     out_ref[...] = total.astype(BF)
+
+
+def chip_of(step):
+    return step // 2, (step + 1) // 2 % 2
+
+
+def grad_sum_kernel(at_ref, left_ref, right_ref, *refs):
+    *more, came_ref, own_ref, fast_ref, slow_ref = refs
+    left = left_ref[...]
+    if more:
+        both = more[0][...]
+        lanes = both.shape[1] // 2
+        left = jnp.concatenate(
+            [left, jnp.where(at_ref[0] == 0, both[:, :lanes], both[:, lanes:])], axis=1
+        )
+    total = (contract_rows(left, right_ref[...]) + came_ref[...].astype(F32)).astype(BF)
+    own_ref[...] = total
+    slow, fast = chip_of(pl.program_id(0))
+    half = total.shape[0] // 2
+
+    @pl.when(fast == 1)
+    def _():
+        fast_ref[0] = total[:half]
+
+    @pl.when(slow == 1)
+    def _():
+        slow_ref[0] = total[half:]
+
+
+def grad_sums(left, right, rep, came, also=None):
+    tokens, height = left.shape
+    length = right.shape[1]
+    height //= 8
+    extra = 0 if also is None else also.shape[1] // 8
+    total = height + extra
+    block = lambda j, at: 2 * (at[2] ^ chip_of(j)[0]) + (at[1] ^ chip_of(j)[1])
+    half = (1, total // 2, length)
+    return pl.pallas_call(
+        grad_sum_kernel,
+        grid_spec=pltpu.PrefetchScalarGridSpec(
+            num_scalar_prefetch=1,
+            grid=(4,),
+            in_specs=[
+                pl.BlockSpec((tokens, height), lambda j, at: (0, 2 * block(j, at) + at[0])),
+                pl.BlockSpec(memory_space=pltpu.VMEM),
+            ]
+            + (
+                []
+                if also is None
+                else [pl.BlockSpec((tokens, 128), lambda j, at: (0, block(j, at)))]
+            )
+            + [pl.BlockSpec((total, length), lambda j, at: (block(j, at), 0))],
+            out_specs=[
+                pl.BlockSpec((total, length), lambda j, at: (block(j, at), 0)),
+                pl.BlockSpec(half, lambda j, at: (at[2] ^ (j // 2), 0, 0)),
+                pl.BlockSpec(half, lambda j, at: (at[1] ^ (1 - j // 3), 0, 0)),
+            ],
+        ),
+        out_shape=[
+            jax.ShapeDtypeStruct((4 * total, length), BF),
+            jax.ShapeDtypeStruct((2,) + half[1:], BF),
+            jax.ShapeDtypeStruct((2,) + half[1:], BF),
+        ],
+        compiler_params=ROOM,
+        name="grad_sums",
+    )(
+        jnp.stack([rep & 1, (rep >> 1) & 1, rep >> 2]),
+        left,
+        right,
+        *([] if also is None else [also]),
+        came,
+    )
 
 
 def half_grads(left, right, which, reps, came=None, also=None):
@@ -307,7 +411,7 @@
             grid=(reps // 2,),
             in_specs=[
                 pl.BlockSpec((tokens, height), lambda b, w: (0, 2 * b + w[0])),
-                pl.BlockSpec((tokens, length), lambda b, w: (0, 0)),
+                pl.BlockSpec(memory_space=pltpu.VMEM),
             ]
             + more_specs
             + ([] if came is None else [block]),
@@ -400,7 +504,7 @@
         pull_kernel,
         grid=(hidden // tile,),
         in_specs=[
-            pl.BlockSpec((height, width), lambda j: (0, 0)),
+            pl.BlockSpec(memory_space=pltpu.VMEM),
             pl.BlockSpec((tile, width), lambda j: (j, 0)),
         ]
         + [block] * len(slope),
@@ -428,7 +532,7 @@
     height = a.shape[0]
     length = b.shape[0 if transposed else 1]
     tile = min(512, length)
-    full = lambda x: pl.BlockSpec(x.shape, lambda j, z: (0, 0))
+    full = lambda x: pl.BlockSpec(memory_space=pltpu.VMEM)
     if transposed:
         part = lambda x: pl.BlockSpec((tile, x.shape[1]), lambda j, z: (j, 0))
     else:
@@ -445,6 +549,32 @@
         compiler_params=ROOM,
         name="push",
     )(place.reshape(1), a, b, c, d)
+
+
+def project_kernel(rows_ref, weight_ref, bias_ref, *refs):
+    refs[-1][...] = times(rows_ref[...], weight_ref[...]) + bias_ref[...]
+
+
+def project(normed_all, weight, bias, tokens, first, count, before):
+    height, width = normed_all.shape
+    length = weight.shape[1]
+    tile = length // 3
+    here = first // count
+    return pl.pallas_call(
+        project_kernel,
+        grid=(3,),
+        in_specs=[
+            pl.BlockSpec((count * tokens, width), lambda j: (here, 0)),
+            pl.BlockSpec((width, tile), lambda j: (0, j)),
+            pl.BlockSpec((1, tile), lambda j: (0, j)),
+        ]
+        + [ANY] * len(before),
+        out_specs=pl.BlockSpec((count * tokens, tile), lambda j: (here, j)),
+        out_shape=jax.ShapeDtypeStruct((height, length), F32),
+        input_output_aliases={3: 0} if before else {},
+        compiler_params=ROOM,
+        name="project",
+    )(normed_all, weight, bias, *before)
 
 
 def turned(u, turn, sign):
@@ -674,22 +804,18 @@
     def gathered(array):
         return lax.all_gather(array, "rep", axis=0, tiled=True)
 
-    small = jnp.concatenate(
-        [ln_gain, ln_bias, b_qkv, b_dense + b_fc2, positions.astype(F32)]
-    ).reshape(1, -1)
-    small = doubled(small, place, line)
+    owners = [(place + hop) % group for hop in range(group)]
+
     def qkv_rows(w):
-        return jnp.concatenate(
-            [
-                jnp.concatenate(
-                    [
-                        lax.dynamic_slice(w, (rep * slab, at * width + owner * rows), (slab, rows))
-                        for at in range(3)
-                    ],
-                    axis=1,
-                )
-                for owner in range(group)
-            ]
+        return tuple(
+            jnp.concatenate(
+                [
+                    lax.dynamic_slice(w, (rep * slab, at * width + owner * rows), (slab, rows))
+                    for at in range(3)
+                ],
+                axis=1,
+            )
+            for owner in owners
         )
 
     def fc1_rows(w):
@@ -700,19 +826,26 @@
             ]
         )
 
-    qkv_pieces = exchanged(line.step(qkv_rows, w_qkv))
+    qkv_pieces = [
+        piece if hop == 0 else ring(piece, "shard", hop)
+        for hop, piece in enumerate(line.step(qkv_rows, w_qkv))
+    ]
     fc1_pieces = exchanged(line.step(fc1_rows, w_fc1))
+    small = jnp.concatenate(
+        [ln_gain, ln_bias, b_qkv, b_dense + b_fc2, positions.astype(F32)]
+    ).reshape(1, -1)
+    small = doubled(small, place, line)
     gain = small[:, :rows].reshape(width)
     shift = small[:, rows : 2 * rows].reshape(width)
     bias_qkv = lax.dynamic_slice_in_dim(
         small[:, 2 * rows : 5 * rows].reshape(3, width), place * rows, rows, 1
-    ).reshape(3 * rows)
+    ).reshape(1, 3 * rows)
     bias_out = small[:, 5 * rows : 6 * rows].reshape(width)
     group_positions = small[:, 6 * rows :]
 
     normed = [line.step(lambda *o: ln_forward(*o, reps, group), inputs, gain, shift)]
     normed.append(ring(line.hold(normed[0]), "shard", 1))
-    qkv_cols = gathered(line.hold(qkv_pieces))
+    qkv_cols = gathered(line.step(lambda *p: placed(p, place), *qkv_pieces))
 
     ring_order = [(place - hop) % group for hop in range(group)]
     ring_positions = jnp.concatenate(
@@ -758,6 +891,15 @@
 
     normed_all = line.step(begin, normed[0])
     cot_all = line.step(begin, cotangent)
+    def project_some(first, count, *before):
+        return line.step(
+            lambda a, b, c, *d: project(a, b, c, tokens, first, count, d),
+            normed_all,
+            qkv_cols,
+            bias_qkv,
+            *before,
+        )
+
     for hop in range(1, group):
         normed[hop] = line.hold(normed[hop])
         if hop == 1:
@@ -768,10 +910,10 @@
             cots = [line.hold(cotangent)]
             cots.append(ring(cots[0], "shard", 1))
         normed_all = line.step(put(hop), normed_all, normed[hop])
-
-    projected = line.step(
-        lambda a, b, c: by_seq(times(a, b) + c), normed_all, qkv_cols, bias_qkv
-    )
+        if hop == group - 2:
+            projected = project_some(0, group - 1)
+
+    projected = by_seq(project_some(group - 1, 1, projected))
     calls = 2 if pairs > 1 else 1
     each = pairs // calls
     kept = []
@@ -814,6 +956,13 @@
         return swap(sent, "rep", 1)
 
     def grad_sum(left, right, came, *also):
+        if reps == 8 and not (left.shape[1] // reps % 128):
+            own, *sent = line.step(
+                lambda a, b, c, *d: grad_sums(a, b, rep, c, *d), left, right, came, *also
+            )
+            halving = Halving(rep, own, 2)
+            halving.send(line, sent)
+            return halving
         own = line.step(
             lambda a, b, c, *d: half_grads(a, b, core, reps, c, *d), left, right, came, *also
         )

time: 595 us -> 587 us (0.987)
  Pallas kernels: 213 us -> 236 us
  waiting for transfers between devices: 163 us -> 148 us
  matrix products: 33.4 us -> 21.9 us
  local copies, waits for them, and re-layouts: 49.6 us -> 42 us
    pallas_call x0 -> x6, Pallas kernels: none -> 52.2 us  [the longest x3 33.8 us: grad_sums(): pl.pallas_call(grad_sum_kernel, grid_spec=pltpu.PrefetchScalarGridSpec(nu...]
    pallas_call x6 -> x3, Pallas kernels: 56.7 us -> 27.1 us  [half_grads(): pl.pallas_call(grad_kernel, grid_spec=pltpu.PrefetchScalarGridSpec(num_sc...]
    all_to_all x3 -> x2, waiting for transfers between devices: 24.2 us -> 6.57 us  [exchanged(): return lax.all_to_all(array, 'shard', 0, 0, tiled=True)]
    dot_general x3 -> x2, matrix products: 33.4 us -> 21.9 us  [times(): return jnp.dot(left_side, right_side, preferred_element_type=F32)]
    reshape x12 -> x6, local copies, waits for them, and re-layouts: 14.6 us -> 4.21 us  [pick(): return half.reshape(half.shape[:axis] + half.shape[axis + 1:])]
    ppermute x9 -> x12, waiting for transfers between devices: 88.6 us -> 86 us  [ring(): lax.ppermute(array, axis, [(i, (i + distance) % size) for i in range(size)])]
    all_to_all x3 -> x2, starting transfers between devices: 12 us -> 10.1 us  [exchanged(): return lax.all_to_all(array, 'shard', 0, 0, tiled=True)]
  transfers between devices with their start and end apart: 47 -> 49, of which waited for: 22 -> 24; matrix products, arithmetic and copies ran while one was open for 20% -> 16% of each run, Pallas kernels for 33% -> 37%
where the time goes in v4:
time: 587 us; the launch traced here: 579 us
  Pallas kernels  236 us (40%)
  waiting for transfers between devices  148 us (25%)
  starting transfers between devices  48.2 us (8%)
  other arithmetic  44.8 us (8%)
  local copies, waits for them, and re-layouts  42 us (7%)
  blocking collectives  23.7 us (4%)
  matrix products  21.9 us (4%)
  between operations  15 us (3%)
    ppermute x12, waiting for transfers between devices, ring(): lax.ppermute(array, axis, [(i, (i + distance) % size) for i in range(size)])  86 us
    ppermute x30, waiting for transfers between devices, swap(): return lax.ppermute(array, axis, [(i, i ^ mask) for i in range(size)])  55 us
    pallas_call x2, Pallas kernels, push(): pl.pallas_call(functools.partial(push_kernel, transposed, size), grid_spe...  37 us
    pallas_call x2, Pallas kernels, attend_back(): pl.pallas_call(functools.partial(attend_back_kernel, block), grid_spec=pl...  36.2 us
    pallas_call x3, Pallas kernels, grad_sums(): pl.pallas_call(grad_sum_kernel, grid_spec=pltpu.PrefetchScalarGridSpec(nu...  33.8 us
    pallas_call x2, Pallas kernels, attend(): pl.pallas_call(functools.partial(attend_kernel, block), grid_spec=pltpu.P...  29.1 us
    ppermute x30, starting transfers between devices, swap(): return lax.ppermute(array, axis, [(i, i ^ mask) for i in range(size)])  27.2 us
    pallas_call x3, Pallas kernels, half_grads(): pl.pallas_call(grad_kernel, grid_spec=pltpu.PrefetchScalarGridSpec(num_sc...  27.1 us
  transfers between devices with their start and end apart: 49, of which 24 were waited for; matrix products, arithmetic and copies ran while one was open for 16% of the time, Pallas kernels for 37%

profile of v4, /device:TPU:0, one launch (start us, length us, event | category | flops | bytes accessed | tf_op | source)
XLA Modules:
  0.0 579.0 jit_solution(677296276565741583)
XLA Ops:
  15.2 3.0 collective-permute-start
  19.9 3.1 collective-permute-start.1
  28.2 3.2 ln_forward.1
  32.7 6.1 %collective-permute-done.3.refs_2_ = bf16[64,1536]{1,0:T(8,128)(2,1)S(1)} collective-permute-done((bf16[64,1536]{1,0:T(8,128)(2,1)S(1)}, bf16[64,1536]{1,0:T(8,128)(2,1)S(1)}, u32[]{:S(2)}, u32[]{:S(2)}) %collective-permute-start.3) | collective-permute-done | bytes 196640 | tf_op jit(solution)/shard_map/ppermute | solution.py:22
  41.7 6.6 %all-to-all-start = ((bf16[4,64,2048]{2,1,0:T(8,128)(2,1)}), bf16[4,64,2048]{2,1,0:T(8,128)(2,1)}, u32[]{:S(2)}, u32[]{:S(2)}) async-start(bf16[4,64,2048]{2,1,0:T(8,128)(2,1)} %bitcast.10), calls=%async_computation | async-start | bytes 2097152 | tf_op jit(solution)/shard_map/all_to_all | solution.py:205
  48.3 2.4 collective-permute-start.5
  57.5 3.8 concatenate.75
  61.3 2.4 concatenate.76
  63.8 27.8 %collective-permute-done.5 = bf16[256,2048]{1,0:T(8,128)(2,1)} collective-permute-done((bf16[256,2048]{1,0:T(8,128)(2,1)}, bf16[256,2048]{1,0:T(8,128)(2,1)}, u32[]{:S(2)}, u32[]{:S(2)}) %collective-permute-start.5) | collective-permute-done | bytes 1048608 | tf_op jit(solution)/shard_map/ppermute | solution.py:22
  91.6 4.6 all-to-all-done
  98.8 23.6 %collective-permute-done.6 = bf16[256,2048]{1,0:T(8,128)(2,1)S(1)} collective-permute-done((bf16[256,2048]{1,0:T(8,128)(2,1)}, bf16[256,2048]{1,0:T(8,128)(2,1)S(1)}, u32[]{:S(2)}, u32[]{:S(2)}) %collective-permute-start.6) | collective-permute-done | bytes 1048608 | tf_op jit(solution)/shard_map/ppermute | solution.py:22
  124.1 10.2 %project.2.refs_0_ = f32[1024,1536]{1,0:T(8,128)} custom-call(bf16[1024,2048]{1,0:T(8,128)(2,1)} %constant_dynamic-update-slice_fusion.11.rows_ref, bf16[2048,1536]{1,0:T(8,128)(2,1)} %all-gather.5.cloned.1.call-done.weight_ref.b_ref, f32[1,1536]{1,0:T(1,128)} %bitcast.104), custom_call_target="tpu_custom_call" | custom-call | tf_op jit(solution)/shard_map/project/pallas_call | solution.py:563
  134.3 13.1 %collective-permute-done.7 = bf16[256,2048]{1,0:T(8,128)(2,1)S(1)} collective-permute-done((bf16[256,2048]{1,0:T(8,128)(2,1)S(1)}, bf16[256,2048]{1,0:T(8,128)(2,1)S(1)}, u32[]{:S(2)}, u32[]{:S(2)}) %collective-permute-start.7) | collective-permute-done | bytes 1048608 | tf_op jit(solution)/shard_map/ppermute | solution.py:22
  149.2 6.1 %project.3.q_ref.k_ref.v_ref = f32[1024,1536]{1,0:T(8,128)} custom-call(bf16[1024,2048]{1,0:T(8,128)(2,1)} %constant_dynamic-update-slice_fusion.10.rows_ref.left_ref, bf16[2048,1536]{1,0:T(8,128)(2,1)} %all-gather.5.cloned.1.call-done.weight_ref.b_ref, f32[1,1536]{1,0:T(1,128)} %bitcast.105, ...), custom_call_target="tpu_custom_call", output_to_operand_aliasing={{}: (3, {})} | custom-call | tf_op jit(solution)/shard_map/project/pallas_call | solution.py:563
  155.3 14.5 %attend.2 = (bf16[1024,512]{1,0:T(8,128)(2,1)}, bf16[1,4,2560,256]{3,2,1,0:T(8,128)(2,1)}, bf16[3,1024,256]{2,1,0:T(8,128)(2,1)}) custom-call(s32[1]{0:T(128)} %bitcast.place_ref, f32[1024,1536]{1,0:T(8,128)} %project.3.q_ref.k_ref.v_ref, f32[1024,1536]{1,0:T(8,128)} %project.3.q_ref.k_ref.v_ref, f32[1024,1536]{1,0:T(8,128)} %project.3.q_ref.k_ref.v_ref, ...), custom_call_target="tpu_custom_call" | custom-call | tf_op jit(solution)/shard_map/attend/pallas_call | solution.py:636
  172.7 18.8 %add_convert_fusion = (bf16[1024,2048]{1,0:T(8,128)(2,1)}, bf16[1024,2048]{1,0:T(8,128)(2,1)}) fusion(f32[2048]{0:T(1024)S(1)} %copy-done.23, bf16[1024,2048]{1,0:T(8,128)(2,1)} %constant_dynamic-update-slice_fusion.10.rows_ref.left_ref, bf16[2048,2048]{1,0:T(8,128)(2,1)} %all-gather.7.cloned.1.call-done.d_ref), kind=kOutput, calls=%fused_computation | convolution fusion | flops 8631877632 | bytes 20979712 | tf_op jit(solution)/shard_map/dot_general | solution.py:43
  191.5 3.2 collective-permute-done.9
  196.2 14.5 %attend.3 = (bf16[1024,512]{1,0:T(8,128)(2,1)}, bf16[1,4,2560,256]{3,2,1,0:T(8,128)(2,1)}, bf16[3,1024,256]{2,1,0:T(8,128)(2,1)}) custom-call(s32[1]{0:T(128)} %bitcast.place_ref, f32[1024,1536]{1,0:T(8,128)} %project.3.q_ref.k_ref.v_ref, f32[1024,1536]{1,0:T(8,128)} %project.3.q_ref.k_ref.v_ref, ...), custom_call_target="tpu_custom_call", output_to_operand_aliasing={{0}: (6, {})} | custom-call | tf_op jit(solution)/shard_map/attend/pallas_call | solution.py:636
  210.7 15.8 %push.2 = bf16[1024,2048]{1,0:T(8,128)(2,1)} custom-call(s32[1]{0:T(128)} %bitcast.place_ref, bf16[1024,512]{1,0:T(8,128)(2,1)} %get-tuple-element.264.a_ref.refs_0_, bf16[512,2048]{1,0:T(8,128)(2,1)} %weight_ref.1, bf16[1024,2048]{1,0:T(8,128)(2,1)} %get-tuple-element.262.c_ref.left_ref, bf16[2048,2048]{1,0:T(8,128)(2,1)} %weight_ref), custom_call_target="tpu_custom_call" | custom-call | tf_op jit(solution)/shard_map/push/pallas_call | solution.py:540
  227.6 10.9 %half_grads.3 = bf16[1280,2048]{1,0:T(8,128)(2,1)} custom-call(s32[1]{0:T(128)} %bitcast.12.which_ref, bf16[1024,2048]{1,0:T(8,128)(2,1)} %get-tuple-element.262.c_ref.left_ref, bf16[1024,2048]{1,0:T(8,128)(2,1)} %constant_dynamic-update-slice_fusion.7.right_ref.cot_ref, bf16[1024,512]{1,0:T(8,128)(2,1)} %get-tuple-element.264.a_ref.refs_0_), custom_call_target="tpu_custom_call" | custom-call | tf_op jit(solution)/shard_map/half_grads/pallas_call | solution.py:407
  238.5 14.4 %pull.2.right_ref.c_ref = bf16[1024,2048]{1,0:T(8,128)(2,1)} custom-call(bf16[1024,2048]{1,0:T(8,128)(2,1)} %constant_dynamic-update-slice_fusion.7.right_ref.cot_ref, bf16[2048,2048]{1,0:T(8,128)(2,1)} %weight_ref, bf16[1024,2048]{1,0:T(8,128)(2,1)} %get-tuple-element.259.refs_0_), custom_call_target="tpu_custom_call" | custom-call | tf_op jit(solution)/shard_map/pull/pallas_call | solution.py:503
  252.9 8.8 %half_grads.4 = bf16[1024,2048]{1,0:T(8,128)(2,1)} custom-call(s32[1]{0:T(128)} %bitcast.12.which_ref, bf16[1024,2048]{1,0:T(8,128)(2,1)} %constant_dynamic-update-slice_fusion.10.rows_ref.left_ref, bf16[1024,2048]{1,0:T(8,128)(2,1)} %pull.2.right_ref.c_ref), custom_call_target="tpu_custom_call" | custom-call | tf_op jit(solution)/shard_map/half_grads/pallas_call | solution.py:407
  263.1 13.5 %grad_sums.3 = (bf16[1280,2048]{1,0:T(8,128)(2,1)}, bf16[2,160,2048]{2,1,0:T(8,128)(2,1)}, bf16[2,160,2048]{2,1,0:T(8,128)(2,1)}) custom-call(s32[3]{0:T(128)} %pad_add_fusion.at_ref, bf16[1024,2048]{1,0:T(8,128)(2,1)} %get-tuple-element.262.c_ref.left_ref, bf16[1024,2048]{1,0:T(8,128)(2,1)} %constant_dynamic-update-slice_fusion.7.right_ref.cot_ref, ...), custom_call_target="tpu_custom_call" | custom-call | tf_op jit(solution)/shard_map/grad_sums/pallas_call | solution.py:349
  279.5 6.2 %pull.3.datt_ref = bf16[1024,512]{1,0:T(8,128)(2,1)} custom-call(bf16[1024,2048]{1,0:T(8,128)(2,1)} %constant_dynamic-update-slice_fusion.7.right_ref.cot_ref, bf16[512,2048]{1,0:T(8,128)(2,1)} %weight_ref.1), custom_call_target="tpu_custom_call" | custom-call | tf_op jit(solution)/shard_map/pull/pallas_call | solution.py:503
  285.7 18.0 %attend_back.2 = (bf16[1024,1536]{1,0:T(8,128)(2,1)}, f32[1,1,1536]{2,1,0:T(1,128)}) custom-call(s32[1]{0:T(128)} %bitcast.place_ref, bf16[1,4,2560,256]{3,2,1,0:T(8,128)(2,1)} %get-tuple-element.231.prob_ref, bf16[3,1024,256]{2,1,0:T(8,128)(2,1)} %get-tuple-element.232.low_ref, bf16[1024,512]{1,0:T(8,128)(2,1)} %pull.3.datt_ref, ...), custom_call_target="tpu_custom_call" | custom-call | tf_op jit(solution)/shard_map/attend_back/pallas_call | solution.py:721
  303.7 10.9 %grad_sums.4 = (bf16[1024,2048]{1,0:T(8,128)(2,1)}, bf16[2,128,2048]{2,1,0:T(8,128)(2,1)}, bf16[2,128,2048]{2,1,0:T(8,128)(2,1)}) custom-call(s32[3]{0:T(128)} %pad_add_fusion.at_ref, bf16[1024,2048]{1,0:T(8,128)(2,1)} %constant_dynamic-update-slice_fusion.10.rows_ref.left_ref, bf16[1024,2048]{1,0:T(8,128)(2,1)} %pull.2.right_ref.c_ref, ...), custom_call_target="tpu_custom_call" | custom-call | tf_op jit(solution)/shard_map/grad_sums/pallas_call | solution.py:349
  314.6 3.3 fusion
  323.0 18.2 %attend_back.3 = (bf16[1024,1536]{1,0:T(8,128)(2,1)}, f32[1,1,1536]{2,1,0:T(1,128)}) custom-call(s32[1]{0:T(128)} %bitcast.place_ref, bf16[1,4,2560,256]{3,2,1,0:T(8,128)(2,1)} %get-tuple-element.245.prob_ref, bf16[3,1024,256]{2,1,0:T(8,128)(2,1)} %get-tuple-element.246.low_ref, ...), custom_call_target="tpu_custom_call", output_to_operand_aliasing={{0}: (5, {}), {1}: (6, {})} | custom-call | tf_op jit(solution)/shard_map/attend_back/pallas_call | solution.py:721
  341.2 21.2 %push.3 = bf16[1024,2048]{1,0:T(8,128)(2,1)} custom-call(s32[1]{0:T(128)} %bitcast.place_ref, bf16[1024,1536]{1,0:T(8,128)(2,1)} %get-tuple-element.315.a_ref.right_ref, bf16[2048,1536]{1,0:T(8,128)(2,1)} %all-gather.5.cloned.1.call-done.weight_ref.b_ref, bf16[1024,2048]{1,0:T(8,128)(2,1)} %pull.2.right_ref.c_ref, ...), custom_call_target="tpu_custom_call" | custom-call | tf_op jit(solution)/shard_map/push/pallas_call | solution.py:540
  362.4 2.5 slice.62
  370.2 7.5 %half_grads.5 = bf16[1024,1536]{1,0:T(8,128)(2,1)} custom-call(s32[1]{0:T(128)} %bitcast.12.which_ref, bf16[1024,2048]{1,0:T(8,128)(2,1)} %constant_dynamic-update-slice_fusion.10.rows_ref.left_ref, bf16[1024,1536]{1,0:T(8,128)(2,1)} %get-tuple-element.315.a_ref.right_ref), custom_call_target="tpu_custom_call" | custom-call | tf_op jit(solution)/shard_map/half_grads/pallas_call | solution.py:407
  379.3 3.1 convert_add_fusion.4
  383.7 9.5 %grad_sums.5 = (bf16[1024,1536]{1,0:T(8,128)(2,1)}, bf16[2,128,1536]{2,1,0:T(8,128)(2,1)}, bf16[2,128,1536]{2,1,0:T(8,128)(2,1)}) custom-call(s32[3]{0:T(128)} %pad_add_fusion.at_ref, bf16[1024,2048]{1,0:T(8,128)(2,1)} %constant_dynamic-update-slice_fusion.10.rows_ref.left_ref, bf16[1024,1536]{1,0:T(8,128)(2,1)} %get-tuple-element.315.a_ref.right_ref, ...), custom_call_target="tpu_custom_call" | custom-call | tf_op jit(solution)/shard_map/grad_sums/pallas_call | solution.py:349
  395.0 8.9 %collective-permute-done.20 = bf16[128,2048]{1,0:T(8,128)(2,1)} collective-permute-done((bf16[128,2048]{1,0:T(8,128)(2,1)}, bf16[128,2048]{1,0:T(8,128)(2,1)}, u32[]{:S(2)}, u32[]{:S(2)}) %collective-permute-start.20) | collective-permute-done | bytes 524320 | tf_op jit(solution)/shard_map/ppermute | solution.py:27
  408.5 2.9 add_convert_fusion.2
  411.4 2.6 collective-permute-start.23
  414.1 3.5 all-to-all-start.1
  417.6 11.5 %collective-permute-done.24 = bf16[2,128,1536]{2,1,0:T(8,128)(2,1)} collective-permute-done((bf16[2,128,1536]{2,1,0:T(8,128)(2,1)}, bf16[2,128,1536]{2,1,0:T(8,128)(2,1)}, u32[]{:S(2)}, u32[]{:S(2)}) %collective-permute-start.24) | collective-permute-done | bytes 786464 | tf_op jit(solution)/shard_map/ppermute | solution.py:27
  437.0 3.1 fusion.14
  440.2 14.6 %collective-permute-done.26 = bf16[128,1536]{1,0:T(8,128)(2,1)S(1)} collective-permute-done((bf16[128,1536]{1,0:T(8,128)(2,1)}, bf16[128,1536]{1,0:T(8,128)(2,1)S(1)}, u32[]{:S(2)}, u32[]{:S(2)}) %collective-permute-start.26) | collective-permute-done | bytes 393248 | tf_op jit(solution)/shard_map/ppermute | solution.py:27
  462.8 23.7 %all_to_all.36 = bf16[4,64,1536]{2,1,0:T(8,128)(2,1)} all-to-all(bf16[4,64,1536]{2,1,0:T(8,128)(2,1)S(1)} %bitcast.92), channel_id=1, replica_groups=mesh['rep'=8,'shard'=4] {'shard'}, dimensions={0} | all-to-all | bytes 1572864 | tf_op jit(solution)/shard_map/all_to_all | solution.py:205
  490.9 2.6 slice.78.a_ref
  495.1 12.1 %split_rows.1 = (f32[2048,2048]{1,0:T(8,128)}, f32[512,2048]{1,0:T(8,128)}) custom-call(bf16[2560,2048]{1,0:T(8,128)(2,1)} %all-gather.9.cloned.1.call-done.in_ref), custom_call_target="tpu_custom_call" | custom-call | tf_op jit(solution)/shard_map/split_rows/pallas_call | solution.py:237
  507.2 9.1 %collective-permute-done.28.b_ref = bf16[256,2048]{1,0:T(8,128)(2,1)} collective-permute-done((bf16[256,2048]{1,0:T(8,128)(2,1)S(1)}, bf16[256,2048]{1,0:T(8,128)(2,1)}, u32[]{:S(2)}, u32[]{:S(2)}) %collective-permute-start.28) | collective-permute-done | bytes 1048608 | tf_op jit(solution)/shard_map/ppermute | solution.py:22
  516.3 5.5 ln_backward.1
  522.8 6.9 %collective-permute-done.30.refs_2_ = bf16[64,6144]{1,0:T(8,128)(2,1)S(1)} collective-permute-done((bf16[64,6144]{1,0:T(8,128)(2,1)S(1)}, bf16[64,6144]{1,0:T(8,128)(2,1)S(1)}, u32[]{:S(2)}, u32[]{:S(2)}) %collective-permute-start.30) | collective-permute-done | bytes 786464 | tf_op jit(solution)/shard_map/ppermute | solution.py:27
  538.1 11.8 %convert_element_type.255 = f32[512,8192]{1,0:T(8,128)} convert(bf16[512,8192]{1,0:T(8,128)(2,1)} %all-gather.11.cloned.1.call-done) | non-fusion elementwise | flops 4194304 | bytes 25165824 | tf_op jit(solution)/shard_map/convert_element_type | solution.py:1060
  563.1 8.4 %assemble.1 = f32[512,6144]{1,0:T(8,128)} custom-call(s32[1]{0:T(128)} %bitcast.44.rep_ref, bf16[64,6144]{1,0:T(8,128)(2,1)} %widened.3.refs_0_, bf16[64,6144]{1,0:T(8,128)(2,1)} %copy-done.12, bf16[64,6144]{1,0:T(8,128)(2,1)} %copy-done.9, bf16[64,6144]{1,0:T(8,128)(2,1)} %copy-done.13, bf16[64,6144]{1,0:T(8,128)(2,1)} %copy-done.10, ...), custom_call_target="tpu_custom_call" | custom-call | tf_op jit(solution)/shard_map/assemble/pallas_call | solution.py:285
  (233 shorter events, 106.0 us)
Async XLA Ops:
  7.2 116.9 %all-gather.5.cloned.1.call-start = ((), (), s32[]{:S(2)}) async-start(), calls=%async_computation.4 | async-start | bytes 7077888 | tf_op jit(solution)/shard_map/all_gather | solution.py:805
  15.2 4.7 collective-permute-start
  19.9 7.0 %collective-permute-start.1 = (f32[2,3328]{1,0:T(2,128)S(1)}, f32[2,3328]{1,0:T(2,128)S(1)}, u32[]{:S(2)}, u32[]{:S(2)}) collective-permute-start(f32[2,3328]{1,0:T(2,128)S(1)} %pad_maximum_fusion.10), channel_id=1, source_target_pairs={{0,2},{1,3},{2,0},{3,1},{4,6},{5,7},{6,4},{7,5},{8,10},{9,11},{10,... | collective-permute-start | bytes 79880 | tf_op jit(solution)/shard_map/ppermute | solution.py:27
  23.0 9.7 %collective-permute-start.2 = (bf16[64,1536]{1,0:T(8,128)(2,1)S(1)}, bf16[64,1536]{1,0:T(8,128)(2,1)S(1)}, u32[]{:S(2)}, u32[]{:S(2)}) collective-permute-start(bf16[64,1536]{1,0:T(8,128)(2,1)S(1)} %pad_maximum_fusion.7), channel_id=1, source_target_pairs={{0,1},{1,2},{2,3},{3,0},{4,5},{5,6},{6,7},{7,4},{8,9},{9,10},{10,1... | collective-permute-start | bytes 589832 | tf_op jit(solution)/shard_map/ppermute | solution.py:22
  24.6 14.2 %collective-permute-start.3 = (bf16[64,1536]{1,0:T(8,128)(2,1)S(1)}, bf16[64,1536]{1,0:T(8,128)(2,1)S(1)}, u32[]{:S(2)}, u32[]{:S(2)}) collective-permute-start(bf16[64,1536]{1,0:T(8,128)(2,1)S(1)} %pad_maximum_fusion.8), channel_id=1, source_target_pairs={{0,2},{1,3},{2,0},{3,1},{4,6},{5,7},{6,4},{7,5},{8,10},{9,11},{10,... | collective-permute-start | bytes 589832 | tf_op jit(solution)/shard_map/ppermute | solution.py:22
  24.9 13.9 %collective-permute-start.4 = (bf16[64,1536]{1,0:T(8,128)(2,1)S(1)}, bf16[64,1536]{1,0:T(8,128)(2,1)S(1)}, u32[]{:S(2)}, u32[]{:S(2)}) collective-permute-start(bf16[64,1536]{1,0:T(8,128)(2,1)S(1)} %pad_maximum_fusion.9), channel_id=1, source_target_pairs={{0,3},{1,0},{2,1},{3,2},{4,7},{5,4},{6,5},{7,6},{8,11},{9,8},{10,9... | collective-permute-start | bytes 589832 | tf_op jit(solution)/shard_map/ppermute | solution.py:22
  41.7 54.4 %all-to-all-start = ((bf16[4,64,2048]{2,1,0:T(8,128)(2,1)}), bf16[4,64,2048]{2,1,0:T(8,128)(2,1)}, u32[]{:S(2)}, u32[]{:S(2)}) async-start(bf16[4,64,2048]{2,1,0:T(8,128)(2,1)} %bitcast.10), calls=%async_computation | async-start | bytes 2097152 | tf_op jit(solution)/shard_map/all_to_all | solution.py:205
  48.3 124.4 %all-gather.7.cloned.1.call-start = ((), (), s32[]{:S(2)}) async-start(), calls=%async_computation.5 | async-start | bytes 9437184 | tf_op jit(solution)/shard_map/all_gather | solution.py:805
  48.3 43.2 %collective-permute-start.5 = (bf16[256,2048]{1,0:T(8,128)(2,1)}, bf16[256,2048]{1,0:T(8,128)(2,1)}, u32[]{:S(2)}, u32[]{:S(2)}) collective-permute-start(bf16[256,2048]{1,0:T(8,128)(2,1)} %ln_forward.1), channel_id=1, source_target_pairs={{0,1},{1,2},{2,3},{3,0},{4,5},{5,6},{6,7},{7,4},{8,9},{9,10},{10,1... | collective-permute-start | bytes 3145736 | tf_op jit(solution)/shard_map/ppermute | solution.py:22
  96.2 283.1 %reduce-scatter.2.cloned.1.call-start = ((), (), s32[]{:S(2)}) async-start(), calls=%async_computation.6 | async-start | bytes 5242880 | tf_op jit(solution)/shard_map/reduce_scatter | solution.py:948
  96.2 26.2 %collective-permute-start.6 = (bf16[256,2048]{1,0:T(8,128)(2,1)}, bf16[256,2048]{1,0:T(8,128)(2,1)S(1)}, u32[]{:S(2)}, u32[]{:S(2)}) collective-permute-start(bf16[256,2048]{1,0:T(8,128)(2,1)} %collective-permute-done.5), channel_id=1, source_target_pairs={{0,1},{1,2},{2,3},{3,0},{4,5},{5,6},{6,7},{7,4},{8,9},{9,10},{10,1... | collective-permute-start | bytes 3145736 | tf_op jit(solution)/shard_map/ppermute | solution.py:22
  122.4 25.0 %collective-permute-start.7 = (bf16[256,2048]{1,0:T(8,128)(2,1)S(1)}, bf16[256,2048]{1,0:T(8,128)(2,1)S(1)}, u32[]{:S(2)}, u32[]{:S(2)}) collective-permute-start(bf16[256,2048]{1,0:T(8,128)(2,1)S(1)} %collective-permute-done.6), channel_id=1, source_target_pairs={{0,1},{1,2},{2,3},{3,0},{4,5},{5,6},{6,7},{7,4},{8,9},{9,10},{10,1... | collective-permute-start | bytes 3145736 | tf_op jit(solution)/shard_map/ppermute | solution.py:22
  147.4 24.3 %collective-permute-start.8 = (bf16[256,2048]{1,0:T(8,128)(2,1)S(1)}, bf16[256,2048]{1,0:T(8,128)(2,1)S(1)}, u32[]{:S(2)}, u32[]{:S(2)}) collective-permute-start(bf16[256,2048]{1,0:T(8,128)(2,1)S(1)} %copy-done.1), channel_id=1, source_target_pairs={{0,1},{1,2},{2,3},{3,0},{4,5},{5,6},{6,7},{7,4},{8,9},{9,10},{10,1... | collective-permute-start | bytes 3145736 | tf_op jit(solution)/shard_map/ppermute | solution.py:22
  171.6 23.1 %collective-permute-start.9 = (bf16[256,2048]{1,0:T(8,128)(2,1)S(1)}, bf16[256,2048]{1,0:T(8,128)(2,1)S(1)}, u32[]{:S(2)}, u32[]{:S(2)}) collective-permute-start(bf16[256,2048]{1,0:T(8,128)(2,1)S(1)} %collective-permute-done.8), channel_id=1, source_target_pairs={{0,1},{1,2},{2,3},{3,0},{4,5},{5,6},{6,7},{7,4},{8,9},{9,10},{10,1... | collective-permute-start | bytes 3145736 | tf_op jit(solution)/shard_map/ppermute | solution.py:22
  194.8 31.8 %collective-permute-start.10 = (bf16[256,2048]{1,0:T(8,128)(2,1)S(1)}, bf16[256,2048]{1,0:T(8,128)(2,1)S(1)}, u32[]{:S(2)}, u32[]{:S(2)}) collective-permute-start(bf16[256,2048]{1,0:T(8,128)(2,1)S(1)} %collective-permute-done.9), channel_id=1, source_target_pairs={{0,1},{1,2},{2,3},{3,0},{4,5},{5,6},{6,7},{7,4},{8,9},{9,10},{10,1... | collective-permute-start | bytes 3145736 | tf_op jit(solution)/shard_map/ppermute | solution.py:22
  238.5 24.6 %collective-permute-start.11 = (bf16[1280,2048]{1,0:T(8,128)(2,1)}, bf16[1280,2048]{1,0:T(8,128)(2,1)}, u32[]{:S(2)}, u32[]{:S(2)}) collective-permute-start(bf16[1280,2048]{1,0:T(8,128)(2,1)} %half_grads.3), channel_id=1, source_target_pairs={{0,4},{4,0},{8,12},{12,8},{16,20},{20,16},{24,28},{28,24},{1,5},{5... | collective-permute-start | bytes 15728648 | tf_op jit(solution)/shard_map/ppermute | solution.py:27
  261.6 42.1 %collective-permute-start.14 = (bf16[1024,2048]{1,0:T(8,128)(2,1)}, bf16[1024,2048]{1,0:T(8,128)(2,1)}, u32[]{:S(2)}, u32[]{:S(2)}) collective-permute-start(bf16[1024,2048]{1,0:T(8,128)(2,1)} %half_grads.4), channel_id=1, source_target_pairs={{0,4},{4,0},{8,12},{12,8},{16,20},{20,16},{24,28},{28,24},{1,5},{5... | collective-permute-start | bytes 12582920 | tf_op jit(solution)/shard_map/ppermute | solution.py:27
  262.2 233.0 %all-gather.9.cloned.1.call-start = ((), (), s32[]{:S(2)}) async-start(), calls=%async_computation.7 | async-start | bytes 11796480 | tf_op jit(solution)/shard_map/all_gather | solution.py:805
  276.5 38.0 %collective-permute-start.12 = (bf16[2,160,2048]{2,1,0:T(8,128)(2,1)}, bf16[2,160,2048]{2,1,0:T(8,128)(2,1)S(1)}, u32[]{:S(2)}, u32[]{:S(2)}) collective-permute-start(bf16[2,160,2048]{2,1,0:T(8,128)(2,1)} %get-tuple-element.267), channel_id=1, source_target_pairs={{0,8},{4,12},{8,0},{12,4},{16,24},{20,28},{24,16},{28,20},{1,9},{5... | collective-permute-start | bytes 3932168 | tf_op jit(solution)/shard_map/ppermute | solution.py:27
  278.0 36.6 %collective-permute-start.13 = (bf16[2,160,2048]{2,1,0:T(8,128)(2,1)}, bf16[2,160,2048]{2,1,0:T(8,128)(2,1)}, u32[]{:S(2)}, u32[]{:S(2)}) collective-permute-start(bf16[2,160,2048]{2,1,0:T(8,128)(2,1)} %get-tuple-element.268), channel_id=1, source_target_pairs={{0,16},{4,20},{8,24},{12,28},{16,0},{20,4},{24,8},{28,12},{1,17},{... | collective-permute-start | bytes 3932168 | tf_op jit(solution)/shard_map/ppermute | solution.py:27
  318.0 46.9 %collective-permute-start.15 = (bf16[160,2048]{1,0:T(8,128)(2,1)S(1)}, bf16[160,2048]{1,0:T(8,128)(2,1)S(1)}, u32[]{:S(2)}, u32[]{:S(2)}) collective-permute-start(bf16[160,2048]{1,0:T(8,128)(2,1)S(1)} %dynamic-slice_bitcast_fusion.1), channel_id=1, source_target_pairs={{0,16},{4,20},{8,24},{12,28},{16,0},{20,4},{24,8},{28,12},{1,17},{... | collective-permute-start | bytes 1966088 | tf_op jit(solution)/shard_map/ppermute | solution.py:27
  319.5 45.4 %collective-permute-start.16 = (bf16[160,2048]{1,0:T(8,128)(2,1)}, bf16[160,2048]{1,0:T(8,128)(2,1)}, u32[]{:S(2)}, u32[]{:S(2)}) collective-permute-start(bf16[160,2048]{1,0:T(8,128)(2,1)} %dynamic-slice_bitcast_fusion), channel_id=1, source_target_pairs={{0,8},{4,12},{8,0},{12,4},{16,24},{20,28},{24,16},{28,20},{1,9},{5... | collective-permute-start | bytes 1966088 | tf_op jit(solution)/shard_map/ppermute | solution.py:27
  320.1 46.3 %collective-permute-start.17 = (bf16[2,128,2048]{2,1,0:T(8,128)(2,1)}, bf16[2,128,2048]{2,1,0:T(8,128)(2,1)S(1)}, u32[]{:S(2)}, u32[]{:S(2)}) collective-permute-start(bf16[2,128,2048]{2,1,0:T(8,128)(2,1)} %get-tuple-element.279), channel_id=1, source_target_pairs={{0,8},{4,12},{8,0},{12,4},{16,24},{20,28},{24,16},{28,20},{1,9},{5... | collective-permute-start | bytes 3145736 | tf_op jit(solution)/shard_map/ppermute | solution.py:27
  321.5 44.9 %collective-permute-start.18 = (bf16[2,128,2048]{2,1,0:T(8,128)(2,1)}, bf16[2,128,2048]{2,1,0:T(8,128)(2,1)S(1)}, u32[]{:S(2)}, u32[]{:S(2)}) collective-permute-start(bf16[2,128,2048]{2,1,0:T(8,128)(2,1)} %get-tuple-element.280), channel_id=1, source_target_pairs={{0,16},{4,20},{8,24},{12,28},{16,0},{20,4},{24,8},{28,12},{1,17},{... | collective-permute-start | bytes 3145736 | tf_op jit(solution)/shard_map/ppermute | solution.py:27
  377.7 6.0 %collective-permute-start.22 = (bf16[1024,1536]{1,0:T(8,128)(2,1)}, bf16[1024,1536]{1,0:T(8,128)(2,1)}, u32[]{:S(2)}, u32[]{:S(2)}) collective-permute-start(bf16[1024,1536]{1,0:T(8,128)(2,1)} %half_grads.5), channel_id=1, source_target_pairs={{0,4},{4,0},{8,12},{12,8},{16,20},{20,16},{24,28},{28,24},{1,5},{5... | collective-permute-start | bytes 9437192 | tf_op jit(solution)/shard_map/ppermute | solution.py:27
  377.7 30.8 %collective-permute-start.19 = (bf16[256,2048]{1,0:T(8,128)(2,1)}, bf16[256,2048]{1,0:T(8,128)(2,1)}, u32[]{:S(2)}, u32[]{:S(2)}) collective-permute-start(bf16[256,2048]{1,0:T(8,128)(2,1)} %slice.62), channel_id=1, source_target_pairs={{0,1},{1,2},{2,3},{3,0},{4,5},{5,6},{6,7},{7,4},{8,9},{9,10},{10,1... | collective-permute-start | bytes 3145736 | tf_op jit(solution)/shard_map/ppermute | solution.py:22
  378.2 25.8 %collective-permute-start.20 = (bf16[128,2048]{1,0:T(8,128)(2,1)}, bf16[128,2048]{1,0:T(8,128)(2,1)}, u32[]{:S(2)}, u32[]{:S(2)}) collective-permute-start(bf16[128,2048]{1,0:T(8,128)(2,1)} %dynamic-slice_bitcast_fusion.3), channel_id=1, source_target_pairs={{0,16},{4,20},{8,24},{12,28},{16,0},{20,4},{24,8},{28,12},{1,17},{... | collective-permute-start | bytes 1572872 | tf_op jit(solution)/shard_map/ppermute | solution.py:27
  378.8 26.2 %collective-permute-start.21 = (bf16[128,2048]{1,0:T(8,128)(2,1)}, bf16[128,2048]{1,0:T(8,128)(2,1)}, u32[]{:S(2)}, u32[]{:S(2)}) collective-permute-start(bf16[128,2048]{1,0:T(8,128)(2,1)} %dynamic-slice_bitcast_fusion.2), channel_id=1, source_target_pairs={{0,8},{4,12},{8,0},{12,4},{16,24},{20,28},{24,16},{28,20},{1,9},{5... | collective-permute-start | bytes 1572872 | tf_op jit(solution)/shard_map/ppermute | solution.py:27
  393.2 36.0 %collective-permute-start.24 = (bf16[2,128,1536]{2,1,0:T(8,128)(2,1)}, bf16[2,128,1536]{2,1,0:T(8,128)(2,1)}, u32[]{:S(2)}, u32[]{:S(2)}) collective-permute-start(bf16[2,128,1536]{2,1,0:T(8,128)(2,1)} %get-tuple-element.318), channel_id=1, source_target_pairs={{0,8},{4,12},{8,0},{12,4},{16,24},{20,28},{24,16},{28,20},{1,9},{5... | collective-permute-start | bytes 2359304 | tf_op jit(solution)/shard_map/ppermute | solution.py:27
  393.8 36.0 %collective-permute-start.25 = (bf16[2,128,1536]{2,1,0:T(8,128)(2,1)}, bf16[2,128,1536]{2,1,0:T(8,128)(2,1)}, u32[]{:S(2)}, u32[]{:S(2)}) collective-permute-start(bf16[2,128,1536]{2,1,0:T(8,128)(2,1)} %get-tuple-element.319), channel_id=1, source_target_pairs={{0,16},{4,20},{8,24},{12,28},{16,0},{20,4},{24,8},{28,12},{1,17},{... | collective-permute-start | bytes 2359304 | tf_op jit(solution)/shard_map/ppermute | solution.py:27
  411.4 46.1 %collective-permute-start.23 = (bf16[256,2048]{1,0:T(8,128)(2,1)}, bf16[256,2048]{1,0:T(8,128)(2,1)}, u32[]{:S(2)}, u32[]{:S(2)}) collective-permute-start(bf16[256,2048]{1,0:T(8,128)(2,1)} %add_convert_fusion.2), channel_id=1, source_target_pairs={{0,1},{1,2},{2,3},{3,0},{4,5},{5,6},{6,7},{7,4},{8,9},{9,10},{10,1... | collective-permute-start | bytes 3145736 | tf_op jit(solution)/shard_map/ppermute | solution.py:22
  414.1 45.5 %all-to-all-start.1 = ((bf16[4,64,2048]{2,1,0:T(8,128)(2,1)}), bf16[4,64,2048]{2,1,0:T(8,128)(2,1)S(1)}, u32[]{:S(2)}, u32[]{:S(2)}) async-start(bf16[4,64,2048]{2,1,0:T(8,128)(2,1)} %bitcast.38), calls=%async_computation.2 | async-start | bytes 2097152 | tf_op jit(solution)/shard_map/all_to_all | solution.py:205
  417.6 120.5 %all-gather.11.cloned.1.call-start = ((), (), s32[]{:S(2)}) async-start(), calls=%async_computation.8 | async-start | bytes 9437184 | tf_op jit(solution)/shard_map/all_gather | solution.py:805
  434.6 20.2 %collective-permute-start.26 = (bf16[128,1536]{1,0:T(8,128)(2,1)}, bf16[128,1536]{1,0:T(8,128)(2,1)S(1)}, u32[]{:S(2)}, u32[]{:S(2)}) collective-permute-start(bf16[128,1536]{1,0:T(8,128)(2,1)} %dynamic-slice_bitcast_fusion.5), channel_id=1, source_target_pairs={{0,16},{4,20},{8,24},{12,28},{16,0},{20,4},{24,8},{28,12},{1,17},{... | collective-permute-start | bytes 1179656 | tf_op jit(solution)/shard_map/ppermute | solution.py:27
  436.3 20.0 %collective-permute-start.27 = (bf16[128,1536]{1,0:T(8,128)(2,1)}, bf16[128,1536]{1,0:T(8,128)(2,1)}, u32[]{:S(2)}, u32[]{:S(2)}) collective-permute-start(bf16[128,1536]{1,0:T(8,128)(2,1)} %dynamic-slice_bitcast_fusion.4), channel_id=1, source_target_pairs={{0,8},{4,12},{8,0},{12,4},{16,24},{20,28},{24,16},{28,20},{1,9},{5... | collective-permute-start | bytes 1179656 | tf_op jit(solution)/shard_map/ppermute | solution.py:27
  490.6 25.6 %collective-permute-start.28 = (bf16[256,2048]{1,0:T(8,128)(2,1)S(1)}, bf16[256,2048]{1,0:T(8,128)(2,1)}, u32[]{:S(2)}, u32[]{:S(2)}) collective-permute-start(bf16[256,2048]{1,0:T(8,128)(2,1)S(1)} %add_convert_fusion.1), channel_id=1, source_target_pairs={{0,1},{1,2},{2,3},{3,0},{4,5},{5,6},{6,7},{7,4},{8,9},{9,10},{10,1... | collective-permute-start | bytes 3145736 | tf_op jit(solution)/shard_map/ppermute | solution.py:22
  493.5 36.2 %collective-permute-start.30 = (bf16[64,6144]{1,0:T(8,128)(2,1)S(1)}, bf16[64,6144]{1,0:T(8,128)(2,1)S(1)}, u32[]{:S(2)}, u32[]{:S(2)}) collective-permute-start(bf16[64,6144]{1,0:T(8,128)(2,1)S(1)} %copy-done.5), channel_id=1, source_target_pairs={{0,8},{4,12},{8,0},{12,4},{16,24},{20,28},{24,16},{28,20},{1,9},{5... | collective-permute-start | bytes 2359304 | tf_op jit(solution)/shard_map/ppermute | solution.py:27
  493.8 36.2 %collective-permute-start.31 = (bf16[64,6144]{1,0:T(8,128)(2,1)S(1)}, bf16[64,6144]{1,0:T(8,128)(2,1)S(1)}, u32[]{:S(2)}, u32[]{:S(2)}) collective-permute-start(bf16[64,6144]{1,0:T(8,128)(2,1)S(1)} %copy-done.5), channel_id=1, source_target_pairs={{0,16},{4,20},{8,24},{12,28},{16,0},{20,4},{24,8},{28,12},{1,17},{... | collective-permute-start | bytes 2359304 | tf_op jit(solution)/shard_map/ppermute | solution.py:27
  522.7 7.4 %collective-permute-start.29 = (f32[2,3072]{1,0:T(2,128)S(1)}, f32[2,3072]{1,0:T(2,128)S(1)}, u32[]{:S(2)}, u32[]{:S(2)}) collective-permute-start(f32[2,3072]{1,0:T(2,128)S(1)} %constant_dynamic-slice_fusion.5), channel_id=1, source_target_pairs={{0,2},{1,3},{2,0},{3,1},{4,6},{5,7},{6,4},{7,5},{8,10},{9,11},{10,... | collective-permute-start | bytes 73736 | tf_op jit(solution)/shard_map/ppermute | solution.py:27
  531.5 4.0 collective-permute-start.32
  532.0 17.9 %collective-permute-start.35 = (bf16[32,6144]{1,0:T(8,128)(2,1)S(1)}, bf16[32,6144]{1,0:T(8,128)(2,1)S(1)}, u32[]{:S(2)}, u32[]{:S(2)}) collective-permute-start(bf16[32,6144]{1,0:T(8,128)(2,1)S(1)} %slice.69), channel_id=1, source_target_pairs={{0,16},{4,20},{8,24},{12,28},{16,0},{20,4},{24,8},{28,12},{1,17},{... | collective-permute-start | bytes 1179656 | tf_op jit(solution)/shard_map/ppermute | solution.py:27
  533.4 16.5 %collective-permute-start.36 = (bf16[32,6144]{1,0:T(8,128)(2,1)S(1)}, bf16[32,6144]{1,0:T(8,128)(2,1)}, u32[]{:S(2)}, u32[]{:S(2)}) collective-permute-start(bf16[32,6144]{1,0:T(8,128)(2,1)S(1)} %slice.70), channel_id=1, source_target_pairs={{0,8},{4,12},{8,0},{12,4},{16,24},{20,28},{24,16},{28,20},{1,9},{5... | collective-permute-start | bytes 1179656 | tf_op jit(solution)/shard_map/ppermute | solution.py:27
  551.0 10.5 %collective-permute-start.38 = (bf16[64,6144]{1,0:T(8,128)(2,1)S(1)}, bf16[64,6144]{1,0:T(8,128)(2,1)S(1)}, u32[]{:S(2)}, u32[]{:S(2)}) collective-permute-start(bf16[64,6144]{1,0:T(8,128)(2,1)S(1)} %copy-done.5), channel_id=1, source_target_pairs={{0,4},{4,0},{8,12},{12,8},{16,20},{20,16},{24,28},{28,24},{1,5},{5... | collective-permute-start | bytes 2359304 | tf_op jit(solution)/shard_map/ppermute | solution.py:27
  551.2 10.2 %collective-permute-start.39 = (bf16[64,6144]{1,0:T(8,128)(2,1)S(1)}, bf16[64,6144]{1,0:T(8,128)(2,1)S(1)}, u32[]{:S(2)}, u32[]{:S(2)}) collective-permute-start(bf16[64,6144]{1,0:T(8,128)(2,1)S(1)} %collective-permute-done.30.refs_2_), channel_id=1, source_target_pairs={{0,4},{4,0},{8,12},{12,8},{16,20},{20,16},{24,28},{28,24},{1,5},{5... | collective-permute-start | bytes 2359304 | tf_op jit(solution)/shard_map/ppermute | solution.py:27
  551.5 9.9 %collective-permute-start.40 = (bf16[64,6144]{1,0:T(8,128)(2,1)S(1)}, bf16[64,6144]{1,0:T(8,128)(2,1)S(1)}, u32[]{:S(2)}, u32[]{:S(2)}) collective-permute-start(bf16[64,6144]{1,0:T(8,128)(2,1)S(1)} %collective-permute-done.31.refs_4_), channel_id=1, source_target_pairs={{0,4},{4,0},{8,12},{12,8},{16,20},{20,16},{24,28},{28,24},{1,5},{5... | collective-permute-start | bytes 2359304 | tf_op jit(solution)/shard_map/ppermute | solution.py:27
  551.7 9.8 %collective-permute-start.41 = (bf16[64,6144]{1,0:T(8,128)(2,1)S(1)}, bf16[64,6144]{1,0:T(8,128)(2,1)S(1)}, u32[]{:S(2)}, u32[]{:S(2)}) collective-permute-start(bf16[64,6144]{1,0:T(8,128)(2,1)S(1)} %pad_maximum_fusion.5.refs_6_), channel_id=1, source_target_pairs={{0,4},{4,0},{8,12},{12,8},{16,20},{20,16},{24,28},{28,24},{1,5},{5... | collective-permute-start | bytes 2359304 | tf_op jit(solution)/shard_map/ppermute | solution.py:27
  552.0 3.8 collective-permute-start.34
  555.8 3.8 collective-permute-start.37
  (25 other events, 185.4 us)
Sparse Core Ops, SparseCore 0:
  41.9 48.4 all-gather.4
  96.3 54.1 all-gather.6
  262.3 78.2 reduce-scatter.1
  370.3 91.5 all-gather.8
  463.9 71.1 all-gather.10

commit v5 on v4

--- a/solution.py
+++ b/solution.py
@@ -131,8 +131,9 @@
             self.spans[part] = (0, self.spans[part][1])
 
     def further(self, line):
-        self.take(line)
-        self.send(line)
+        if len(self.todo[0]) > 1:
+            self.take(line)
+            self.send(line)
 
     def end(self, line):
         while len(self.todo[0]) > 1:
@@ -763,17 +764,39 @@
     )
 
 
+def feed_kernel(tokens, rows_ref, weight_ref, bias_ref, act_ref, slope_ref):
+    root = (2.0 / jnp.pi) ** 0.5
+    for first in range(0, rows_ref.shape[0], tokens):
+        here = slice(first, first + tokens)
+        pre_act = times(rows_ref[here], weight_ref[...]) + bias_ref[...]
+        square = pre_act * pre_act
+        curve = jnp.tanh(root * pre_act * (1.0 + 0.044715 * square))
+        half = 0.5 * (1.0 + curve)
+        act_ref[here] = (pre_act * half).astype(BF)
+        slope_ref[here] = (
+            half
+            + 0.5 * pre_act * (1.0 - curve * curve) * root * (1.0 + 3 * 0.044715 * square)
+        ).astype(BF)
+
+
 def feed_forward(normed_all, fc1_cols, bias):
-    pre_act = times(normed_all, fc1_cols) + bias
-    root = (2.0 / jnp.pi) ** 0.5
-    square = pre_act * pre_act
-    curve = jnp.tanh(root * pre_act * (1.0 + 0.044715 * square))
-    activation = (0.5 * pre_act * (1.0 + curve)).astype(BF)
-    slope = (
-        0.5 * (1.0 + curve)
-        + 0.5 * pre_act * (1.0 - curve * curve) * root * (1.0 + 3 * 0.044715 * square)
-    ).astype(BF)
-    return activation, slope
+    height, width = normed_all.shape
+    hidden = fc1_cols.shape[1]
+    tile = min(512, hidden)
+    block = pl.BlockSpec((height, tile), lambda j: (0, j))
+    return pl.pallas_call(
+        functools.partial(feed_kernel, min(256, height)),
+        grid=(hidden // tile,),
+        in_specs=[
+            pl.BlockSpec(memory_space=pltpu.VMEM),
+            pl.BlockSpec((width, tile), lambda j: (0, j)),
+            pl.BlockSpec((1, tile), lambda j: (0, j)),
+        ],
+        out_specs=[block, block],
+        out_shape=[jax.ShapeDtypeStruct((height, hidden), BF)] * 2,
+        compiler_params=ROOM,
+        name="feed_forward",
+    )(normed_all, fc1_cols, bias.reshape(1, hidden))
 
 
 def shards(
@@ -984,7 +1007,9 @@
     d_pre = line.step(pull, cot_all, w_fc2, slope)
     fc1_came = grad(normed_all, d_pre)
     out_grads = grad_sum(activation, cot_all, out_came, attended)
-    d_attended = by_seq(line.step(pull, cot_all, w_dense))
+    d_attended = by_seq(
+        line.step(lambda c, w: times_transpose(c, w).astype(BF), cot_all, w_dense)
+    )
     back = attend_back_some(0, ())
     fc1_sum = grad_sum(normed_all, d_pre, fc1_came)
     out_grads.further(line)
@@ -1057,7 +1082,7 @@
     sums = owned_sum(line, sums, place)
     sums = line.hold(jnp.concatenate([sums, d_bias_fc1]))
     sums = line.hold(sums + swap(sums, "rep", 1))
-    fc1_total = line.step(lambda a: a.astype(F32), fc1_whole)
+    (fc1_total,) = line.step(lambda a: split_rows(a, reps, (slab,)), fc1_whole)
     qkv_spread = qkv_spread.shared()
     bit = 2
     while bit < reps:

time: 587 us -> 586 us (level)
  Pallas kernels: 236 us -> 258 us
  matrix products: 21.9 us -> 8.61 us
  other arithmetic: 44.8 us -> 33.6 us
    dot_general x2 -> x1, matrix products: 21.9 us -> 3.08 us  [times(): return jnp.dot(left_side, right_side, preferred_element_type=F32)]
    pallas_call x0 -> x1, Pallas kernels: none -> 18.3 us  [feed_forward(): pl.pallas_call(functools.partial(feed_kernel, min(256, height)), grid=(hi...]
    convert_element_type x1 -> x0, other arithmetic: 11.8 us -> none  [shards(): fc1_total = line.step(lambda a: a.astype(F32), fc1_whole)]
    pallas_call x1 -> x2, Pallas kernels: 12.1 us -> 22.3 us  [split_rows(): pl.pallas_call(split_kernel, grid=(reps,), in_specs=[pl.BlockSpec((rows /...]
    pallas_call x2 -> x1, Pallas kernels: 20.6 us -> 14.4 us  [pull(): pl.pallas_call(pull_kernel, grid=(hidden // tile,), in_specs=[pl.BlockSpe...]
  transfers between devices with their start and end apart: 49 -> 49, of which waited for: 24 -> 23; matrix products, arithmetic and copies ran while one was open for 16% -> 12% of each run, Pallas kernels for 37% -> 41%
where the time goes in v5:
time: 586 us; the launch traced here: 577 us
  Pallas kernels  258 us (44%)
  waiting for transfers between devices  148 us (25%)
  starting transfers between devices  48.2 us (8%)
  local copies, waits for them, and re-layouts  42 us (7%)
  other arithmetic  33.6 us (6%)
  blocking collectives  23.7 us (4%)
  between operations  15 us (3%)
  matrix products  8.61 us (1%)
    ppermute x12, waiting for transfers between devices, ring(): lax.ppermute(array, axis, [(i, (i + distance) % size) for i in range(size)])  86.8 us
    ppermute x30, waiting for transfers between devices, swap(): return lax.ppermute(array, axis, [(i, i ^ mask) for i in range(size)])  54.4 us
    pallas_call x2, Pallas kernels, push(): pl.pallas_call(functools.partial(push_kernel, transposed, size), grid_spe...  37 us
    pallas_call x2, Pallas kernels, attend_back(): pl.pallas_call(functools.partial(attend_back_kernel, block), grid_spec=pl...  36.2 us
    pallas_call x3, Pallas kernels, grad_sums(): pl.pallas_call(grad_sum_kernel, grid_spec=pltpu.PrefetchScalarGridSpec(nu...  34 us
    pallas_call x2, Pallas kernels, attend(): pl.pallas_call(functools.partial(attend_kernel, block), grid_spec=pltpu.P...  29.1 us
    pallas_call x3, Pallas kernels, half_grads(): pl.pallas_call(grad_kernel, grid_spec=pltpu.PrefetchScalarGridSpec(num_sc...  27.1 us
    ppermute x30, starting transfers between devices, swap(): return lax.ppermute(array, axis, [(i, i ^ mask) for i in range(size)])  27 us
  transfers between devices with their start and end apart: 49, of which 23 were waited for; matrix products, arithmetic and copies ran while one was open for 12% of the time, Pallas kernels for 41%

profile of v5, /device:TPU:0, one launch (start us, length us, event | category | flops | bytes accessed | tf_op | source)
XLA Modules:
  0.0 577.4 jit_solution(15573943099555378548)
XLA Ops:
  15.2 3.0 collective-permute-start
  19.9 3.1 collective-permute-start.1
  28.2 3.2 ln_forward.1
  32.7 6.1 %collective-permute-done.3.refs_2_ = bf16[64,1536]{1,0:T(8,128)(2,1)S(1)} collective-permute-done((bf16[64,1536]{1,0:T(8,128)(2,1)S(1)}, bf16[64,1536]{1,0:T(8,128)(2,1)S(1)}, u32[]{:S(2)}, u32[]{:S(2)}) %collective-permute-start.3) | collective-permute-done | bytes 196640 | tf_op jit(solution)/shard_map/ppermute | solution.py:22
  41.7 6.6 %all-to-all-start = ((bf16[4,64,2048]{2,1,0:T(8,128)(2,1)}), bf16[4,64,2048]{2,1,0:T(8,128)(2,1)}, u32[]{:S(2)}, u32[]{:S(2)}) async-start(bf16[4,64,2048]{2,1,0:T(8,128)(2,1)} %bitcast.10), calls=%async_computation | async-start | bytes 2097152 | tf_op jit(solution)/shard_map/all_to_all | solution.py:206
  48.3 2.4 collective-permute-start.5
  57.5 3.8 concatenate.75
  61.3 2.4 concatenate.76
  63.8 27.8 %collective-permute-done.5 = bf16[256,2048]{1,0:T(8,128)(2,1)} collective-permute-done((bf16[256,2048]{1,0:T(8,128)(2,1)}, bf16[256,2048]{1,0:T(8,128)(2,1)}, u32[]{:S(2)}, u32[]{:S(2)}) %collective-permute-start.5) | collective-permute-done | bytes 1048608 | tf_op jit(solution)/shard_map/ppermute | solution.py:22
  91.6 4.6 all-to-all-done
  98.8 23.6 %collective-permute-done.6 = bf16[256,2048]{1,0:T(8,128)(2,1)S(1)} collective-permute-done((bf16[256,2048]{1,0:T(8,128)(2,1)}, bf16[256,2048]{1,0:T(8,128)(2,1)S(1)}, u32[]{:S(2)}, u32[]{:S(2)}) %collective-permute-start.6) | collective-permute-done | bytes 1048608 | tf_op jit(solution)/shard_map/ppermute | solution.py:22
  124.1 10.2 %project.2.refs_0_ = f32[1024,1536]{1,0:T(8,128)} custom-call(bf16[1024,2048]{1,0:T(8,128)(2,1)} %constant_dynamic-update-slice_fusion.11.rows_ref, bf16[2048,1536]{1,0:T(8,128)(2,1)} %all-gather.5.cloned.1.call-done.weight_ref.b_ref, f32[1,1536]{1,0:T(1,128)} %bitcast.105), custom_call_target="tpu_custom_call" | custom-call | tf_op jit(solution)/shard_map/project/pallas_call | solution.py:564
  134.3 13.1 %collective-permute-done.7 = bf16[256,2048]{1,0:T(8,128)(2,1)S(1)} collective-permute-done((bf16[256,2048]{1,0:T(8,128)(2,1)S(1)}, bf16[256,2048]{1,0:T(8,128)(2,1)S(1)}, u32[]{:S(2)}, u32[]{:S(2)}) %collective-permute-start.7) | collective-permute-done | bytes 1048608 | tf_op jit(solution)/shard_map/ppermute | solution.py:22
  149.2 6.1 %project.3.q_ref.k_ref.v_ref = f32[1024,1536]{1,0:T(8,128)} custom-call(bf16[1024,2048]{1,0:T(8,128)(2,1)} %constant_dynamic-update-slice_fusion.10.rows_ref.left_ref, bf16[2048,1536]{1,0:T(8,128)(2,1)} %all-gather.5.cloned.1.call-done.weight_ref.b_ref, f32[1,1536]{1,0:T(1,128)} %bitcast.106, ...), custom_call_target="tpu_custom_call", output_to_operand_aliasing={{}: (3, {})} | custom-call | tf_op jit(solution)/shard_map/project/pallas_call | solution.py:564
  155.3 14.5 %attend.2 = (bf16[1024,512]{1,0:T(8,128)(2,1)}, bf16[1,4,2560,256]{3,2,1,0:T(8,128)(2,1)}, bf16[3,1024,256]{2,1,0:T(8,128)(2,1)}) custom-call(s32[1]{0:T(128)} %bitcast.place_ref, f32[1024,1536]{1,0:T(8,128)} %project.3.q_ref.k_ref.v_ref, f32[1024,1536]{1,0:T(8,128)} %project.3.q_ref.k_ref.v_ref, f32[1024,1536]{1,0:T(8,128)} %project.3.q_ref.k_ref.v_ref, ...), custom_call_target="tpu_custom_call" | custom-call | tf_op jit(solution)/shard_map/attend/pallas_call | solution.py:637
  172.7 18.3 %feed_forward.1 = (bf16[1024,2048]{1,0:T(8,128)(2,1)}, bf16[1024,2048]{1,0:T(8,128)(2,1)}) custom-call(bf16[1024,2048]{1,0:T(8,128)(2,1)} %constant_dynamic-update-slice_fusion.10.rows_ref.left_ref, bf16[2048,2048]{1,0:T(8,128)(2,1)} %all-gather.7.cloned.1.call-done.weight_ref.d_ref, f32[1,2048]{1,0:T(1,128)} %bitcast.111), custom_call_target="tpu_custom_call" | custom-call | tf_op jit(solution)/shard_map/feed_forward/pallas_call | solution.py:787
  191.0 3.7 collective-permute-done.9
  196.2 14.5 %attend.3 = (bf16[1024,512]{1,0:T(8,128)(2,1)}, bf16[1,4,2560,256]{3,2,1,0:T(8,128)(2,1)}, bf16[3,1024,256]{2,1,0:T(8,128)(2,1)}) custom-call(s32[1]{0:T(128)} %bitcast.place_ref, f32[1024,1536]{1,0:T(8,128)} %project.3.q_ref.k_ref.v_ref, f32[1024,1536]{1,0:T(8,128)} %project.3.q_ref.k_ref.v_ref, ...), custom_call_target="tpu_custom_call", output_to_operand_aliasing={{0}: (6, {})} | custom-call | tf_op jit(solution)/shard_map/attend/pallas_call | solution.py:637
  210.7 15.8 %push.2 = bf16[1024,2048]{1,0:T(8,128)(2,1)} custom-call(s32[1]{0:T(128)} %bitcast.place_ref, bf16[1024,512]{1,0:T(8,128)(2,1)} %get-tuple-element.268.a_ref.refs_0_, bf16[512,2048]{1,0:T(8,128)(2,1)} %b_ref, bf16[1024,2048]{1,0:T(8,128)(2,1)} %get-tuple-element.266.c_ref.left_ref, bf16[2048,2048]{1,0:T(8,128)(2,1)} %weight_ref), custom_call_target="tpu_custom_call" | custom-call | tf_op jit(solution)/shard_map/push/pallas_call | solution.py:541
  227.6 10.9 %half_grads.3 = bf16[1280,2048]{1,0:T(8,128)(2,1)} custom-call(s32[1]{0:T(128)} %bitcast.13.which_ref, bf16[1024,2048]{1,0:T(8,128)(2,1)} %get-tuple-element.266.c_ref.left_ref, bf16[1024,2048]{1,0:T(8,128)(2,1)} %constant_dynamic-update-slice_fusion.7.right_ref.cot_ref, bf16[1024,512]{1,0:T(8,128)(2,1)} %get-tuple-element.268.a_ref.refs_0_), custom_call_target="tpu_custom_call" | custom-call | tf_op jit(solution)/shard_map/half_grads/pallas_call | solution.py:408
  238.5 14.4 %pull.1.right_ref.c_ref = bf16[1024,2048]{1,0:T(8,128)(2,1)} custom-call(bf16[1024,2048]{1,0:T(8,128)(2,1)} %constant_dynamic-update-slice_fusion.7.right_ref.cot_ref, bf16[2048,2048]{1,0:T(8,128)(2,1)} %weight_ref, bf16[1024,2048]{1,0:T(8,128)(2,1)} %get-tuple-element.263.refs_0_), custom_call_target="tpu_custom_call" | custom-call | tf_op jit(solution)/shard_map/pull/pallas_call | solution.py:504
  252.9 8.8 %half_grads.4 = bf16[1024,2048]{1,0:T(8,128)(2,1)} custom-call(s32[1]{0:T(128)} %bitcast.13.which_ref, bf16[1024,2048]{1,0:T(8,128)(2,1)} %constant_dynamic-update-slice_fusion.10.rows_ref.left_ref, bf16[1024,2048]{1,0:T(8,128)(2,1)} %pull.1.right_ref.c_ref), custom_call_target="tpu_custom_call" | custom-call | tf_op jit(solution)/shard_map/half_grads/pallas_call | solution.py:408
  263.1 13.6 %grad_sums.3 = (bf16[1280,2048]{1,0:T(8,128)(2,1)}, bf16[2,160,2048]{2,1,0:T(8,128)(2,1)}, bf16[2,160,2048]{2,1,0:T(8,128)(2,1)}) custom-call(s32[3]{0:T(128)} %pad_add_fusion.at_ref, bf16[1024,2048]{1,0:T(8,128)(2,1)} %get-tuple-element.266.c_ref.left_ref, bf16[1024,2048]{1,0:T(8,128)(2,1)} %constant_dynamic-update-slice_fusion.7.right_ref.cot_ref, ...), custom_call_target="tpu_custom_call" | custom-call | tf_op jit(solution)/shard_map/grad_sums/pallas_call | solution.py:350
  279.6 5.5 convolution_convert_fusion.datt_ref
  285.2 18.0 %attend_back.2 = (bf16[1024,1536]{1,0:T(8,128)(2,1)}, f32[1,1,1536]{2,1,0:T(1,128)}) custom-call(s32[1]{0:T(128)} %bitcast.place_ref, bf16[1,4,2560,256]{3,2,1,0:T(8,128)(2,1)} %get-tuple-element.233.prob_ref, bf16[3,1024,256]{2,1,0:T(8,128)(2,1)} %get-tuple-element.234.low_ref, bf16[1024,512]{1,0:T(8,128)(2,1)} %convolution_convert_fusion.datt_ref, ...), custom_call_target="tpu_custom_call" | custom-call | tf_op jit(solution)/shard_map/attend_back/pallas_call | solution.py:722
  303.1 10.9 %grad_sums.4 = (bf16[1024,2048]{1,0:T(8,128)(2,1)}, bf16[2,128,2048]{2,1,0:T(8,128)(2,1)}, bf16[2,128,2048]{2,1,0:T(8,128)(2,1)}) custom-call(s32[3]{0:T(128)} %pad_add_fusion.at_ref, bf16[1024,2048]{1,0:T(8,128)(2,1)} %constant_dynamic-update-slice_fusion.10.rows_ref.left_ref, bf16[1024,2048]{1,0:T(8,128)(2,1)} %pull.1.right_ref.c_ref, ...), custom_call_target="tpu_custom_call" | custom-call | tf_op jit(solution)/shard_map/grad_sums/pallas_call | solution.py:350
  314.1 3.8 fusion
  323.0 18.2 %attend_back.3 = (bf16[1024,1536]{1,0:T(8,128)(2,1)}, f32[1,1,1536]{2,1,0:T(1,128)}) custom-call(s32[1]{0:T(128)} %bitcast.place_ref, bf16[1,4,2560,256]{3,2,1,0:T(8,128)(2,1)} %get-tuple-element.249.prob_ref, bf16[3,1024,256]{2,1,0:T(8,128)(2,1)} %get-tuple-element.250.low_ref, ...), custom_call_target="tpu_custom_call", output_to_operand_aliasing={{0}: (5, {}), {1}: (6, {})} | custom-call | tf_op jit(solution)/shard_map/attend_back/pallas_call | solution.py:722
  341.3 21.2 %push.3 = bf16[1024,2048]{1,0:T(8,128)(2,1)} custom-call(s32[1]{0:T(128)} %bitcast.place_ref, bf16[1024,1536]{1,0:T(8,128)(2,1)} %get-tuple-element.319.a_ref.right_ref, bf16[2048,1536]{1,0:T(8,128)(2,1)} %all-gather.5.cloned.1.call-done.weight_ref.b_ref, bf16[1024,2048]{1,0:T(8,128)(2,1)} %pull.1.right_ref.c_ref, ...), custom_call_target="tpu_custom_call" | custom-call | tf_op jit(solution)/shard_map/push/pallas_call | solution.py:541
  362.5 2.5 slice.62
  370.2 7.5 %half_grads.5 = bf16[1024,1536]{1,0:T(8,128)(2,1)} custom-call(s32[1]{0:T(128)} %bitcast.13.which_ref, bf16[1024,2048]{1,0:T(8,128)(2,1)} %constant_dynamic-update-slice_fusion.10.rows_ref.left_ref, bf16[1024,1536]{1,0:T(8,128)(2,1)} %get-tuple-element.319.a_ref.right_ref), custom_call_target="tpu_custom_call" | custom-call | tf_op jit(solution)/shard_map/half_grads/pallas_call | solution.py:408
  379.1 3.1 convert_add_fusion.4
  383.7 9.5 %grad_sums.5 = (bf16[1024,1536]{1,0:T(8,128)(2,1)}, bf16[2,128,1536]{2,1,0:T(8,128)(2,1)}, bf16[2,128,1536]{2,1,0:T(8,128)(2,1)}) custom-call(s32[3]{0:T(128)} %pad_add_fusion.at_ref, bf16[1024,2048]{1,0:T(8,128)(2,1)} %constant_dynamic-update-slice_fusion.10.rows_ref.left_ref, bf16[1024,1536]{1,0:T(8,128)(2,1)} %get-tuple-element.319.a_ref.right_ref, ...), custom_call_target="tpu_custom_call" | custom-call | tf_op jit(solution)/shard_map/grad_sums/pallas_call | solution.py:350
  395.0 9.0 %collective-permute-done.20 = bf16[128,2048]{1,0:T(8,128)(2,1)} collective-permute-done((bf16[128,2048]{1,0:T(8,128)(2,1)}, bf16[128,2048]{1,0:T(8,128)(2,1)}, u32[]{:S(2)}, u32[]{:S(2)}) %collective-permute-start.20) | collective-permute-done | bytes 524320 | tf_op jit(solution)/shard_map/ppermute | solution.py:27
  408.3 2.9 add_convert_fusion.1
  411.2 2.8 collective-permute-start.23
  414.0 3.5 all-to-all-start.1
  417.6 11.5 %collective-permute-done.24 = bf16[2,128,1536]{2,1,0:T(8,128)(2,1)} collective-permute-done((bf16[2,128,1536]{2,1,0:T(8,128)(2,1)}, bf16[2,128,1536]{2,1,0:T(8,128)(2,1)}, u32[]{:S(2)}, u32[]{:S(2)}) %collective-permute-start.24) | collective-permute-done | bytes 786464 | tf_op jit(solution)/shard_map/ppermute | solution.py:27
  436.9 3.1 fusion.14
  440.1 14.8 %collective-permute-done.26 = bf16[128,1536]{1,0:T(8,128)(2,1)S(1)} collective-permute-done((bf16[128,1536]{1,0:T(8,128)(2,1)}, bf16[128,1536]{1,0:T(8,128)(2,1)S(1)}, u32[]{:S(2)}, u32[]{:S(2)}) %collective-permute-start.26) | collective-permute-done | bytes 393248 | tf_op jit(solution)/shard_map/ppermute | solution.py:27
  462.9 23.7 %all_to_all.36 = bf16[4,64,1536]{2,1,0:T(8,128)(2,1)} all-to-all(bf16[4,64,1536]{2,1,0:T(8,128)(2,1)S(1)} %bitcast.93), channel_id=1, replica_groups=mesh['rep'=8,'shard'=4] {'shard'}, dimensions={0} | all-to-all | bytes 1572864 | tf_op jit(solution)/shard_map/all_to_all | solution.py:206
  491.0 2.6 slice.78.a_ref
  495.0 12.1 %split_rows.2 = (f32[2048,2048]{1,0:T(8,128)}, f32[512,2048]{1,0:T(8,128)}) custom-call(bf16[2560,2048]{1,0:T(8,128)(2,1)} %all-gather.9.cloned.1.call-done.in_ref), custom_call_target="tpu_custom_call" | custom-call | tf_op jit(solution)/shard_map/split_rows/pallas_call | solution.py:238
  507.1 9.3 %collective-permute-done.28.b_ref = bf16[256,2048]{1,0:T(8,128)(2,1)} collective-permute-done((bf16[256,2048]{1,0:T(8,128)(2,1)S(1)}, bf16[256,2048]{1,0:T(8,128)(2,1)}, u32[]{:S(2)}, u32[]{:S(2)}) %collective-permute-start.28) | collective-permute-done | bytes 1048608 | tf_op jit(solution)/shard_map/ppermute | solution.py:22
  516.4 5.5 ln_backward.1
  522.9 6.9 %collective-permute-done.30.refs_2_ = bf16[64,6144]{1,0:T(8,128)(2,1)S(1)} collective-permute-done((bf16[64,6144]{1,0:T(8,128)(2,1)S(1)}, bf16[64,6144]{1,0:T(8,128)(2,1)S(1)}, u32[]{:S(2)}, u32[]{:S(2)}) %collective-permute-start.30) | collective-permute-done | bytes 786464 | tf_op jit(solution)/shard_map/ppermute | solution.py:27
  538.0 10.3 %split_rows.3 = f32[512,8192]{1,0:T(8,128)} custom-call(bf16[512,8192]{1,0:T(8,128)(2,1)} %all-gather.11.cloned.1.call-done.in_ref), custom_call_target="tpu_custom_call" | custom-call | tf_op jit(solution)/shard_map/split_rows/pallas_call | solution.py:238
  561.5 8.4 %assemble.1 = f32[512,6144]{1,0:T(8,128)} custom-call(s32[1]{0:T(128)} %bitcast.45.rep_ref, bf16[64,6144]{1,0:T(8,128)(2,1)} %widened.3.refs_0_, bf16[64,6144]{1,0:T(8,128)(2,1)} %copy-done.13, bf16[64,6144]{1,0:T(8,128)(2,1)} %copy-done.10, bf16[64,6144]{1,0:T(8,128)(2,1)} %copy-done.14, bf16[64,6144]{1,0:T(8,128)(2,1)} %copy-done.11, ...), custom_call_target="tpu_custom_call" | custom-call | tf_op jit(solution)/shard_map/assemble/pallas_call | solution.py:286
  (233 shorter events, 105.2 us)
Async XLA Ops:
  7.2 116.9 %all-gather.5.cloned.1.call-start = ((), (), s32[]{:S(2)}) async-start(), calls=%async_computation.4 | async-start | bytes 7077888 | tf_op jit(solution)/shard_map/all_gather | solution.py:828
  15.2 4.7 collective-permute-start
  19.9 7.0 %collective-permute-start.1 = (f32[2,3328]{1,0:T(2,128)S(1)}, f32[2,3328]{1,0:T(2,128)S(1)}, u32[]{:S(2)}, u32[]{:S(2)}) collective-permute-start(f32[2,3328]{1,0:T(2,128)S(1)} %pad_maximum_fusion.10), channel_id=1, source_target_pairs={{0,2},{1,3},{2,0},{3,1},{4,6},{5,7},{6,4},{7,5},{8,10},{9,11},{10,... | collective-permute-start | bytes 79880 | tf_op jit(solution)/shard_map/ppermute | solution.py:27
  23.0 9.7 %collective-permute-start.2 = (bf16[64,1536]{1,0:T(8,128)(2,1)S(1)}, bf16[64,1536]{1,0:T(8,128)(2,1)S(1)}, u32[]{:S(2)}, u32[]{:S(2)}) collective-permute-start(bf16[64,1536]{1,0:T(8,128)(2,1)S(1)} %pad_maximum_fusion.7), channel_id=1, source_target_pairs={{0,1},{1,2},{2,3},{3,0},{4,5},{5,6},{6,7},{7,4},{8,9},{9,10},{10,1... | collective-permute-start | bytes 589832 | tf_op jit(solution)/shard_map/ppermute | solution.py:22
  24.6 14.2 %collective-permute-start.3 = (bf16[64,1536]{1,0:T(8,128)(2,1)S(1)}, bf16[64,1536]{1,0:T(8,128)(2,1)S(1)}, u32[]{:S(2)}, u32[]{:S(2)}) collective-permute-start(bf16[64,1536]{1,0:T(8,128)(2,1)S(1)} %pad_maximum_fusion.8), channel_id=1, source_target_pairs={{0,2},{1,3},{2,0},{3,1},{4,6},{5,7},{6,4},{7,5},{8,10},{9,11},{10,... | collective-permute-start | bytes 589832 | tf_op jit(solution)/shard_map/ppermute | solution.py:22
  24.9 13.9 %collective-permute-start.4 = (bf16[64,1536]{1,0:T(8,128)(2,1)S(1)}, bf16[64,1536]{1,0:T(8,128)(2,1)S(1)}, u32[]{:S(2)}, u32[]{:S(2)}) collective-permute-start(bf16[64,1536]{1,0:T(8,128)(2,1)S(1)} %pad_maximum_fusion.9), channel_id=1, source_target_pairs={{0,3},{1,0},{2,1},{3,2},{4,7},{5,4},{6,5},{7,6},{8,11},{9,8},{10,9... | collective-permute-start | bytes 589832 | tf_op jit(solution)/shard_map/ppermute | solution.py:22
  41.7 54.4 %all-to-all-start = ((bf16[4,64,2048]{2,1,0:T(8,128)(2,1)}), bf16[4,64,2048]{2,1,0:T(8,128)(2,1)}, u32[]{:S(2)}, u32[]{:S(2)}) async-start(bf16[4,64,2048]{2,1,0:T(8,128)(2,1)} %bitcast.10), calls=%async_computation | async-start | bytes 2097152 | tf_op jit(solution)/shard_map/all_to_all | solution.py:206
  48.3 124.4 %all-gather.7.cloned.1.call-start = ((), (), s32[]{:S(2)}) async-start(), calls=%async_computation.5 | async-start | bytes 9437184 | tf_op jit(solution)/shard_map/all_gather | solution.py:828
  48.3 43.2 %collective-permute-start.5 = (bf16[256,2048]{1,0:T(8,128)(2,1)}, bf16[256,2048]{1,0:T(8,128)(2,1)}, u32[]{:S(2)}, u32[]{:S(2)}) collective-permute-start(bf16[256,2048]{1,0:T(8,128)(2,1)} %ln_forward.1), channel_id=1, source_target_pairs={{0,1},{1,2},{2,3},{3,0},{4,5},{5,6},{6,7},{7,4},{8,9},{9,10},{10,1... | collective-permute-start | bytes 3145736 | tf_op jit(solution)/shard_map/ppermute | solution.py:22
  96.2 282.9 %reduce-scatter.2.cloned.1.call-start = ((), (), s32[]{:S(2)}) async-start(), calls=%async_computation.6 | async-start | bytes 5242880 | tf_op jit(solution)/shard_map/reduce_scatter | solution.py:971
  96.2 26.2 %collective-permute-start.6 = (bf16[256,2048]{1,0:T(8,128)(2,1)}, bf16[256,2048]{1,0:T(8,128)(2,1)S(1)}, u32[]{:S(2)}, u32[]{:S(2)}) collective-permute-start(bf16[256,2048]{1,0:T(8,128)(2,1)} %collective-permute-done.5), channel_id=1, source_target_pairs={{0,1},{1,2},{2,3},{3,0},{4,5},{5,6},{6,7},{7,4},{8,9},{9,10},{10,1... | collective-permute-start | bytes 3145736 | tf_op jit(solution)/shard_map/ppermute | solution.py:22
  122.4 25.0 %collective-permute-start.7 = (bf16[256,2048]{1,0:T(8,128)(2,1)S(1)}, bf16[256,2048]{1,0:T(8,128)(2,1)S(1)}, u32[]{:S(2)}, u32[]{:S(2)}) collective-permute-start(bf16[256,2048]{1,0:T(8,128)(2,1)S(1)} %collective-permute-done.6), channel_id=1, source_target_pairs={{0,1},{1,2},{2,3},{3,0},{4,5},{5,6},{6,7},{7,4},{8,9},{9,10},{10,1... | collective-permute-start | bytes 3145736 | tf_op jit(solution)/shard_map/ppermute | solution.py:22
  147.4 24.3 %collective-permute-start.8 = (bf16[256,2048]{1,0:T(8,128)(2,1)S(1)}, bf16[256,2048]{1,0:T(8,128)(2,1)S(1)}, u32[]{:S(2)}, u32[]{:S(2)}) collective-permute-start(bf16[256,2048]{1,0:T(8,128)(2,1)S(1)} %copy-done.1), channel_id=1, source_target_pairs={{0,1},{1,2},{2,3},{3,0},{4,5},{5,6},{6,7},{7,4},{8,9},{9,10},{10,1... | collective-permute-start | bytes 3145736 | tf_op jit(solution)/shard_map/ppermute | solution.py:22
  171.6 23.1 %collective-permute-start.9 = (bf16[256,2048]{1,0:T(8,128)(2,1)S(1)}, bf16[256,2048]{1,0:T(8,128)(2,1)S(1)}, u32[]{:S(2)}, u32[]{:S(2)}) collective-permute-start(bf16[256,2048]{1,0:T(8,128)(2,1)S(1)} %collective-permute-done.8), channel_id=1, source_target_pairs={{0,1},{1,2},{2,3},{3,0},{4,5},{5,6},{6,7},{7,4},{8,9},{9,10},{10,1... | collective-permute-start | bytes 3145736 | tf_op jit(solution)/shard_map/ppermute | solution.py:22
  194.8 31.8 %collective-permute-start.10 = (bf16[256,2048]{1,0:T(8,128)(2,1)S(1)}, bf16[256,2048]{1,0:T(8,128)(2,1)S(1)}, u32[]{:S(2)}, u32[]{:S(2)}) collective-permute-start(bf16[256,2048]{1,0:T(8,128)(2,1)S(1)} %collective-permute-done.9), channel_id=1, source_target_pairs={{0,1},{1,2},{2,3},{3,0},{4,5},{5,6},{6,7},{7,4},{8,9},{9,10},{10,1... | collective-permute-start | bytes 3145736 | tf_op jit(solution)/shard_map/ppermute | solution.py:22
  238.5 24.6 %collective-permute-start.11 = (bf16[1280,2048]{1,0:T(8,128)(2,1)}, bf16[1280,2048]{1,0:T(8,128)(2,1)}, u32[]{:S(2)}, u32[]{:S(2)}) collective-permute-start(bf16[1280,2048]{1,0:T(8,128)(2,1)} %half_grads.3), channel_id=1, source_target_pairs={{0,4},{4,0},{8,12},{12,8},{16,20},{20,16},{24,28},{28,24},{1,5},{5... | collective-permute-start | bytes 15728648 | tf_op jit(solution)/shard_map/ppermute | solution.py:27
  261.6 41.5 %collective-permute-start.14 = (bf16[1024,2048]{1,0:T(8,128)(2,1)}, bf16[1024,2048]{1,0:T(8,128)(2,1)}, u32[]{:S(2)}, u32[]{:S(2)}) collective-permute-start(bf16[1024,2048]{1,0:T(8,128)(2,1)} %half_grads.4), channel_id=1, source_target_pairs={{0,4},{4,0},{8,12},{12,8},{16,20},{20,16},{24,28},{28,24},{1,5},{5... | collective-permute-start | bytes 12582920 | tf_op jit(solution)/shard_map/ppermute | solution.py:27
  262.2 232.8 %all-gather.9.cloned.1.call-start = ((), (), s32[]{:S(2)}) async-start(), calls=%async_computation.7 | async-start | bytes 11796480 | tf_op jit(solution)/shard_map/all_gather | solution.py:828
  276.6 37.4 %collective-permute-start.12 = (bf16[2,160,2048]{2,1,0:T(8,128)(2,1)}, bf16[2,160,2048]{2,1,0:T(8,128)(2,1)}, u32[]{:S(2)}, u32[]{:S(2)}) collective-permute-start(bf16[2,160,2048]{2,1,0:T(8,128)(2,1)} %get-tuple-element.271), channel_id=1, source_target_pairs={{0,8},{4,12},{8,0},{12,4},{16,24},{20,28},{24,16},{28,20},{1,9},{5... | collective-permute-start | bytes 3932168 | tf_op jit(solution)/shard_map/ppermute | solution.py:27
  278.1 36.0 %collective-permute-start.13 = (bf16[2,160,2048]{2,1,0:T(8,128)(2,1)}, bf16[2,160,2048]{2,1,0:T(8,128)(2,1)}, u32[]{:S(2)}, u32[]{:S(2)}) collective-permute-start(bf16[2,160,2048]{2,1,0:T(8,128)(2,1)} %get-tuple-element.272), channel_id=1, source_target_pairs={{0,16},{4,20},{8,24},{12,28},{16,0},{20,4},{24,8},{28,12},{1,17},{... | collective-permute-start | bytes 3932168 | tf_op jit(solution)/shard_map/ppermute | solution.py:27
  318.0 46.9 %collective-permute-start.15 = (bf16[160,2048]{1,0:T(8,128)(2,1)S(1)}, bf16[160,2048]{1,0:T(8,128)(2,1)S(1)}, u32[]{:S(2)}, u32[]{:S(2)}) collective-permute-start(bf16[160,2048]{1,0:T(8,128)(2,1)S(1)} %dynamic-slice_bitcast_fusion.1), channel_id=1, source_target_pairs={{0,16},{4,20},{8,24},{12,28},{16,0},{20,4},{24,8},{28,12},{1,17},{... | collective-permute-start | bytes 1966088 | tf_op jit(solution)/shard_map/ppermute | solution.py:27
  319.5 45.5 %collective-permute-start.16 = (bf16[160,2048]{1,0:T(8,128)(2,1)}, bf16[160,2048]{1,0:T(8,128)(2,1)}, u32[]{:S(2)}, u32[]{:S(2)}) collective-permute-start(bf16[160,2048]{1,0:T(8,128)(2,1)} %dynamic-slice_bitcast_fusion), channel_id=1, source_target_pairs={{0,8},{4,12},{8,0},{12,4},{16,24},{20,28},{24,16},{28,20},{1,9},{5... | collective-permute-start | bytes 1966088 | tf_op jit(solution)/shard_map/ppermute | solution.py:27
  320.0 46.4 %collective-permute-start.17 = (bf16[2,128,2048]{2,1,0:T(8,128)(2,1)}, bf16[2,128,2048]{2,1,0:T(8,128)(2,1)S(1)}, u32[]{:S(2)}, u32[]{:S(2)}) collective-permute-start(bf16[2,128,2048]{2,1,0:T(8,128)(2,1)} %get-tuple-element.283), channel_id=1, source_target_pairs={{0,8},{4,12},{8,0},{12,4},{16,24},{20,28},{24,16},{28,20},{1,9},{5... | collective-permute-start | bytes 3145736 | tf_op jit(solution)/shard_map/ppermute | solution.py:27
  321.5 44.9 %collective-permute-start.18 = (bf16[2,128,2048]{2,1,0:T(8,128)(2,1)}, bf16[2,128,2048]{2,1,0:T(8,128)(2,1)S(1)}, u32[]{:S(2)}, u32[]{:S(2)}) collective-permute-start(bf16[2,128,2048]{2,1,0:T(8,128)(2,1)} %get-tuple-element.284), channel_id=1, source_target_pairs={{0,16},{4,20},{8,24},{12,28},{16,0},{20,4},{24,8},{28,12},{1,17},{... | collective-permute-start | bytes 3145736 | tf_op jit(solution)/shard_map/ppermute | solution.py:27
  377.7 6.0 %collective-permute-start.22 = (bf16[1024,1536]{1,0:T(8,128)(2,1)}, bf16[1024,1536]{1,0:T(8,128)(2,1)}, u32[]{:S(2)}, u32[]{:S(2)}) collective-permute-start(bf16[1024,1536]{1,0:T(8,128)(2,1)} %half_grads.5), channel_id=1, source_target_pairs={{0,4},{4,0},{8,12},{12,8},{16,20},{20,16},{24,28},{28,24},{1,5},{5... | collective-permute-start | bytes 9437192 | tf_op jit(solution)/shard_map/ppermute | solution.py:27
  377.7 30.6 %collective-permute-start.19 = (bf16[256,2048]{1,0:T(8,128)(2,1)}, bf16[256,2048]{1,0:T(8,128)(2,1)}, u32[]{:S(2)}, u32[]{:S(2)}) collective-permute-start(bf16[256,2048]{1,0:T(8,128)(2,1)} %slice.62), channel_id=1, source_target_pairs={{0,1},{1,2},{2,3},{3,0},{4,5},{5,6},{6,7},{7,4},{8,9},{9,10},{10,1... | collective-permute-start | bytes 3145736 | tf_op jit(solution)/shard_map/ppermute | solution.py:22
  378.2 25.8 %collective-permute-start.20 = (bf16[128,2048]{1,0:T(8,128)(2,1)}, bf16[128,2048]{1,0:T(8,128)(2,1)}, u32[]{:S(2)}, u32[]{:S(2)}) collective-permute-start(bf16[128,2048]{1,0:T(8,128)(2,1)} %dynamic-slice_bitcast_fusion.3), channel_id=1, source_target_pairs={{0,16},{4,20},{8,24},{12,28},{16,0},{20,4},{24,8},{28,12},{1,17},{... | collective-permute-start | bytes 1572872 | tf_op jit(solution)/shard_map/ppermute | solution.py:27
  378.6 26.2 %collective-permute-start.21 = (bf16[128,2048]{1,0:T(8,128)(2,1)}, bf16[128,2048]{1,0:T(8,128)(2,1)}, u32[]{:S(2)}, u32[]{:S(2)}) collective-permute-start(bf16[128,2048]{1,0:T(8,128)(2,1)} %dynamic-slice_bitcast_fusion.2), channel_id=1, source_target_pairs={{0,8},{4,12},{8,0},{12,4},{16,24},{20,28},{24,16},{28,20},{1,9},{5... | collective-permute-start | bytes 1572872 | tf_op jit(solution)/shard_map/ppermute | solution.py:27
  393.2 35.9 %collective-permute-start.24 = (bf16[2,128,1536]{2,1,0:T(8,128)(2,1)}, bf16[2,128,1536]{2,1,0:T(8,128)(2,1)}, u32[]{:S(2)}, u32[]{:S(2)}) collective-permute-start(bf16[2,128,1536]{2,1,0:T(8,128)(2,1)} %get-tuple-element.322), channel_id=1, source_target_pairs={{0,8},{4,12},{8,0},{12,4},{16,24},{20,28},{24,16},{28,20},{1,9},{5... | collective-permute-start | bytes 2359304 | tf_op jit(solution)/shard_map/ppermute | solution.py:27
  393.8 36.0 %collective-permute-start.25 = (bf16[2,128,1536]{2,1,0:T(8,128)(2,1)}, bf16[2,128,1536]{2,1,0:T(8,128)(2,1)}, u32[]{:S(2)}, u32[]{:S(2)}) collective-permute-start(bf16[2,128,1536]{2,1,0:T(8,128)(2,1)} %get-tuple-element.323), channel_id=1, source_target_pairs={{0,16},{4,20},{8,24},{12,28},{16,0},{20,4},{24,8},{28,12},{1,17},{... | collective-permute-start | bytes 2359304 | tf_op jit(solution)/shard_map/ppermute | solution.py:27
  411.2 46.2 %collective-permute-start.23 = (bf16[256,2048]{1,0:T(8,128)(2,1)}, bf16[256,2048]{1,0:T(8,128)(2,1)}, u32[]{:S(2)}, u32[]{:S(2)}) collective-permute-start(bf16[256,2048]{1,0:T(8,128)(2,1)} %add_convert_fusion.1), channel_id=1, source_target_pairs={{0,1},{1,2},{2,3},{3,0},{4,5},{5,6},{6,7},{7,4},{8,9},{9,10},{10,1... | collective-permute-start | bytes 3145736 | tf_op jit(solution)/shard_map/ppermute | solution.py:22
  414.0 45.6 %all-to-all-start.1 = ((bf16[4,64,2048]{2,1,0:T(8,128)(2,1)}), bf16[4,64,2048]{2,1,0:T(8,128)(2,1)S(1)}, u32[]{:S(2)}, u32[]{:S(2)}) async-start(bf16[4,64,2048]{2,1,0:T(8,128)(2,1)} %bitcast.39), calls=%async_computation.2 | async-start | bytes 2097152 | tf_op jit(solution)/shard_map/all_to_all | solution.py:206
  417.5 120.5 %all-gather.11.cloned.1.call-start = ((), (), s32[]{:S(2)}) async-start(), calls=%async_computation.8 | async-start | bytes 9437184 | tf_op jit(solution)/shard_map/all_gather | solution.py:828
  434.6 20.2 %collective-permute-start.26 = (bf16[128,1536]{1,0:T(8,128)(2,1)}, bf16[128,1536]{1,0:T(8,128)(2,1)S(1)}, u32[]{:S(2)}, u32[]{:S(2)}) collective-permute-start(bf16[128,1536]{1,0:T(8,128)(2,1)} %dynamic-slice_bitcast_fusion.5), channel_id=1, source_target_pairs={{0,16},{4,20},{8,24},{12,28},{16,0},{20,4},{24,8},{28,12},{1,17},{... | collective-permute-start | bytes 1179656 | tf_op jit(solution)/shard_map/ppermute | solution.py:27
  436.1 20.1 %collective-permute-start.27 = (bf16[128,1536]{1,0:T(8,128)(2,1)}, bf16[128,1536]{1,0:T(8,128)(2,1)}, u32[]{:S(2)}, u32[]{:S(2)}) collective-permute-start(bf16[128,1536]{1,0:T(8,128)(2,1)} %dynamic-slice_bitcast_fusion.4), channel_id=1, source_target_pairs={{0,8},{4,12},{8,0},{12,4},{16,24},{20,28},{24,16},{28,20},{1,9},{5... | collective-permute-start | bytes 1179656 | tf_op jit(solution)/shard_map/ppermute | solution.py:27
  490.7 25.6 %collective-permute-start.28 = (bf16[256,2048]{1,0:T(8,128)(2,1)S(1)}, bf16[256,2048]{1,0:T(8,128)(2,1)}, u32[]{:S(2)}, u32[]{:S(2)}) collective-permute-start(bf16[256,2048]{1,0:T(8,128)(2,1)S(1)} %add_convert_fusion), channel_id=1, source_target_pairs={{0,1},{1,2},{2,3},{3,0},{4,5},{5,6},{6,7},{7,4},{8,9},{9,10},{10,1... | collective-permute-start | bytes 3145736 | tf_op jit(solution)/shard_map/ppermute | solution.py:22
  493.6 36.2 %collective-permute-start.30 = (bf16[64,6144]{1,0:T(8,128)(2,1)S(1)}, bf16[64,6144]{1,0:T(8,128)(2,1)S(1)}, u32[]{:S(2)}, u32[]{:S(2)}) collective-permute-start(bf16[64,6144]{1,0:T(8,128)(2,1)S(1)} %copy-done.5), channel_id=1, source_target_pairs={{0,8},{4,12},{8,0},{12,4},{16,24},{20,28},{24,16},{28,20},{1,9},{5... | collective-permute-start | bytes 2359304 | tf_op jit(solution)/shard_map/ppermute | solution.py:27
  493.6 36.2 %collective-permute-start.31 = (bf16[64,6144]{1,0:T(8,128)(2,1)S(1)}, bf16[64,6144]{1,0:T(8,128)(2,1)S(1)}, u32[]{:S(2)}, u32[]{:S(2)}) collective-permute-start(bf16[64,6144]{1,0:T(8,128)(2,1)S(1)} %copy-done.5), channel_id=1, source_target_pairs={{0,16},{4,20},{8,24},{12,28},{16,0},{20,4},{24,8},{28,12},{1,17},{... | collective-permute-start | bytes 2359304 | tf_op jit(solution)/shard_map/ppermute | solution.py:27
  522.8 7.1 %collective-permute-start.29 = (f32[2,3072]{1,0:T(2,128)S(1)}, f32[2,3072]{1,0:T(2,128)S(1)}, u32[]{:S(2)}, u32[]{:S(2)}) collective-permute-start(f32[2,3072]{1,0:T(2,128)S(1)} %constant_dynamic-slice_fusion.5), channel_id=1, source_target_pairs={{0,2},{1,3},{2,0},{3,1},{4,6},{5,7},{6,4},{7,5},{8,10},{9,11},{10,... | collective-permute-start | bytes 73736 | tf_op jit(solution)/shard_map/ppermute | solution.py:27
  531.3 4.0 collective-permute-start.32
  531.9 16.3 %collective-permute-start.35 = (bf16[32,6144]{1,0:T(8,128)(2,1)S(1)}, bf16[32,6144]{1,0:T(8,128)(2,1)S(1)}, u32[]{:S(2)}, u32[]{:S(2)}) collective-permute-start(bf16[32,6144]{1,0:T(8,128)(2,1)S(1)} %slice.69), channel_id=1, source_target_pairs={{0,16},{4,20},{8,24},{12,28},{16,0},{20,4},{24,8},{28,12},{1,17},{... | collective-permute-start | bytes 1179656 | tf_op jit(solution)/shard_map/ppermute | solution.py:27
  533.3 15.0 %collective-permute-start.36 = (bf16[32,6144]{1,0:T(8,128)(2,1)S(1)}, bf16[32,6144]{1,0:T(8,128)(2,1)}, u32[]{:S(2)}, u32[]{:S(2)}) collective-permute-start(bf16[32,6144]{1,0:T(8,128)(2,1)S(1)} %slice.70), channel_id=1, source_target_pairs={{0,8},{4,12},{8,0},{12,4},{16,24},{20,28},{24,16},{28,20},{1,9},{5... | collective-permute-start | bytes 1179656 | tf_op jit(solution)/shard_map/ppermute | solution.py:27
  549.3 10.5 %collective-permute-start.38 = (bf16[64,6144]{1,0:T(8,128)(2,1)S(1)}, bf16[64,6144]{1,0:T(8,128)(2,1)S(1)}, u32[]{:S(2)}, u32[]{:S(2)}) collective-permute-start(bf16[64,6144]{1,0:T(8,128)(2,1)S(1)} %copy-done.5), channel_id=1, source_target_pairs={{0,4},{4,0},{8,12},{12,8},{16,20},{20,16},{24,28},{28,24},{1,5},{5... | collective-permute-start | bytes 2359304 | tf_op jit(solution)/shard_map/ppermute | solution.py:27
  549.6 10.2 %collective-permute-start.39 = (bf16[64,6144]{1,0:T(8,128)(2,1)S(1)}, bf16[64,6144]{1,0:T(8,128)(2,1)S(1)}, u32[]{:S(2)}, u32[]{:S(2)}) collective-permute-start(bf16[64,6144]{1,0:T(8,128)(2,1)S(1)} %collective-permute-done.30.refs_2_), channel_id=1, source_target_pairs={{0,4},{4,0},{8,12},{12,8},{16,20},{20,16},{24,28},{28,24},{1,5},{5... | collective-permute-start | bytes 2359304 | tf_op jit(solution)/shard_map/ppermute | solution.py:27
  549.9 9.9 %collective-permute-start.40 = (bf16[64,6144]{1,0:T(8,128)(2,1)S(1)}, bf16[64,6144]{1,0:T(8,128)(2,1)S(1)}, u32[]{:S(2)}, u32[]{:S(2)}) collective-permute-start(bf16[64,6144]{1,0:T(8,128)(2,1)S(1)} %collective-permute-done.31.refs_4_), channel_id=1, source_target_pairs={{0,4},{4,0},{8,12},{12,8},{16,20},{20,16},{24,28},{28,24},{1,5},{5... | collective-permute-start | bytes 2359304 | tf_op jit(solution)/shard_map/ppermute | solution.py:27
  550.1 9.8 %collective-permute-start.41 = (bf16[64,6144]{1,0:T(8,128)(2,1)S(1)}, bf16[64,6144]{1,0:T(8,128)(2,1)S(1)}, u32[]{:S(2)}, u32[]{:S(2)}) collective-permute-start(bf16[64,6144]{1,0:T(8,128)(2,1)S(1)} %pad_maximum_fusion.5.refs_6_), channel_id=1, source_target_pairs={{0,4},{4,0},{8,12},{12,8},{16,20},{20,16},{24,28},{28,24},{1,5},{5... | collective-permute-start | bytes 2359304 | tf_op jit(solution)/shard_map/ppermute | solution.py:27
  550.4 3.8 collective-permute-start.34
  554.2 3.8 collective-permute-start.37
  (25 other events, 178.4 us)
Sparse Core Ops, SparseCore 0:
  41.9 48.4 all-gather.4
  96.3 54.1 all-gather.6
  262.3 78.2 reduce-scatter.1
  370.4 91.5 all-gather.8
  463.8 71.0 all-gather.10

commit v6 on v5

--- a/solution.py
+++ b/solution.py
@@ -854,6 +854,7 @@
         for hop, piece in enumerate(line.step(qkv_rows, w_qkv))
     ]
     fc1_pieces = exchanged(line.step(fc1_rows, w_fc1))
+    qkv_cols = gathered(line.step(lambda *p: placed(p, place), *qkv_pieces))
     small = jnp.concatenate(
         [ln_gain, ln_bias, b_qkv, b_dense + b_fc2, positions.astype(F32)]
     ).reshape(1, -1)
@@ -868,7 +869,6 @@
 
     normed = [line.step(lambda *o: ln_forward(*o, reps, group), inputs, gain, shift)]
     normed.append(ring(line.hold(normed[0]), "shard", 1))
-    qkv_cols = gathered(line.step(lambda *p: placed(p, place), *qkv_pieces))
 
     ring_order = [(place - hop) % group for hop in range(group)]
     ring_positions = jnp.concatenate(

time: 586 us -> 579 us (0.988)
  transfers between devices with their start and end apart: 49 -> 49, of which waited for: 23 -> 24; matrix products, arithmetic and copies ran while one was open for 12% -> 13% of each run, Pallas kernels for 41% -> 41%
where the time goes in v6:
time: 579 us; the launch traced here: 571 us
  Pallas kernels  258 us (45%)
  waiting for transfers between devices  144 us (25%)
  starting transfers between devices  48.6 us (8%)
  local copies, waits for them, and re-layouts  39.4 us (7%)
  other arithmetic  33.2 us (6%)
  blocking collectives  23.7 us (4%)
  between operations  15.1 us (3%)
  matrix products  8.63 us (1%)
    ppermute x12, waiting for transfers between devices, ring(): lax.ppermute(array, axis, [(i, (i + distance) % size) for i in range(size)])  82.7 us
    ppermute x30, waiting for transfers between devices, swap(): return lax.ppermute(array, axis, [(i, i ^ mask) for i in range(size)])  54.9 us
    pallas_call x2, Pallas kernels, push(): pl.pallas_call(functools.partial(push_kernel, transposed, size), grid_spe...  37 us
    pallas_call x2, Pallas kernels, attend_back(): pl.pallas_call(functools.partial(attend_back_kernel, block), grid_spec=pl...  36.3 us
    pallas_call x3, Pallas kernels, grad_sums(): pl.pallas_call(grad_sum_kernel, grid_spec=pltpu.PrefetchScalarGridSpec(nu...  33.9 us
    pallas_call x2, Pallas kernels, attend(): pl.pallas_call(functools.partial(attend_kernel, block), grid_spec=pltpu.P...  29.1 us
    pallas_call x3, Pallas kernels, half_grads(): pl.pallas_call(grad_kernel, grid_spec=pltpu.PrefetchScalarGridSpec(num_sc...  27.1 us
    ppermute x30, starting transfers between devices, swap(): return lax.ppermute(array, axis, [(i, i ^ mask) for i in range(size)])  27.1 us
  transfers between devices with their start and end apart: 49, of which 24 were waited for; matrix products, arithmetic and copies ran while one was open for 13% of the time, Pallas kernels for 41%

profile of v6, /device:TPU:0, one launch (start us, length us, event | category | flops | bytes accessed | tf_op | source)
XLA Modules:
  0.0 570.8 jit_solution(14012411545683687680)
XLA Ops:
  8.6 3.1 collective-permute-start
  11.7 2.7 collective-permute-start.1
  19.5 7.6 %collective-permute-done.1.refs_2_ = bf16[64,1536]{1,0:T(8,128)(2,1)S(1)} collective-permute-done((bf16[64,1536]{1,0:T(8,128)(2,1)S(1)}, bf16[64,1536]{1,0:T(8,128)(2,1)S(1)}, u32[]{:S(2)}, u32[]{:S(2)}) %collective-permute-start.1) | collective-permute-done | bytes 196640 | tf_op jit(solution)/shard_map/ppermute | solution.py:22
  30.2 4.7 collective-permute-start.3
  38.4 4.3 all-to-all-start
  44.0 3.2 ln_forward.1
  57.6 2.5 concatenate.75
  60.2 2.5 concatenate.76
  62.6 22.1 %collective-permute-done.5 = bf16[256,2048]{1,0:T(8,128)(2,1)} collective-permute-done((bf16[256,2048]{1,0:T(8,128)(2,1)}, bf16[256,2048]{1,0:T(8,128)(2,1)}, u32[]{:S(2)}, u32[]{:S(2)}) %collective-permute-start.5) | collective-permute-done | bytes 1048608 | tf_op jit(solution)/shard_map/ppermute | solution.py:22
  84.7 4.7 all-to-all-done
  91.9 23.8 %collective-permute-done.6 = bf16[256,2048]{1,0:T(8,128)(2,1)S(1)} collective-permute-done((bf16[256,2048]{1,0:T(8,128)(2,1)}, bf16[256,2048]{1,0:T(8,128)(2,1)S(1)}, u32[]{:S(2)}, u32[]{:S(2)}) %collective-permute-start.6) | collective-permute-done | bytes 1048608 | tf_op jit(solution)/shard_map/ppermute | solution.py:22
  117.4 9.5 %project.2.refs_0_ = f32[1024,1536]{1,0:T(8,128)} custom-call(bf16[1024,2048]{1,0:T(8,128)(2,1)} %constant_dynamic-update-slice_fusion.11.rows_ref, bf16[2048,1536]{1,0:T(8,128)(2,1)} %all-gather.5.cloned.1.call-done.weight_ref.b_ref, f32[1,1536]{1,0:T(1,128)} %bitcast.105), custom_call_target="tpu_custom_call" | custom-call | tf_op jit(solution)/shard_map/project/pallas_call | solution.py:564
  126.8 13.8 %collective-permute-done.7 = bf16[256,2048]{1,0:T(8,128)(2,1)S(1)} collective-permute-done((bf16[256,2048]{1,0:T(8,128)(2,1)S(1)}, bf16[256,2048]{1,0:T(8,128)(2,1)S(1)}, u32[]{:S(2)}, u32[]{:S(2)}) %collective-permute-start.7) | collective-permute-done | bytes 1048608 | tf_op jit(solution)/shard_map/ppermute | solution.py:22
  142.5 6.1 %project.3.q_ref.k_ref.v_ref = f32[1024,1536]{1,0:T(8,128)} custom-call(bf16[1024,2048]{1,0:T(8,128)(2,1)} %constant_dynamic-update-slice_fusion.10.rows_ref.left_ref, bf16[2048,1536]{1,0:T(8,128)(2,1)} %all-gather.5.cloned.1.call-done.weight_ref.b_ref, f32[1,1536]{1,0:T(1,128)} %bitcast.106, ...), custom_call_target="tpu_custom_call", output_to_operand_aliasing={{}: (3, {})} | custom-call | tf_op jit(solution)/shard_map/project/pallas_call | solution.py:564
  148.6 14.5 %attend.2 = (bf16[1024,512]{1,0:T(8,128)(2,1)}, bf16[1,4,2560,256]{3,2,1,0:T(8,128)(2,1)}, bf16[3,1024,256]{2,1,0:T(8,128)(2,1)}) custom-call(s32[1]{0:T(128)} %bitcast.place_ref, f32[1024,1536]{1,0:T(8,128)} %project.3.q_ref.k_ref.v_ref, f32[1024,1536]{1,0:T(8,128)} %project.3.q_ref.k_ref.v_ref, f32[1024,1536]{1,0:T(8,128)} %project.3.q_ref.k_ref.v_ref, ...), custom_call_target="tpu_custom_call" | custom-call | tf_op jit(solution)/shard_map/attend/pallas_call | solution.py:637
  166.0 18.4 %feed_forward.1 = (bf16[1024,2048]{1,0:T(8,128)(2,1)}, bf16[1024,2048]{1,0:T(8,128)(2,1)}) custom-call(bf16[1024,2048]{1,0:T(8,128)(2,1)} %constant_dynamic-update-slice_fusion.10.rows_ref.left_ref, bf16[2048,2048]{1,0:T(8,128)(2,1)} %all-gather.7.cloned.1.call-done.weight_ref.d_ref, f32[1,2048]{1,0:T(1,128)} %bitcast.111), custom_call_target="tpu_custom_call" | custom-call | tf_op jit(solution)/shard_map/feed_forward/pallas_call | solution.py:787
  184.4 3.7 collective-permute-done.9
  189.5 14.5 %attend.3 = (bf16[1024,512]{1,0:T(8,128)(2,1)}, bf16[1,4,2560,256]{3,2,1,0:T(8,128)(2,1)}, bf16[3,1024,256]{2,1,0:T(8,128)(2,1)}) custom-call(s32[1]{0:T(128)} %bitcast.place_ref, f32[1024,1536]{1,0:T(8,128)} %project.3.q_ref.k_ref.v_ref, f32[1024,1536]{1,0:T(8,128)} %project.3.q_ref.k_ref.v_ref, ...), custom_call_target="tpu_custom_call", output_to_operand_aliasing={{0}: (6, {})} | custom-call | tf_op jit(solution)/shard_map/attend/pallas_call | solution.py:637
  204.0 15.8 %push.2 = bf16[1024,2048]{1,0:T(8,128)(2,1)} custom-call(s32[1]{0:T(128)} %bitcast.place_ref, bf16[1024,512]{1,0:T(8,128)(2,1)} %get-tuple-element.268.a_ref.refs_0_, bf16[512,2048]{1,0:T(8,128)(2,1)} %b_ref, bf16[1024,2048]{1,0:T(8,128)(2,1)} %get-tuple-element.266.c_ref.left_ref, bf16[2048,2048]{1,0:T(8,128)(2,1)} %weight_ref), custom_call_target="tpu_custom_call" | custom-call | tf_op jit(solution)/shard_map/push/pallas_call | solution.py:541
  220.8 10.9 %half_grads.3 = bf16[1280,2048]{1,0:T(8,128)(2,1)} custom-call(s32[1]{0:T(128)} %bitcast.13.which_ref, bf16[1024,2048]{1,0:T(8,128)(2,1)} %get-tuple-element.266.c_ref.left_ref, bf16[1024,2048]{1,0:T(8,128)(2,1)} %constant_dynamic-update-slice_fusion.7.right_ref.cot_ref, bf16[1024,512]{1,0:T(8,128)(2,1)} %get-tuple-element.268.a_ref.refs_0_), custom_call_target="tpu_custom_call" | custom-call | tf_op jit(solution)/shard_map/half_grads/pallas_call | solution.py:408
  231.7 14.4 %pull.1.right_ref.c_ref = bf16[1024,2048]{1,0:T(8,128)(2,1)} custom-call(bf16[1024,2048]{1,0:T(8,128)(2,1)} %constant_dynamic-update-slice_fusion.7.right_ref.cot_ref, bf16[2048,2048]{1,0:T(8,128)(2,1)} %weight_ref, bf16[1024,2048]{1,0:T(8,128)(2,1)} %get-tuple-element.263.refs_0_), custom_call_target="tpu_custom_call" | custom-call | tf_op jit(solution)/shard_map/pull/pallas_call | solution.py:504
  246.1 8.7 %half_grads.4 = bf16[1024,2048]{1,0:T(8,128)(2,1)} custom-call(s32[1]{0:T(128)} %bitcast.13.which_ref, bf16[1024,2048]{1,0:T(8,128)(2,1)} %constant_dynamic-update-slice_fusion.10.rows_ref.left_ref, bf16[1024,2048]{1,0:T(8,128)(2,1)} %pull.1.right_ref.c_ref), custom_call_target="tpu_custom_call" | custom-call | tf_op jit(solution)/shard_map/half_grads/pallas_call | solution.py:408
  256.2 13.6 %grad_sums.3 = (bf16[1280,2048]{1,0:T(8,128)(2,1)}, bf16[2,160,2048]{2,1,0:T(8,128)(2,1)}, bf16[2,160,2048]{2,1,0:T(8,128)(2,1)}) custom-call(s32[3]{0:T(128)} %pad_add_fusion.at_ref, bf16[1024,2048]{1,0:T(8,128)(2,1)} %get-tuple-element.266.c_ref.left_ref, bf16[1024,2048]{1,0:T(8,128)(2,1)} %constant_dynamic-update-slice_fusion.7.right_ref.cot_ref, ...), custom_call_target="tpu_custom_call" | custom-call | tf_op jit(solution)/shard_map/grad_sums/pallas_call | solution.py:350
  272.8 5.6 convolution_convert_fusion.datt_ref
  278.3 18.0 %attend_back.2 = (bf16[1024,1536]{1,0:T(8,128)(2,1)}, f32[1,1,1536]{2,1,0:T(1,128)}) custom-call(s32[1]{0:T(128)} %bitcast.place_ref, bf16[1,4,2560,256]{3,2,1,0:T(8,128)(2,1)} %get-tuple-element.233.prob_ref, bf16[3,1024,256]{2,1,0:T(8,128)(2,1)} %get-tuple-element.234.low_ref, bf16[1024,512]{1,0:T(8,128)(2,1)} %convolution_convert_fusion.datt_ref, ...), custom_call_target="tpu_custom_call" | custom-call | tf_op jit(solution)/shard_map/attend_back/pallas_call | solution.py:722
  296.4 10.9 %grad_sums.4 = (bf16[1024,2048]{1,0:T(8,128)(2,1)}, bf16[2,128,2048]{2,1,0:T(8,128)(2,1)}, bf16[2,128,2048]{2,1,0:T(8,128)(2,1)}) custom-call(s32[3]{0:T(128)} %pad_add_fusion.at_ref, bf16[1024,2048]{1,0:T(8,128)(2,1)} %constant_dynamic-update-slice_fusion.10.rows_ref.left_ref, bf16[1024,2048]{1,0:T(8,128)(2,1)} %pull.1.right_ref.c_ref, ...), custom_call_target="tpu_custom_call" | custom-call | tf_op jit(solution)/shard_map/grad_sums/pallas_call | solution.py:350
  307.3 3.8 fusion
  316.2 18.3 %attend_back.3 = (bf16[1024,1536]{1,0:T(8,128)(2,1)}, f32[1,1,1536]{2,1,0:T(1,128)}) custom-call(s32[1]{0:T(128)} %bitcast.place_ref, bf16[1,4,2560,256]{3,2,1,0:T(8,128)(2,1)} %get-tuple-element.249.prob_ref, bf16[3,1024,256]{2,1,0:T(8,128)(2,1)} %get-tuple-element.250.low_ref, ...), custom_call_target="tpu_custom_call", output_to_operand_aliasing={{0}: (5, {}), {1}: (6, {})} | custom-call | tf_op jit(solution)/shard_map/attend_back/pallas_call | solution.py:722
  334.5 21.2 %push.3 = bf16[1024,2048]{1,0:T(8,128)(2,1)} custom-call(s32[1]{0:T(128)} %bitcast.place_ref, bf16[1024,1536]{1,0:T(8,128)(2,1)} %get-tuple-element.319.a_ref.right_ref, bf16[2048,1536]{1,0:T(8,128)(2,1)} %all-gather.5.cloned.1.call-done.weight_ref.b_ref, bf16[1024,2048]{1,0:T(8,128)(2,1)} %pull.1.right_ref.c_ref, ...), custom_call_target="tpu_custom_call" | custom-call | tf_op jit(solution)/shard_map/push/pallas_call | solution.py:541
  363.5 7.5 %half_grads.5 = bf16[1024,1536]{1,0:T(8,128)(2,1)} custom-call(s32[1]{0:T(128)} %bitcast.13.which_ref, bf16[1024,2048]{1,0:T(8,128)(2,1)} %constant_dynamic-update-slice_fusion.10.rows_ref.left_ref, bf16[1024,1536]{1,0:T(8,128)(2,1)} %get-tuple-element.319.a_ref.right_ref), custom_call_target="tpu_custom_call" | custom-call | tf_op jit(solution)/shard_map/half_grads/pallas_call | solution.py:408
  372.3 3.1 convert_add_fusion.4
  376.9 9.5 %grad_sums.5 = (bf16[1024,1536]{1,0:T(8,128)(2,1)}, bf16[2,128,1536]{2,1,0:T(8,128)(2,1)}, bf16[2,128,1536]{2,1,0:T(8,128)(2,1)}) custom-call(s32[3]{0:T(128)} %pad_add_fusion.at_ref, bf16[1024,2048]{1,0:T(8,128)(2,1)} %constant_dynamic-update-slice_fusion.10.rows_ref.left_ref, bf16[1024,1536]{1,0:T(8,128)(2,1)} %get-tuple-element.319.a_ref.right_ref, ...), custom_call_target="tpu_custom_call" | custom-call | tf_op jit(solution)/shard_map/grad_sums/pallas_call | solution.py:350
  388.2 9.0 %collective-permute-done.20 = bf16[128,2048]{1,0:T(8,128)(2,1)} collective-permute-done((bf16[128,2048]{1,0:T(8,128)(2,1)}, bf16[128,2048]{1,0:T(8,128)(2,1)}, u32[]{:S(2)}, u32[]{:S(2)}) %collective-permute-start.20) | collective-permute-done | bytes 524320 | tf_op jit(solution)/shard_map/ppermute | solution.py:27
  401.5 2.9 add_convert_fusion.1
  404.4 2.8 collective-permute-start.23
  407.2 3.5 all-to-all-start.1
  410.8 11.5 %collective-permute-done.24 = bf16[2,128,1536]{2,1,0:T(8,128)(2,1)} collective-permute-done((bf16[2,128,1536]{2,1,0:T(8,128)(2,1)}, bf16[2,128,1536]{2,1,0:T(8,128)(2,1)}, u32[]{:S(2)}, u32[]{:S(2)}) %collective-permute-start.24) | collective-permute-done | bytes 786464 | tf_op jit(solution)/shard_map/ppermute | solution.py:27
  430.2 3.1 fusion.14
  433.3 14.7 %collective-permute-done.26 = bf16[128,1536]{1,0:T(8,128)(2,1)S(1)} collective-permute-done((bf16[128,1536]{1,0:T(8,128)(2,1)}, bf16[128,1536]{1,0:T(8,128)(2,1)S(1)}, u32[]{:S(2)}, u32[]{:S(2)}) %collective-permute-start.26) | collective-permute-done | bytes 393248 | tf_op jit(solution)/shard_map/ppermute | solution.py:27
  456.1 23.7 %all_to_all.36 = bf16[4,64,1536]{2,1,0:T(8,128)(2,1)} all-to-all(bf16[4,64,1536]{2,1,0:T(8,128)(2,1)S(1)} %bitcast.93), channel_id=1, replica_groups=mesh['rep'=8,'shard'=4] {'shard'}, dimensions={0} | all-to-all | bytes 1572864 | tf_op jit(solution)/shard_map/all_to_all | solution.py:206
  484.2 2.6 slice.78.a_ref
  488.3 12.1 %split_rows.2 = (f32[2048,2048]{1,0:T(8,128)}, f32[512,2048]{1,0:T(8,128)}) custom-call(bf16[2560,2048]{1,0:T(8,128)(2,1)} %all-gather.9.cloned.1.call-done.in_ref), custom_call_target="tpu_custom_call" | custom-call | tf_op jit(solution)/shard_map/split_rows/pallas_call | solution.py:238
  500.4 9.2 %collective-permute-done.28.b_ref = bf16[256,2048]{1,0:T(8,128)(2,1)} collective-permute-done((bf16[256,2048]{1,0:T(8,128)(2,1)S(1)}, bf16[256,2048]{1,0:T(8,128)(2,1)}, u32[]{:S(2)}, u32[]{:S(2)}) %collective-permute-start.28) | collective-permute-done | bytes 1048608 | tf_op jit(solution)/shard_map/ppermute | solution.py:22
  509.6 5.5 ln_backward.1
  516.1 6.9 %collective-permute-done.30.refs_2_ = bf16[64,6144]{1,0:T(8,128)(2,1)S(1)} collective-permute-done((bf16[64,6144]{1,0:T(8,128)(2,1)S(1)}, bf16[64,6144]{1,0:T(8,128)(2,1)S(1)}, u32[]{:S(2)}, u32[]{:S(2)}) %collective-permute-start.30) | collective-permute-done | bytes 786464 | tf_op jit(solution)/shard_map/ppermute | solution.py:27
  531.4 10.3 %split_rows.3 = f32[512,8192]{1,0:T(8,128)} custom-call(bf16[512,8192]{1,0:T(8,128)(2,1)} %all-gather.11.cloned.1.call-done.in_ref), custom_call_target="tpu_custom_call" | custom-call | tf_op jit(solution)/shard_map/split_rows/pallas_call | solution.py:238
  548.9 2.5 collective-permute-done.37
  554.9 8.4 %assemble.1 = f32[512,6144]{1,0:T(8,128)} custom-call(s32[1]{0:T(128)} %bitcast.45.rep_ref, bf16[64,6144]{1,0:T(8,128)(2,1)} %widened.3.refs_0_, bf16[64,6144]{1,0:T(8,128)(2,1)} %copy-done.14, bf16[64,6144]{1,0:T(8,128)(2,1)} %copy-done.11, bf16[64,6144]{1,0:T(8,128)(2,1)} %copy-done.15, bf16[64,6144]{1,0:T(8,128)(2,1)} %copy-done.12, ...), custom_call_target="tpu_custom_call" | custom-call | tf_op jit(solution)/shard_map/assemble/pallas_call | solution.py:286
  (247 shorter events, 104.2 us)
Async XLA Ops:
  7.2 110.2 %all-gather.5.cloned.1.call-start = ((), (), s32[]{:S(2)}) async-start(), calls=%async_computation.4 | async-start | bytes 7077888 | tf_op jit(solution)/shard_map/all_gather | solution.py:828
  8.6 10.9 %collective-permute-start = (bf16[64,1536]{1,0:T(8,128)(2,1)S(1)}, bf16[64,1536]{1,0:T(8,128)(2,1)S(1)}, u32[]{:S(2)}, u32[]{:S(2)}) collective-permute-start(bf16[64,1536]{1,0:T(8,128)(2,1)S(1)} %pad_maximum_fusion.7), channel_id=1, source_target_pairs={{0,1},{1,2},{2,3},{3,0},{4,5},{5,6},{6,7},{7,4},{8,9},{9,10},{10,1... | collective-permute-start | bytes 589832 | tf_op jit(solution)/shard_map/ppermute | solution.py:22
  11.7 15.4 %collective-permute-start.1 = (bf16[64,1536]{1,0:T(8,128)(2,1)S(1)}, bf16[64,1536]{1,0:T(8,128)(2,1)S(1)}, u32[]{:S(2)}, u32[]{:S(2)}) collective-permute-start(bf16[64,1536]{1,0:T(8,128)(2,1)S(1)} %pad_maximum_fusion.8), channel_id=1, source_target_pairs={{0,2},{1,3},{2,0},{3,1},{4,6},{5,7},{6,4},{7,5},{8,10},{9,11},{10,... | collective-permute-start | bytes 589832 | tf_op jit(solution)/shard_map/ppermute | solution.py:22
  14.4 12.8 %collective-permute-start.2 = (bf16[64,1536]{1,0:T(8,128)(2,1)S(1)}, bf16[64,1536]{1,0:T(8,128)(2,1)S(1)}, u32[]{:S(2)}, u32[]{:S(2)}) collective-permute-start(bf16[64,1536]{1,0:T(8,128)(2,1)S(1)} %pad_maximum_fusion.9), channel_id=1, source_target_pairs={{0,3},{1,0},{2,1},{3,2},{4,7},{5,4},{6,5},{7,6},{8,11},{9,8},{10,9... | collective-permute-start | bytes 589832 | tf_op jit(solution)/shard_map/ppermute | solution.py:22
  30.2 6.4 %collective-permute-start.3 = (f32[1,3328]{1,0:T(1,128)S(1)}, f32[1,3328]{1,0:T(1,128)S(1)}, u32[]{:S(2)}, u32[]{:S(2)}) collective-permute-start(f32[1,3328]{1,0:T(1,128)S(1)} %reshape.180), channel_id=1, source_target_pairs={{0,1},{1,0},{2,3},{3,2},{4,5},{5,4},{6,7},{7,6},{8,9},{9,8},{10,11... | collective-permute-start | bytes 39944 | tf_op jit(solution)/shard_map/ppermute | solution.py:27
  36.6 6.1 %collective-permute-start.4 = (f32[2,3328]{1,0:T(2,128)S(1)}, f32[2,3328]{1,0:T(2,128)S(1)}, u32[]{:S(2)}, u32[]{:S(2)}) collective-permute-start(f32[2,3328]{1,0:T(2,128)S(1)} %pad_maximum_fusion.10), channel_id=1, source_target_pairs={{0,2},{1,3},{2,0},{3,1},{4,6},{5,7},{6,4},{7,5},{8,10},{9,11},{10,... | collective-permute-start | bytes 79880 | tf_op jit(solution)/shard_map/ppermute | solution.py:27
  38.4 51.0 %all-to-all-start = ((bf16[4,64,2048]{2,1,0:T(8,128)(2,1)}), bf16[4,64,2048]{2,1,0:T(8,128)(2,1)}, u32[]{:S(2)}, u32[]{:S(2)}) async-start(bf16[4,64,2048]{2,1,0:T(8,128)(2,1)} %bitcast.10), calls=%async_computation | async-start | bytes 2097152 | tf_op jit(solution)/shard_map/all_to_all | solution.py:206
  42.7 123.3 %all-gather.7.cloned.1.call-start = ((), (), s32[]{:S(2)}) async-start(), calls=%async_computation.5 | async-start | bytes 9437184 | tf_op jit(solution)/shard_map/all_gather | solution.py:828
  47.2 37.5 %collective-permute-start.5 = (bf16[256,2048]{1,0:T(8,128)(2,1)}, bf16[256,2048]{1,0:T(8,128)(2,1)}, u32[]{:S(2)}, u32[]{:S(2)}) collective-permute-start(bf16[256,2048]{1,0:T(8,128)(2,1)} %ln_forward.1), channel_id=1, source_target_pairs={{0,1},{1,2},{2,3},{3,0},{4,5},{5,6},{6,7},{7,4},{8,9},{9,10},{10,1... | collective-permute-start | bytes 3145736 | tf_op jit(solution)/shard_map/ppermute | solution.py:22
  89.4 282.9 %reduce-scatter.2.cloned.1.call-start = ((), (), s32[]{:S(2)}) async-start(), calls=%async_computation.6 | async-start | bytes 5242880 | tf_op jit(solution)/shard_map/reduce_scatter | solution.py:971
  89.5 26.2 %collective-permute-start.6 = (bf16[256,2048]{1,0:T(8,128)(2,1)}, bf16[256,2048]{1,0:T(8,128)(2,1)S(1)}, u32[]{:S(2)}, u32[]{:S(2)}) collective-permute-start(bf16[256,2048]{1,0:T(8,128)(2,1)} %collective-permute-done.5), channel_id=1, source_target_pairs={{0,1},{1,2},{2,3},{3,0},{4,5},{5,6},{6,7},{7,4},{8,9},{9,10},{10,1... | collective-permute-start | bytes 3145736 | tf_op jit(solution)/shard_map/ppermute | solution.py:22
  115.6 25.0 %collective-permute-start.7 = (bf16[256,2048]{1,0:T(8,128)(2,1)S(1)}, bf16[256,2048]{1,0:T(8,128)(2,1)S(1)}, u32[]{:S(2)}, u32[]{:S(2)}) collective-permute-start(bf16[256,2048]{1,0:T(8,128)(2,1)S(1)} %collective-permute-done.6), channel_id=1, source_target_pairs={{0,1},{1,2},{2,3},{3,0},{4,5},{5,6},{6,7},{7,4},{8,9},{9,10},{10,1... | collective-permute-start | bytes 3145736 | tf_op jit(solution)/shard_map/ppermute | solution.py:22
  140.6 24.3 %collective-permute-start.8 = (bf16[256,2048]{1,0:T(8,128)(2,1)S(1)}, bf16[256,2048]{1,0:T(8,128)(2,1)S(1)}, u32[]{:S(2)}, u32[]{:S(2)}) collective-permute-start(bf16[256,2048]{1,0:T(8,128)(2,1)S(1)} %copy-done.1), channel_id=1, source_target_pairs={{0,1},{1,2},{2,3},{3,0},{4,5},{5,6},{6,7},{7,4},{8,9},{9,10},{10,1... | collective-permute-start | bytes 3145736 | tf_op jit(solution)/shard_map/ppermute | solution.py:22
  164.9 23.1 %collective-permute-start.9 = (bf16[256,2048]{1,0:T(8,128)(2,1)S(1)}, bf16[256,2048]{1,0:T(8,128)(2,1)S(1)}, u32[]{:S(2)}, u32[]{:S(2)}) collective-permute-start(bf16[256,2048]{1,0:T(8,128)(2,1)S(1)} %collective-permute-done.8), channel_id=1, source_target_pairs={{0,1},{1,2},{2,3},{3,0},{4,5},{5,6},{6,7},{7,4},{8,9},{9,10},{10,1... | collective-permute-start | bytes 3145736 | tf_op jit(solution)/shard_map/ppermute | solution.py:22
  188.1 31.7 %collective-permute-start.10 = (bf16[256,2048]{1,0:T(8,128)(2,1)S(1)}, bf16[256,2048]{1,0:T(8,128)(2,1)S(1)}, u32[]{:S(2)}, u32[]{:S(2)}) collective-permute-start(bf16[256,2048]{1,0:T(8,128)(2,1)S(1)} %collective-permute-done.9), channel_id=1, source_target_pairs={{0,1},{1,2},{2,3},{3,0},{4,5},{5,6},{6,7},{7,4},{8,9},{9,10},{10,1... | collective-permute-start | bytes 3145736 | tf_op jit(solution)/shard_map/ppermute | solution.py:22
  231.7 24.5 %collective-permute-start.11 = (bf16[1280,2048]{1,0:T(8,128)(2,1)}, bf16[1280,2048]{1,0:T(8,128)(2,1)}, u32[]{:S(2)}, u32[]{:S(2)}) collective-permute-start(bf16[1280,2048]{1,0:T(8,128)(2,1)} %half_grads.3), channel_id=1, source_target_pairs={{0,4},{4,0},{8,12},{12,8},{16,20},{20,16},{24,28},{28,24},{1,5},{5... | collective-permute-start | bytes 15728648 | tf_op jit(solution)/shard_map/ppermute | solution.py:27
  254.8 41.5 %collective-permute-start.14 = (bf16[1024,2048]{1,0:T(8,128)(2,1)}, bf16[1024,2048]{1,0:T(8,128)(2,1)}, u32[]{:S(2)}, u32[]{:S(2)}) collective-permute-start(bf16[1024,2048]{1,0:T(8,128)(2,1)} %half_grads.4), channel_id=1, source_target_pairs={{0,4},{4,0},{8,12},{12,8},{16,20},{20,16},{24,28},{28,24},{1,5},{5... | collective-permute-start | bytes 12582920 | tf_op jit(solution)/shard_map/ppermute | solution.py:27
  255.4 232.9 %all-gather.9.cloned.1.call-start = ((), (), s32[]{:S(2)}) async-start(), calls=%async_computation.7 | async-start | bytes 11796480 | tf_op jit(solution)/shard_map/all_gather | solution.py:828
  269.8 37.5 %collective-permute-start.12 = (bf16[2,160,2048]{2,1,0:T(8,128)(2,1)}, bf16[2,160,2048]{2,1,0:T(8,128)(2,1)}, u32[]{:S(2)}, u32[]{:S(2)}) collective-permute-start(bf16[2,160,2048]{2,1,0:T(8,128)(2,1)} %get-tuple-element.271), channel_id=1, source_target_pairs={{0,8},{4,12},{8,0},{12,4},{16,24},{20,28},{24,16},{28,20},{1,9},{5... | collective-permute-start | bytes 3932168 | tf_op jit(solution)/shard_map/ppermute | solution.py:27
  271.3 36.0 %collective-permute-start.13 = (bf16[2,160,2048]{2,1,0:T(8,128)(2,1)}, bf16[2,160,2048]{2,1,0:T(8,128)(2,1)}, u32[]{:S(2)}, u32[]{:S(2)}) collective-permute-start(bf16[2,160,2048]{2,1,0:T(8,128)(2,1)} %get-tuple-element.272), channel_id=1, source_target_pairs={{0,16},{4,20},{8,24},{12,28},{16,0},{20,4},{24,8},{28,12},{1,17},{... | collective-permute-start | bytes 3932168 | tf_op jit(solution)/shard_map/ppermute | solution.py:27
  311.2 47.0 %collective-permute-start.15 = (bf16[160,2048]{1,0:T(8,128)(2,1)S(1)}, bf16[160,2048]{1,0:T(8,128)(2,1)S(1)}, u32[]{:S(2)}, u32[]{:S(2)}) collective-permute-start(bf16[160,2048]{1,0:T(8,128)(2,1)S(1)} %dynamic-slice_bitcast_fusion.1), channel_id=1, source_target_pairs={{0,16},{4,20},{8,24},{12,28},{16,0},{20,4},{24,8},{28,12},{1,17},{... | collective-permute-start | bytes 1966088 | tf_op jit(solution)/shard_map/ppermute | solution.py:27
  312.6 45.5 %collective-permute-start.16 = (bf16[160,2048]{1,0:T(8,128)(2,1)}, bf16[160,2048]{1,0:T(8,128)(2,1)}, u32[]{:S(2)}, u32[]{:S(2)}) collective-permute-start(bf16[160,2048]{1,0:T(8,128)(2,1)} %dynamic-slice_bitcast_fusion), channel_id=1, source_target_pairs={{0,8},{4,12},{8,0},{12,4},{16,24},{20,28},{24,16},{28,20},{1,9},{5... | collective-permute-start | bytes 1966088 | tf_op jit(solution)/shard_map/ppermute | solution.py:27
  313.2 46.4 %collective-permute-start.17 = (bf16[2,128,2048]{2,1,0:T(8,128)(2,1)}, bf16[2,128,2048]{2,1,0:T(8,128)(2,1)S(1)}, u32[]{:S(2)}, u32[]{:S(2)}) collective-permute-start(bf16[2,128,2048]{2,1,0:T(8,128)(2,1)} %get-tuple-element.283), channel_id=1, source_target_pairs={{0,8},{4,12},{8,0},{12,4},{16,24},{20,28},{24,16},{28,20},{1,9},{5... | collective-permute-start | bytes 3145736 | tf_op jit(solution)/shard_map/ppermute | solution.py:27
  314.6 45.0 %collective-permute-start.18 = (bf16[2,128,2048]{2,1,0:T(8,128)(2,1)}, bf16[2,128,2048]{2,1,0:T(8,128)(2,1)S(1)}, u32[]{:S(2)}, u32[]{:S(2)}) collective-permute-start(bf16[2,128,2048]{2,1,0:T(8,128)(2,1)} %get-tuple-element.284), channel_id=1, source_target_pairs={{0,16},{4,20},{8,24},{12,28},{16,0},{20,4},{24,8},{28,12},{1,17},{... | collective-permute-start | bytes 3145736 | tf_op jit(solution)/shard_map/ppermute | solution.py:27
  370.9 6.0 %collective-permute-start.22 = (bf16[1024,1536]{1,0:T(8,128)(2,1)}, bf16[1024,1536]{1,0:T(8,128)(2,1)}, u32[]{:S(2)}, u32[]{:S(2)}) collective-permute-start(bf16[1024,1536]{1,0:T(8,128)(2,1)} %half_grads.5), channel_id=1, source_target_pairs={{0,4},{4,0},{8,12},{12,8},{16,20},{20,16},{24,28},{28,24},{1,5},{5... | collective-permute-start | bytes 9437192 | tf_op jit(solution)/shard_map/ppermute | solution.py:27
  370.9 30.6 %collective-permute-start.19 = (bf16[256,2048]{1,0:T(8,128)(2,1)}, bf16[256,2048]{1,0:T(8,128)(2,1)}, u32[]{:S(2)}, u32[]{:S(2)}) collective-permute-start(bf16[256,2048]{1,0:T(8,128)(2,1)} %slice.62), channel_id=1, source_target_pairs={{0,1},{1,2},{2,3},{3,0},{4,5},{5,6},{6,7},{7,4},{8,9},{9,10},{10,1... | collective-permute-start | bytes 3145736 | tf_op jit(solution)/shard_map/ppermute | solution.py:22
  371.4 25.8 %collective-permute-start.20 = (bf16[128,2048]{1,0:T(8,128)(2,1)}, bf16[128,2048]{1,0:T(8,128)(2,1)}, u32[]{:S(2)}, u32[]{:S(2)}) collective-permute-start(bf16[128,2048]{1,0:T(8,128)(2,1)} %dynamic-slice_bitcast_fusion.3), channel_id=1, source_target_pairs={{0,16},{4,20},{8,24},{12,28},{16,0},{20,4},{24,8},{28,12},{1,17},{... | collective-permute-start | bytes 1572872 | tf_op jit(solution)/shard_map/ppermute | solution.py:27
  371.9 26.2 %collective-permute-start.21 = (bf16[128,2048]{1,0:T(8,128)(2,1)}, bf16[128,2048]{1,0:T(8,128)(2,1)}, u32[]{:S(2)}, u32[]{:S(2)}) collective-permute-start(bf16[128,2048]{1,0:T(8,128)(2,1)} %dynamic-slice_bitcast_fusion.2), channel_id=1, source_target_pairs={{0,8},{4,12},{8,0},{12,4},{16,24},{20,28},{24,16},{28,20},{1,9},{5... | collective-permute-start | bytes 1572872 | tf_op jit(solution)/shard_map/ppermute | solution.py:27
  386.4 35.9 %collective-permute-start.24 = (bf16[2,128,1536]{2,1,0:T(8,128)(2,1)}, bf16[2,128,1536]{2,1,0:T(8,128)(2,1)}, u32[]{:S(2)}, u32[]{:S(2)}) collective-permute-start(bf16[2,128,1536]{2,1,0:T(8,128)(2,1)} %get-tuple-element.322), channel_id=1, source_target_pairs={{0,8},{4,12},{8,0},{12,4},{16,24},{20,28},{24,16},{28,20},{1,9},{5... | collective-permute-start | bytes 2359304 | tf_op jit(solution)/shard_map/ppermute | solution.py:27
  387.0 36.0 %collective-permute-start.25 = (bf16[2,128,1536]{2,1,0:T(8,128)(2,1)}, bf16[2,128,1536]{2,1,0:T(8,128)(2,1)}, u32[]{:S(2)}, u32[]{:S(2)}) collective-permute-start(bf16[2,128,1536]{2,1,0:T(8,128)(2,1)} %get-tuple-element.323), channel_id=1, source_target_pairs={{0,16},{4,20},{8,24},{12,28},{16,0},{20,4},{24,8},{28,12},{1,17},{... | collective-permute-start | bytes 2359304 | tf_op jit(solution)/shard_map/ppermute | solution.py:27
  404.4 46.2 %collective-permute-start.23 = (bf16[256,2048]{1,0:T(8,128)(2,1)}, bf16[256,2048]{1,0:T(8,128)(2,1)}, u32[]{:S(2)}, u32[]{:S(2)}) collective-permute-start(bf16[256,2048]{1,0:T(8,128)(2,1)} %add_convert_fusion.1), channel_id=1, source_target_pairs={{0,1},{1,2},{2,3},{3,0},{4,5},{5,6},{6,7},{7,4},{8,9},{9,10},{10,1... | collective-permute-start | bytes 3145736 | tf_op jit(solution)/shard_map/ppermute | solution.py:22
  407.2 45.5 %all-to-all-start.1 = ((bf16[4,64,2048]{2,1,0:T(8,128)(2,1)}), bf16[4,64,2048]{2,1,0:T(8,128)(2,1)S(1)}, u32[]{:S(2)}, u32[]{:S(2)}) async-start(bf16[4,64,2048]{2,1,0:T(8,128)(2,1)} %bitcast.39), calls=%async_computation.2 | async-start | bytes 2097152 | tf_op jit(solution)/shard_map/all_to_all | solution.py:206
  410.8 120.6 %all-gather.11.cloned.1.call-start = ((), (), s32[]{:S(2)}) async-start(), calls=%async_computation.8 | async-start | bytes 9437184 | tf_op jit(solution)/shard_map/all_gather | solution.py:828
  427.8 20.2 %collective-permute-start.26 = (bf16[128,1536]{1,0:T(8,128)(2,1)}, bf16[128,1536]{1,0:T(8,128)(2,1)S(1)}, u32[]{:S(2)}, u32[]{:S(2)}) collective-permute-start(bf16[128,1536]{1,0:T(8,128)(2,1)} %dynamic-slice_bitcast_fusion.5), channel_id=1, source_target_pairs={{0,16},{4,20},{8,24},{12,28},{16,0},{20,4},{24,8},{28,12},{1,17},{... | collective-permute-start | bytes 1179656 | tf_op jit(solution)/shard_map/ppermute | solution.py:27
  429.4 20.0 %collective-permute-start.27 = (bf16[128,1536]{1,0:T(8,128)(2,1)}, bf16[128,1536]{1,0:T(8,128)(2,1)}, u32[]{:S(2)}, u32[]{:S(2)}) collective-permute-start(bf16[128,1536]{1,0:T(8,128)(2,1)} %dynamic-slice_bitcast_fusion.4), channel_id=1, source_target_pairs={{0,8},{4,12},{8,0},{12,4},{16,24},{20,28},{24,16},{28,20},{1,9},{5... | collective-permute-start | bytes 1179656 | tf_op jit(solution)/shard_map/ppermute | solution.py:27
  483.9 25.6 %collective-permute-start.28 = (bf16[256,2048]{1,0:T(8,128)(2,1)S(1)}, bf16[256,2048]{1,0:T(8,128)(2,1)}, u32[]{:S(2)}, u32[]{:S(2)}) collective-permute-start(bf16[256,2048]{1,0:T(8,128)(2,1)S(1)} %add_convert_fusion), channel_id=1, source_target_pairs={{0,1},{1,2},{2,3},{3,0},{4,5},{5,6},{6,7},{7,4},{8,9},{9,10},{10,1... | collective-permute-start | bytes 3145736 | tf_op jit(solution)/shard_map/ppermute | solution.py:22
  486.8 36.2 %collective-permute-start.30 = (bf16[64,6144]{1,0:T(8,128)(2,1)S(1)}, bf16[64,6144]{1,0:T(8,128)(2,1)S(1)}, u32[]{:S(2)}, u32[]{:S(2)}) collective-permute-start(bf16[64,6144]{1,0:T(8,128)(2,1)S(1)} %copy-done.6), channel_id=1, source_target_pairs={{0,8},{4,12},{8,0},{12,4},{16,24},{20,28},{24,16},{28,20},{1,9},{5... | collective-permute-start | bytes 2359304 | tf_op jit(solution)/shard_map/ppermute | solution.py:27
  486.9 36.2 %collective-permute-start.31 = (bf16[64,6144]{1,0:T(8,128)(2,1)S(1)}, bf16[64,6144]{1,0:T(8,128)(2,1)S(1)}, u32[]{:S(2)}, u32[]{:S(2)}) collective-permute-start(bf16[64,6144]{1,0:T(8,128)(2,1)S(1)} %copy-done.6), channel_id=1, source_target_pairs={{0,16},{4,20},{8,24},{12,28},{16,0},{20,4},{24,8},{28,12},{1,17},{... | collective-permute-start | bytes 2359304 | tf_op jit(solution)/shard_map/ppermute | solution.py:27
  516.0 7.3 %collective-permute-start.29 = (f32[2,3072]{1,0:T(2,128)S(1)}, f32[2,3072]{1,0:T(2,128)S(1)}, u32[]{:S(2)}, u32[]{:S(2)}) collective-permute-start(f32[2,3072]{1,0:T(2,128)S(1)} %constant_dynamic-slice_fusion.5), channel_id=1, source_target_pairs={{0,2},{1,3},{2,0},{3,1},{4,6},{5,7},{6,4},{7,5},{8,10},{9,11},{10,... | collective-permute-start | bytes 73736 | tf_op jit(solution)/shard_map/ppermute | solution.py:27
  524.7 4.0 collective-permute-start.32
  525.2 16.5 %collective-permute-start.35 = (bf16[32,6144]{1,0:T(8,128)(2,1)S(1)}, bf16[32,6144]{1,0:T(8,128)(2,1)S(1)}, u32[]{:S(2)}, u32[]{:S(2)}) collective-permute-start(bf16[32,6144]{1,0:T(8,128)(2,1)S(1)} %slice.69), channel_id=1, source_target_pairs={{0,16},{4,20},{8,24},{12,28},{16,0},{20,4},{24,8},{28,12},{1,17},{... | collective-permute-start | bytes 1179656 | tf_op jit(solution)/shard_map/ppermute | solution.py:27
  526.5 15.1 %collective-permute-start.36 = (bf16[32,6144]{1,0:T(8,128)(2,1)S(1)}, bf16[32,6144]{1,0:T(8,128)(2,1)}, u32[]{:S(2)}, u32[]{:S(2)}) collective-permute-start(bf16[32,6144]{1,0:T(8,128)(2,1)S(1)} %slice.70), channel_id=1, source_target_pairs={{0,8},{4,12},{8,0},{12,4},{16,24},{20,28},{24,16},{28,20},{1,9},{5... | collective-permute-start | bytes 1179656 | tf_op jit(solution)/shard_map/ppermute | solution.py:27
  542.7 10.5 %collective-permute-start.38 = (bf16[64,6144]{1,0:T(8,128)(2,1)S(1)}, bf16[64,6144]{1,0:T(8,128)(2,1)S(1)}, u32[]{:S(2)}, u32[]{:S(2)}) collective-permute-start(bf16[64,6144]{1,0:T(8,128)(2,1)S(1)} %copy-done.6), channel_id=1, source_target_pairs={{0,4},{4,0},{8,12},{12,8},{16,20},{20,16},{24,28},{28,24},{1,5},{5... | collective-permute-start | bytes 2359304 | tf_op jit(solution)/shard_map/ppermute | solution.py:27
  543.0 10.2 %collective-permute-start.39 = (bf16[64,6144]{1,0:T(8,128)(2,1)S(1)}, bf16[64,6144]{1,0:T(8,128)(2,1)S(1)}, u32[]{:S(2)}, u32[]{:S(2)}) collective-permute-start(bf16[64,6144]{1,0:T(8,128)(2,1)S(1)} %collective-permute-done.30.refs_2_), channel_id=1, source_target_pairs={{0,4},{4,0},{8,12},{12,8},{16,20},{20,16},{24,28},{28,24},{1,5},{5... | collective-permute-start | bytes 2359304 | tf_op jit(solution)/shard_map/ppermute | solution.py:27
  543.3 9.9 %collective-permute-start.40 = (bf16[64,6144]{1,0:T(8,128)(2,1)S(1)}, bf16[64,6144]{1,0:T(8,128)(2,1)S(1)}, u32[]{:S(2)}, u32[]{:S(2)}) collective-permute-start(bf16[64,6144]{1,0:T(8,128)(2,1)S(1)} %collective-permute-done.31.refs_4_), channel_id=1, source_target_pairs={{0,4},{4,0},{8,12},{12,8},{16,20},{20,16},{24,28},{28,24},{1,5},{5... | collective-permute-start | bytes 2359304 | tf_op jit(solution)/shard_map/ppermute | solution.py:27
  543.5 9.8 %collective-permute-start.41 = (bf16[64,6144]{1,0:T(8,128)(2,1)S(1)}, bf16[64,6144]{1,0:T(8,128)(2,1)S(1)}, u32[]{:S(2)}, u32[]{:S(2)}) collective-permute-start(bf16[64,6144]{1,0:T(8,128)(2,1)S(1)} %pad_maximum_fusion.5.refs_6_), channel_id=1, source_target_pairs={{0,4},{4,0},{8,12},{12,8},{16,20},{20,16},{24,28},{28,24},{1,5},{5... | collective-permute-start | bytes 2359304 | tf_op jit(solution)/shard_map/ppermute | solution.py:27
  543.8 3.8 collective-permute-start.34
  547.6 3.8 collective-permute-start.37
  (32 other events, 257.3 us)
Sparse Core Ops, SparseCore 0:
  30.2 48.8 all-gather.4
  89.5 52.5 all-gather.6
  255.5 78.1 reduce-scatter.1
  363.6 91.5 all-gather.8
  457.1 71.0 all-gather.10
